TPU v7x, 32 devices: a whole 2x2x4 slice. The times are simulated.
32 devices in a mesh: dp: 4 (over y, core), mp: 8 (over z, x).
Axes of the slice: x: 2, y: 2, z: 4, core: 2. Of those that a mesh axis runs over, the one named last changes fastest.
Arguments:
- frames: bfloat16 [16384, 768], P(('dp', 'mp')), may hold values from -6 to 6
- seg_ids: int32 [32, 512], P('dp'), may hold values from 0 to 3, never falling along the last dimension, each value on 1 to 384 neighbouring positions
- text: bfloat16 [128, 77, 768], P(('dp', 'mp')), may hold values from -6 to 6
- text_lens: int32 [128], P('dp'), may hold values from 1 to 77, as said below
- step_ids: int32 [128], P('dp'), may hold values from 0 to 999
- step_table: bfloat16 [1000, 768], P(None, 'mp'), may hold values from -6 to 6
- ada_weight: bfloat16 [768, 4608], P('mp'), may hold values from -0.21875 to 0.21875
- ada_bias: bfloat16 [4608], replicated, may hold values from -3 to 3
- query_w: bfloat16 [768, 768], P(None, 'mp'), may hold values from -0.21875 to 0.21875
- key_w: bfloat16 [768, 768], P(None, 'mp'), may hold values from -0.21875 to 0.21875
- value_w: bfloat16 [768, 768], P(None, 'mp'), may hold values from -0.21875 to 0.21875
- out_w: bfloat16 [768, 768], P('mp'), may hold values from -1.25 to 1.25
- cross_query_w: bfloat16 [768, 768], P(None, 'mp'), may hold values from -0.21875 to 0.21875
- cross_key_w: bfloat16 [768, 768], P(None, 'mp'), may hold values from -0.21875 to 0.21875
- cross_value_w: bfloat16 [768, 768], P(None, 'mp'), may hold values from -0.21875 to 0.21875
- cross_out_w: bfloat16 [768, 768], P('mp'), may hold values from -1.25 to 1.25
- up_weight: bfloat16 [768, 3072], P(None, 'mp'), may hold values from -0.21875 to 0.21875
- down_weight: bfloat16 [3072, 768], P('mp'), may hold values from -0.21875 to 0.21875
- out_grad: bfloat16 [16384, 768], P(('dp', 'mp')), may hold values from -6 to 6
Outputs:
- layer_out: bfloat16 [16384, 768], P(('dp', 'mp'))
- grad_frames: float32 [16384, 768], P(('dp', 'mp'))
- grad_text: float32 [128, 77, 768], P(('dp', 'mp'))
- grad_step_table: float32 [1000, 768], P(None, 'mp')
- grad_ada_weight: float32 [768, 4608], P('mp')
- grad_ada_bias: float32 [4608], replicated
- grad_query_w: float32 [768, 768], P(None, 'mp')
- grad_key_w: float32 [768, 768], P(None, 'mp')
- grad_value_w: float32 [768, 768], P(None, 'mp')
- grad_out_w: float32 [768, 768], P('mp')
- grad_cross_query_w: float32 [768, 768], P(None, 'mp')
- grad_cross_key_w: float32 [768, 768], P(None, 'mp')
- grad_cross_value_w: float32 [768, 768], P(None, 'mp')
- grad_cross_out_w: float32 [768, 768], P('mp')
- grad_up_weight: float32 [768, 3072], P(None, 'mp')
- grad_down_weight: float32 [3072, 768], P('mp')
Inputs may be any that keep to these rules, and one draw needn't show every extreme that they name: `seg_ids`: within a row the clip number never falls, each of the 4 numbers appears, no clip has more than 384 frames and some clip in each row has exactly 384. A caption's first text_lens tokens are real; its other rows are padding that no frame attends to.
All inputs are finite; a program needn't handle non-finite values.
Results may differ from a plain program's by a relative error of at most 0.022.
Values may be sent and summed in bfloat16 or wider, within the bound.
No kernel may reach another device: no remote copies, remote signals or barrier semaphores. Data moves between devices by JAX's collectives and lax.ppermute only.
A program may use at most 320 MiB of HBM per device.

v0:
```python
from functools import partial

import jax
import jax.numpy as jnp
from jax import lax
from jax.sharding import PartitionSpec as P

HEADS = 12
HD = 64
CAPTION = 77
SEGS = 4
GROUP = 4


highest = lax.Precision.HIGHEST
epsilon = 1e-06
masked_score = -1e30


def swapped(block, axis, stride):
    count = lax.axis_size(axis)
    route = []
    for low in range(count):
        high = low | 1 << stride
        if high != low and high < count:
            route += [(low, high), (high, low)]
    return lax.ppermute(block, axis, route)


def from_behind(value, axis, steps):
    count = lax.axis_size(axis)
    pairs = [(source, (source + steps) % count) for source in range(count)]
    return lax.ppermute(value, axis, pairs)


def normalize(values):
    centre = values - jnp.mean(values, axis=-1, keepdims=True)
    inverse = lax.rsqrt(jnp.mean(centre * centre, axis=-1, keepdims=True) + epsilon)
    return (centre * inverse, inverse)


def norm_back(normed, inverse, upstream):
    mean_grad = jnp.mean(upstream, axis=-1, keepdims=True)
    mean_both = jnp.mean(upstream * normed, axis=-1, keepdims=True)
    return inverse * (upstream - mean_grad - normed * mean_both)


def matmul(left, right):
    return jnp.dot(left, right, preferred_element_type=jnp.float32)


def inner_rows(left, right):
    return lax.dot_general(
        left, right, (((0,), (0,)), ((), ())), preferred_element_type=jnp.float32
    )


def outer_cols(left, right):
    return lax.dot_general(
        left, right, (((1,), (1,)), ((), ())), preferred_element_type=jnp.float32
    )


def gelu_back(pre_act, upstream):
    return jax.vjp(partial(jax.nn.gelu, approximate=True), pre_act)[1](upstream)[0]


def silu_back(inputs, upstream):
    return jax.vjp(jax.nn.silu, inputs)[1](upstream)[0]


def head_cols(block, head):
    return block[:, head * HD : (head + 1) * HD]


def attend_rows(query, keys, values, allowed, score_scale):
    head_count = query.shape[2] // HD

    def one_row(block_item):
        row_query, row_keys, row_values, row_allowed = block_item
        mixed_parts = []
        total_parts = []
        for head in range(head_count):
            scores = outer_cols(head_cols(row_query, head), head_cols(row_keys, head)) * score_scale
            scores = jnp.where(row_allowed, scores, masked_score)
            highest_score = jnp.max(scores, axis=-1, keepdims=True)
            shifted = jnp.exp(scores - highest_score)
            row_total = jnp.sum(shifted, axis=-1, keepdims=True)
            weights = (shifted / row_total).astype(jnp.bfloat16)
            mixed_parts.append(matmul(weights, head_cols(row_values, head)).astype(jnp.bfloat16))
            total_parts.append((highest_score + jnp.log(row_total))[:, 0])
        return (jnp.concatenate(mixed_parts, axis=1), jnp.stack(total_parts))

    return lax.map(one_row, (query, keys, values, allowed))


def attend_back(query, keys, values, allowed, score_scale, log_total, grad_mix):
    head_count = query.shape[2] // HD

    def one_row(block_item):
        row_query, row_keys, row_values, row_allowed, row_total, row_grad = block_item
        query_parts = []
        key_parts = []
        value_parts = []
        for head in range(head_count):
            head_query = head_cols(row_query, head)
            head_keys = head_cols(row_keys, head)
            head_grad = head_cols(row_grad, head)
            scores = outer_cols(head_query, head_keys) * score_scale
            scores = jnp.where(row_allowed, scores, masked_score)
            weights = jnp.exp(scores - row_total[head][:, None])
            value_parts.append(
                inner_rows(weights.astype(jnp.bfloat16), head_grad).astype(jnp.bfloat16)
            )
            grad_weights = outer_cols(head_grad, head_cols(row_values, head))
            grad_scores = (
                weights * (grad_weights - jnp.sum(weights * grad_weights, axis=-1, keepdims=True))
            ).astype(jnp.bfloat16)
            query_parts.append((matmul(grad_scores, head_keys) * score_scale).astype(jnp.bfloat16))
            key_parts.append(
                (inner_rows(grad_scores, head_query) * score_scale).astype(jnp.bfloat16)
            )
        return (
            jnp.concatenate(query_parts, axis=1),
            jnp.concatenate(key_parts, axis=1),
            jnp.concatenate(value_parts, axis=1),
        )

    return lax.map(one_row, (query, keys, values, allowed, log_total, grad_mix))


def collect_bits(stacked, offset, group_span):
    for bit in range(group_span.bit_length() - 1):
        other = swapped(stacked, "mp", bit)
        upper = offset >> bit & 1 == 1
        stacked = jnp.where(
            upper, jnp.concatenate([other, stacked], 0), jnp.concatenate([stacked, other], 0)
        )
    return stacked


def reduce_bits(stacked, offset, group_span):
    for bit in reversed(range(group_span.bit_length() - 1)):
        half_count = stacked.shape[0] // 2
        lower_half = stacked[:half_count]
        upper_half = stacked[half_count:]
        upper = offset >> bit & 1 == 1
        keeping = jnp.where(upper, upper_half, lower_half)
        sending = jnp.where(upper, lower_half, upper_half)
        stacked = keeping + swapped(sending.astype(jnp.bfloat16), "mp", bit).astype(sending.dtype)
    return stacked[0]


def group_rows(piece_rows, member, group_span):
    pieces = [piece_rows]
    for stride in range(1, GROUP):
        pieces.append(from_behind(piece_rows, "mp", stride * group_span))
    order = (member - jnp.arange(GROUP)) % GROUP
    return jnp.take(jnp.stack(pieces), order, axis=0)


def group_sums(partial_sum, member, group_span):
    running = lax.dynamic_index_in_dim(partial_sum, member, 0, keepdims=False)
    for stride in range(1, GROUP):
        sending = lax.dynamic_index_in_dim(
            partial_sum, (member + stride) % GROUP, 0, keepdims=False
        )
        running = running + from_behind(sending, "mp", stride * group_span)
    return running


def shards(
    frames,
    seg_ids,
    text,
    text_lens,
    step_ids,
    step_table,
    ada_weight,
    ada_bias,
    query_w,
    key_w,
    value_w,
    out_w,
    cross_query_w,
    cross_key_w,
    cross_value_w,
    cross_out_w,
    up_weight,
    down_weight,
    out_grad,
):
    model_width = frames.shape[1]
    axis_count = lax.axis_size("mp")
    group_span = axis_count // GROUP
    position = lax.axis_index("mp")
    member = position // group_span
    offset = position % group_span
    rows_dev = seg_ids.shape[0] // axis_count
    frames_row = seg_ids.shape[1]
    tok_dev = rows_dev * frames_row
    segs_dev = rows_dev * SEGS
    text_rows = segs_dev * CAPTION
    score_scale = HD ** (-0.5)
    my_ids = lax.dynamic_slice_in_dim(seg_ids, position * rows_dev, rows_dev, 0)
    choose_step = (step_ids[:, None] == jnp.arange(step_table.shape[0])[None, :]).astype(
        jnp.float32
    )
    cond_cols = jnp.dot(choose_step, step_table.astype(jnp.float32), precision=highest)
    silu_cols = jax.nn.silu(cond_cols).astype(jnp.bfloat16)
    modulation = lax.psum_scatter(
        matmul(silu_cols, ada_weight), "mp", scatter_dimension=0, tiled=True
    ) + ada_bias.astype(jnp.float32)
    chooser = (my_ids[:, :, None] == jnp.arange(SEGS)[None, None, :]).astype(jnp.float32)
    mod_rows = modulation.reshape(rows_dev, SEGS, 6 * model_width)
    per_frame = jnp.zeros((rows_dev, frames_row, 6 * model_width), jnp.float32)
    for segment in range(SEGS):
        per_frame = (
            per_frame + chooser[:, :, segment : segment + 1] * mod_rows[:, segment : segment + 1, :]
        )
    shift_one, scale_one, gate_one, shift_two, scale_two, gate_two = jnp.split(
        per_frame.reshape(tok_dev, 6 * model_width), 6, axis=1
    )
    heads_here = HEADS // GROUP
    column_stack = jnp.stack(
        [query_w, key_w, value_w, out_w.T, cross_query_w, cross_key_w, cross_value_w, cross_out_w.T]
    )[None]
    collected = collect_bits(column_stack, offset, group_span)
    gathered_cols = jnp.moveaxis(collected, 0, 2).reshape(8, model_width, -1)
    query_heads, key_heads, value_heads = (gathered_cols[0], gathered_cols[1], gathered_cols[2])
    out_heads = gathered_cols[3].T
    cquery_heads, ckey_heads, cvalue_heads = (gathered_cols[4], gathered_cols[5], gathered_cols[6])
    cout_heads = gathered_cols[7].T
    ids_rows = lax.dynamic_index_in_dim(
        seg_ids.reshape(GROUP, group_span, rows_dev, frames_row), offset, 1, keepdims=False
    ).reshape(GROUP * rows_dev, frames_row)
    lens_rows = lax.dynamic_index_in_dim(
        text_lens.reshape(GROUP, group_span, segs_dev), offset, 1, keepdims=False
    )

    def bring(piece_rows):
        return group_rows(piece_rows, member, group_span)

    def settle(partial_sum):
        return group_sums(partial_sum, member, group_span)

    rows_here = ids_rows.shape[0]
    head_width = heads_here * HD
    head_shape = (rows_here, frames_row, head_width)
    text_shape = (rows_here, SEGS * CAPTION, head_width)
    base = frames.astype(jnp.float32)
    normed_one, inverse_one = normalize(base)
    first_in = (normed_one * (1.0 + scale_one) + shift_one).astype(jnp.bfloat16)
    packed = bring(jnp.concatenate([first_in, text.reshape(text_rows, model_width)], axis=0))
    first_group = packed[:, :tok_dev].reshape(-1, model_width)
    text_group = packed[:, tok_dev:].reshape(-1, model_width)
    query = matmul(first_group, query_heads).astype(jnp.bfloat16).reshape(head_shape)
    keys = matmul(first_group, key_heads).astype(jnp.bfloat16).reshape(head_shape)
    values = matmul(first_group, value_heads).astype(jnp.bfloat16).reshape(head_shape)
    same_seg = ids_rows[:, :, None] == ids_rows[:, None, :]
    self_mix, self_total = attend_rows(query, keys, values, same_seg, score_scale)
    self_flat = self_mix.reshape(-1, head_width)
    self_out = settle(matmul(self_flat, out_heads).reshape(-1, tok_dev, model_width))
    resid_one = base + gate_one * self_out
    normed_two, inverse_two = normalize(resid_one)
    second_in = normed_two.astype(jnp.bfloat16)
    second_group = bring(second_in).reshape(-1, model_width)
    cross_query = matmul(second_group, cquery_heads).astype(jnp.bfloat16).reshape(head_shape)
    cross_keys = matmul(text_group, ckey_heads).astype(jnp.bfloat16).reshape(text_shape)
    cross_values = matmul(text_group, cvalue_heads).astype(jnp.bfloat16).reshape(text_shape)
    key_segment = jnp.arange(SEGS * CAPTION) // CAPTION
    valid_key = (jnp.arange(CAPTION)[None, None, :] < lens_rows[:, :, None]).reshape(
        rows_here, SEGS * CAPTION
    )
    allowed = (ids_rows[:, :, None] == key_segment[None, None, :]) & valid_key[:, None, :]
    cross_mix, cross_total = attend_rows(
        cross_query, cross_keys, cross_values, allowed, score_scale
    )
    cross_flat = cross_mix.reshape(-1, head_width)
    cross_out = settle(matmul(cross_flat, cout_heads).reshape(-1, tok_dev, model_width))
    resid_two = resid_one + cross_out
    normed_three, inverse_three = normalize(resid_two)
    third_in = (normed_three * (1.0 + scale_two) + shift_two).astype(jnp.bfloat16)
    third_all = lax.all_gather(third_in, "mp", axis=0, tiled=True)
    pre_act = matmul(third_all, up_weight)
    activated = jax.nn.gelu(pre_act, approximate=True).astype(jnp.bfloat16)
    mlp_out = lax.psum_scatter(
        matmul(activated, down_weight).astype(jnp.bfloat16), "mp", scatter_dimension=0, tiled=True
    ).astype(jnp.float32)
    layer_out = (resid_two + gate_two * mlp_out).astype(jnp.bfloat16)
    upstream = out_grad.astype(jnp.float32)
    grad_gate_two = upstream * mlp_out
    grad_mlp = (gate_two * upstream).astype(jnp.bfloat16)
    received = lax.all_gather(grad_mlp, "mp", axis=0, tiled=True)
    grad_rows = gelu_back(pre_act, outer_cols(received, down_weight)).astype(jnp.bfloat16)
    grad_down = inner_rows(activated, received)
    grad_up = inner_rows(third_all, grad_rows)
    grad_third = lax.psum_scatter(
        outer_cols(grad_rows, up_weight), "mp", scatter_dimension=0, tiled=True
    )
    grad_resid_two = upstream + norm_back(
        normed_three, inverse_three, grad_third * (1.0 + scale_two)
    )
    grad_cross = grad_resid_two.astype(jnp.bfloat16)
    grad_cross_group = bring(grad_cross).reshape(-1, model_width)
    grad_cout = inner_rows(cross_flat, grad_cross_group)
    grad_cross_mix = (
        outer_cols(grad_cross_group, cout_heads).astype(jnp.bfloat16).reshape(head_shape)
    )
    grad_cq, grad_ck, grad_cv = attend_back(
        cross_query, cross_keys, cross_values, allowed, score_scale, cross_total, grad_cross_mix
    )
    grad_cq = grad_cq.reshape(-1, head_width)
    grad_ck = grad_ck.reshape(-1, head_width)
    grad_cv = grad_cv.reshape(-1, head_width)
    grad_cquery = inner_rows(second_group, grad_cq)
    grad_ckey = inner_rows(text_group, grad_ck)
    grad_cvalue = inner_rows(text_group, grad_cv)
    grad_second_part = outer_cols(grad_cq, cquery_heads).reshape(-1, tok_dev, model_width)
    grad_text_part = (outer_cols(grad_ck, ckey_heads) + outer_cols(grad_cv, cvalue_heads)).reshape(
        -1, text_rows, model_width
    )
    settled = settle(jnp.concatenate([grad_second_part, grad_text_part], axis=1))
    grad_second = settled[:tok_dev]
    grad_text = settled[tok_dev:].reshape(segs_dev, CAPTION, model_width)
    grad_resid_one = grad_resid_two + norm_back(normed_two, inverse_two, grad_second)
    grad_gate_one = grad_resid_one * self_out
    grad_self = (gate_one * grad_resid_one).astype(jnp.bfloat16)
    grad_self_group = bring(grad_self).reshape(-1, model_width)
    grad_outp = inner_rows(self_flat, grad_self_group)
    grad_self_mix = outer_cols(grad_self_group, out_heads).astype(jnp.bfloat16).reshape(head_shape)
    grad_sq, grad_sk, grad_sv = attend_back(
        query, keys, values, same_seg, score_scale, self_total, grad_self_mix
    )
    grad_sq = grad_sq.reshape(-1, head_width)
    grad_sk = grad_sk.reshape(-1, head_width)
    grad_sv = grad_sv.reshape(-1, head_width)
    grad_query = inner_rows(first_group, grad_sq)
    grad_key = inner_rows(first_group, grad_sk)
    grad_value = inner_rows(first_group, grad_sv)
    grad_first_part = (
        outer_cols(grad_sq, query_heads)
        + outer_cols(grad_sk, key_heads)
        + outer_cols(grad_sv, value_heads)
    )
    grad_first = settle(grad_first_part.reshape(-1, tok_dev, model_width))
    grad_frames = grad_resid_one + norm_back(
        normed_one, inverse_one, grad_first * (1.0 + scale_one)
    )
    grad_frame_mod = jnp.concatenate(
        [
            grad_first,
            grad_first * normed_one,
            grad_gate_one,
            grad_third,
            grad_third * normed_three,
            grad_gate_two,
        ],
        axis=1,
    )
    grad_mod_mine = jnp.einsum(
        "rsk,rsc->rkc",
        chooser,
        grad_frame_mod.reshape(rows_dev, frames_row, 6 * model_width),
        precision=highest,
    ).reshape(segs_dev, 6 * model_width)
    grad_mod_all = lax.all_gather(
        grad_mod_mine.astype(jnp.bfloat16), "mp", axis=0, tiled=True
    ).astype(grad_mod_mine.dtype)
    grad_ada_w = lax.dot_general(
        silu_cols.astype(jnp.float32), grad_mod_all, (((0,), (0,)), ((), ())), precision=highest
    )
    grad_ada_b = jnp.sum(grad_mod_all, axis=0)
    grad_silu = lax.dot_general(
        grad_mod_all, ada_weight.astype(jnp.float32), (((1,), (1,)), ((), ())), precision=highest
    )
    grad_cond = silu_back(cond_cols, grad_silu)
    grad_table = lax.dot_general(
        choose_step, grad_cond, (((0,), (0,)), ((), ())), precision=highest
    )
    head_grads = jnp.stack(
        [
            grad_query,
            grad_key,
            grad_value,
            grad_outp.T,
            grad_cquery,
            grad_ckey,
            grad_cvalue,
            grad_cout.T,
        ]
    )
    spread_out = jnp.moveaxis(head_grads.reshape(8, model_width, group_span, -1), 2, 0)
    reduced = reduce_bits(spread_out, offset, group_span)
    shard_query, shard_key, shard_value = (reduced[0], reduced[1], reduced[2])
    shard_out = reduced[3].T
    shard_cquery, shard_ckey, shard_cvalue = (reduced[4], reduced[5], reduced[6])
    shard_cout = reduced[7].T
    shard_up, shard_down = (grad_up, grad_down)
    summed = (
        lax.psum(grad_table.astype(jnp.bfloat16), "dp").astype(jnp.float32),
        lax.psum(grad_ada_w.astype(jnp.bfloat16), "dp").astype(jnp.float32),
        lax.psum(grad_ada_b.astype(jnp.bfloat16), "dp").astype(jnp.float32),
        lax.psum(shard_query.astype(jnp.bfloat16), "dp").astype(jnp.float32),
        lax.psum(shard_key.astype(jnp.bfloat16), "dp").astype(jnp.float32),
        lax.psum(shard_value.astype(jnp.bfloat16), "dp").astype(jnp.float32),
        lax.psum(shard_out.astype(jnp.bfloat16), "dp").astype(jnp.float32),
        lax.psum(shard_cquery.astype(jnp.bfloat16), "dp").astype(jnp.float32),
        lax.psum(shard_ckey.astype(jnp.bfloat16), "dp").astype(jnp.float32),
        lax.psum(shard_cvalue.astype(jnp.bfloat16), "dp").astype(jnp.float32),
        lax.psum(shard_cout.astype(jnp.bfloat16), "dp").astype(jnp.float32),
        lax.psum(shard_up.astype(jnp.bfloat16), "dp").astype(jnp.float32),
        lax.psum(shard_down.astype(jnp.bfloat16), "dp").astype(jnp.float32),
    )
    return (
        layer_out,
        grad_frames,
        grad_text,
        summed[0],
        summed[1],
        summed[2],
        summed[3],
        summed[4],
        summed[5],
        summed[6],
        summed[7],
        summed[8],
        summed[9],
        summed[10],
        summed[11],
        summed[12],
    )


def solution(mesh):
    return jax.shard_map(
        shards,
        mesh=mesh,
        in_specs=(
            P(("dp", "mp"), None),
            P("dp", None),
            P(("dp", "mp"), None, None),
            P("dp"),
            P("dp"),
            P(None, "mp"),
            P("mp", None),
            P(),
            P(None, "mp"),
            P(None, "mp"),
            P(None, "mp"),
            P("mp", None),
            P(None, "mp"),
            P(None, "mp"),
            P(None, "mp"),
            P("mp", None),
            P(None, "mp"),
            P("mp", None),
            P(("dp", "mp"), None),
        ),
        out_specs=(
            P(("dp", "mp"), None),
            P(("dp", "mp"), None),
            P(("dp", "mp"), None, None),
            P(None, "mp"),
            P("mp", None),
            P(),
            P(None, "mp"),
            P(None, "mp"),
            P(None, "mp"),
            P("mp", None),
            P(None, "mp"),
            P(None, "mp"),
            P(None, "mp"),
            P("mp", None),
            P(None, "mp"),
            P("mp", None),
        ),
        check_vma=False,
    )
```

profile of v0, /device:TPU:0, one launch (start us, length us, event | category | flops | bytes accessed | tf_op | source)
XLA Modules:
  0.0 2013.7 jit_solution(15626463957406197515)
XLA Ops:
  22.7 67.4 %all-reduce.5.cloned.1.call-done = f32[32,4608]{1,0:T(8,128)} async-done(((f32[32,4608]{1,0:T(8,128)}), f32[32,4608]{1,0:T(8,128)}) %all-reduce.5.cloned.1.call-update) | async-done | bytes 589840
  110.3 73.7 %collective-permute-done.1 = bf16[820,768]{1,0:T(8,128)(2,1)} collective-permute-done((bf16[820,768]{1,0:T(8,128)(2,1)}, bf16[820,768]{1,0:T(8,128)(2,1)}, u32[]{:S(2)}, u32[]{:S(2)}) %collective-permute-start.1) | collective-permute-done | bytes 1259552 | tf_op jit(solution)/shard_map/ppermute | solution.py:33
  215.0 18.2 while.52
  240.3 26.9 %collective-permute-start.4 = (f32[512,768]{1,0:T(8,128)}, f32[512,768]{1,0:T(8,128)S(1)}, u32[]{:S(2)}, u32[]{:S(2)}) collective-permute-start(f32[512,768]{1,0:T(8,128)} %get-tuple-element.516), channel_id=1, source_target_pairs={{0,2},{1,3},{2,4},{3,5},{4,6},{5,7},{6,0},{7,1},{8,10},{9,11},{10,... | collective-permute-start | bytes 4718600 | tf_op jit(solution)/shard_map/ppermute | solution.py:33
  276.1 26.2 %collective-permute-done.4 = f32[512,768]{1,0:T(8,128)S(1)} collective-permute-done((f32[512,768]{1,0:T(8,128)}, f32[512,768]{1,0:T(8,128)S(1)}, u32[]{:S(2)}, u32[]{:S(2)}) %collective-permute-start.4) | collective-permute-done | bytes 1572896 | tf_op jit(solution)/shard_map/ppermute | solution.py:33
  302.3 33.7 %collective-permute-done.6 = f32[512,768]{1,0:T(8,128)} collective-permute-done((f32[512,768]{1,0:T(8,128)}, f32[512,768]{1,0:T(8,128)}, u32[]{:S(2)}, u32[]{:S(2)}) %collective-permute-start.6) | collective-permute-done | bytes 1572896 | tf_op jit(solution)/shard_map/ppermute | solution.py:33
  336.1 42.3 %collective-permute-done.5 = f32[512,768]{1,0:T(8,128)} collective-permute-done((f32[512,768]{1,0:T(8,128)}, f32[512,768]{1,0:T(8,128)}, u32[]{:S(2)}, u32[]{:S(2)}) %collective-permute-start.5) | collective-permute-done | bytes 1572896 | tf_op jit(solution)/shard_map/ppermute | solution.py:33
  384.8 45.3 %collective-permute-start.7 = (bf16[512,768]{1,0:T(8,128)(2,1)}, bf16[512,768]{1,0:T(8,128)(2,1)}, u32[]{:S(2)}, u32[]{:S(2)}) collective-permute-start(bf16[512,768]{1,0:T(8,128)(2,1)} %fusion.172), channel_id=1, source_target_pairs={{0,2},{1,3},{2,4},{3,5},{4,6},{5,7},{6,0},{7,1},{8,10},{9,11},{10,... | collective-permute-start | bytes 2359304 | tf_op jit(solution)/shard_map/ppermute | solution.py:33
  444.3 21.0 %collective-permute-done.7 = bf16[512,768]{1,0:T(8,128)(2,1)} collective-permute-done((bf16[512,768]{1,0:T(8,128)(2,1)}, bf16[512,768]{1,0:T(8,128)(2,1)}, u32[]{:S(2)}, u32[]{:S(2)}) %collective-permute-start.7) | collective-permute-done | bytes 786464 | tf_op jit(solution)/shard_map/ppermute | solution.py:33
  482.0 20.0 while.53
  504.5 15.5 collective-permute-start.10
  523.3 33.3 %collective-permute-done.10 = f32[512,768]{1,0:T(8,128)S(1)} collective-permute-done((f32[512,768]{1,0:T(8,128)S(1)}, f32[512,768]{1,0:T(8,128)S(1)}, u32[]{:S(2)}, u32[]{:S(2)}) %collective-permute-start.10) | collective-permute-done | bytes 1572896 | tf_op jit(solution)/shard_map/ppermute | solution.py:33
  556.6 32.0 %collective-permute-done.12 = f32[512,768]{1,0:T(8,128)S(1)} collective-permute-done((f32[512,768]{1,0:T(8,128)S(1)}, f32[512,768]{1,0:T(8,128)S(1)}, u32[]{:S(2)}, u32[]{:S(2)}) %collective-permute-start.12) | collective-permute-done | bytes 1572896 | tf_op jit(solution)/shard_map/ppermute | solution.py:33
  588.6 67.4 %collective-permute-done.11 = f32[512,768]{1,0:T(8,128)S(1)} collective-permute-done((f32[512,768]{1,0:T(8,128)S(1)}, f32[512,768]{1,0:T(8,128)S(1)}, u32[]{:S(2)}, u32[]{:S(2)}) %collective-permute-start.11) | collective-permute-done | bytes 1572896 | tf_op jit(solution)/shard_map/ppermute | solution.py:33
  659.7 96.7 %all-gather.6.cloned.1.call-done = bf16[4096,768]{1,0:T(8,128)(2,1)} async-done(((bf16[512,768]{1,0:T(8,128)(2,1)}), bf16[4096,768]{1,0:T(8,128)(2,1)}) %all-gather.6.cloned.1.call-update) | async-done | bytes 6291472 | tf_op jit(solution)/shard_map/all_gather | solution.py:294
  765.4 91.2 %all-gather.4.cloned.1.call-done = bf16[4096,768]{1,0:T(8,128)(2,1)} async-done(((bf16[512,768]{1,0:T(8,128)(2,1)}), bf16[4096,768]{1,0:T(8,128)(2,1)}) %all-gather.4.cloned.1.call-update) | async-done | bytes 6291472 | tf_op jit(solution)/shard_map/all_gather | solution.py:284
  856.6 13.4 fusion.130
  888.6 195.1 %reduce-scatter.5.cloned.1.call-done = f32[512,768]{1,0:T(8,128)} async-done(((f32[4096,768]{1,0:T(8,128)}), f32[512,768]{1,0:T(8,128)}) %reduce-scatter.5.cloned.1.call-update) | async-done | bytes 1572880 | tf_op jit(solution)/shard_map/reduce_scatter | solution.py:298
  1086.6 118.0 %reduce-scatter.3.cloned.1.call-done = bf16[512,768]{1,0:T(8,128)(2,1)} async-done(((bf16[4096,768]{1,0:T(8,128)(2,1)}), bf16[512,768]{1,0:T(8,128)(2,1)}) %reduce-scatter.3.cloned.1.call-update) | async-done | bytes 786448 | tf_op jit(solution)/shard_map/reduce_scatter | solution.py:287
  1213.3 16.2 collective-permute-done.15
  1229.5 50.3 %collective-permute-done.14 = bf16[512,768]{1,0:T(8,128)(2,1)} collective-permute-done((bf16[512,768]{1,0:T(8,128)(2,1)}, bf16[512,768]{1,0:T(8,128)(2,1)}, u32[]{:S(2)}, u32[]{:S(2)}) %collective-permute-start.14) | collective-permute-done | bytes 786464 | tf_op jit(solution)/shard_map/ppermute | solution.py:33
  1296.5 36.5 %while.54 = (s32[]{:T(128)}, bf16[4,512,192]{1,2,0:T(8,128)(2,1)}, bf16[4,308,192]{1,2,0:T(8,128)(2,1)}, bf16[4,308,192]{1,2,0:T(8,128)(2,1)}, pred[4,512,308]{1...) while((s32[]{:T(128)}, bf16[4,512,192]{1,2,0:T(8,128)(2,1)}, ...), condition=%wide.region_31.33_spmd, body=%wide.region_27.32_spmd.sunk | while | flops 308706048 | bytes 19685584 | solution.py:129
  1369.5 43.4 %collective-permute-done.16 = f32[820,768]{1,0:T(8,128)} collective-permute-done((f32[820,768]{1,0:T(8,128)}, f32[820,768]{1,0:T(8,128)}, u32[]{:S(2)}, u32[]{:S(2)}) %collective-permute-start.16) | collective-permute-done | bytes 2519072 | tf_op jit(solution)/shard_map/ppermute | solution.py:33
  1413.0 106.2 %collective-permute-done.17 = f32[820,768]{1,0:T(8,128)} collective-permute-done((f32[820,768]{1,0:T(8,128)}, f32[820,768]{1,0:T(8,128)}, u32[]{:S(2)}, u32[]{:S(2)}) %collective-permute-start.17) | collective-permute-done | bytes 2519072 | tf_op jit(solution)/shard_map/ppermute | solution.py:33
  1529.0 56.9 %collective-permute-start.21 = (bf16[512,768]{1,0:T(8,128)(2,1)S(1)}, bf16[512,768]{1,0:T(8,128)(2,1)S(1)}, u32[]{:S(2)}, u32[]{:S(2)}) collective-permute-start(bf16[512,768]{1,0:T(8,128)(2,1)S(1)} %get-tuple-element.453), channel_id=1, source_target_pairs={{0,6},{1,7},{2,0},{3,1},{4,2},{5,3},{6,4},{7,5},{8,14},{9,15},{10,... | collective-permute-start | bytes 2359304 | tf_op jit(solution)/shard_map/ppermute | solution.py:33
  1604.0 49.2 %collective-permute-done.20 = bf16[512,768]{1,0:T(8,128)(2,1)S(1)} collective-permute-done((bf16[512,768]{1,0:T(8,128)(2,1)S(1)}, bf16[512,768]{1,0:T(8,128)(2,1)S(1)}, u32[]{:S(2)}, u32[]{:S(2)}) %collective-permute-start.20) | collective-permute-done | bytes 786464 | tf_op jit(solution)/shard_map/ppermute | solution.py:33
  1669.8 44.3 %while.55 = (s32[]{:T(128)}, bf16[4,512,192]{1,2,0:T(8,128)(2,1)}, bf16[4,512,192]{1,2,0:T(8,128)(2,1)}, bf16[4,512,192]{1,2,0:T(8,128)(2,1)}, pred[4,512,512]{1...) while((s32[]{:T(128)}, bf16[4,512,192]{1,2,0:T(8,128)(2,1)}, ...), condition=%wide.region_38.40_spmd, body=%wide.region_34.39_spmd.sunk | while | flops 512653824 | bytes 30505168 | solution.py:129
  1754.4 15.7 collective-permute-done.22
  1770.1 30.7 %collective-permute-done.24 = f32[512,768]{1,0:T(8,128)S(1)} collective-permute-done((f32[512,768]{1,0:T(8,128)S(1)}, f32[512,768]{1,0:T(8,128)S(1)}, u32[]{:S(2)}, u32[]{:S(2)}) %collective-permute-start.24) | collective-permute-done | bytes 1572896 | tf_op jit(solution)/shard_map/ppermute | solution.py:33
  1800.7 68.3 %collective-permute-done.23 = f32[512,768]{1,0:T(8,128)S(1)} collective-permute-done((f32[512,768]{1,0:T(8,128)S(1)}, f32[512,768]{1,0:T(8,128)S(1)}, u32[]{:S(2)}, u32[]{:S(2)}) %collective-permute-start.23) | collective-permute-done | bytes 1572896 | tf_op jit(solution)/shard_map/ppermute | solution.py:33
  1883.0 30.9 %all-gather = bf16[8,4,4608]{2,1,0:T(4,128)(2,1)S(1)} all-gather(bf16[1,4,4608]{2,1,0:T(4,128)(2,1)S(1)} %fusion.131), channel_id=1, replica_groups=mesh['dp'=4,'mp'=8] {'mp'}, dimensions={0}, use_global_device_ids=true | all-gather | bytes 331776 | tf_op jit(solution)/shard_map/all_gather | solution.py:367
  1931.6 59.2 %all-reduce.7.cloned.1.call-done = (bf16[1000,96]{0,1:T(8,128)(2,1)}, bf16[96,4608]{1,0:T(8,128)(2,1)}, bf16[768,96]{0,1:T(8,128)(2,1)}, bf16[768,96]{0,1:T(8,12...) async-done(((bf16[1000,96]{0,1:T(8,128)(2,1)}, ...) | async-done | bytes 3436048 | tf_op jit(solution)/shard_map/psum | solution.py:401
  (745 shorter events, 469.7 us)
Async XLA Ops:
  7.3 82.8 %all-reduce.5.cloned.1.call-start = ((), (), s32[]{:S(2)}) async-start(), calls=%async_computation.6 | async-start | bytes 1179648
  10.3 746.0 %all-gather.6.cloned.1.call-start = ((), (), s32[]{:S(2)}) async-start(), calls=%async_computation.4 | async-start | bytes 7077888 | tf_op jit(solution)/shard_map/all_gather | solution.py:294
  16.8 89.2 %collective-permute-start.3 = (bf16[1,8,768,96]{2,3,1,0:T(8,128)(2,1)}, bf16[1,8,768,96]{2,3,1,0:T(8,128)(2,1)}, u32[]{:S(2)}, u32[]{:S(2)}) collective-permute-start(bf16[1,8,768,96]{2,3,1,0:T(8,128)(2,1)} %bitcast.62), channel_id=1, source_target_pairs={{0,1},{1,0},{2,3},{3,2},{4,5},{5,4},{6,7},{7,6},{8,9},{9,8},{10,11... | collective-permute-start | bytes 3538952 | tf_op jit(solution)/shard_map/ppermute | solution.py:27
  99.9 84.1 %collective-permute-start.1 = (bf16[820,768]{1,0:T(8,128)(2,1)}, bf16[820,768]{1,0:T(8,128)(2,1)}, u32[]{:S(2)}, u32[]{:S(2)}) collective-permute-start(bf16[820,768]{1,0:T(8,128)(2,1)} %get-tuple-element.530), channel_id=1, source_target_pairs={{0,4},{1,5},{2,6},{3,7},{4,0},{5,1},{6,2},{7,3},{8,12},{9,13},{10,... | collective-permute-start | bytes 3778568 | tf_op jit(solution)/shard_map/ppermute | solution.py:33
  101.2 82.8 %collective-permute-start = (bf16[820,768]{1,0:T(8,128)(2,1)}, bf16[820,768]{1,0:T(8,128)(2,1)}, u32[]{:S(2)}, u32[]{:S(2)}) collective-permute-start(bf16[820,768]{1,0:T(8,128)(2,1)} %get-tuple-element.530), channel_id=1, source_target_pairs={{0,2},{1,3},{2,4},{3,5},{4,6},{5,7},{6,0},{7,1},{8,10},{9,11},{10,... | collective-permute-start | bytes 3778568 | tf_op jit(solution)/shard_map/ppermute | solution.py:33
  102.5 81.5 %collective-permute-start.2 = (bf16[820,768]{1,0:T(8,128)(2,1)}, bf16[820,768]{1,0:T(8,128)(2,1)}, u32[]{:S(2)}, u32[]{:S(2)}) collective-permute-start(bf16[820,768]{1,0:T(8,128)(2,1)} %get-tuple-element.530), channel_id=1, source_target_pairs={{0,6},{1,7},{2,0},{3,1},{4,2},{5,3},{6,4},{7,5},{8,14},{9,15},{10,... | collective-permute-start | bytes 3778568 | tf_op jit(solution)/shard_map/ppermute | solution.py:33
  240.3 62.1 %collective-permute-start.4 = (f32[512,768]{1,0:T(8,128)}, f32[512,768]{1,0:T(8,128)S(1)}, u32[]{:S(2)}, u32[]{:S(2)}) collective-permute-start(f32[512,768]{1,0:T(8,128)} %get-tuple-element.516), channel_id=1, source_target_pairs={{0,2},{1,3},{2,4},{3,5},{4,6},{5,7},{6,0},{7,1},{8,10},{9,11},{10,... | collective-permute-start | bytes 4718600 | tf_op jit(solution)/shard_map/ppermute | solution.py:33
  267.1 68.9 %collective-permute-start.6 = (f32[512,768]{1,0:T(8,128)}, f32[512,768]{1,0:T(8,128)}, u32[]{:S(2)}, u32[]{:S(2)}) collective-permute-start(f32[512,768]{1,0:T(8,128)} %get-tuple-element.517), channel_id=1, source_target_pairs={{0,6},{1,7},{2,0},{3,1},{4,2},{5,3},{6,4},{7,5},{8,14},{9,15},{10,... | collective-permute-start | bytes 4718600 | tf_op jit(solution)/shard_map/ppermute | solution.py:33
  267.1 111.2 %collective-permute-start.5 = (f32[512,768]{1,0:T(8,128)}, f32[512,768]{1,0:T(8,128)}, u32[]{:S(2)}, u32[]{:S(2)}) collective-permute-start(f32[512,768]{1,0:T(8,128)} %get-tuple-element.518), channel_id=1, source_target_pairs={{0,4},{1,5},{2,6},{3,7},{4,0},{5,1},{6,2},{7,3},{8,12},{9,13},{10,... | collective-permute-start | bytes 4718600 | tf_op jit(solution)/shard_map/ppermute | solution.py:33
  384.8 59.5 %collective-permute-start.8 = (bf16[512,768]{1,0:T(8,128)(2,1)}, bf16[512,768]{1,0:T(8,128)(2,1)}, u32[]{:S(2)}, u32[]{:S(2)}) collective-permute-start(bf16[512,768]{1,0:T(8,128)(2,1)} %fusion.172), channel_id=1, source_target_pairs={{0,4},{1,5},{2,6},{3,7},{4,0},{5,1},{6,2},{7,3},{8,12},{9,13},{10,... | collective-permute-start | bytes 2359304 | tf_op jit(solution)/shard_map/ppermute | solution.py:33
  384.8 80.4 %collective-permute-start.7 = (bf16[512,768]{1,0:T(8,128)(2,1)}, bf16[512,768]{1,0:T(8,128)(2,1)}, u32[]{:S(2)}, u32[]{:S(2)}) collective-permute-start(bf16[512,768]{1,0:T(8,128)(2,1)} %fusion.172), channel_id=1, source_target_pairs={{0,2},{1,3},{2,4},{3,5},{4,6},{5,7},{6,0},{7,1},{8,10},{9,11},{10,... | collective-permute-start | bytes 2359304 | tf_op jit(solution)/shard_map/ppermute | solution.py:33
  430.1 35.4 %collective-permute-start.9 = (bf16[512,768]{1,0:T(8,128)(2,1)}, bf16[512,768]{1,0:T(8,128)(2,1)}, u32[]{:S(2)}, u32[]{:S(2)}) collective-permute-start(bf16[512,768]{1,0:T(8,128)(2,1)} %fusion.172), channel_id=1, source_target_pairs={{0,6},{1,7},{2,0},{3,1},{4,2},{5,3},{6,4},{7,5},{8,14},{9,15},{10,... | collective-permute-start | bytes 2359304 | tf_op jit(solution)/shard_map/ppermute | solution.py:33
  504.5 52.1 %collective-permute-start.10 = (f32[512,768]{1,0:T(8,128)S(1)}, f32[512,768]{1,0:T(8,128)S(1)}, u32[]{:S(2)}, u32[]{:S(2)}) collective-permute-start(f32[512,768]{1,0:T(8,128)S(1)} %get-tuple-element.513), channel_id=1, source_target_pairs={{0,2},{1,3},{2,4},{3,5},{4,6},{5,7},{6,0},{7,1},{8,10},{9,11},{10,... | collective-permute-start | bytes 4718600 | tf_op jit(solution)/shard_map/ppermute | solution.py:33
  520.0 68.5 %collective-permute-start.12 = (f32[512,768]{1,0:T(8,128)S(1)}, f32[512,768]{1,0:T(8,128)S(1)}, u32[]{:S(2)}, u32[]{:S(2)}) collective-permute-start(f32[512,768]{1,0:T(8,128)S(1)} %get-tuple-element.514), channel_id=1, source_target_pairs={{0,6},{1,7},{2,0},{3,1},{4,2},{5,3},{6,4},{7,5},{8,14},{9,15},{10,... | collective-permute-start | bytes 4718600 | tf_op jit(solution)/shard_map/ppermute | solution.py:33
  521.3 134.7 %collective-permute-start.11 = (f32[512,768]{1,0:T(8,128)S(1)}, f32[512,768]{1,0:T(8,128)S(1)}, u32[]{:S(2)}, u32[]{:S(2)}) collective-permute-start(f32[512,768]{1,0:T(8,128)S(1)} %get-tuple-element.515), channel_id=1, source_target_pairs={{0,4},{1,5},{2,6},{3,7},{4,0},{5,1},{6,2},{7,3},{8,12},{9,13},{10,... | collective-permute-start | bytes 4718600 | tf_op jit(solution)/shard_map/ppermute | solution.py:33
  658.6 198.0 %all-gather.4.cloned.1.call-start = ((), (), s32[]{:S(2)}) async-start(), calls=%async_computation.2 | async-start | bytes 7077888 | tf_op jit(solution)/shard_map/all_gather | solution.py:284
  659.4 424.4 %reduce-scatter.5.cloned.1.call-start = ((), (), s32[]{:S(2)}) async-start(), calls=%async_computation.5 | async-start | bytes 14155776 | tf_op jit(solution)/shard_map/reduce_scatter | solution.py:298
  878.1 326.6 %reduce-scatter.3.cloned.1.call-start = ((), (), s32[]{:S(2)}) async-start(), calls=%async_computation.3 | async-start | bytes 7077888 | tf_op jit(solution)/shard_map/reduce_scatter | solution.py:287
  888.6 1102.3 %all-reduce.7.cloned.1.call-start = ((), (), s32[]{:S(2)}) async-start(), calls=%async_computation.7 | async-start | bytes 6881280 | tf_op jit(solution)/shard_map/psum | solution.py:401
  1209.6 19.9 collective-permute-start.15
  1211.1 68.6 %collective-permute-start.14 = (bf16[512,768]{1,0:T(8,128)(2,1)}, bf16[512,768]{1,0:T(8,128)(2,1)}, u32[]{:S(2)}, u32[]{:S(2)}) collective-permute-start(bf16[512,768]{1,0:T(8,128)(2,1)} %get-tuple-element.455), channel_id=1, source_target_pairs={{0,4},{1,5},{2,6},{3,7},{4,0},{5,1},{6,2},{7,3},{8,12},{9,13},{10,... | collective-permute-start | bytes 2359304 | tf_op jit(solution)/shard_map/ppermute | solution.py:33
  1211.8 68.0 %collective-permute-start.13 = (bf16[512,768]{1,0:T(8,128)(2,1)}, bf16[512,768]{1,0:T(8,128)(2,1)}, u32[]{:S(2)}, u32[]{:S(2)}) collective-permute-start(bf16[512,768]{1,0:T(8,128)(2,1)} %get-tuple-element.455), channel_id=1, source_target_pairs={{0,2},{1,3},{2,4},{3,5},{4,6},{5,7},{6,0},{7,1},{8,10},{9,11},{10,... | collective-permute-start | bytes 2359304 | tf_op jit(solution)/shard_map/ppermute | solution.py:33
  1352.9 60.1 %collective-permute-start.16 = (f32[820,768]{1,0:T(8,128)}, f32[820,768]{1,0:T(8,128)}, u32[]{:S(2)}, u32[]{:S(2)}) collective-permute-start(f32[820,768]{1,0:T(8,128)} %get-tuple-element.505), channel_id=1, source_target_pairs={{0,2},{1,3},{2,4},{3,5},{4,6},{5,7},{6,0},{7,1},{8,10},{9,11},{10,... | collective-permute-start | bytes 7557128 | tf_op jit(solution)/shard_map/ppermute | solution.py:33
  1353.4 165.8 %collective-permute-start.17 = (f32[820,768]{1,0:T(8,128)}, f32[820,768]{1,0:T(8,128)}, u32[]{:S(2)}, u32[]{:S(2)}) collective-permute-start(f32[820,768]{1,0:T(8,128)} %get-tuple-element.506), channel_id=1, source_target_pairs={{0,4},{1,5},{2,6},{3,7},{4,0},{5,1},{6,2},{7,3},{8,12},{9,13},{10,... | collective-permute-start | bytes 7557128 | tf_op jit(solution)/shard_map/ppermute | solution.py:33
  1355.3 163.9 %collective-permute-start.18 = (f32[820,768]{1,0:T(8,128)}, f32[820,768]{1,0:T(8,128)}, u32[]{:S(2)}, u32[]{:S(2)}) collective-permute-start(f32[820,768]{1,0:T(8,128)} %get-tuple-element.507), channel_id=1, source_target_pairs={{0,6},{1,7},{2,0},{3,1},{4,2},{5,3},{6,4},{7,5},{8,14},{9,15},{10,... | collective-permute-start | bytes 7557128 | tf_op jit(solution)/shard_map/ppermute | solution.py:33
  1529.0 74.9 %collective-permute-start.21 = (bf16[512,768]{1,0:T(8,128)(2,1)S(1)}, bf16[512,768]{1,0:T(8,128)(2,1)S(1)}, u32[]{:S(2)}, u32[]{:S(2)}) collective-permute-start(bf16[512,768]{1,0:T(8,128)(2,1)S(1)} %get-tuple-element.453), channel_id=1, source_target_pairs={{0,6},{1,7},{2,0},{3,1},{4,2},{5,3},{6,4},{7,5},{8,14},{9,15},{10,... | collective-permute-start | bytes 2359304 | tf_op jit(solution)/shard_map/ppermute | solution.py:33
  1585.9 67.3 %collective-permute-start.20 = (bf16[512,768]{1,0:T(8,128)(2,1)S(1)}, bf16[512,768]{1,0:T(8,128)(2,1)S(1)}, u32[]{:S(2)}, u32[]{:S(2)}) collective-permute-start(bf16[512,768]{1,0:T(8,128)(2,1)S(1)} %get-tuple-element.453), channel_id=1, source_target_pairs={{0,4},{1,5},{2,6},{3,7},{4,0},{5,1},{6,2},{7,3},{8,12},{9,13},{10,... | collective-permute-start | bytes 2359304 | tf_op jit(solution)/shard_map/ppermute | solution.py:33
  1585.9 67.3 %collective-permute-start.19 = (bf16[512,768]{1,0:T(8,128)(2,1)S(1)}, bf16[512,768]{1,0:T(8,128)(2,1)S(1)}, u32[]{:S(2)}, u32[]{:S(2)}) collective-permute-start(bf16[512,768]{1,0:T(8,128)(2,1)S(1)} %get-tuple-element.453), channel_id=1, source_target_pairs={{0,2},{1,3},{2,4},{3,5},{4,6},{5,7},{6,0},{7,1},{8,10},{9,11},{10,... | collective-permute-start | bytes 2359304 | tf_op jit(solution)/shard_map/ppermute | solution.py:33
  1725.8 27.1 %collective-permute-start.25 = (bf16[1,8,768,96]{2,3,1,0:T(8,128)(2,1)S(1)}, bf16[1,8,768,96]{2,3,1,0:T(8,128)(2,1)S(1)}, u32[]{:S(2)}, u32[]{:S(2)}) collective-permute-start(bf16[1,8,768,96]{2,3,1,0:T(8,128)(2,1)S(1)} %select_convert_fusion), channel_id=1, source_target_pairs={{0,1},{1,0},{2,3},{3,2},{4,5},{5,4},{6,7},{7,6},{8,9},{9,8},{10,11... | collective-permute-start | bytes 3538952 | tf_op jit(solution)/shard_map/ppermute | solution.py:27
  1730.9 39.2 %collective-permute-start.22 = (f32[512,768]{1,0:T(8,128)S(1)}, f32[512,768]{1,0:T(8,128)S(1)}, u32[]{:S(2)}, u32[]{:S(2)}) collective-permute-start(f32[512,768]{1,0:T(8,128)S(1)} %get-tuple-element.510), channel_id=1, source_target_pairs={{0,2},{1,3},{2,4},{3,5},{4,6},{5,7},{6,0},{7,1},{8,10},{9,11},{10,... | collective-permute-start | bytes 4718600 | tf_op jit(solution)/shard_map/ppermute | solution.py:33
  1731.3 69.5 %collective-permute-start.24 = (f32[512,768]{1,0:T(8,128)S(1)}, f32[512,768]{1,0:T(8,128)S(1)}, u32[]{:S(2)}, u32[]{:S(2)}) collective-permute-start(f32[512,768]{1,0:T(8,128)S(1)} %get-tuple-element.511), channel_id=1, source_target_pairs={{0,6},{1,7},{2,0},{3,1},{4,2},{5,3},{6,4},{7,5},{8,14},{9,15},{10,... | collective-permute-start | bytes 4718600 | tf_op jit(solution)/shard_map/ppermute | solution.py:33
  1734.9 134.1 %collective-permute-start.23 = (f32[512,768]{1,0:T(8,128)S(1)}, f32[512,768]{1,0:T(8,128)S(1)}, u32[]{:S(2)}, u32[]{:S(2)}) collective-permute-start(f32[512,768]{1,0:T(8,128)S(1)} %get-tuple-element.512), channel_id=1, source_target_pairs={{0,4},{1,5},{2,6},{3,7},{4,0},{5,1},{6,2},{7,3},{8,12},{9,13},{10,... | collective-permute-start | bytes 4718600 | tf_op jit(solution)/shard_map/ppermute | solution.py:33
  (98 other events, 3667.1 us)
Sparse Core Ops, SparseCore 0:
  12.1 78.0 all-reduce.4
  658.7 97.5 all-gather.5
  759.4 97.1 all-gather.3
  878.2 205.4 reduce-scatter.4
  1087.6 117.0 reduce-scatter.2
  1917.0 73.7 all-reduce.6
where the time goes:
time: 2020 us; the launch traced here: 2010 us
  waiting for transfers between devices  1360 us (67%)
  starting transfers between devices  176 us (9%)
  matrix products  167 us (8%)
  local copies, waits for them, and re-layouts  135 us (7%)
  other arithmetic  117 us (6%)
  blocking collectives  42 us (2%)
    ppermute x24, waiting for transfers between devices, from_behind(): return lax.ppermute(value, axis, pairs)  722 us
    reduce_scatter x1, waiting for transfers between devices, shards(): lax.psum_scatter(outer_cols(grad_rows, up_weight), 'mp', scatter_dimensio...  195 us
    ppermute x24, starting transfers between devices, from_behind(): return lax.ppermute(value, axis, pairs)  170 us
    reduce_scatter x1, waiting for transfers between devices, shards(): lax.psum_scatter(matmul(activated, down_weight).astype(jnp.bfloat16), 'mp...  118 us
    all_gather x1, waiting for transfers between devices, shards(): received = lax.all_gather(grad_mlp, 'mp', axis=0, tiled=True)  96.7 us
    all_gather x1, waiting for transfers between devices, shards(): third_all = lax.all_gather(third_in, 'mp', axis=0, tiled=True)  91.2 us
    unnamed x7, waiting for transfers between devices  68.2 us
    psum x1, waiting for transfers between devices, shards(): lax.psum(grad_table.astype(jnp.bfloat16), 'dp').astype(jnp.float32)  59.2 us
  transfers between devices with their start and end apart: 32, of which 25 were waited for; matrix products, arithmetic and copies ran while one was open for 5% of the time, Pallas kernels for 0%

commit v1 on v0

v1 whole, which is shorter than its diff:
```python
from functools import partial

import jax
import jax.numpy as jnp
from jax import lax
from jax.experimental import pallas as pl
from jax.experimental.pallas import tpu as pltpu
from jax.sharding import Mesh, PartitionSpec as P

HEADS = 12
HD = 64
CAPTION = 77
SEGS = 4

PAIR = 2 * HD
highest = lax.Precision.HIGHEST
epsilon = 1e-06
masked_score = -1e30
bf16 = jnp.bfloat16
f32 = jnp.float32
FINE = ("y", "core", "z", "x")
WEIGHT_ORDER = ("z", "x", "y", "core")
VMEM = 48 << 20


def shifted(value, axis, steps):
    count = lax.axis_size(axis)
    return lax.ppermute(value, axis, [(k, (k + steps) % count) for k in range(count)])


def gather_axis(value, axis):
    count = lax.axis_size(axis)
    if count == 1:
        return value[None]
    me = lax.axis_index(axis)
    pieces = [value] + [shifted(value, axis, s) for s in range(1, count)]
    if count == 2:
        first = me == 0
        return jnp.stack(
            [jnp.where(first, pieces[0], pieces[1]), jnp.where(first, pieces[1], pieces[0])]
        )
    turned = jnp.stack(pieces[::-1] + pieces[::-1])
    return lax.dynamic_slice_in_dim(turned, count - 1 - me, count, 0)


def scatter_axis(value, axis, dim):
    count = lax.axis_size(axis)
    me = lax.axis_index(axis)

    def piece(which):
        return lax.dynamic_index_in_dim(value, which % count, dim, keepdims=False)

    arrived = [shifted(piece(me + s), axis, s) for s in range(1, count)]
    total = piece(me).astype(f32)
    for part in arrived:
        total = total + part.astype(f32)
    return total


def gather_weights(shards):
    count, rows, width = len(shards), shards[0].shape[0], shards[0].shape[1]
    copies = lax.axis_size("y") * lax.axis_size("core")
    part = rows // copies
    mine = lax.axis_index("y") * lax.axis_size("core") + lax.axis_index("core")
    stacked = jnp.stack([lax.dynamic_slice_in_dim(s, mine * part, part, 0) for s in shards])
    column = gather_axis(stacked, "z")
    half = width // 2
    left = gather_axis(gather_axis(column[..., :half], "x"), "y")
    right = gather_axis(gather_axis(column[..., half:], "y"), "x")
    left = gather_axis(left, "core").transpose(4, 3, 2, 1, 0, 5, 6)
    right = gather_axis(right, "core").transpose(4, 3, 1, 2, 0, 5, 6)
    whole = jnp.concatenate([left, right], axis=-1)
    return whole.reshape(count, -1, width)


def pair_product(left, right):
    half = right.shape[1] // 2
    me = lax.axis_index("core")
    mine = lax.dynamic_slice_in_dim(right, me * half, half, 1)
    other = lax.dynamic_slice_in_dim(right, (1 - me) * half, half, 1)
    sent = shifted(inner_rows(left, other).astype(bf16), "core", 1)
    return (inner_rows(left, mine) + sent.astype(f32)).astype(bf16)


def reduce_grads(grads):
    nz, nx, ny = (lax.axis_size(a) for a in ("z", "x", "y"))
    width = grads[0].shape[1]
    stacked = [g.reshape(nz, nx, ny, -1, width) for g in grads]
    half = stacked[0].shape[3] // 2
    first = jnp.stack([g[:, :, :, :half] for g in stacked])
    second = jnp.stack([g[:, :, :, half:] for g in stacked])
    first = scatter_axis(first, "x", 2).astype(bf16)
    second = scatter_axis(second, "y", 3).astype(bf16)
    first = scatter_axis(first, "y", 2).astype(bf16)
    second = scatter_axis(second, "x", 2).astype(bf16)
    both = jnp.concatenate([first, second], axis=2)
    done = scatter_axis(both, "z", 1).astype(bf16)
    done = gather_axis(gather_axis(done, "y"), "core")
    done = done.transpose(2, 1, 3, 0, 4)
    return done.reshape(len(grads), -1, width * lax.axis_size("core"))


def gather_all(rows):
    value = gather_axis(gather_axis(rows, "z"), "x")
    value = gather_axis(gather_axis(value, "y"), "core")
    value = value.transpose(1, 0, 3, 2, 4, 5)
    return value.reshape(-1, rows.shape[-1])


def normalize(values):
    centre = values - jnp.mean(values, axis=-1, keepdims=True)
    inverse = lax.rsqrt(jnp.mean(centre * centre, axis=-1, keepdims=True) + epsilon)
    return (centre * inverse, inverse)


def norm_back(normed, inverse, upstream):
    mean_grad = jnp.mean(upstream, axis=-1, keepdims=True)
    mean_both = jnp.mean(upstream * normed, axis=-1, keepdims=True)
    return inverse * (upstream - mean_grad - normed * mean_both)


def matmul(left, right):
    return jnp.dot(left, right, preferred_element_type=f32)


def inner_rows(left, right):
    return lax.dot_general(left, right, (((0,), (0,)), ((), ())), preferred_element_type=f32)


def outer_cols(left, right):
    return lax.dot_general(left, right, (((1,), (1,)), ((), ())), preferred_element_type=f32)


def gelu_back(pre_act, upstream):
    return jax.vjp(partial(jax.nn.gelu, approximate=True), pre_act)[1](upstream)[0]


def silu_back(inputs, upstream):
    return jax.vjp(jax.nn.silu, inputs)[1](upstream)[0]


def half_lanes(head):
    lane = lax.broadcasted_iota(jnp.int32, (1, PAIR), 1)
    return lane < HD if head == 0 else lane >= HD


def forward_kernel(q_ref, k_ref, v_ref, bias_ref, mix_ref):
    query = q_ref[...] * bf16(HD**-0.5)
    keys, values, bias = k_ref[...], v_ref[...], bias_ref[0]
    parts = []
    for head in range(2):
        own = jnp.where(half_lanes(head), query, bf16(0))
        scores = outer_cols(own, keys) + bias
        shifted_scores = jnp.exp(scores - jnp.max(scores, axis=1, keepdims=True))
        total = jnp.sum(shifted_scores, axis=1, keepdims=True)
        parts.append(matmul(shifted_scores.astype(bf16), values) / total)
    mix_ref[...] = jnp.where(half_lanes(0), parts[0], parts[1]).astype(bf16)


def backward_kernel(q_ref, k_ref, v_ref, bias_ref, g_ref, gq_ref, gk_ref, gv_ref):
    query = q_ref[...] * bf16(HD**-0.5)
    keys, values, bias, grad = k_ref[...], v_ref[...], bias_ref[0], g_ref[...]
    gq, gk, gv = [], [], []
    for head in range(2):
        own = half_lanes(head)
        scores = outer_cols(keys, jnp.where(own, query, bf16(0))) + bias
        raised = jnp.exp(scores - jnp.max(scores, axis=0, keepdims=True))
        weights = raised * (1.0 / jnp.sum(raised, axis=0, keepdims=True))
        grad_weights = outer_cols(jnp.where(own, values, bf16(0)), grad)
        mean = jnp.sum(weights * grad_weights, axis=0, keepdims=True)
        grad_scores = (weights * (grad_weights - mean)).astype(bf16)
        gv.append(matmul(weights.astype(bf16), grad))
        gk.append(matmul(grad_scores, query))
        gq.append(inner_rows(grad_scores, keys))
    gq_ref[...] = (jnp.where(half_lanes(0), gq[0], gq[1]) * HD**-0.5).astype(bf16)
    gk_ref[...] = jnp.where(half_lanes(0), gk[0], gk[1]).astype(bf16)
    gv_ref[...] = jnp.where(half_lanes(0), gv[0], gv[1]).astype(bf16)


def attend(query, keys, values, bias):
    rows, frames, tokens = bias.shape
    pairs = query.shape[1] // PAIR
    blocks = [pl.BlockSpec((n, PAIR), lambda r, h: (r, h)) for n in (frames, tokens, tokens)]
    return pl.pallas_call(
        forward_kernel,
        grid=(rows, pairs),
        in_specs=blocks + [pl.BlockSpec((1, frames, tokens), lambda r, h: (r, 0, 0))],
        out_specs=blocks[0],
        out_shape=jax.ShapeDtypeStruct(query.shape, bf16),
        compiler_params=pltpu.CompilerParams(vmem_limit_bytes=VMEM),
        cost_estimate=pl.CostEstimate(
            flops=4 * rows * frames * tokens * query.shape[1] * 2,
            transcendentals=rows * frames * tokens * pairs * 2,
            bytes_accessed=8 * query.size,
        ),
    )(query, keys, values, bias)


def attend_back(query, keys, values, bias, grad):
    rows, tokens, frames = bias.shape
    pairs = query.shape[1] // PAIR
    wide = pl.BlockSpec((frames, PAIR), lambda r, h: (r, h))
    held = pl.BlockSpec((tokens, PAIR), lambda r, h: (r, h))
    return pl.pallas_call(
        backward_kernel,
        grid=(rows, pairs),
        in_specs=[wide, held, held, pl.BlockSpec((1, tokens, frames), lambda r, h: (r, 0, 0)), wide],
        out_specs=[wide, held, held],
        out_shape=[jax.ShapeDtypeStruct(a.shape, bf16) for a in (query, keys, values)],
        compiler_params=pltpu.CompilerParams(vmem_limit_bytes=VMEM),
        cost_estimate=pl.CostEstimate(
            flops=10 * rows * frames * tokens * query.shape[1] * 2,
            transcendentals=rows * frames * tokens * pairs * 2,
            bytes_accessed=16 * query.size,
        ),
    )(query, keys, values, bias, grad)


def shards(
    frames,
    seg_ids,
    text,
    text_lens,
    step_ids,
    step_table,
    ada_weight,
    ada_bias,
    query_w,
    key_w,
    value_w,
    out_w,
    cross_query_w,
    cross_key_w,
    cross_value_w,
    cross_out_w,
    up_weight,
    down_weight,
    out_grad,
):
    width = frames.shape[1]
    mp = lax.axis_size("z") * lax.axis_size("x")
    position = lax.axis_index("z") * lax.axis_size("x") + lax.axis_index("x")
    rows_dev = seg_ids.shape[0] // mp
    frames_row = seg_ids.shape[1]
    segs_dev = rows_dev * SEGS
    my_ids = lax.dynamic_slice_in_dim(seg_ids, position * rows_dev, rows_dev, 0)
    my_lens = lax.dynamic_slice_in_dim(text_lens, position * segs_dev, segs_dev, 0)

    qkv = gather_weights([query_w.T, key_w.T, value_w.T]).reshape(-1, width)
    others = gather_weights([out_w, cross_query_w.T, cross_key_w.T, cross_value_w.T, cross_out_w])
    out_full, cquery_t, cout_full = others[0], others[1], others[4]
    ckv_t = others[2:4].reshape(-1, width)
    copies = lax.axis_size("y") * lax.axis_size("core")
    mine = lax.axis_index("y") * lax.axis_size("core") + lax.axis_index("core")
    hidden_part = down_weight.shape[0] // copies
    ff_mine = lax.dynamic_slice_in_dim(
        jnp.concatenate([up_weight.T, down_weight], axis=1), mine * hidden_part, hidden_part, 0
    )
    ff_full = lax.all_gather(ff_mine, WEIGHT_ORDER, axis=0, tiled=True)
    up_t, down_full = ff_full[:, :width], ff_full[:, width:]

    table_low = step_table
    choose_step = (step_ids[:, None] == jnp.arange(step_table.shape[0])[None, :]).astype(bf16)
    silu_mine = jax.nn.silu(matmul(choose_step, table_low)).astype(bf16)
    partial_mod = matmul(silu_mine, ada_weight).astype(bf16)
    partial_mod = partial_mod.reshape(
        lax.axis_size("z"), lax.axis_size("x"), segs_dev, partial_mod.shape[1]
    )
    modulation = scatter_axis(scatter_axis(partial_mod, "x", 1).astype(bf16), "z", 0)
    modulation = modulation + ada_bias.astype(f32)
    flat_ids = my_ids.reshape(-1)
    row_of = jnp.arange(flat_ids.shape[0]) // frames_row
    clip = flat_ids + row_of * SEGS
    chosen = clip[:, None] == jnp.arange(segs_dev)[None, :]

    def per_frame(index):
        table = modulation[:, index * width : (index + 1) * width]
        value = jnp.broadcast_to(table[0:1], (clip.shape[0], width))
        for segment in range(1, segs_dev):
            value = jnp.where(chosen[:, segment : segment + 1], table[segment : segment + 1], value)
        return value

    shift_one, scale_one, gate_one, shift_two, scale_two, gate_two = map(per_frame, range(6))

    same_seg = my_ids[:, :, None] == my_ids[:, None, :]
    self_bias = jnp.where(same_seg, 0.0, masked_score).astype(f32)
    key_segment = jnp.arange(SEGS * CAPTION) // CAPTION
    valid_key = (
        jnp.arange(CAPTION)[None, None, :] < my_lens.reshape(rows_dev, SEGS)[:, :, None]
    ).reshape(rows_dev, SEGS * CAPTION)
    allowed = (my_ids[:, :, None] == key_segment[None, None, :]) & valid_key[:, None, :]
    cross_bias = jnp.where(allowed, 0.0, masked_score).astype(f32)
    allowed_t = (my_ids[:, None, :] == key_segment[None, :, None]) & valid_key[:, :, None]
    cross_bias_t = jnp.where(allowed_t, 0.0, masked_score).astype(f32)

    base = frames.astype(f32)
    text_flat = text.reshape(-1, width)
    normed_one, inverse_one = normalize(base)
    first_in = (normed_one * (1.0 + scale_one) + shift_one).astype(bf16)
    query, keys, values = (
        outer_cols(first_in, qkv[i * width : (i + 1) * width]).astype(bf16) for i in range(3)
    )
    self_mix = attend(query, keys, values, self_bias)
    self_out = matmul(self_mix, out_full)
    resid_one = base + gate_one * self_out
    normed_two, inverse_two = normalize(resid_one)
    second_in = normed_two.astype(bf16)
    cross_query = outer_cols(second_in, cquery_t).astype(bf16)
    cross_keys = outer_cols(text_flat, ckv_t[:width]).astype(bf16)
    cross_values = outer_cols(text_flat, ckv_t[width:]).astype(bf16)
    cross_mix = attend(cross_query, cross_keys, cross_values, cross_bias)
    resid_two = resid_one + matmul(cross_mix, cout_full)
    normed_three, inverse_three = normalize(resid_two)
    third_in = (normed_three * (1.0 + scale_two) + shift_two).astype(bf16)
    pre_act = outer_cols(third_in, up_t)
    activated = jax.nn.gelu(pre_act, approximate=True).astype(bf16)
    mlp_out = matmul(activated, down_full)
    layer_out = (resid_two + gate_two * mlp_out).astype(bf16)

    upstream = out_grad.astype(f32)
    grad_gate_two = upstream * mlp_out
    grad_mlp = (gate_two * upstream).astype(bf16)
    grad_pre = gelu_back(pre_act, outer_cols(grad_mlp, down_full)).astype(bf16)
    grad_down = pair_product(activated, grad_mlp)
    grad_up_t = pair_product(grad_pre, third_in)
    grad_third = matmul(grad_pre, up_t)
    shard_up, shard_down = reduce_grads([grad_up_t, grad_down])
    grad_resid_two = upstream + norm_back(
        normed_three, inverse_three, grad_third * (1.0 + scale_two)
    )
    grad_cross = grad_resid_two.astype(bf16)
    grad_cout = pair_product(cross_mix, grad_cross)
    grad_cross_mix = outer_cols(grad_cross, cout_full).astype(bf16)
    grad_cq, grad_ck, grad_cv = attend_back(
        cross_query, cross_keys, cross_values, cross_bias_t, grad_cross_mix
    )
    grad_cquery_t = pair_product(grad_cq, second_in)
    grad_ckey_t = pair_product(grad_ck, text_flat)
    grad_cvalue_t = pair_product(grad_cv, text_flat)
    grad_second = matmul(grad_cq, cquery_t)
    grad_text = matmul(grad_ck, ckv_t[:width]) + matmul(grad_cv, ckv_t[width:])
    grad_resid_one = grad_resid_two + norm_back(normed_two, inverse_two, grad_second)
    grad_gate_one = grad_resid_one * self_out
    grad_self = (gate_one * grad_resid_one).astype(bf16)
    grad_out = pair_product(self_mix, grad_self)
    shard_out, shard_cout, shard_cquery, shard_ckey, shard_cvalue = reduce_grads(
        [grad_out, grad_cout, grad_cquery_t, grad_ckey_t, grad_cvalue_t]
    )
    grad_self_mix = outer_cols(grad_self, out_full).astype(bf16)
    grad_sq, grad_sk, grad_sv = attend_back(query, keys, values, self_bias, grad_self_mix)
    grad_query_t = pair_product(grad_sq, first_in)
    grad_key_t = pair_product(grad_sk, first_in)
    grad_value_t = pair_product(grad_sv, first_in)
    shard_query, shard_key, shard_value = reduce_grads([grad_query_t, grad_key_t, grad_value_t])
    grad_first = (
        matmul(grad_sq, qkv[:width])
        + matmul(grad_sk, qkv[width : 2 * width])
        + matmul(grad_sv, qkv[2 * width :])
    )
    grad_frames = grad_resid_one + norm_back(
        normed_one, inverse_one, grad_first * (1.0 + scale_one)
    )

    chooser = chosen.astype(f32)

    def clip_sums(value):
        return lax.dot_general(chooser, value, (((0,), (0,)), ((), ())), precision=highest)

    late = jnp.concatenate([clip_sums(grad_first), clip_sums(grad_first * normed_one)], axis=1)
    early = jnp.concatenate(
        [
            clip_sums(grad_gate_one),
            clip_sums(grad_third),
            clip_sums(grad_third * normed_three),
            clip_sums(grad_gate_two),
        ],
        axis=1,
    )
    early_all = gather_all(early.astype(bf16))
    late_all = gather_all(late.astype(bf16))
    grad_mod_all = jnp.concatenate([late_all, early_all], axis=1)
    steps_all = gather_axis(gather_axis(step_ids.astype(f32), "y"), "core")
    steps_all = steps_all.transpose(1, 0, 2).reshape(-1)
    choose_all = (
        steps_all[:, None] == jnp.arange(step_table.shape[0]).astype(f32)[None, :]
    ).astype(bf16)
    cond_all = matmul(choose_all, table_low)
    silu_all = jax.nn.silu(cond_all).astype(bf16)
    grad_ada_w = inner_rows(silu_all, grad_mod_all)
    grad_ada_b = jnp.sum(grad_mod_all.astype(f32), axis=0)
    grad_cond = silu_back(cond_all, outer_cols(grad_mod_all, ada_weight))
    grad_table = lax.dot_general(
        choose_all.astype(f32), grad_cond, (((0,), (0,)), ((), ())), precision=highest
    )

    def columns(value):
        return value.T.astype(f32)

    return (
        layer_out,
        grad_frames,
        grad_text.reshape(text.shape),
        grad_table,
        grad_ada_w,
        grad_ada_b,
        columns(shard_query),
        columns(shard_key),
        columns(shard_value),
        shard_out.astype(f32),
        columns(shard_cquery),
        columns(shard_ckey),
        columns(shard_cvalue),
        shard_cout.astype(f32),
        columns(shard_up),
        shard_down.astype(f32),
    )


def solution(mesh):
    dp, mp = mesh.shape["dp"], mesh.shape["mp"]
    fine = Mesh(mesh.devices.reshape(dp // 2, 2, mp // 2, 2), FINE)
    dp_axes, mp_axes = ("y", "core"), ("z", "x")
    return jax.shard_map(
        shards,
        mesh=fine,
        in_specs=(
            P(FINE, None),
            P(dp_axes, None),
            P(FINE, None, None),
            P(dp_axes),
            P(dp_axes),
            P(None, mp_axes),
            P(mp_axes, None),
            P(),
            P(None, mp_axes),
            P(None, mp_axes),
            P(None, mp_axes),
            P(mp_axes, None),
            P(None, mp_axes),
            P(None, mp_axes),
            P(None, mp_axes),
            P(mp_axes, None),
            P(None, mp_axes),
            P(mp_axes, None),
            P(FINE, None),
        ),
        out_specs=(
            P(FINE, None),
            P(FINE, None),
            P(FINE, None, None),
            P(None, mp_axes),
            P(mp_axes, None),
            P(),
            P(None, mp_axes),
            P(None, mp_axes),
            P(None, mp_axes),
            P(mp_axes, None),
            P(None, mp_axes),
            P(None, mp_axes),
            P(None, mp_axes),
            P(mp_axes, None),
            P(None, mp_axes),
            P(mp_axes, None),
        ),
        check_vma=False,
    )
```

time: 2020 us -> 482 us (0.24)
  waiting for transfers between devices: 1360 us -> 134 us
  starting transfers between devices: 176 us -> 76.9 us
  matrix products: 167 us -> 91.1 us
  other arithmetic: 117 us -> 42 us
  local copies, waits for them, and re-layouts: 135 us -> 74.8 us
  blocking collectives: 42 us -> 0 us
  Pallas kernels: 0 us -> 38.5 us
    ppermute x26 -> x73, waiting for transfers between devices: 731 us -> 134 us  [shifted(): lax.ppermute(value, axis, [(k, (k + steps) % count) for k in range(count)])]
    reduce_scatter x2 -> x0, waiting for transfers between devices: 313 us -> none  [the longest x1 195 us: shards(): lax.psum_scatter(outer_cols(grad_rows, up_weight), 'mp', scatter_dimensio...]
    all_gather x2 -> x1, waiting for transfers between devices: 188 us -> 0.02 us  [shards(): ff_full = lax.all_gather(ff_mine, WEIGHT_ORDER, axis=0, tiled=True)]
    ppermute x26 -> x73, starting transfers between devices: 175 us -> 76.9 us  [shifted(): lax.ppermute(value, axis, [(k, (k + steps) % count) for k in range(count)])]
    unnamed x7 -> x1, waiting for transfers between devices: 68.2 us -> 0.02 us
    psum x1 -> x0, waiting for transfers between devices: 59.2 us -> none  [shards(): lax.psum(grad_table.astype(jnp.bfloat16), 'dp').astype(jnp.float32)]
    pallas_call x0 -> x4, Pallas kernels: none -> 38.5 us  [the longest x2 25.4 us: attend_back(): pl.pallas_call(backward_kernel, grid=(rows, pairs), in_specs=[wide, held,...]
    dot_general x64 -> x19, matrix products: 63.9 us -> 29.3 us  [the longest x12 23.7 us: matmul(): return jnp.dot(left, right, preferred_element_type=f32)]
  transfers between devices with their start and end apart: 32 -> 74, of which waited for: 25 -> 21; matrix products, arithmetic and copies ran while one was open for 5% -> 32% of each run, Pallas kernels for 0% -> 3%
where the time goes in v1:
time: 482 us; the launch traced here: 474 us
  waiting for transfers between devices  134 us (28%)
  matrix products  91.1 us (19%)
  starting transfers between devices  76.9 us (16%)
  local copies, waits for them, and re-layouts  74.8 us (16%)
  other arithmetic  42 us (9%)
  Pallas kernels  38.5 us (8%)
  between operations  16.8 us (3%)
    ppermute x73, waiting for transfers between devices, shifted(): lax.ppermute(value, axis, [(k, (k + steps) % count) for k in range(count)])  134 us
    ppermute x73, starting transfers between devices, shifted(): lax.ppermute(value, axis, [(k, (k + steps) % count) for k in range(count)])  76.9 us
    unnamed x287, local copies, waits for them, and re-layouts  43.2 us
    dot_general x21, matrix products, inner_rows(): lax.dot_general(left, right, (((0,), (0,)), ((), ())), preferred_element_...  37.6 us
    pallas_call x2, Pallas kernels, attend_back(): pl.pallas_call(backward_kernel, grid=(rows, pairs), in_specs=[wide, held,...  25.4 us
    dot_general x11, matrix products, outer_cols(): lax.dot_general(left, right, (((1,), (1,)), ((), ())), preferred_element_...  24.3 us
    dot_general x12, matrix products, matmul(): return jnp.dot(left, right, preferred_element_type=f32)  23.7 us
    pallas_call x2, Pallas kernels, attend(): pl.pallas_call(forward_kernel, grid=(rows, pairs), in_specs=blocks + [pl....  13.1 us
  transfers between devices with their start and end apart: 74, of which 21 were waited for; matrix products, arithmetic and copies ran while one was open for 32% of the time, Pallas kernels for 3%

profile of v1, /device:TPU:0, one launch (start us, length us, event | category | flops | bytes accessed | tf_op | source)
XLA Modules:
  0.0 474.5 jit_solution(8866965221291635148)
XLA Ops:
  9.6 5.0 %collective-permute-start.4 = (bf16[3,24,768]{2,1,0:T(8,128)(2,1)}, bf16[3,24,768]{2,1,0:T(8,128)(2,1)}, u32[]{:S(2)}, u32[]{:S(2)}) collective-permute-start(bf16[3,24,768]{2,1,0:T(8,128)(2,1)} %pad_maximum_fusion.18), channel_id=1, source_target_pairs={{0,6},{2,0},{4,2},{6,4},{1,7},{3,1},{5,3},{7,5},{8,14},{10,8},{12,... | collective-permute-start | bytes 331784 | tf_op jit(solution)/shard_map/ppermute | solution.py:28
  19.6 2.9 collective-permute-start.13
  64.4 3.7 collective-permute-start.3
  70.2 3.7 collective-permute-start.1
  78.2 3.1 fusion.34
  89.1 4.2 collective-permute-done.16
  94.4 17.8 %collective-permute-done.11 = bf16[2,4,3,24,384]{4,3,1,2,0:T(8,128)(2,1)S(1)} collective-permute-done((bf16[2,4,3,24,384]{4,3,1,2,0:T(8,128)(2,1)S(1)}, bf16[2,4,3,24,384]{4,3,1,2,0:T(8,128)(2,1)S(1)}, u32[]{:S(2)}, u32[]{:S(2)}) %collective-permute-start.11) | collective-permute-done | bytes 442400 | tf_op jit(solution)/shard_map/ppermute | solution.py:28
  113.4 14.3 %collective-permute-done.20 = bf16[2,4,5,24,384]{4,3,1,2,0:T(8,128)(2,1)S(1)} collective-permute-done((bf16[2,4,5,24,384]{4,3,1,2,0:T(8,128)(2,1)S(1)}, bf16[2,4,5,24,384]{4,3,1,2,0:T(8,128)(2,1)S(1)}, u32[]{:S(2)}, u32[]{:S(2)}) %collective-permute-start.20) | collective-permute-done | bytes 737312 | tf_op jit(solution)/shard_map/ppermute | solution.py:28
  135.9 7.0 %shard_map.306 = bf16[512,768]{1,0:T(8,128)(2,1)S(1)} custom-call(bf16[512,768]{1,0:T(8,128)(2,1)S(1)} %convolution_convert_fusion.8.q_ref, bf16[512,768]{1,0:T(8,128)(2,1)S(1)} %convolution_convert_fusion.7.k_ref, bf16[512,768]{1,0:T(8,128)(2,1)S(1)} %convolution_convert_fusion.6.v_ref, f32[1,512,512]{2,1,0:T(8,128)S(1)} %compare_select_fusion.bias_ref), custom_call_target="tpu_custom_call" | custom-call | flops 1610612736 | bytes 3145728 | tf_op jit(solution)/shard_map/pallas_call | solution.py:184
  156.6 6.1 %shard_map.307 = bf16[512,768]{1,0:T(8,128)(2,1)S(1)} custom-call(bf16[512,768]{1,0:T(8,128)(2,1)S(1)} %convolution_convert_fusion.5.q_ref, bf16[308,768]{1,0:T(8,128)(2,1)S(1)} %fusion.44.k_ref, bf16[308,768]{1,0:T(8,128)(2,1)S(1)} %fusion.45.v_ref, f32[1,512,308]{2,1,0:T(8,128)S(1)} %and_select_fusion.bias_ref), custom_call_target="tpu_custom_call" | custom-call | flops 968884224 | bytes 3145728 | tf_op jit(solution)/shard_map/pallas_call | solution.py:184
  167.3 8.7 %multiply_convert_fusion = (bf16[512,3072]{1,0:T(8,128)(2,1)S(1)}, f32[512,3072]{1,0:T(8,128)}) fusion(bf16[512,768]{1,0:T(8,128)(2,1)S(1)} %add_convert_fusion.3, bf16[3072,1536]{1,0:T(8,128)(2,1)} %all-gather.2.cloned.1.call-done), kind=kOutput, calls=%fused_computation.17 | convolution fusion | flops 2430074880 | bytes 14942208 | tf_op jit(solution)/shard_map/dot_general | solution.py:131
  176.1 9.1 %fusion.6 = bf16[512,3072]{1,0:T(8,128)(2,1)S(1)} fusion(f32[512,3072]{1,0:T(8,128)} %get-tuple-element.235, bf16[512,768]{1,0:T(8,128)(2,1)S(1)} %copy-done.67, bf16[3072,1536]{1,0:T(8,128)(2,1)S(1)} %copy-done.101), kind=kOutput, calls=%fused_computation.16 | convolution fusion | flops 2447376384 | bytes 14942208 | tf_op jit(solution)/shard_map/dot_general | solution.py:131
  185.2 3.0 fusion.233
  188.3 5.0 %fusion.236 = (bf16[512,768]{1,0:T(8,128)(2,1)S(1)}, f32[512,768]{1,0:T(8,128)}, bf16[512,768]{1,0:T(8,128)(2,1)}, f32[512,768]{1,0:T(8,128)}) fusion(f32[512]{0:T(512)S(1)} %broadcast_multiply_fusion.4, f32[512,768]{1,0:T(8,128)S(1)} %copy-done.27, f32[512]{0:T(512)S(1)} %broadcast_multiply_fusion.6, f32[512]{0:T(512)S(1)} %broadcast_multiply_fusion.5, ...), kind=kOutput, calls=%fused_computation.565 | convolution fusion | flops 2423783424 | bytes 16557568 | tf_op jit(solution)/shard_map/dot_general | solution.py:123
  195.1 10.2 %shard_map.308 = (bf16[512,768]{1,0:T(8,128)(2,1)S(1)}, bf16[308,768]{1,0:T(8,128)(2,1)S(1)}, bf16[308,768]{1,0:T(8,128)(2,1)S(1)}) custom-call(bf16[512,768]{1,0:T(8,128)(2,1)S(1)} %copy-done.13, bf16[308,768]{1,0:T(8,128)(2,1)S(1)} %copy-done.9, bf16[308,768]{1,0:T(8,128)(2,1)S(1)} %copy-done.11, f32[1,308,512]{2,1,0:T(8,128)S(1)} %and_select_fusion.1.bias_ref, ...), custom_call_target="tpu_custom_call" | custom-call | flops 2422210560 | bytes 6291456 | tf_op jit(solution)/shard_map/pallas_call | solution.py:204
  211.1 15.2 %shard_map.309 = (bf16[512,768]{1,0:T(8,128)(2,1)S(1)}, bf16[512,768]{1,0:T(8,128)(2,1)S(1)}, bf16[512,768]{1,0:T(8,128)(2,1)S(1)}) custom-call(bf16[512,768]{1,0:T(8,128)(2,1)S(1)} %copy-done.19, bf16[512,768]{1,0:T(8,128)(2,1)S(1)} %copy-done.21, bf16[512,768]{1,0:T(8,128)(2,1)S(1)} %copy-done.23, f32[1,512,512]{2,1,0:T(8,128)} %copy-done.1, ...), custom_call_target="tpu_custom_call" | custom-call | flops 4026531840 | bytes 6291456 | tf_op jit(solution)/shard_map/pallas_call | solution.py:204
  239.8 4.3 collective-permute-start.30
  255.3 3.4 convolution_convert_fusion.2
  258.7 3.3 convolution_convert_fusion.1
  274.2 3.5 collective-permute-done.32
  289.0 3.0 collective-permute-done.28
  294.1 3.7 collective-permute-done.34
  343.8 18.0 %collective-permute-done.40 = bf16[3,4,24,384]{3,2,1,0:T(8,128)(2,1)S(1)} collective-permute-done((bf16[3,4,24,384]{3,2,1,0:T(8,128)(2,1)S(1)}, bf16[3,4,24,384]{3,2,1,0:T(8,128)(2,1)S(1)}, u32[]{:S(2)}, u32[]{:S(2)}) %collective-permute-start.40) | collective-permute-done | bytes 221216 | tf_op jit(solution)/shard_map/ppermute | solution.py:28
  363.0 4.6 collective-permute-done.42
  373.2 3.6 add_convert_fusion.1
  379.0 3.6 add_convert_fusion
  387.1 3.5 collective-permute-done.46
  393.6 16.6 %collective-permute-done.64 = bf16[2,4,2,96,384]{4,3,0,1,2:T(8,128)(2,1)S(1)} collective-permute-done((bf16[2,4,2,96,384]{4,3,0,1,2:T(8,128)(2,1)S(1)}, bf16[2,4,2,96,384]{4,3,0,1,2:T(8,128)(2,1)S(1)}, u32[]{:S(2)}, u32[]{:S(2)}) %collective-permute-start.64) | collective-permute-done | bytes 1179680 | tf_op jit(solution)/shard_map/ppermute | solution.py:28
  415.1 8.8 %collective-permute-done.65 = bf16[2,4,96,384]{3,2,0,1:T(8,128)(2,1)S(1)} collective-permute-done((bf16[2,4,96,384]{3,2,0,1:T(8,128)(2,1)S(1)}, bf16[2,4,96,384]{3,2,0,1:T(8,128)(2,1)S(1)}, u32[]{:S(2)}, u32[]{:S(2)}) %collective-permute-start.65) | collective-permute-done | bytes 589856 | tf_op jit(solution)/shard_map/ppermute | solution.py:28
  425.8 2.9 collective-permute-start.70
  436.2 14.0 %collective-permute-done.69 = bf16[2,192,384]{2,1,0:T(8,128)(2,1)S(1)} collective-permute-done((bf16[2,192,384]{2,1,0:T(8,128)(2,1)S(1)}, bf16[2,192,384]{2,1,0:T(8,128)(2,1)S(1)}, u32[]{:S(2)}, u32[]{:S(2)}) %collective-permute-start.69) | collective-permute-done | bytes 294944 | tf_op jit(solution)/shard_map/ppermute | solution.py:28
  451.0 6.2 %collective-permute-done.71 = bf16[2,192,384]{2,1,0:T(8,128)(2,1)S(1)} collective-permute-done((bf16[2,192,384]{2,1,0:T(8,128)(2,1)S(1)}, bf16[2,192,384]{2,1,0:T(8,128)(2,1)S(1)}, u32[]{:S(2)}, u32[]{:S(2)}) %collective-permute-start.71) | collective-permute-done | bytes 294944 | tf_op jit(solution)/shard_map/ppermute | solution.py:28
  (638 shorter events, 235.9 us)
Async XLA Ops:
  7.2 160.0 %all-gather.2.cloned.1.call-start = ((), (), s32[]{:S(2)}) async-start(), calls=%async_computation | async-start | bytes 9732096 | tf_op jit(solution)/shard_map/all_gather | solution.py:259
  9.6 42.3 %collective-permute-start.4 = (bf16[3,24,768]{2,1,0:T(8,128)(2,1)}, bf16[3,24,768]{2,1,0:T(8,128)(2,1)}, u32[]{:S(2)}, u32[]{:S(2)}) collective-permute-start(bf16[3,24,768]{2,1,0:T(8,128)(2,1)} %pad_maximum_fusion.18), channel_id=1, source_target_pairs={{0,6},{2,0},{4,2},{6,4},{1,7},{3,1},{5,3},{7,5},{8,14},{10,8},{12,... | collective-permute-start | bytes 331784 | tf_op jit(solution)/shard_map/ppermute | solution.py:28
  14.7 38.2 %collective-permute-start.5 = (bf16[3,24,768]{2,1,0:T(8,128)(2,1)}, bf16[3,24,768]{2,1,0:T(8,128)(2,1)}, u32[]{:S(2)}, u32[]{:S(2)}) collective-permute-start(bf16[3,24,768]{2,1,0:T(8,128)(2,1)} %pad_maximum_fusion.18), channel_id=1, source_target_pairs={{0,4},{2,6},{4,0},{6,2},{1,5},{3,7},{5,1},{7,3},{8,12},{10,14},{12... | collective-permute-start | bytes 331784 | tf_op jit(solution)/shard_map/ppermute | solution.py:28
  14.7 40.8 %collective-permute-start.6 = (bf16[3,24,768]{2,1,0:T(8,128)(2,1)}, bf16[3,24,768]{2,1,0:T(8,128)(2,1)}, u32[]{:S(2)}, u32[]{:S(2)}) collective-permute-start(bf16[3,24,768]{2,1,0:T(8,128)(2,1)} %pad_maximum_fusion.18), channel_id=1, source_target_pairs={{0,2},{2,4},{4,6},{6,0},{1,3},{3,5},{5,7},{7,1},{8,10},{10,12},{12... | collective-permute-start | bytes 331784 | tf_op jit(solution)/shard_map/ppermute | solution.py:28
  19.6 44.8 %collective-permute-start.13 = (bf16[5,24,768]{2,1,0:T(8,128)(2,1)S(1)}, bf16[5,24,768]{2,1,0:T(8,128)(2,1)}, u32[]{:S(2)}, u32[]{:S(2)}) collective-permute-start(bf16[5,24,768]{2,1,0:T(8,128)(2,1)S(1)} %constant_dynamic-update-slice_fusion), channel_id=1, source_target_pairs={{0,6},{2,0},{4,2},{6,4},{1,7},{3,1},{5,3},{7,5},{8,14},{10,8},{12,... | collective-permute-start | bytes 552968 | tf_op jit(solution)/shard_map/ppermute | solution.py:28
  46.3 23.0 %collective-permute-start.14 = (bf16[5,24,768]{2,1,0:T(8,128)(2,1)S(1)}, bf16[5,24,768]{2,1,0:T(8,128)(2,1)}, u32[]{:S(2)}, u32[]{:S(2)}) collective-permute-start(bf16[5,24,768]{2,1,0:T(8,128)(2,1)S(1)} %constant_dynamic-update-slice_fusion), channel_id=1, source_target_pairs={{0,4},{2,6},{4,0},{6,2},{1,5},{3,7},{5,1},{7,3},{8,12},{10,14},{12... | collective-permute-start | bytes 552968 | tf_op jit(solution)/shard_map/ppermute | solution.py:28
  60.0 21.3 %collective-permute-start.10 = (bf16[4,3,24,384]{3,2,0,1:T(8,128)(2,1)S(1)}, bf16[4,3,24,384]{3,2,0,1:T(8,128)(2,1)S(1)}, u32[]{:S(2)}, u32[]{:S(2)}) collective-permute-start(bf16[4,3,24,384]{3,2,0,1:T(8,128)(2,1)S(1)} %get-tuple-element.167), channel_id=1, source_target_pairs={{0,16},{16,0},{1,17},{17,1},{2,18},{18,2},{3,19},{19,3},{4,20},{20... | collective-permute-start | bytes 663560 | tf_op jit(solution)/shard_map/ppermute | solution.py:28
  81.4 30.9 %collective-permute-start.11 = (bf16[2,4,3,24,384]{4,3,1,2,0:T(8,128)(2,1)S(1)}, bf16[2,4,3,24,384]{4,3,1,2,0:T(8,128)(2,1)S(1)}, u32[]{:S(2)}, u32[]{:S(2)}) collective-permute-start(bf16[2,4,3,24,384]{4,3,1,2,0:T(8,128)(2,1)S(1)} %pad_maximum_fusion.12), channel_id=1, source_target_pairs={{0,1},{1,0},{2,3},{3,2},{4,5},{5,4},{6,7},{7,6},{8,9},{9,8},{10,11... | collective-permute-start | bytes 1327112 | tf_op jit(solution)/shard_map/ppermute | solution.py:28
  82.7 29.9 %collective-permute-start.8 = (bf16[2,4,3,24,384]{4,3,0,1,2:T(8,128)(2,1)S(1)}, bf16[2,4,3,24,384]{4,3,0,1,2:T(8,128)(2,1)S(1)}, u32[]{:S(2)}, u32[]{:S(2)}) collective-permute-start(bf16[2,4,3,24,384]{4,3,0,1,2:T(8,128)(2,1)S(1)} %pad_maximum_fusion.11), channel_id=1, source_target_pairs={{0,16},{16,0},{1,17},{17,1},{2,18},{18,2},{3,19},{19,3},{4,20},{20... | collective-permute-start | bytes 1327112 | tf_op jit(solution)/shard_map/ppermute | solution.py:28
  86.9 40.9 %collective-permute-start.20 = (bf16[2,4,5,24,384]{4,3,1,2,0:T(8,128)(2,1)S(1)}, bf16[2,4,5,24,384]{4,3,1,2,0:T(8,128)(2,1)S(1)}, u32[]{:S(2)}, u32[]{:S(2)}) collective-permute-start(bf16[2,4,5,24,384]{4,3,1,2,0:T(8,128)(2,1)S(1)} %pad_maximum_fusion.9), channel_id=1, source_target_pairs={{0,1},{1,0},{2,3},{3,2},{4,5},{5,4},{6,7},{7,6},{8,9},{9,8},{10,11... | collective-permute-start | bytes 2211848 | tf_op jit(solution)/shard_map/ppermute | solution.py:28
  93.4 36.0 %collective-permute-start.17 = (bf16[2,4,5,24,384]{4,3,0,1,2:T(8,128)(2,1)S(1)}, bf16[2,4,5,24,384]{4,3,0,1,2:T(8,128)(2,1)S(1)}, u32[]{:S(2)}, u32[]{:S(2)}) collective-permute-start(bf16[2,4,5,24,384]{4,3,0,1,2:T(8,128)(2,1)S(1)} %pad_maximum_fusion.8), channel_id=1, source_target_pairs={{0,16},{16,0},{1,17},{17,1},{2,18},{18,2},{3,19},{19,3},{4,20},{20... | collective-permute-start | bytes 2211848 | tf_op jit(solution)/shard_map/ppermute | solution.py:28
  233.5 38.4 %collective-permute-start.24 = (bf16[4,1536]{1,0:T(4,128)(2,1)S(1)}, bf16[4,1536]{1,0:T(4,128)(2,1)S(1)}, u32[]{:S(2)}, u32[]{:S(2)}) collective-permute-start(bf16[4,1536]{1,0:T(4,128)(2,1)S(1)} %pad_maximum_fusion.22), channel_id=1, source_target_pairs={{0,6},{2,0},{4,2},{6,4},{1,7},{3,1},{5,3},{7,5},{8,14},{10,8},{12,... | collective-permute-start | bytes 36872 | tf_op jit(solution)/shard_map/ppermute | solution.py:28
  235.0 37.6 %collective-permute-start.25 = (bf16[4,1536]{1,0:T(4,128)(2,1)S(1)}, bf16[4,1536]{1,0:T(4,128)(2,1)S(1)}, u32[]{:S(2)}, u32[]{:S(2)}) collective-permute-start(bf16[4,1536]{1,0:T(4,128)(2,1)S(1)} %pad_maximum_fusion.22), channel_id=1, source_target_pairs={{0,4},{2,6},{4,0},{6,2},{1,5},{3,7},{5,1},{7,3},{8,12},{10,14},{12... | collective-permute-start | bytes 36872 | tf_op jit(solution)/shard_map/ppermute | solution.py:28
  236.2 36.6 %collective-permute-start.26 = (bf16[4,1536]{1,0:T(4,128)(2,1)S(1)}, bf16[4,1536]{1,0:T(4,128)(2,1)S(1)}, u32[]{:S(2)}, u32[]{:S(2)}) collective-permute-start(bf16[4,1536]{1,0:T(4,128)(2,1)S(1)} %pad_maximum_fusion.22), channel_id=1, source_target_pairs={{0,2},{2,4},{4,6},{6,0},{1,3},{3,5},{5,7},{7,1},{8,10},{10,12},{12... | collective-permute-start | bytes 36872 | tf_op jit(solution)/shard_map/ppermute | solution.py:28
  239.8 33.6 %collective-permute-start.30 = (bf16[4,3072]{1,0:T(4,128)(2,1)S(1)}, bf16[4,3072]{1,0:T(4,128)(2,1)S(1)}, u32[]{:S(2)}, u32[]{:S(2)}) collective-permute-start(bf16[4,3072]{1,0:T(4,128)(2,1)S(1)} %pad_maximum_fusion.20), channel_id=1, source_target_pairs={{0,6},{2,0},{4,2},{6,4},{1,7},{3,1},{5,3},{7,5},{8,14},{10,8},{12,... | collective-permute-start | bytes 73736 | tf_op jit(solution)/shard_map/ppermute | solution.py:28
  244.2 29.4 %collective-permute-start.31 = (bf16[4,3072]{1,0:T(4,128)(2,1)S(1)}, bf16[4,3072]{1,0:T(4,128)(2,1)S(1)}, u32[]{:S(2)}, u32[]{:S(2)}) collective-permute-start(bf16[4,3072]{1,0:T(4,128)(2,1)S(1)} %pad_maximum_fusion.20), channel_id=1, source_target_pairs={{0,4},{2,6},{4,0},{6,2},{1,5},{3,7},{5,1},{7,3},{8,12},{10,14},{12... | collective-permute-start | bytes 73736 | tf_op jit(solution)/shard_map/ppermute | solution.py:28
  272.7 32.6 %collective-permute-start.38 = (bf16[768,384]{1,0:T(8,128)(2,1)}, bf16[768,384]{1,0:T(8,128)(2,1)}, u32[]{:S(2)}, u32[]{:S(2)}) collective-permute-start(bf16[768,384]{1,0:T(8,128)(2,1)} %convolution_convert_fusion.14), channel_id=1, source_target_pairs={{0,8},{8,0},{1,9},{9,1},{2,10},{10,2},{3,11},{11,3},{4,12},{12,4},... | collective-permute-start | bytes 1769480 | tf_op jit(solution)/shard_map/ppermute | solution.py:28
  272.8 34.8 %collective-permute-start.37 = (bf16[768,384]{1,0:T(8,128)(2,1)}, bf16[768,384]{1,0:T(8,128)(2,1)}, u32[]{:S(2)}, u32[]{:S(2)}) collective-permute-start(bf16[768,384]{1,0:T(8,128)(2,1)} %convolution_convert_fusion.15), channel_id=1, source_target_pairs={{0,8},{8,0},{1,9},{9,1},{2,10},{10,2},{3,11},{11,3},{4,12},{12,4},... | collective-permute-start | bytes 1769480 | tf_op jit(solution)/shard_map/ppermute | solution.py:28
  273.5 36.4 %collective-permute-start.36 = (bf16[768,384]{1,0:T(8,128)(2,1)}, bf16[768,384]{1,0:T(8,128)(2,1)}, u32[]{:S(2)}, u32[]{:S(2)}) collective-permute-start(bf16[768,384]{1,0:T(8,128)(2,1)} %convolution_convert_fusion.16), channel_id=1, source_target_pairs={{0,8},{8,0},{1,9},{9,1},{2,10},{10,2},{3,11},{11,3},{4,12},{12,4},... | collective-permute-start | bytes 1769480 | tf_op jit(solution)/shard_map/ppermute | solution.py:28
  273.6 39.1 %collective-permute-start.48 = (bf16[768,384]{1,0:T(8,128)(2,1)}, bf16[768,384]{1,0:T(8,128)(2,1)}, u32[]{:S(2)}, u32[]{:S(2)}) collective-permute-start(bf16[768,384]{1,0:T(8,128)(2,1)} %convolution_convert_fusion.13), channel_id=1, source_target_pairs={{0,8},{8,0},{1,9},{9,1},{2,10},{10,2},{3,11},{11,3},{4,12},{12,4},... | collective-permute-start | bytes 1769480 | tf_op jit(solution)/shard_map/ppermute | solution.py:28
  312.7 60.1 %collective-permute-start.62 = (bf16[3072,384]{1,0:T(8,128)(2,1)}, bf16[3072,384]{1,0:T(8,128)(2,1)}, u32[]{:S(2)}, u32[]{:S(2)}) collective-permute-start(bf16[3072,384]{1,0:T(8,128)(2,1)} %convolution_convert_fusion.2), channel_id=1, source_target_pairs={{0,8},{8,0},{1,9},{9,1},{2,10},{10,2},{3,11},{11,3},{4,12},{12,4},... | collective-permute-start | bytes 7077896 | tf_op jit(solution)/shard_map/ppermute | solution.py:28
  315.1 62.2 %collective-permute-start.63 = (bf16[3072,384]{1,0:T(8,128)(2,1)}, bf16[3072,384]{1,0:T(8,128)(2,1)}, u32[]{:S(2)}, u32[]{:S(2)}) collective-permute-start(bf16[3072,384]{1,0:T(8,128)(2,1)} %convolution_convert_fusion.1), channel_id=1, source_target_pairs={{0,8},{8,0},{1,9},{9,1},{2,10},{10,2},{3,11},{11,3},{4,12},{12,4},... | collective-permute-start | bytes 7077896 | tf_op jit(solution)/shard_map/ppermute | solution.py:28
  328.3 40.2 %collective-permute-start.53 = (bf16[5,4,2,24,384]{4,3,1,0,2:T(8,128)(2,1)}, bf16[5,4,2,24,384]{4,3,1,0,2:T(8,128)(2,1)}, u32[]{:S(2)}, u32[]{:S(2)}) collective-permute-start(bf16[5,4,2,24,384]{4,3,1,0,2:T(8,128)(2,1)} %dynamic-slice_bitcast_fusion.1), channel_id=1, source_target_pairs={{0,1},{1,0},{2,3},{3,2},{4,5},{5,4},{6,7},{7,6},{8,9},{9,8},{10,11... | collective-permute-start | bytes 2211848 | tf_op jit(solution)/shard_map/ppermute | solution.py:28
  339.3 31.3 %collective-permute-start.55 = (bf16[5,4,2,24,384]{4,3,2,1,0:T(8,128)(2,1)S(1)}, bf16[5,4,2,24,384]{4,3,2,1,0:T(8,128)(2,1)S(1)}, u32[]{:S(2)}, u32[]{:S(2)}) collective-permute-start(bf16[5,4,2,24,384]{4,3,2,1,0:T(8,128)(2,1)S(1)} %copy-done.76), channel_id=1, source_target_pairs={{0,16},{16,0},{1,17},{17,1},{2,18},{18,2},{3,19},{19,3},{4,20},{20... | collective-permute-start | bytes 2211848 | tf_op jit(solution)/shard_map/ppermute | solution.py:28
  383.1 27.0 %collective-permute-start.64 = (bf16[2,4,2,96,384]{4,3,0,1,2:T(8,128)(2,1)S(1)}, bf16[2,4,2,96,384]{4,3,0,1,2:T(8,128)(2,1)S(1)}, u32[]{:S(2)}, u32[]{:S(2)}) collective-permute-start(bf16[2,4,2,96,384]{4,3,0,1,2:T(8,128)(2,1)S(1)} %fusion.52), channel_id=1, source_target_pairs={{0,1},{1,0},{2,3},{3,2},{4,5},{5,4},{6,7},{7,6},{8,9},{9,8},{10,11... | collective-permute-start | bytes 3538952 | tf_op jit(solution)/shard_map/ppermute | solution.py:28
  386.6 24.9 %collective-permute-start.66 = (bf16[2,4,2,96,384]{4,3,0,1,2:T(8,128)(2,1)S(1)}, bf16[2,4,2,96,384]{4,3,0,1,2:T(8,128)(2,1)S(1)}, u32[]{:S(2)}, u32[]{:S(2)}) collective-permute-start(bf16[2,4,2,96,384]{4,3,0,1,2:T(8,128)(2,1)S(1)} %fusion.48), channel_id=1, source_target_pairs={{0,16},{16,0},{1,17},{17,1},{2,18},{18,2},{3,19},{19,3},{4,20},{20... | collective-permute-start | bytes 3538952 | tf_op jit(solution)/shard_map/ppermute | solution.py:28
  390.6 23.0 %collective-permute-start.47 = (bf16[2,3,48,384]{3,2,1,0:T(8,128)(2,1)S(1)}, bf16[2,3,48,384]{3,2,1,0:T(8,128)(2,1)S(1)}, u32[]{:S(2)}, u32[]{:S(2)}) collective-permute-start(bf16[2,3,48,384]{3,2,1,0:T(8,128)(2,1)S(1)} %pad_maximum_fusion.15), channel_id=1, source_target_pairs={{0,8},{8,0},{1,9},{9,1},{2,10},{10,2},{3,11},{11,3},{4,12},{12,4},... | collective-permute-start | bytes 663560 | tf_op jit(solution)/shard_map/ppermute | solution.py:28
  391.0 37.7 %collective-permute-start.59 = (bf16[5,48,384]{2,1,0:T(8,128)(2,1)S(1)}, bf16[5,48,384]{2,1,0:T(8,128)(2,1)S(1)}, u32[]{:S(2)}, u32[]{:S(2)}) collective-permute-start(bf16[5,48,384]{2,1,0:T(8,128)(2,1)S(1)} %get-tuple-element.182), channel_id=1, source_target_pairs={{0,6},{2,0},{4,2},{6,4},{1,7},{3,1},{5,3},{7,5},{8,14},{10,8},{12,... | collective-permute-start | bytes 552968 | tf_op jit(solution)/shard_map/ppermute | solution.py:28
  393.0 39.9 %collective-permute-start.58 = (bf16[5,48,384]{2,1,0:T(8,128)(2,1)S(1)}, bf16[5,48,384]{2,1,0:T(8,128)(2,1)S(1)}, u32[]{:S(2)}, u32[]{:S(2)}) collective-permute-start(bf16[5,48,384]{2,1,0:T(8,128)(2,1)S(1)} %get-tuple-element.181), channel_id=1, source_target_pairs={{0,4},{2,6},{4,0},{6,2},{1,5},{3,7},{5,1},{7,3},{8,12},{10,14},{12... | collective-permute-start | bytes 552968 | tf_op jit(solution)/shard_map/ppermute | solution.py:28
  410.1 22.8 %collective-permute-start.57 = (bf16[5,48,384]{2,1,0:T(8,128)(2,1)S(1)}, bf16[5,48,384]{2,1,0:T(8,128)(2,1)S(1)}, u32[]{:S(2)}, u32[]{:S(2)}) collective-permute-start(bf16[5,48,384]{2,1,0:T(8,128)(2,1)S(1)} %get-tuple-element.180), channel_id=1, source_target_pairs={{0,2},{2,4},{4,6},{6,0},{1,3},{3,5},{5,7},{7,1},{8,10},{10,12},{12... | collective-permute-start | bytes 552968 | tf_op jit(solution)/shard_map/ppermute | solution.py:28
  428.7 21.5 %collective-permute-start.69 = (bf16[2,192,384]{2,1,0:T(8,128)(2,1)S(1)}, bf16[2,192,384]{2,1,0:T(8,128)(2,1)S(1)}, u32[]{:S(2)}, u32[]{:S(2)}) collective-permute-start(bf16[2,192,384]{2,1,0:T(8,128)(2,1)S(1)} %get-tuple-element.163), channel_id=1, source_target_pairs={{0,4},{2,6},{4,0},{6,2},{1,5},{3,7},{5,1},{7,3},{8,12},{10,14},{12... | collective-permute-start | bytes 884744 | tf_op jit(solution)/shard_map/ppermute | solution.py:28
  428.7 21.5 %collective-permute-start.68 = (bf16[2,192,384]{2,1,0:T(8,128)(2,1)S(1)}, bf16[2,192,384]{2,1,0:T(8,128)(2,1)S(1)}, u32[]{:S(2)}, u32[]{:S(2)}) collective-permute-start(bf16[2,192,384]{2,1,0:T(8,128)(2,1)S(1)} %get-tuple-element.162), channel_id=1, source_target_pairs={{0,2},{2,4},{4,6},{6,0},{1,3},{3,5},{5,7},{7,1},{8,10},{10,12},{12... | collective-permute-start | bytes 884744 | tf_op jit(solution)/shard_map/ppermute | solution.py:28
  (156 other events, 1282.4 us)
Sparse Core Ops, SparseCore 0:
  24.7 106.0 all-gather.1

commit v2 on v1

v2 whole, which is shorter than its diff:
```python
from functools import partial

import jax
import jax.numpy as jnp
from jax import lax
from jax.experimental import pallas as pl
from jax.experimental.pallas import tpu as pltpu
from jax.sharding import Mesh, PartitionSpec as P

HEADS = 12
HD = 64
CAPTION = 77
SEGS = 4

QUAD = 4 * HD
highest = lax.Precision.HIGHEST
epsilon = 1e-06
masked_score = -1e30
bf16 = jnp.bfloat16
f32 = jnp.float32
FINE = ("y", "core", "za", "zb", "x")
MP_AXES = ("za", "zb", "x")
VMEM = 48 << 20


def shifted(value, axis, steps):
    count = lax.axis_size(axis)
    with jax.named_scope(f"to_{axis}_{steps}"):
        return lax.ppermute(value, axis, [(k, (k + steps) % count) for k in range(count)])


def gather_axis(value, axis, *hold):
    count = lax.axis_size(axis)
    me = lax.axis_index(axis)
    pieces = [shifted(value, axis, s) for s in range(1, count)]
    if hold:
        pieces = [after(piece, *hold) for piece in pieces]
    pieces = [value] + pieces

    def at(place):
        turn = (me - place) % count
        chosen = pieces[0]
        for s in range(1, count):
            chosen = jnp.where(turn == s, pieces[s], chosen)
        return chosen

    return jnp.stack([at(place) for place in range(count)])


def after(value, *done):
    return lax.optimization_barrier((value, *done))[0]


def picked(terms, dim, which):
    return [lax.dynamic_index_in_dim(t, which, dim, keepdims=False) for t in terms]


def summed(terms):
    total = terms[0].astype(f32)
    for term in terms[1:]:
        total = total + term.astype(f32)
    return total


def launch(terms, axis, dim):
    count = lax.axis_size(axis)
    me = lax.axis_index(axis)
    sent = [
        summed(picked(terms, dim, (me + s) % count)).astype(bf16) for s in range(1, count)
    ]
    arrived = [shifted(part, axis, s) for s, part in enumerate(sent, 1)]
    return picked(terms, dim, me), sent, arrived


def launch_wide(value, axis, dim):
    count = lax.axis_size(axis)
    me = lax.axis_index(axis)
    sent = [picked([value], dim, (me + s) % count)[0] for s in range(1, count)]
    arrived = [shifted(part, axis, s) for s, part in enumerate(sent, 1)]
    return picked([value], dim, me), sent, arrived


def landed(started, *done):
    kept, _, arrived = started
    if done:
        arrived = [after(part, *done) for part in arrived]
    return kept + arrived


def split_rows(part):
    grid = [lax.axis_size(a) for a in (*MP_AXES, "y")]
    return part.reshape(part.shape[0], *grid, -1, part.shape[-1])


def first_stage(mine_a, mine_b, other_a, other_b, *done):
    other_a, other_b = shifted(other_a, "core", 1), shifted(other_b, "core", 1)
    if done:
        other_a, other_b = after(other_a, *done), after(other_b, *done)
    left = [split_rows(mine_a), split_rows(other_a)]
    right = [split_rows(mine_b), split_rows(other_b)]
    return launch(left, "x", 3), launch(right, "y", 4)


def second_stage(stage, *done):
    left = launch(landed(stage[0], *done), "y", 3)
    right = launch(landed(stage[1], *done), "x", 3)
    return left, right


def third_stage(stage, *done):
    left, right = (summed(landed(part, *done)).astype(bf16) for part in stage)
    return launch([jnp.stack([left, right])], "zb", 3)


def fourth_stage(stage, *done):
    return launch(landed(stage, *done), "za", 2)


def sends(stage):
    return stage[0][1] + stage[1][1]


def assemble(left, right):
    left = left.transpose(5, 4, 3, 2, 1, 0, 6, 7)
    right = right.transpose(5, 4, 3, 1, 2, 0, 6, 7)
    whole = jnp.concatenate([left, right], axis=-1)
    return whole.reshape(whole.shape[0], -1, whole.shape[-1])


def parts_kernel(mine_ref, *refs):
    *sources, up_ref, down_ref, first_ref, more_ref, feed_ref, turned_ref, tall_ref = refs
    rows, hidden = first_ref.shape[1], feed_ref.shape[1]
    width = down_ref.shape[1]

    def own(ref, count):
        return ref[pl.ds(pl.multiple_of(mine_ref[0] * count, 8), count), :]

    for which, source in enumerate(sources):
        shard = source[...].astype(f32)
        turned_ref[...] = shard.T if shard.shape[1] < width else shard
        target, place = (first_ref, which) if which < 3 else (more_ref, which - 3)
        target[place] = own(turned_ref, rows).astype(bf16)
    tall_ref[...] = up_ref[...].astype(f32).T
    feed_ref[0] = own(tall_ref, hidden).astype(bf16)
    tall_ref[...] = down_ref[...].astype(f32)
    feed_ref[1] = own(tall_ref, hidden).astype(bf16)


def weight_parts(weights, up_weight, down_weight):
    copies = lax.axis_size("y") * lax.axis_size("core")
    mine = lax.axis_index("y") * lax.axis_size("core") + lax.axis_index("core")
    hidden, width = down_weight.shape
    shard = min(weights[0].shape)
    rows = shard // copies
    if rows % 8 or hidden // copies % 8:

        def own(value):
            part = value.shape[0] // copies
            return lax.dynamic_slice_in_dim(value, mine * part, part, 0)

        turned = [own(w.T if w.shape[1] < width else w) for w in weights]
        feed_part = jnp.stack([own(up_weight.T), own(down_weight)])
        return jnp.stack(turned[:3]), jnp.stack(turned[3:]), feed_part
    shapes = [
        (3, rows, width),
        (len(weights) - 3, rows, width),
        (2, hidden // copies, width),
    ]

    def whole(shape):
        return pl.BlockSpec(shape, lambda i: (0,) * len(shape))

    sources = [*weights, up_weight, down_weight]
    return pl.pallas_call(
        parts_kernel,
        grid=(1,),
        in_specs=[pl.BlockSpec(memory_space=pltpu.SMEM)] + [whole(w.shape) for w in sources],
        out_specs=[whole(shape) for shape in shapes],
        out_shape=[jax.ShapeDtypeStruct(shape, bf16) for shape in shapes],
        scratch_shapes=[pltpu.VMEM((shard, width), f32), pltpu.VMEM((hidden, width), f32)],
        compiler_params=pltpu.CompilerParams(vmem_limit_bytes=VMEM),
    )(mine.reshape(1), *sources)


def columns_whole(done):
    done = gather_axis(gather_axis(done, "y"), "core")
    done = done.transpose(2, 3, 1, 4, 0, 5)
    return done.reshape(-1, done.shape[2] * done.shape[3], done.shape[4] * done.shape[5])


def rows_whole(done):
    done = gather_axis(gather_axis(done, "y"), "core")
    done = done.transpose(2, 3, 0, 1, 4, 5)
    return done.reshape(done.shape[0], -1, done.shape[5])


def normalize(values):
    centre = values - jnp.mean(values, axis=-1, keepdims=True)
    inverse = lax.rsqrt(jnp.mean(centre * centre, axis=-1, keepdims=True) + epsilon)
    return (centre * inverse, inverse)


def norm_back(normed, inverse, upstream):
    mean_grad = jnp.mean(upstream, axis=-1, keepdims=True)
    mean_both = jnp.mean(upstream * normed, axis=-1, keepdims=True)
    return inverse * (upstream - mean_grad - normed * mean_both)


def matmul(left, right):
    return jnp.dot(left, right, preferred_element_type=f32)


def inner_rows(left, right):
    return lax.dot_general(left, right, (((0,), (0,)), ((), ())), preferred_element_type=f32)


def outer_cols(left, right):
    return lax.dot_general(left, right, (((1,), (1,)), ((), ())), preferred_element_type=f32)


def gelu_back(pre_act, upstream):
    return jax.vjp(partial(jax.nn.gelu, approximate=True), pre_act)[1](upstream)[0]


def silu_back(inputs, upstream):
    return jax.vjp(jax.nn.silu, inputs)[1](upstream)[0]


def own_lanes(head):
    lane = lax.broadcasted_iota(jnp.int32, (1, QUAD), 1)
    return (lane >= head * HD) & (lane < (head + 1) * HD)


def merged(parts):
    whole = parts[0]
    for head in range(1, len(parts)):
        whole = jnp.where(own_lanes(head), parts[head], whole)
    return whole


def forward_kernel(q_ref, k_ref, v_ref, bias_ref, mix_ref):
    query = q_ref[...] * bf16(HD**-0.5)
    keys, values, bias = k_ref[...], v_ref[...], bias_ref[0]
    parts = []
    for head in range(QUAD // HD):
        own = jnp.where(own_lanes(head), query, bf16(0))
        scores = outer_cols(own, keys) + bias
        raised = jnp.exp(scores - jnp.max(scores, axis=1, keepdims=True))
        total = jnp.sum(raised, axis=1, keepdims=True)
        parts.append(matmul(raised.astype(bf16), values) / total)
    mix_ref[...] = merged(parts).astype(bf16)


def backward_kernel(
    core_ref,
    q_ref,
    k_ref,
    v_ref,
    mix_ref,
    bias_ref,
    out_w_ref,
    q_w_ref,
    k_w_ref,
    v_w_ref,
    back_ref,
    x_ref,
    *rest,
):
    *source, in_ref, mine_a, mine_b, other_a, other_b = rest
    text_ref, text_grad_ref = source if source else (x_ref, in_ref)
    query = q_ref[...] * bf16(HD**-0.5)
    keys, values, bias = k_ref[...], v_ref[...], bias_ref[0]
    back = back_ref[...]
    grad = outer_cols(back, out_w_ref[...]).astype(bf16)
    gq, gk, gv = [], [], []
    for head in range(QUAD // HD):
        own = own_lanes(head)
        scores = outer_cols(keys, jnp.where(own, query, bf16(0))) + bias
        raised = jnp.exp(scores - jnp.max(scores, axis=0, keepdims=True))
        weights = raised * (1.0 / jnp.sum(raised, axis=0, keepdims=True))
        grad_weights = outer_cols(jnp.where(own, values, bf16(0)), grad)
        mean = jnp.sum(weights * grad_weights, axis=0, keepdims=True)
        grad_scores = (weights * (grad_weights - mean)).astype(bf16)
        gv.append(matmul(weights.astype(bf16), grad))
        gk.append(matmul(grad_scores, query))
        gq.append(inner_rows(grad_scores, keys))
    gq = (merged(gq) * HD**-0.5).astype(bf16)
    gk, gv = merged(gk).astype(bf16), merged(gv).astype(bf16)

    @pl.when(pl.program_id(1) == 0)
    def _():
        in_ref[...] = jnp.zeros_like(in_ref)
        if source:
            text_grad_ref[...] = jnp.zeros_like(text_grad_ref)

    if source:
        in_ref[...] += matmul(gq, q_w_ref[...])
        text_grad_ref[...] += matmul(gk, k_w_ref[...]) + matmul(gv, v_w_ref[...])
    else:
        in_ref[...] += (
            matmul(gq, q_w_ref[...]) + matmul(gk, k_w_ref[...]) + matmul(gv, v_w_ref[...])
        )
    half = mine_a.shape[-1]
    first = core_ref[0] == 0
    mine, other = (mine_a, mine_b), (other_a, other_b)
    pairs = [(mix_ref[...], back), (gq, x_ref[...]), (gk, text_ref[...]), (gv, text_ref[...])]
    for which, (left, right) in enumerate(pairs):
        whole = inner_rows(left, right).astype(bf16)
        low, high = whole[:, :half], whole[:, half:]
        mine[which // 2][which % 2] = jnp.where(first, low, high)
        other[which // 2][which % 2] = jnp.where(first, high, low)


def attend(query, keys, values, bias):
    rows, frames, tokens = bias.shape
    pairs = query.shape[1] // QUAD
    blocks = [pl.BlockSpec((n, QUAD), lambda r, h: (r, h)) for n in (frames, tokens, tokens)]
    return pl.pallas_call(
        forward_kernel,
        grid=(rows, pairs),
        in_specs=blocks + [pl.BlockSpec((1, frames, tokens), lambda r, h: (r, 0, 0))],
        out_specs=blocks[0],
        out_shape=jax.ShapeDtypeStruct(query.shape, bf16),
        compiler_params=pltpu.CompilerParams(vmem_limit_bytes=VMEM),
        cost_estimate=pl.CostEstimate(flops=0, transcendentals=0, bytes_accessed=0),
    )(query, keys, values, bias)


def attend_back(core, query, keys, values, mix, bias, weights, back, x, text=None):
    rows, tokens, frames = bias.shape
    width = query.shape[1]
    pairs, half = width // QUAD, width // 2
    wide = pl.BlockSpec((frames, QUAD), lambda r, h, c: (r, h))
    held = pl.BlockSpec((tokens, QUAD), lambda r, h, c: (r, h))
    matrix = pl.BlockSpec((QUAD, width), lambda r, h, c: (h, 0))
    frames_all = pl.BlockSpec((frames, width), lambda r, h, c: (r, 0))
    tokens_all = pl.BlockSpec((tokens, width), lambda r, h, c: (r, 0))
    grads = pl.BlockSpec((2, QUAD, half), lambda r, h, c: (0, h, 0))
    grads_shape = jax.ShapeDtypeStruct((2, width, half), bf16)
    cross = text is not None
    return pl.pallas_call(
        backward_kernel,
        grid_spec=pltpu.PrefetchScalarGridSpec(
            num_scalar_prefetch=1,
            grid=(rows, pairs),
            in_specs=[wide, held, held, wide]
            + [pl.BlockSpec((1, tokens, frames), lambda r, h, c: (r, 0, 0))]
            + [matrix] * 4
            + [frames_all] * 2
            + [tokens_all] * cross,
            out_specs=[tokens_all] * cross + [frames_all] + [grads] * 4,
        ),
        out_shape=[jax.ShapeDtypeStruct((rows * tokens, width), f32)] * cross
        + [jax.ShapeDtypeStruct(x.shape, f32)]
        + [grads_shape] * 4,
        compiler_params=pltpu.CompilerParams(vmem_limit_bytes=VMEM),
        cost_estimate=pl.CostEstimate(flops=0, transcendentals=0, bytes_accessed=0),
    )(core, query, keys, values, mix, bias, *weights, back, x, *([text] if cross else []))


def feed_kernel(
    core_ref, x_ref, g_ref, up_ref, down_ref, up_far, down_far, out_ref, back_ref, *rest
):
    *grads, xt_ref, gt_ref = rest
    slope = (2.0 / jnp.pi) ** 0.5

    @pl.when(pl.program_id(0) == 0)
    def _():
        out_ref[...] = jnp.zeros_like(out_ref)
        back_ref[...] = jnp.zeros_like(back_ref)
        xt_ref[...] = x_ref[...].T
        gt_ref[...] = g_ref[...].T

    def joined(near, far):
        first = core_ref[0] == 0
        parts = []
        for x in range(near.shape[1]):
            for y in range(near.shape[0]):
                here, there = near[y, x, 0, 0], far[y, x, 0, 0]
                parts += [jnp.where(first, here, there), jnp.where(first, there, here)]
        return jnp.concatenate(parts, axis=0)

    up, down = joined(up_ref, up_far), joined(down_ref, down_far)
    pre = outer_cols(x_ref[...], up)
    square = pre * pre
    bent = jnp.tanh(slope * pre * (1.0 + 0.044715 * square))
    rise = 0.5 * (1.0 + bent)
    active = (pre * rise).astype(bf16)
    steep = rise + 0.5 * pre * (1.0 - bent * bent) * (slope * (1.0 + 0.134145 * square))
    grad_pre = (outer_cols(g_ref[...], down) * steep).astype(bf16)
    out_ref[...] += matmul(active, down)
    back_ref[...] += matmul(grad_pre, up)
    shards, half, block = grads[0].shape
    lanes = [slice(n * block, (n + 1) * block) for n in range(shards)]
    for which, (left, right) in enumerate([(xt_ref, grad_pre), (gt_ref, active)]):
        for target, core in ((grads[which], core_ref[0]), (grads[which + 2], 1 - core_ref[0])):
            rows = left[pl.ds(pl.multiple_of(core * half, half), half), :]
            product = matmul(rows, right).astype(bf16)
            for n in range(shards):
                target[n] = product[:, lanes[n]]


def feed(core, third_in, grad_mlp, weights):
    tokens, width = third_in.shape
    ny, nx, zb, za, rows, _ = weights[0].shape
    nz = za * zb
    block, half = ny * rows * 2, width // 2
    whole = pl.BlockSpec((tokens, width), lambda j, c: (0, 0))
    parts = pl.BlockSpec((nx, half, block), lambda j, c: (j, 0, 0))
    matrix = pl.BlockSpec(
        (ny, nx, 1, 1, rows, width), lambda j, c: (0, 0, j % zb, j // zb, 0, 0)
    )
    hidden = nx * nz * block
    return pl.pallas_call(
        feed_kernel,
        grid_spec=pltpu.PrefetchScalarGridSpec(
            num_scalar_prefetch=1,
            grid=(nz,),
            in_specs=[whole] * 2 + [matrix] * 4,
            out_specs=[whole] * 2 + [parts] * 4,
            scratch_shapes=[pltpu.VMEM((width, tokens), bf16)] * 2,
        ),
        out_shape=[
            jax.ShapeDtypeStruct((tokens, width), f32),
            jax.ShapeDtypeStruct((tokens, width), f32),
        ]
        + [jax.ShapeDtypeStruct((nx * nz, half, block), bf16)] * 4,
        compiler_params=pltpu.CompilerParams(vmem_limit_bytes=VMEM),
        cost_estimate=pl.CostEstimate(flops=0, transcendentals=0, bytes_accessed=0),
    )(core, third_in, grad_mlp, *weights)


def shards(
    frames,
    seg_ids,
    text,
    text_lens,
    step_ids,
    step_table,
    ada_weight,
    ada_bias,
    query_w,
    key_w,
    value_w,
    out_w,
    cross_query_w,
    cross_key_w,
    cross_value_w,
    cross_out_w,
    up_weight,
    down_weight,
    out_grad,
):
    width = frames.shape[1]
    za, zb, nx = (lax.axis_size(axis) for axis in MP_AXES)
    mp = za * zb * nx
    position = (lax.axis_index("za") * zb + lax.axis_index("zb")) * nx + lax.axis_index("x")
    rows_dev = seg_ids.shape[0] // mp
    frames_row = seg_ids.shape[1]
    segs_dev = rows_dev * SEGS
    my_ids = lax.dynamic_slice_in_dim(seg_ids, position * rows_dev, rows_dev, 0)
    my_lens = lax.dynamic_slice_in_dim(text_lens, position * segs_dev, segs_dev, 0)

    half = width // 2
    first, more, feed_part = weight_parts(
        [
            query_w,
            key_w,
            value_w,
            out_w,
            cross_query_w,
            cross_key_w,
            cross_value_w,
            cross_out_w,
        ],
        up_weight,
        down_weight,
    )
    first = gather_axis(gather_axis(first, "za"), "zb")
    more = gather_axis(more, "za", first)
    first_left = gather_axis(first[..., :half], "x")
    first_right = gather_axis(first[..., half:], "y")
    more = gather_axis(more, "zb", first_left, first_right)
    first_left = gather_axis(first_left, "y")
    first_right = gather_axis(first_right, "x")
    feed_part = gather_axis(feed_part, "za", more)
    more_left = gather_axis(more[..., :half], "x", first_left, first_right)
    more_right = gather_axis(more[..., half:], "y", first_left, first_right)
    qkv = assemble(gather_axis(first_left, "core"), gather_axis(first_right, "core"))
    qkv = qkv.reshape(-1, width)
    feed_part = gather_axis(feed_part, "zb", more_left, more_right)

    table_low = step_table
    choose_step = (step_ids[:, None] == jnp.arange(step_table.shape[0])[None, :]).astype(bf16)
    silu_mine = jax.nn.silu(matmul(choose_step, table_low)).astype(bf16)
    partial_mod = matmul(silu_mine, ada_weight)
    partial_mod = partial_mod.reshape(za, zb, nx, segs_dev, partial_mod.shape[1])
    modulation = summed(landed(launch_wide(partial_mod, "x", 2))).astype(bf16)
    modulation = summed(landed(launch([modulation], "zb", 1))).astype(bf16)
    modulation = summed(landed(launch([modulation], "za", 0)))
    modulation = modulation + ada_bias.astype(f32)
    flat_ids = my_ids.reshape(-1)
    row_of = jnp.arange(flat_ids.shape[0]) // frames_row
    clip = flat_ids + row_of * SEGS
    chosen = clip[:, None] == jnp.arange(segs_dev)[None, :]

    def per_frame(index):
        table = modulation[:, index * width : (index + 1) * width]
        value = jnp.broadcast_to(table[0:1], (clip.shape[0], width))
        for segment in range(1, segs_dev):
            value = jnp.where(chosen[:, segment : segment + 1], table[segment : segment + 1], value)
        return value

    shift_one, scale_one, gate_one, shift_two, scale_two, gate_two = map(per_frame, range(6))

    same_seg = my_ids[:, :, None] == my_ids[:, None, :]
    self_bias = jnp.where(same_seg, 0.0, masked_score).astype(f32)
    key_segment = jnp.arange(SEGS * CAPTION) // CAPTION
    valid_key = (
        jnp.arange(CAPTION)[None, None, :] < my_lens.reshape(rows_dev, SEGS)[:, :, None]
    ).reshape(rows_dev, SEGS * CAPTION)
    allowed = (my_ids[:, :, None] == key_segment[None, None, :]) & valid_key[:, None, :]
    cross_bias = jnp.where(allowed, 0.0, masked_score).astype(f32)
    allowed_t = (my_ids[:, None, :] == key_segment[None, :, None]) & valid_key[:, :, None]
    cross_bias_t = jnp.where(allowed_t, 0.0, masked_score).astype(f32)

    base = frames.astype(f32)
    text_flat = text.reshape(-1, width)
    normed_one, inverse_one = normalize(base)
    first_in = (normed_one * (1.0 + scale_one) + shift_one).astype(bf16)
    query, keys, values = (
        outer_cols(first_in, qkv[i * width : (i + 1) * width]).astype(bf16) for i in range(3)
    )
    self_mix = attend(query, keys, values, self_bias)
    more_left = gather_axis(more_left, "y", self_mix)
    more_right = gather_axis(more_right, "x", self_mix)
    feed_up = gather_axis(feed_part[:, :, 0], "x", self_mix)
    feed_down = gather_axis(feed_part[:, :, 1], "y", self_mix)
    whole = assemble(gather_axis(more_left, "core"), gather_axis(more_right, "core"))
    out_full, cquery_t, cout_full = whole[0], whole[1], whole[4]
    ckv_t = whole[2:4].reshape(-1, width)
    self_out = matmul(self_mix, out_full)
    resid_one = base + gate_one * self_out
    normed_two, inverse_two = normalize(resid_one)
    second_in = normed_two.astype(bf16)
    cross_query = outer_cols(second_in, cquery_t).astype(bf16)
    cross_keys = outer_cols(text_flat, ckv_t[:width]).astype(bf16)
    cross_values = outer_cols(text_flat, ckv_t[width:]).astype(bf16)
    cross_mix = attend(cross_query, cross_keys, cross_values, cross_bias)
    resid_two = resid_one + matmul(cross_mix, cout_full)
    normed_three, inverse_three = normalize(resid_two)
    third_in = (normed_three * (1.0 + scale_two) + shift_two).astype(bf16)
    upstream = out_grad.astype(f32)
    grad_mlp = (gate_two * upstream).astype(bf16)
    core = lax.axis_index("core").reshape(1)
    feed_up = gather_axis(feed_up, "y", cross_mix)
    feed_down = gather_axis(feed_down, "x", cross_mix).swapaxes(0, 1)
    feed_weights = [feed_up, feed_down] + [shifted(w, "core", 1) for w in (feed_up, feed_down)]
    mlp_out, grad_third, *ff_parts = feed(core, third_in, grad_mlp, feed_weights)
    layer_out = (resid_two + gate_two * mlp_out).astype(bf16)

    grad_gate_two = upstream * mlp_out
    with jax.named_scope("feed_sums_first_stage"):
        feed_sums = first_stage(*[part[None] for part in ff_parts])
    grad_resid_two = upstream + norm_back(
        normed_three, inverse_three, grad_third * (1.0 + scale_two)
    )
    grad_cross = after(grad_resid_two.astype(bf16), *sends(feed_sums))
    grad_text, grad_second, *cross_parts = attend_back(
        core,
        cross_query,
        cross_keys,
        cross_values,
        cross_mix,
        cross_bias_t,
        [cout_full, cquery_t, ckv_t[:width], ckv_t[width:]],
        grad_cross,
        second_in,
        text_flat,
    )
    with jax.named_scope("cross_sums_first_stage"):
        cross_sums = first_stage(*cross_parts)
    with jax.named_scope("feed_sums_second_stage"):
        feed_sums = second_stage(feed_sums, grad_second)
    grad_resid_one = grad_resid_two + norm_back(normed_two, inverse_two, grad_second)
    grad_gate_one = grad_resid_one * self_out
    grad_self = after(
        (gate_one * grad_resid_one).astype(bf16), *sends(cross_sums), *sends(feed_sums)
    )
    grad_first, *self_parts = attend_back(
        core,
        query,
        keys,
        values,
        self_mix,
        self_bias,
        [out_full, qkv[:width], qkv[width : 2 * width], qkv[2 * width :]],
        grad_self,
        first_in,
    )
    with jax.named_scope("feed_sums_third_stage"):
        feed_sums = third_stage(feed_sums, grad_first)
    with jax.named_scope("self_sums_first_stage"):
        self_sums = first_stage(*self_parts, *feed_sums[1])
    with jax.named_scope("cross_sums_second_stage"):
        cross_sums = second_stage(cross_sums, *sends(self_sums))

    chooser = chosen.astype(f32)
    grad_first = after(grad_first, *sends(cross_sums))
    mod_parts = [
        grad_first,
        grad_first * normed_one,
        grad_gate_one,
        grad_third,
        grad_third * normed_three,
        grad_gate_two,
    ]
    grad_mod = jnp.stack(
        [
            lax.dot_general(chooser, v, (((0,), (0,)), ((), ())), precision=highest)
            for v in mod_parts
        ]
    ).astype(bf16)
    steps_all = after(step_ids.astype(f32), grad_mod)
    with jax.named_scope("self_sums_second_stage"):
        self_sums = second_stage(self_sums, grad_mod)
    with jax.named_scope("cross_sums_third_stage"):
        cross_sums = third_stage(cross_sums, *sends(self_sums))
    gathered = gather_axis(grad_mod, "za", *cross_sums[1])
    with jax.named_scope("self_sums_third_stage"):
        self_sums = third_stage(self_sums, gathered)
    gathered = gather_axis(gathered, "zb", *self_sums[1])
    feed_sums = fourth_stage(feed_sums, gathered)
    gathered = gather_axis(gathered, "x", *feed_sums[1])
    cross_sums = fourth_stage(cross_sums, gathered)
    self_sums = fourth_stage(self_sums, *cross_sums[1])
    feed_done = summed(landed(feed_sums, gathered)).astype(bf16)
    gathered = gather_axis(gathered, "y", feed_done)
    steps_all = gather_axis(steps_all, "y", feed_done)
    cross_done = summed(landed(cross_sums, gathered)).astype(bf16)
    gathered = gather_axis(gathered, "core", cross_done)
    steps_all = gather_axis(steps_all, "core", cross_done).transpose(1, 0, 2).reshape(-1)
    grad_mod_all = gathered.transpose(1, 0, 4, 3, 2, 6, 5, 7).reshape(-1, 6 * width)
    grad_frames = grad_resid_one + norm_back(
        normed_one, inverse_one, after(grad_first, cross_done) * (1.0 + scale_one)
    )
    self_done = summed(landed(self_sums, grad_frames)).astype(bf16)
    shard_up, shard_down = rows_whole(feed_done)
    shard_cout, shard_cquery, shard_ckey, shard_cvalue = columns_whole(cross_done)
    shard_out, shard_query, shard_key, shard_value = columns_whole(self_done)

    choose_all = (
        steps_all[:, None] == jnp.arange(step_table.shape[0]).astype(f32)[None, :]
    ).astype(bf16)
    cond_all = matmul(choose_all, table_low)
    silu_all = jax.nn.silu(cond_all).astype(bf16)
    grad_ada_w = inner_rows(silu_all, grad_mod_all)
    grad_ada_b = jnp.sum(grad_mod_all.astype(f32), axis=0)
    grad_cond = silu_back(cond_all, outer_cols(grad_mod_all, ada_weight))
    grad_table = lax.dot_general(
        choose_all.astype(f32), grad_cond, (((0,), (0,)), ((), ())), precision=highest
    )

    def columns(value):
        return value.T.astype(f32)

    return (
        layer_out,
        grad_frames,
        grad_text.reshape(text.shape),
        grad_table,
        grad_ada_w,
        grad_ada_b,
        columns(shard_query),
        columns(shard_key),
        columns(shard_value),
        shard_out.astype(f32),
        columns(shard_cquery),
        columns(shard_ckey),
        columns(shard_cvalue),
        shard_cout.astype(f32),
        shard_up.astype(f32),
        columns(shard_down),
    )


def solution(mesh):
    dp, mp = mesh.shape["dp"], mesh.shape["mp"]
    fine = Mesh(mesh.devices.reshape(dp // 2, 2, mp // 4, 2, 2), FINE)
    dp_axes, mp_axes = ("y", "core"), MP_AXES
    return jax.shard_map(
        shards,
        mesh=fine,
        in_specs=(
            P(FINE, None),
            P(dp_axes, None),
            P(FINE, None, None),
            P(dp_axes),
            P(dp_axes),
            P(None, mp_axes),
            P(mp_axes, None),
            P(),
            P(None, mp_axes),
            P(None, mp_axes),
            P(None, mp_axes),
            P(mp_axes, None),
            P(None, mp_axes),
            P(None, mp_axes),
            P(None, mp_axes),
            P(mp_axes, None),
            P(None, mp_axes),
            P(mp_axes, None),
            P(FINE, None),
        ),
        out_specs=(
            P(FINE, None),
            P(FINE, None),
            P(FINE, None, None),
            P(None, mp_axes),
            P(mp_axes, None),
            P(),
            P(None, mp_axes),
            P(None, mp_axes),
            P(None, mp_axes),
            P(mp_axes, None),
            P(None, mp_axes),
            P(None, mp_axes),
            P(None, mp_axes),
            P(mp_axes, None),
            P(None, mp_axes),
            P(mp_axes, None),
        ),
        check_vma=False,
    )
```

time: 482 us -> 376 us (0.78)
  matrix products: 91.1 us -> 17.7 us
  local copies, waits for them, and re-layouts: 74.8 us -> 32.4 us
  other arithmetic: 42 us -> 80 us
  Pallas kernels: 38.5 us -> 71 us
  waiting for transfers between devices: 134 us -> 103 us
  between operations: 16.8 us -> 3.46 us
  starting transfers between devices: 76.9 us -> 63.6 us
    dot_general x21 -> x1, matrix products: 37.6 us -> 1.6 us  [inner_rows(): lax.dot_general(left, right, (((0,), (0,)), ((), ())), preferred_element_...]
    pallas_call x2 -> x4, Pallas kernels: 25.4 us -> 60.1 us  [the longest x2 38.6 us: attend_back(): pl.pallas_call(backward_kernel, grid_spec=pltpu.PrefetchScalarGridSpec(nu...]
    ppermute x73 -> x64, waiting for transfers between devices: 134 us -> 103 us  [shifted(): lax.ppermute(value, axis, [(k, (k + steps) % count) for k in range(count)])]
    unnamed x287 -> x292, local copies, waits for them, and re-layouts: 43.2 us -> 20.1 us
    dot_general x11 -> x7, matrix products: 24.3 us -> 4.9 us  [outer_cols(): lax.dot_general(left, right, (((1,), (1,)), ((), ())), preferred_element_...]
    another operation x48 -> x66, other arithmetic: 13.5 us -> 32.6 us  [the longest x60 28.1 us: gather_axis(): return jnp.stack([at(place) for place in range(count)])]
    dot_general x12 -> x4, matrix products: 23.7 us -> 5.55 us  [matmul(): return jnp.dot(left, right, preferred_element_type=f32)]
    convert_element_type x19 -> x25, other arithmetic: 7.81 us -> 24.5 us  [the longest x15 14.3 us: launch(): summed(picked(terms, dim, (me + s) % count)).astype(bf16)]
  transfers between devices with their start and end apart: 74 -> 64, of which waited for: 21 -> 29; matrix products, arithmetic and copies ran while one was open for 32% -> 30% of each run, Pallas kernels for 3% -> 14%
where the time goes in v2:
time: 376 us; the launch traced here: 371 us
  waiting for transfers between devices  103 us (27%)
  other arithmetic  80 us (21%)
  Pallas kernels  71 us (19%)
  starting transfers between devices  63.6 us (17%)
  local copies, waits for them, and re-layouts  32.4 us (9%)
  matrix products  17.7 us (5%)
    ppermute x64, waiting for transfers between devices, shifted(): lax.ppermute(value, axis, [(k, (k + steps) % count) for k in range(count)])  103 us
    ppermute x64, starting transfers between devices, shifted(): lax.ppermute(value, axis, [(k, (k + steps) % count) for k in range(count)])  63.6 us
    pallas_call x2, Pallas kernels, attend_back(): pl.pallas_call(backward_kernel, grid_spec=pltpu.PrefetchScalarGridSpec(nu...  38.6 us
    another operation x60, other arithmetic, gather_axis(): return jnp.stack([at(place) for place in range(count)])  28.1 us
    pallas_call x1, Pallas kernels, feed(): pl.pallas_call(feed_kernel, grid_spec=pltpu.PrefetchScalarGridSpec(num_sc...  20.2 us
    unnamed x292, local copies, waits for them, and re-layouts  20.1 us
    convert_element_type x15, other arithmetic, launch(): summed(picked(terms, dim, (me + s) % count)).astype(bf16)  14.3 us
    pallas_call x2, Pallas kernels, attend(): pl.pallas_call(forward_kernel, grid=(rows, pairs), in_specs=blocks + [pl....  10.8 us
  transfers between devices with their start and end apart: 64, of which 29 were waited for; matrix products, arithmetic and copies ran while one was open for 30% of the time, Pallas kernels for 14%

profile of v2, /device:TPU:0, one launch (start us, length us, event | category | flops | bytes accessed | tf_op | source)
XLA Modules:
  0.0 370.7 jit_solution(4626569432519735593)
XLA Ops:
  4.4 2.9 collective-permute-start
  11.7 2.6 collective-permute-start.3
  14.6 2.6 collective-permute-start.19
  22.1 9.1 %collective-permute-done.3 = bf16[3,24,768]{2,1,0:T(8,128)(2,1)} collective-permute-done((bf16[3,24,768]{2,1,0:T(8,128)(2,1)}, bf16[3,24,768]{2,1,0:T(8,128)(2,1)}, u32[]{:S(2)}, u32[]{:S(2)}) %collective-permute-start.3) | collective-permute-done | bytes 110624 | tf_op jit(solution)/shard_map/to_za_1/ppermute | solution.py:29
  32.3 2.9 collective-permute-done.11
  42.3 2.8 collective-permute-done.4
  45.1 9.4 %collective-permute-done.1 = bf16[2,4,4608]{2,1,0:T(4,128)(2,1)S(1)} collective-permute-done((bf16[2,4,4608]{2,1,0:T(4,128)(2,1)S(1)}, bf16[2,4,4608]{2,1,0:T(4,128)(2,1)S(1)}, u32[]{:S(2)}, u32[]{:S(2)}) %collective-permute-start.1) | collective-permute-done | bytes 73760 | tf_op jit(solution)/shard_map/to_zb_1/ppermute | solution.py:29
  68.0 8.6 %collective-permute-done.9 = bf16[2,2,2,3,24,384]{5,4,3,2,1,0:T(8,128)(2,1)S(1)} collective-permute-done((bf16[2,2,2,3,24,384]{5,4,3,2,1,0:T(8,128)(2,1)S(1)}, bf16[2,2,2,3,24,384]{5,4,3,2,1,0:T(8,128)(2,1)S(1)}, u32[]{:S(2)}, u32[]{:S(2)}) %collective-permute-start.9) | collective-permute-done | bytes 442400 | tf_op jit(solution)/shard_map/to_x_1/ppermute | solution.py:29
  78.2 5.0 %collective-permute-done.16 = bf16[2,2,5,24,384]{4,3,2,1,0:T(8,128)(2,1)S(1)} collective-permute-done((bf16[2,2,5,24,384]{4,3,2,1,0:T(8,128)(2,1)S(1)}, bf16[2,2,5,24,384]{4,3,2,1,0:T(8,128)(2,1)S(1)}, u32[]{:S(2)}, u32[]{:S(2)}) %collective-permute-start.16) | collective-permute-done | bytes 368672 | tf_op jit(solution)/shard_map/to_y_1/ppermute | solution.py:29
  93.7 5.5 %shard_map.307.mix_ref = bf16[512,768]{1,0:T(8,128)(2,1)S(1)} custom-call(bf16[512,768]{1,0:T(8,128)(2,1)S(1)} %convolution_convert_fusion.3.q_ref, bf16[512,768]{1,0:T(8,128)(2,1)S(1)} %convolution_convert_fusion.2.k_ref, bf16[512,768]{1,0:T(8,128)(2,1)S(1)} %convolution_convert_fusion.1.v_ref, f32[1,512,512]{2,1,0:T(8,128)S(1)} %compare_select_fusion.bias_ref), custom_call_target="tpu_custom_call" | custom-call | tf_op jit(solution)/shard_map/pallas_call | solution.py:318
  99.2 4.7 %collective-permute-done.17 = bf16[2,2,2,5,24,384]{5,4,3,2,1,0:T(8,128)(2,1)} collective-permute-done((bf16[2,2,2,5,24,384]{5,4,3,2,1,0:T(8,128)(2,1)}, bf16[2,2,2,5,24,384]{5,4,3,2,1,0:T(8,128)(2,1)}, u32[]{:S(2)}, u32[]{:S(2)}) %collective-permute-start.17) | collective-permute-done | bytes 737312 | tf_op jit(solution)/shard_map/to_x_1/ppermute | solution.py:29
  107.9 5.2 %collective-permute-done.21 = bf16[2,2,96,768]{3,2,1,0:T(8,128)(2,1)} collective-permute-done((bf16[2,2,96,768]{3,2,1,0:T(8,128)(2,1)S(1)}, bf16[2,2,96,768]{3,2,1,0:T(8,128)(2,1)}, u32[]{:S(2)}, u32[]{:S(2)}) %collective-permute-start.21) | collective-permute-done | bytes 589856 | tf_op jit(solution)/shard_map/to_x_1/ppermute | solution.py:29
  116.5 6.4 %collective-permute-done.23 = bf16[2,2,96,768]{3,2,1,0:T(8,128)(2,1)S(1)} collective-permute-done((bf16[2,2,96,768]{3,2,1,0:T(8,128)(2,1)S(1)}, bf16[2,2,96,768]{3,2,1,0:T(8,128)(2,1)S(1)}, u32[]{:S(2)}, u32[]{:S(2)}) %collective-permute-start.23) | collective-permute-done | bytes 589856 | tf_op jit(solution)/shard_map/to_y_1/ppermute | solution.py:29
  136.3 5.4 %shard_map.308.mix_ref = bf16[512,768]{1,0:T(8,128)(2,1)S(1)} custom-call(bf16[512,768]{1,0:T(8,128)(2,1)S(1)} %convolution_convert_fusion.q_ref, bf16[308,768]{1,0:T(8,128)(2,1)S(1)} %fusion.24.k_ref, bf16[308,768]{1,0:T(8,128)(2,1)S(1)} %fusion.25.v_ref, f32[1,512,308]{2,1,0:T(8,128)S(1)} %and_select_fusion.bias_ref), custom_call_target="tpu_custom_call" | custom-call | tf_op jit(solution)/shard_map/pallas_call | solution.py:318
  141.7 5.6 %collective-permute-done.22 = bf16[2,2,2,96,768]{4,3,2,1,0:T(8,128)(2,1)} collective-permute-done((bf16[2,2,2,96,768]{4,3,2,1,0:T(8,128)(2,1)}, bf16[2,2,2,96,768]{4,3,2,1,0:T(8,128)(2,1)}, u32[]{:S(2)}, u32[]{:S(2)}) %collective-permute-start.22) | collective-permute-done | bytes 1179680 | tf_op jit(solution)/shard_map/to_y_1/ppermute | solution.py:29
  161.7 20.2 %shard_map.309 = (f32[512,768]{1,0:T(8,128)S(1)}, f32[512,768]{1,0:T(8,128)S(1)}, bf16[8,384,384]{2,1,0:T(8,128)(2,1)}, bf16[8,384,384]{2,1,0:T(8,128)(2,1)}, bf...) custom-call(s32[1]{0:T(128)} %bitcast.56.core_ref, bf16[512,768]{1,0:T(8,128)(2,1)S(1)} %add_convert_fusion.3.x_ref, ...), custom_call_target="tpu_custom_call" | custom-call | tf_op jit(solution)/shard_map/pallas_call | solution.py:414
  187.9 2.7 fusion.27
  191.7 2.8 fusion.28
  198.7 17.4 %shard_map.310 = (f32[308,768]{1,0:T(8,128)S(1)}, f32[512,768]{1,0:T(8,128)}, bf16[2,768,384]{2,1,0:T(8,128)(2,1)}, bf16[2,768,384]{2,1,0:T(8,128)(2,1)}, bf16[2...) custom-call(s32[1]{0:T(128)} %bitcast.56.core_ref, bf16[512,768]{1,0:T(8,128)(2,1)S(1)} %copy-done.18, ...), custom_call_target="tpu_custom_call" | custom-call | tf_op jit(solution)/shard_map/pallas_call | solution.py:341
  219.1 2.6 multiply_convert_fusion
  232.9 21.1 %shard_map.311 = (f32[512,768]{1,0:T(8,128)}, bf16[2,768,384]{2,1,0:T(8,128)(2,1)}, bf16[2,768,384]{2,1,0:T(8,128)(2,1)}, bf16[2,768,384]{2,1,0:T(8,128)(2,1)}, bf16[2,768,384]{2,1,0:T(8,128)(2,1)}) custom-call(s32[1]{0:T(128)} %bitcast.56.core_ref, bf16[512,768]{1,0:T(8,128)(2,1)S(1)} %copy-done.6, bf16[512,768]{1,0:T(8,128)(2,1)S(1)} %copy-done.8, ...), custom_call_target="tpu_custom_call" | custom-call | tf_op jit(solution)/shard_map/pallas_call | solution.py:341
  261.8 3.3 collective-permute-start.49
  268.0 3.3 collective-permute-done.33
  280.1 3.8 %collective-permute-done.40 = bf16[2,2,2,2,48,384]{5,4,2,1,0,3:T(8,128)(2,1)S(1)} collective-permute-done((bf16[2,2,2,2,48,384]{5,4,2,1,0,3:T(8,128)(2,1)S(1)}, bf16[2,2,2,2,48,384]{5,4,2,1,0,3:T(8,128)(2,1)S(1)}, u32[]{:S(2)}, u32[]{:S(2)}) %collective-permute-start.40) | collective-permute-done | bytes 589856 | tf_op jit(solution)/shard_map/self_sums_first_stage/to_x_1/ppermute | solution.py:29
  284.0 2.6 collective-permute-start.44
  287.4 4.4 %collective-permute-done.39 = bf16[2,2,2,48,384]{4,3,0,2,1:T(8,128)(2,1)S(1)} collective-permute-done((bf16[2,2,2,48,384]{4,3,0,2,1:T(8,128)(2,1)S(1)}, bf16[2,2,2,48,384]{4,3,0,2,1:T(8,128)(2,1)S(1)}, u32[]{:S(2)}, u32[]{:S(2)}) %collective-permute-start.39) | collective-permute-done | bytes 294944 | tf_op jit(solution)/shard_map/cross_sums_second_stage/to_y_1/ppermute | solution.py:29
  293.9 3.4 collective-permute-start.45
  302.7 2.8 copy.181
  306.0 2.9 collective-permute-start.43
  314.2 9.9 %collective-permute-done.43 = bf16[2,2,2,48,384]{4,3,1,0,2:T(8,128)(2,1)S(1)} collective-permute-done((bf16[2,2,2,48,384]{4,3,1,0,2:T(8,128)(2,1)S(1)}, bf16[2,2,2,48,384]{4,3,1,0,2:T(8,128)(2,1)S(1)}, u32[]{:S(2)}, u32[]{:S(2)}) %collective-permute-start.43) | collective-permute-done | bytes 294944 | tf_op jit(solution)/shard_map/cross_sums_third_stage/to_zb_1/ppermute | solution.py:29
  330.1 3.5 collective-permute-start.57
  342.9 4.2 %collective-permute-done.58 = bf16[2,2,48,384]{3,2,1,0:T(8,128)(2,1)S(1)} collective-permute-done((bf16[2,2,48,384]{3,2,1,0:T(8,128)(2,1)S(1)}, bf16[2,2,48,384]{3,2,1,0:T(8,128)(2,1)S(1)}, u32[]{:S(2)}, u32[]{:S(2)}) %collective-permute-start.58) | collective-permute-done | bytes 147488 | tf_op jit(solution)/shard_map/to_y_1/ppermute | solution.py:29
  (593 shorter events, 177.6 us)
Async XLA Ops:
  4.4 31.8 %collective-permute-start = (f32[2,2,4,4608]{3,2,1,0:T(4,128)}, f32[2,2,4,4608]{3,2,1,0:T(4,128)}, u32[]{:S(2)}, u32[]{:S(2)}) collective-permute-start(f32[2,2,4,4608]{3,2,1,0:T(4,128)} %dynamic-slice_bitcast_fusion), channel_id=1, source_target_pairs={{0,1},{1,0},{2,3},{3,2},{4,5},{5,4},{6,7},{7,6},{8,9},{9,8},{10,11... | collective-permute-start | bytes 884744 | tf_op jit(solution)/shard_map/to_x_1/ppermute | solution.py:29
  11.7 19.5 %collective-permute-start.3 = (bf16[3,24,768]{2,1,0:T(8,128)(2,1)}, bf16[3,24,768]{2,1,0:T(8,128)(2,1)}, u32[]{:S(2)}, u32[]{:S(2)}) collective-permute-start(bf16[3,24,768]{2,1,0:T(8,128)(2,1)} %get-tuple-element.80), channel_id=1, source_target_pairs={{0,4},{4,0},{1,5},{5,1},{2,6},{6,2},{3,7},{7,3},{8,12},{12,8},{9,1... | collective-permute-start | bytes 331784 | tf_op jit(solution)/shard_map/to_za_1/ppermute | solution.py:29
  14.2 20.9 %collective-permute-start.11 = (bf16[5,24,768]{2,1,0:T(8,128)(2,1)}, bf16[5,24,768]{2,1,0:T(8,128)(2,1)S(1)}, u32[]{:S(2)}, u32[]{:S(2)}) collective-permute-start(bf16[5,24,768]{2,1,0:T(8,128)(2,1)} %get-tuple-element.81), channel_id=1, source_target_pairs={{0,4},{4,0},{1,5},{5,1},{2,6},{6,2},{3,7},{7,3},{8,12},{12,8},{9,1... | collective-permute-start | bytes 552968 | tf_op jit(solution)/shard_map/to_za_1/ppermute | solution.py:29
  14.6 25.8 %collective-permute-start.19 = (bf16[2,96,768]{2,1,0:T(8,128)(2,1)}, bf16[2,96,768]{2,1,0:T(8,128)(2,1)}, u32[]{:S(2)}, u32[]{:S(2)}) collective-permute-start(bf16[2,96,768]{2,1,0:T(8,128)(2,1)} %get-tuple-element.88), channel_id=1, source_target_pairs={{0,4},{4,0},{1,5},{5,1},{2,6},{6,2},{3,7},{7,3},{8,12},{12,8},{9,1... | collective-permute-start | bytes 884744 | tf_op jit(solution)/shard_map/to_za_1/ppermute | solution.py:29
  36.1 29.6 %collective-permute-start.12 = (bf16[2,5,24,768]{3,2,1,0:T(8,128)(2,1)S(1)}, bf16[2,5,24,768]{3,2,1,0:T(8,128)(2,1)S(1)}, u32[]{:S(2)}, u32[]{:S(2)}) collective-permute-start(bf16[2,5,24,768]{3,2,1,0:T(8,128)(2,1)S(1)} %pad_maximum_fusion.19), channel_id=1, source_target_pairs={{0,2},{2,0},{1,3},{3,1},{4,6},{6,4},{5,7},{7,5},{8,10},{10,8},{9,1... | collective-permute-start | bytes 1105928 | tf_op jit(solution)/shard_map/to_zb_1/ppermute | solution.py:29
  37.3 17.2 %collective-permute-start.1 = (bf16[2,4,4608]{2,1,0:T(4,128)(2,1)S(1)}, bf16[2,4,4608]{2,1,0:T(4,128)(2,1)S(1)}, u32[]{:S(2)}, u32[]{:S(2)}) collective-permute-start(bf16[2,4,4608]{2,1,0:T(4,128)(2,1)S(1)} %dynamic-slice_bitcast_fusion.1), channel_id=1, source_target_pairs={{0,2},{2,0},{1,3},{3,1},{4,6},{6,4},{5,7},{7,5},{8,10},{10,8},{9,1... | collective-permute-start | bytes 221192 | tf_op jit(solution)/shard_map/to_zb_1/ppermute | solution.py:29
  41.6 46.2 %collective-permute-start.20 = (bf16[2,2,96,768]{3,2,0,1:T(8,128)(2,1)S(1)}, bf16[2,2,96,768]{3,2,0,1:T(8,128)(2,1)S(1)}, u32[]{:S(2)}, u32[]{:S(2)}) collective-permute-start(bf16[2,2,96,768]{3,2,0,1:T(8,128)(2,1)S(1)} %pad_maximum_fusion.13), channel_id=1, source_target_pairs={{0,2},{2,0},{1,3},{3,1},{4,6},{6,4},{5,7},{7,5},{8,10},{10,8},{9,1... | collective-permute-start | bytes 1769480 | tf_op jit(solution)/shard_map/to_zb_1/ppermute | solution.py:29
  65.9 17.2 %collective-permute-start.16 = (bf16[2,2,5,24,384]{4,3,2,1,0:T(8,128)(2,1)S(1)}, bf16[2,2,5,24,384]{4,3,2,1,0:T(8,128)(2,1)S(1)}, u32[]{:S(2)}, u32[]{:S(2)}) collective-permute-start(bf16[2,2,5,24,384]{4,3,2,1,0:T(8,128)(2,1)S(1)} %get-tuple-element.266), channel_id=1, source_target_pairs={{0,16},{16,0},{1,17},{17,1},{2,18},{18,2},{3,19},{19,3},{4,20},{20... | collective-permute-start | bytes 1105928 | tf_op jit(solution)/shard_map/to_y_1/ppermute | solution.py:29
  67.0 18.2 %collective-permute-start.13 = (bf16[2,2,5,24,384]{4,3,2,1,0:T(8,128)(2,1)S(1)}, bf16[2,2,5,24,384]{4,3,2,1,0:T(8,128)(2,1)S(1)}, u32[]{:S(2)}, u32[]{:S(2)}) collective-permute-start(bf16[2,2,5,24,384]{4,3,2,1,0:T(8,128)(2,1)S(1)} %get-tuple-element.267), channel_id=1, source_target_pairs={{0,1},{1,0},{2,3},{3,2},{4,5},{5,4},{6,7},{7,6},{8,9},{9,8},{10,11... | collective-permute-start | bytes 1105928 | tf_op jit(solution)/shard_map/to_x_1/ppermute | solution.py:29
  84.2 19.7 %collective-permute-start.17 = (bf16[2,2,2,5,24,384]{5,4,3,2,1,0:T(8,128)(2,1)}, bf16[2,2,2,5,24,384]{5,4,3,2,1,0:T(8,128)(2,1)}, u32[]{:S(2)}, u32[]{:S(2)}) collective-permute-start(bf16[2,2,2,5,24,384]{5,4,3,2,1,0:T(8,128)(2,1)} %pad_maximum_fusion.11), channel_id=1, source_target_pairs={{0,1},{1,0},{2,3},{3,2},{4,5},{5,4},{6,7},{7,6},{8,9},{9,8},{10,11... | collective-permute-start | bytes 2211848 | tf_op jit(solution)/shard_map/to_x_1/ppermute | solution.py:29
  86.2 19.4 %collective-permute-start.14 = (bf16[2,2,2,5,24,384]{5,4,3,2,1,0:T(8,128)(2,1)}, bf16[2,2,2,5,24,384]{5,4,3,2,1,0:T(8,128)(2,1)S(1)}, u32[]{:S(2)}, u32[]{:S(2)}) collective-permute-start(bf16[2,2,2,5,24,384]{5,4,3,2,1,0:T(8,128)(2,1)} %pad_maximum_fusion.10), channel_id=1, source_target_pairs={{0,16},{16,0},{1,17},{17,1},{2,18},{18,2},{3,19},{19,3},{4,20},{20... | collective-permute-start | bytes 2211848 | tf_op jit(solution)/shard_map/to_y_1/ppermute | solution.py:29
  87.9 25.1 %collective-permute-start.21 = (bf16[2,2,96,768]{3,2,1,0:T(8,128)(2,1)S(1)}, bf16[2,2,96,768]{3,2,1,0:T(8,128)(2,1)}, u32[]{:S(2)}, u32[]{:S(2)}) collective-permute-start(bf16[2,2,96,768]{3,2,1,0:T(8,128)(2,1)S(1)} %get-tuple-element.255), channel_id=1, source_target_pairs={{0,1},{1,0},{2,3},{3,2},{4,5},{5,4},{6,7},{7,6},{8,9},{9,8},{10,11... | collective-permute-start | bytes 1769480 | tf_op jit(solution)/shard_map/to_x_1/ppermute | solution.py:29
  105.6 19.6 %collective-permute-start.18 = (bf16[2,2,2,2,5,24,384]{6,5,4,3,2,0,1:T(8,128)(2,1)S(1)}, bf16[2,2,2,2,5,24,384]{6,5,4,3,2,0,1:T(8,128)(2,1)S(1)}, u32[]{:S(2)}, u32[]{:S(2)}) collective-permute-start(bf16[2,2,2,2,5,24,384]{6,5,4,3,2,0,1:T(8,128)(2,1)S(1)} %copy.125), channel_id=1, source_target_pairs={{0,8},{8,0},{1,9},{9,1},{2,10},{10,2},{3,11},{11,3},{4,12},{12,4},... | collective-permute-start | bytes 4423688 | tf_op jit(solution)/shard_map/to_core_1/ppermute | solution.py:29
  106.0 19.4 %collective-permute-start.15 = (bf16[2,2,2,2,5,24,384]{6,5,4,3,2,0,1:T(8,128)(2,1)S(1)}, bf16[2,2,2,2,5,24,384]{6,5,4,3,2,0,1:T(8,128)(2,1)S(1)}, u32[]{:S(2)}, u32[]{:S(2)}) collective-permute-start(bf16[2,2,2,2,5,24,384]{6,5,4,3,2,0,1:T(8,128)(2,1)S(1)} %pad_maximum_fusion.1), channel_id=1, source_target_pairs={{0,8},{8,0},{1,9},{9,1},{2,10},{10,2},{3,11},{11,3},{4,12},{12,4},... | collective-permute-start | bytes 4423688 | tf_op jit(solution)/shard_map/to_core_1/ppermute | solution.py:29
  115.4 31.9 %collective-permute-start.22 = (bf16[2,2,2,96,768]{4,3,2,1,0:T(8,128)(2,1)}, bf16[2,2,2,96,768]{4,3,2,1,0:T(8,128)(2,1)}, u32[]{:S(2)}, u32[]{:S(2)}) collective-permute-start(bf16[2,2,2,96,768]{4,3,2,1,0:T(8,128)(2,1)} %pad_maximum_fusion.5), channel_id=1, source_target_pairs={{0,16},{16,0},{1,17},{17,1},{2,18},{18,2},{3,19},{19,3},{4,20},{20... | collective-permute-start | bytes 3538952 | tf_op jit(solution)/shard_map/to_y_1/ppermute | solution.py:29
  124.2 26.4 %collective-permute-start.24 = (bf16[2,2,2,96,768]{4,3,2,1,0:T(8,128)(2,1)}, bf16[2,2,2,96,768]{4,3,2,1,0:T(8,128)(2,1)}, u32[]{:S(2)}, u32[]{:S(2)}) collective-permute-start(bf16[2,2,2,96,768]{4,3,2,1,0:T(8,128)(2,1)} %pad_maximum_fusion.6), channel_id=1, source_target_pairs={{0,1},{1,0},{2,3},{3,2},{4,5},{5,4},{6,7},{7,6},{8,9},{9,8},{10,11... | collective-permute-start | bytes 3538952 | tf_op jit(solution)/shard_map/to_x_1/ppermute | solution.py:29
  190.6 31.1 %collective-permute-start.31 = (bf16[1,2,2,2,192,384]{5,4,2,1,3,0:T(8,128)(2,1)}, bf16[1,2,2,2,192,384]{5,4,2,1,3,0:T(8,128)(2,1)}, u32[]{:S(2)}, u32[]{:S(2)}) collective-permute-start(bf16[1,2,2,2,192,384]{5,4,2,1,3,0:T(8,128)(2,1)} %fusion.27), channel_id=1, source_target_pairs={{0,1},{1,0},{2,3},{3,2},{4,5},{5,4},{6,7},{7,6},{8,9},{9,8},{10,11... | collective-permute-start | bytes 3538952 | tf_op jit(solution)/shard_map/feed_sums_first_stage/to_x_1/ppermute | solution.py:29
  194.5 28.0 %collective-permute-start.32 = (bf16[1,2,2,2,192,384]{5,4,2,1,3,0:T(8,128)(2,1)}, bf16[1,2,2,2,192,384]{5,4,2,1,3,0:T(8,128)(2,1)}, u32[]{:S(2)}, u32[]{:S(2)}) collective-permute-start(bf16[1,2,2,2,192,384]{5,4,2,1,3,0:T(8,128)(2,1)} %fusion.28), channel_id=1, source_target_pairs={{0,16},{16,0},{1,17},{17,1},{2,18},{18,2},{3,19},{19,3},{4,20},{20... | collective-permute-start | bytes 3538952 | tf_op jit(solution)/shard_map/feed_sums_first_stage/to_y_1/ppermute | solution.py:29
  225.1 31.4 %collective-permute-start.35 = (bf16[1,2,2,192,384]{4,3,2,1,0:T(8,128)(2,1)}, bf16[1,2,2,192,384]{4,3,2,1,0:T(8,128)(2,1)}, u32[]{:S(2)}, u32[]{:S(2)}) collective-permute-start(bf16[1,2,2,192,384]{4,3,2,1,0:T(8,128)(2,1)} %fusion.40), channel_id=1, source_target_pairs={{0,16},{16,0},{1,17},{17,1},{2,18},{18,2},{3,19},{19,3},{4,20},{20... | collective-permute-start | bytes 1769480 | tf_op jit(solution)/shard_map/feed_sums_second_stage/to_y_1/ppermute | solution.py:29
  228.9 28.1 %collective-permute-start.36 = (bf16[1,2,2,192,384]{4,3,2,1,0:T(8,128)(2,1)}, bf16[1,2,2,192,384]{4,3,2,1,0:T(8,128)(2,1)}, u32[]{:S(2)}, u32[]{:S(2)}) collective-permute-start(bf16[1,2,2,192,384]{4,3,2,1,0:T(8,128)(2,1)} %fusion.39), channel_id=1, source_target_pairs={{0,1},{1,0},{2,3},{3,2},{4,5},{5,4},{6,7},{7,6},{8,9},{9,8},{10,11... | collective-permute-start | bytes 1769480 | tf_op jit(solution)/shard_map/feed_sums_second_stage/to_x_1/ppermute | solution.py:29
  261.8 47.2 %collective-permute-start.49 = (bf16[2,1,2,192,384]{4,3,0,2,1:T(8,128)(2,1)}, bf16[2,1,2,192,384]{4,3,0,2,1:T(8,128)(2,1)}, u32[]{:S(2)}, u32[]{:S(2)}) collective-permute-start(bf16[2,1,2,192,384]{4,3,0,2,1:T(8,128)(2,1)} %fusion.93), channel_id=1, source_target_pairs={{0,2},{2,0},{1,3},{3,1},{4,6},{6,4},{5,7},{7,5},{8,10},{10,8},{9,1... | collective-permute-start | bytes 1769480 | tf_op jit(solution)/shard_map/feed_sums_third_stage/to_zb_1/ppermute | solution.py:29
  265.3 18.6 %collective-permute-start.40 = (bf16[2,2,2,2,48,384]{5,4,2,1,0,3:T(8,128)(2,1)S(1)}, bf16[2,2,2,2,48,384]{5,4,2,1,0,3:T(8,128)(2,1)S(1)}, u32[]{:S(2)}, u32[]{:S(2)}) collective-permute-start(bf16[2,2,2,2,48,384]{5,4,2,1,0,3:T(8,128)(2,1)S(1)} %fusion.86), channel_id=1, source_target_pairs={{0,1},{1,0},{2,3},{3,2},{4,5},{5,4},{6,7},{7,6},{8,9},{9,8},{10,11... | collective-permute-start | bytes 1769480 | tf_op jit(solution)/shard_map/self_sums_first_stage/to_x_1/ppermute | solution.py:29
  266.5 20.1 %collective-permute-start.41 = (bf16[2,2,2,2,48,384]{5,4,2,1,0,3:T(8,128)(2,1)S(1)}, bf16[2,2,2,2,48,384]{5,4,2,1,0,3:T(8,128)(2,1)S(1)}, u32[]{:S(2)}, u32[]{:S(2)}) collective-permute-start(bf16[2,2,2,2,48,384]{5,4,2,1,0,3:T(8,128)(2,1)S(1)} %fusion.87), channel_id=1, source_target_pairs={{0,16},{16,0},{1,17},{17,1},{2,18},{18,2},{3,19},{19,3},{4,20},{20... | collective-permute-start | bytes 1769480 | tf_op jit(solution)/shard_map/self_sums_first_stage/to_y_1/ppermute | solution.py:29
  272.9 18.8 %collective-permute-start.39 = (bf16[2,2,2,48,384]{4,3,0,2,1:T(8,128)(2,1)S(1)}, bf16[2,2,2,48,384]{4,3,0,2,1:T(8,128)(2,1)S(1)}, u32[]{:S(2)}, u32[]{:S(2)}) collective-permute-start(bf16[2,2,2,48,384]{4,3,0,2,1:T(8,128)(2,1)S(1)} %fusion.109), channel_id=1, source_target_pairs={{0,16},{16,0},{1,17},{17,1},{2,18},{18,2},{3,19},{19,3},{4,20},{20... | collective-permute-start | bytes 884744 | tf_op jit(solution)/shard_map/cross_sums_second_stage/to_y_1/ppermute | solution.py:29
  273.6 19.0 %collective-permute-start.42 = (bf16[2,2,2,48,384]{4,3,0,2,1:T(8,128)(2,1)S(1)}, bf16[2,2,2,48,384]{4,3,0,2,1:T(8,128)(2,1)S(1)}, u32[]{:S(2)}, u32[]{:S(2)}) collective-permute-start(bf16[2,2,2,48,384]{4,3,0,2,1:T(8,128)(2,1)S(1)} %fusion.108), channel_id=1, source_target_pairs={{0,1},{1,0},{2,3},{3,2},{4,5},{5,4},{6,7},{7,6},{8,9},{9,8},{10,11... | collective-permute-start | bytes 884744 | tf_op jit(solution)/shard_map/cross_sums_second_stage/to_x_1/ppermute | solution.py:29
  305.5 24.4 %collective-permute-start.53 = (f32[32]{0:T(128)S(1)}, f32[32]{0:T(128)S(1)}, u32[]{:S(2)}, u32[]{:S(2)}) collective-permute-start(f32[32]{0:T(128)S(1)} %convert_element_type.936), channel_id=1, source_target_pairs={{0,16},{16,0},{1,17},{17,1},{2,18},{18,2},{3,19},{19,3},{4,20},{20... | collective-permute-start | bytes 392 | tf_op jit(solution)/shard_map/to_y_1/ppermute | solution.py:29
  306.0 18.1 %collective-permute-start.43 = (bf16[2,2,2,48,384]{4,3,1,0,2:T(8,128)(2,1)S(1)}, bf16[2,2,2,48,384]{4,3,1,0,2:T(8,128)(2,1)S(1)}, u32[]{:S(2)}, u32[]{:S(2)}) collective-permute-start(bf16[2,2,2,48,384]{4,3,1,0,2:T(8,128)(2,1)S(1)} %copy-done.92), channel_id=1, source_target_pairs={{0,2},{2,0},{1,3},{3,1},{4,6},{6,4},{5,7},{7,5},{8,10},{10,8},{9,1... | collective-permute-start | bytes 884744 | tf_op jit(solution)/shard_map/cross_sums_third_stage/to_zb_1/ppermute | solution.py:29
  308.9 21.1 %collective-permute-start.56 = (bf16[2,2,2,48,384]{4,3,1,0,2:T(8,128)(2,1)S(1)}, bf16[2,2,2,48,384]{4,3,1,0,2:T(8,128)(2,1)S(1)}, u32[]{:S(2)}, u32[]{:S(2)}) collective-permute-start(bf16[2,2,2,48,384]{4,3,1,0,2:T(8,128)(2,1)S(1)} %copy-done.93), channel_id=1, source_target_pairs={{0,2},{2,0},{1,3},{3,1},{4,6},{6,4},{5,7},{7,5},{8,10},{10,8},{9,1... | collective-permute-start | bytes 884744 | tf_op jit(solution)/shard_map/self_sums_third_stage/to_zb_1/ppermute | solution.py:29
  310.0 16.5 %collective-permute-start.52 = (bf16[2,1,192,384]{3,2,0,1:T(8,128)(2,1)S(1)}, bf16[2,1,192,384]{3,2,0,1:T(8,128)(2,1)S(1)}, u32[]{:S(2)}, u32[]{:S(2)}) collective-permute-start(bf16[2,1,192,384]{3,2,0,1:T(8,128)(2,1)S(1)} %fusion.97), channel_id=1, source_target_pairs={{0,4},{4,0},{1,5},{5,1},{2,6},{6,2},{3,7},{7,3},{8,12},{12,8},{9,1... | collective-permute-start | bytes 884744 | tf_op jit(solution)/shard_map/to_za_1/ppermute | solution.py:29
  312.6 21.0 %collective-permute-start.51 = (bf16[2,2,2,6,4,768]{5,4,3,2,1,0:T(4,128)(2,1)S(1)}, bf16[2,2,2,6,4,768]{5,4,3,2,1,0:T(4,128)(2,1)S(1)}, u32[]{:S(2)}, u32[]{:S(2)}) collective-permute-start(bf16[2,2,2,6,4,768]{5,4,3,2,1,0:T(4,128)(2,1)S(1)} %pad_maximum_fusion.20), channel_id=1, source_target_pairs={{0,16},{16,0},{1,17},{17,1},{2,18},{18,2},{3,19},{19,3},{4,20},{20... | collective-permute-start | bytes 884744 | tf_op jit(solution)/shard_map/to_y_1/ppermute | solution.py:29
  328.4 21.1 %collective-permute-start.62 = (bf16[2,1,192,384]{3,2,0,1:T(8,128)(2,1)}, bf16[2,1,192,384]{3,2,0,1:T(8,128)(2,1)}, u32[]{:S(2)}, u32[]{:S(2)}) collective-permute-start(bf16[2,1,192,384]{3,2,0,1:T(8,128)(2,1)} %fusion.96), channel_id=1, source_target_pairs={{0,16},{16,0},{1,17},{17,1},{2,18},{18,2},{3,19},{19,3},{4,20},{20... | collective-permute-start | bytes 884744 | tf_op jit(solution)/shard_map/to_y_1/ppermute | solution.py:29
  335.3 24.1 %collective-permute-start.55 = (bf16[2,2,2,2,6,4,768]{6,5,4,3,2,1,0:T(4,128)(2,1)}, bf16[2,2,2,2,6,4,768]{6,5,4,3,2,1,0:T(4,128)(2,1)}, u32[]{:S(2)}, u32[]{:S(2)}) collective-permute-start(bf16[2,2,2,2,6,4,768]{6,5,4,3,2,1,0:T(4,128)(2,1)} %pad_maximum_fusion.14), channel_id=1, source_target_pairs={{0,8},{8,0},{1,9},{9,1},{2,10},{10,2},{3,11},{11,3},{4,12},{12,4},... | collective-permute-start | bytes 1769480 | tf_op jit(solution)/shard_map/to_core_1/ppermute | solution.py:29
  (173 other events, 1819.2 us)

commit v3 on v2

--- a/solution.py
+++ b/solution.py
@@ -47,6 +47,10 @@
     return jnp.stack([at(place) for place in range(count)])
 
 
+def joined_rows(value, axis, *hold):
+    return gather_axis(value, axis, *hold).reshape(-1, value.shape[-1])
+
+
 def after(value, *done):
     return lax.optimization_barrier((value, *done))[0]
 
@@ -128,29 +132,27 @@
 
 
 def parts_kernel(mine_ref, *refs):
-    *sources, up_ref, down_ref, first_ref, more_ref, feed_ref, turned_ref, tall_ref = refs
+    *sources, up_ref, down_ref, first_ref, more_ref, feed_ref, row_ref, tall_ref = refs
     rows, hidden = first_ref.shape[1], feed_ref.shape[1]
-    width = down_ref.shape[1]
 
     def own(ref, count):
-        return ref[pl.ds(pl.multiple_of(mine_ref[0] * count, 8), count), :]
+        return ref[pl.ds(pl.multiple_of(mine_ref[0] * count, 8), count), :].astype(bf16)
 
     for which, source in enumerate(sources):
-        shard = source[...].astype(f32)
-        turned_ref[...] = shard.T if shard.shape[1] < width else shard
+        row_ref[...] = source[...].astype(f32)
         target, place = (first_ref, which) if which < 3 else (more_ref, which - 3)
-        target[place] = own(turned_ref, rows).astype(bf16)
+        target[place] = own(row_ref, rows)
     tall_ref[...] = up_ref[...].astype(f32).T
-    feed_ref[0] = own(tall_ref, hidden).astype(bf16)
+    feed_ref[0] = own(tall_ref, hidden)
     tall_ref[...] = down_ref[...].astype(f32)
-    feed_ref[1] = own(tall_ref, hidden).astype(bf16)
+    feed_ref[1] = own(tall_ref, hidden)
 
 
 def weight_parts(weights, up_weight, down_weight):
     copies = lax.axis_size("y") * lax.axis_size("core")
     mine = lax.axis_index("y") * lax.axis_size("core") + lax.axis_index("core")
     hidden, width = down_weight.shape
-    shard = min(weights[0].shape)
+    shard = weights[0].shape[0]
     rows = shard // copies
     if rows % 8 or hidden // copies % 8:
 
@@ -158,9 +160,9 @@
             part = value.shape[0] // copies
             return lax.dynamic_slice_in_dim(value, mine * part, part, 0)
 
-        turned = [own(w.T if w.shape[1] < width else w) for w in weights]
+        kept = [own(w) for w in weights]
         feed_part = jnp.stack([own(up_weight.T), own(down_weight)])
-        return jnp.stack(turned[:3]), jnp.stack(turned[3:]), feed_part
+        return jnp.stack(kept[:3]), jnp.stack(kept[3:]), feed_part
     shapes = [
         (3, rows, width),
         (len(weights) - 3, rows, width),
@@ -182,16 +184,52 @@
     )(mine.reshape(1), *sources)
 
 
-def columns_whole(done):
-    done = gather_axis(gather_axis(done, "y"), "core")
-    done = done.transpose(2, 3, 1, 4, 0, 5)
-    return done.reshape(-1, done.shape[2] * done.shape[3], done.shape[4] * done.shape[5])
-
-
-def rows_whole(done):
-    done = gather_axis(gather_axis(done, "y"), "core")
-    done = done.transpose(2, 3, 0, 1, 4, 5)
-    return done.reshape(done.shape[0], -1, done.shape[5])
+def finish_kernel(me_ref, near, far_y, far_core, far_both, *refs):
+    *outs, whole_ref = refs
+    y, core = me_ref[0], me_ref[1]
+    matrices, rows, lanes = near.shape
+    deep = rows == lanes // 2
+
+    def place(which, part, turn_y, turn_core):
+        if deep:
+            row = (core ^ turn_core) * 2 * rows + (y ^ turn_y) * rows
+            whole_ref[pl.ds(pl.multiple_of(row, 8), rows), :] = part[which].astype(f32)
+        else:
+            row, lane = (y ^ turn_y) * rows, (core ^ turn_core) * lanes
+            whole_ref[
+                pl.ds(pl.multiple_of(row, 8), rows), pl.ds(pl.multiple_of(lane, 128), lanes)
+            ] = part[which].astype(f32)
+
+    for which, out in enumerate(outs):
+        for part, turns in ((near, (0, 0)), (far_y, (1, 0)), (far_core, (0, 1)), (far_both, (1, 1))):
+            place(which, part, *turns)
+        out[...] = whole_ref[...] if out.shape == whole_ref.shape else whole_ref[...].T
+
+
+def finish(done, shapes):
+    done = done.reshape(-1, *done.shape[2:])
+    deep = done.shape[1] == done.shape[2] // 2
+    if lax.axis_size("y") != 2 or done.shape[1] % 8 or done.shape[2] % 128:
+        done = gather_axis(gather_axis(done, "y"), "core")
+        axes = (2, 0, 1, 3, 4) if deep else (2, 1, 3, 0, 4)
+        done = done.transpose(axes).reshape(done.shape[2], *shapes[0])
+        return [d.astype(f32) if s == shapes[0] else d.T.astype(f32) for d, s in zip(done, shapes)]
+    far_y = shifted(done, "y", 1)
+    far_core, far_both = shifted(done, "core", 1), shifted(far_y, "core", 1)
+    me = jnp.stack([lax.axis_index("y"), lax.axis_index("core")])
+
+    def whole(shape):
+        return pl.BlockSpec(shape, lambda i: (0,) * len(shape))
+
+    return pl.pallas_call(
+        finish_kernel,
+        grid=(1,),
+        in_specs=[pl.BlockSpec(memory_space=pltpu.SMEM)] + [whole(done.shape)] * 4,
+        out_specs=[whole(shape) for shape in shapes],
+        out_shape=[jax.ShapeDtypeStruct(shape, f32) for shape in shapes],
+        scratch_shapes=[pltpu.VMEM(shapes[0], f32)],
+        compiler_params=pltpu.CompilerParams(vmem_limit_bytes=VMEM),
+    )(me, done, far_y, far_core, far_both)
 
 
 def normalize(values):
@@ -266,8 +304,12 @@
     x_ref,
     *rest,
 ):
-    *source, in_ref, mine_a, mine_b, other_a, other_b = rest
-    text_ref, text_grad_ref = source if source else (x_ref, in_ref)
+    cross = len(rest) > 5
+    if cross:
+        text_ref, text_grad_ref, in_ref, mine_a, mine_b, other_a, other_b = rest
+    else:
+        in_ref, mine_a, mine_b, other_a, other_b = rest
+        text_ref = x_ref
     query = q_ref[...] * bf16(HD**-0.5)
     keys, values, bias = k_ref[...], v_ref[...], bias_ref[0]
     back = back_ref[...]
@@ -290,10 +332,10 @@
     @pl.when(pl.program_id(1) == 0)
     def _():
         in_ref[...] = jnp.zeros_like(in_ref)
-        if source:
+        if cross:
             text_grad_ref[...] = jnp.zeros_like(text_grad_ref)
 
-    if source:
+    if cross:
         in_ref[...] += matmul(gq, q_w_ref[...])
         text_grad_ref[...] += matmul(gk, k_w_ref[...]) + matmul(gv, v_w_ref[...])
     else:
@@ -464,33 +506,35 @@
     half = width // 2
     first, more, feed_part = weight_parts(
         [
-            query_w,
-            key_w,
-            value_w,
+            query_w.T,
+            key_w.T,
+            value_w.T,
             out_w,
-            cross_query_w,
-            cross_key_w,
-            cross_value_w,
+            cross_query_w.T,
+            cross_key_w.T,
+            cross_value_w.T,
             cross_out_w,
         ],
         up_weight,
         down_weight,
     )
-    first = gather_axis(gather_axis(first, "za"), "zb")
-    more = gather_axis(more, "za", first)
-    first_left = gather_axis(first[..., :half], "x")
-    first_right = gather_axis(first[..., half:], "y")
-    more = gather_axis(more, "zb", first_left, first_right)
+    more_rows = more.shape[0] * more.shape[1]
+    gathered_more = lax.all_gather(
+        more.reshape(more_rows, width), (*MP_AXES, "y", "core"), axis=0, tiled=True
+    )
+    first_in_column = gather_axis(gather_axis(first, "za"), "zb")
+    feed_part = after(feed_part, first_in_column)
+    first_left = gather_axis(first_in_column[..., :half], "x")
+    first_right = gather_axis(first_in_column[..., half:], "y")
+    feed_part = gather_axis(feed_part, "za", first_left, first_right)
     first_left = gather_axis(first_left, "y")
     first_right = gather_axis(first_right, "x")
-    feed_part = gather_axis(feed_part, "za", more)
-    more_left = gather_axis(more[..., :half], "x", first_left, first_right)
-    more_right = gather_axis(more[..., half:], "y", first_left, first_right)
+    feed_part = gather_axis(feed_part, "zb", first_left, first_right)
     qkv = assemble(gather_axis(first_left, "core"), gather_axis(first_right, "core"))
     qkv = qkv.reshape(-1, width)
-    feed_part = gather_axis(feed_part, "zb", more_left, more_right)
 
     table_low = step_table
+    step_ids = after(step_ids, first)
     choose_step = (step_ids[:, None] == jnp.arange(step_table.shape[0])[None, :]).astype(bf16)
     silu_mine = jax.nn.silu(matmul(choose_step, table_low)).astype(bf16)
     partial_mod = matmul(silu_mine, ada_weight)
@@ -513,30 +557,33 @@
 
     shift_one, scale_one, gate_one, shift_two, scale_two, gate_two = map(per_frame, range(6))
 
+    my_steps = lax.dynamic_slice_in_dim(step_ids, position * segs_dev, segs_dev, 0)
+    digits = jnp.stack([my_steps // 256, my_steps % 256], axis=1).astype(bf16)
+    digits = jnp.pad(digits, ((0, 0), (0, 126)))
+
     same_seg = my_ids[:, :, None] == my_ids[:, None, :]
     self_bias = jnp.where(same_seg, 0.0, masked_score).astype(f32)
-    key_segment = jnp.arange(SEGS * CAPTION) // CAPTION
+    key_segment = jnp.arange(SEGS * CAPTION) % SEGS
     valid_key = (
-        jnp.arange(CAPTION)[None, None, :] < my_lens.reshape(rows_dev, SEGS)[:, :, None]
+        jnp.arange(CAPTION)[None, :, None] < my_lens.reshape(rows_dev, SEGS)[:, None, :]
     ).reshape(rows_dev, SEGS * CAPTION)
     allowed = (my_ids[:, :, None] == key_segment[None, None, :]) & valid_key[:, None, :]
     cross_bias = jnp.where(allowed, 0.0, masked_score).astype(f32)
     allowed_t = (my_ids[:, None, :] == key_segment[None, :, None]) & valid_key[:, :, None]
     cross_bias_t = jnp.where(allowed_t, 0.0, masked_score).astype(f32)
+    cross_bias = after(cross_bias, cross_bias_t, digits)
 
     base = frames.astype(f32)
-    text_flat = text.reshape(-1, width)
+    text_flat = text.reshape(rows_dev, SEGS, CAPTION, width).swapaxes(1, 2).reshape(-1, width)
     normed_one, inverse_one = normalize(base)
     first_in = (normed_one * (1.0 + scale_one) + shift_one).astype(bf16)
     query, keys, values = (
         outer_cols(first_in, qkv[i * width : (i + 1) * width]).astype(bf16) for i in range(3)
     )
     self_mix = attend(query, keys, values, self_bias)
-    more_left = gather_axis(more_left, "y", self_mix)
-    more_right = gather_axis(more_right, "x", self_mix)
     feed_up = gather_axis(feed_part[:, :, 0], "x", self_mix)
     feed_down = gather_axis(feed_part[:, :, 1], "y", self_mix)
-    whole = assemble(gather_axis(more_left, "core"), gather_axis(more_right, "core"))
+    whole = gathered_more.reshape(-1, *more.shape).swapaxes(0, 1).reshape(more.shape[0], -1, width)
     out_full, cquery_t, cout_full = whole[0], whole[1], whole[4]
     ckv_t = whole[2:4].reshape(-1, width)
     self_out = matmul(self_mix, out_full)
@@ -600,13 +647,13 @@
     )
     with jax.named_scope("feed_sums_third_stage"):
         feed_sums = third_stage(feed_sums, grad_first)
+    with jax.named_scope("cross_sums_second_stage"):
+        cross_sums = second_stage(cross_sums, grad_first)
     with jax.named_scope("self_sums_first_stage"):
-        self_sums = first_stage(*self_parts, *feed_sums[1])
-    with jax.named_scope("cross_sums_second_stage"):
-        cross_sums = second_stage(cross_sums, *sends(self_sums))
-
-    chooser = chosen.astype(f32)
-    grad_first = after(grad_first, *sends(cross_sums))
+        self_sums = first_stage(*self_parts, *sends(cross_sums), *feed_sums[1])
+
+    chooser = chosen.astype(bf16)
+    grad_first = after(grad_first, *sends(self_sums))
     mod_parts = [
         grad_first,
         grad_first * normed_one,
@@ -615,39 +662,44 @@
         grad_third * normed_three,
         grad_gate_two,
     ]
-    grad_mod = jnp.stack(
-        [
-            lax.dot_general(chooser, v, (((0,), (0,)), ((), ())), precision=highest)
-            for v in mod_parts
-        ]
-    ).astype(bf16)
-    steps_all = after(step_ids.astype(f32), grad_mod)
+    grad_mod = jnp.concatenate(
+        [inner_rows(chooser, v.astype(bf16)).astype(bf16) for v in mod_parts] + [digits], axis=1
+    )
+    with jax.named_scope("feed_sums_fourth_stage"):
+        feed_sums = fourth_stage(feed_sums, grad_mod)
+    with jax.named_scope("cross_sums_third_stage"):
+        cross_sums = third_stage(cross_sums, *feed_sums[1])
     with jax.named_scope("self_sums_second_stage"):
-        self_sums = second_stage(self_sums, grad_mod)
-    with jax.named_scope("cross_sums_third_stage"):
-        cross_sums = third_stage(cross_sums, *sends(self_sums))
-    gathered = gather_axis(grad_mod, "za", *cross_sums[1])
+        self_sums = second_stage(self_sums, *cross_sums[1])
+    with jax.named_scope("gather_mod"):
+        gathered = joined_rows(grad_mod, "za", *sends(self_sums))
+    with jax.named_scope("cross_sums_fourth_stage"):
+        cross_sums = fourth_stage(cross_sums, gathered)
+    feed_done = summed(landed(feed_sums, *cross_sums[1])).astype(bf16)
     with jax.named_scope("self_sums_third_stage"):
-        self_sums = third_stage(self_sums, gathered)
-    gathered = gather_axis(gathered, "zb", *self_sums[1])
-    feed_sums = fourth_stage(feed_sums, gathered)
-    gathered = gather_axis(gathered, "x", *feed_sums[1])
-    cross_sums = fourth_stage(cross_sums, gathered)
-    self_sums = fourth_stage(self_sums, *cross_sums[1])
-    feed_done = summed(landed(feed_sums, gathered)).astype(bf16)
-    gathered = gather_axis(gathered, "y", feed_done)
-    steps_all = gather_axis(steps_all, "y", feed_done)
+        self_sums = third_stage(self_sums, feed_done)
+    with jax.named_scope("gather_mod"):
+        gathered = joined_rows(gathered, "zb", *self_sums[1])
     cross_done = summed(landed(cross_sums, gathered)).astype(bf16)
-    gathered = gather_axis(gathered, "core", cross_done)
-    steps_all = gather_axis(steps_all, "core", cross_done).transpose(1, 0, 2).reshape(-1)
-    grad_mod_all = gathered.transpose(1, 0, 4, 3, 2, 6, 5, 7).reshape(-1, 6 * width)
+    with jax.named_scope("self_sums_fourth_stage"):
+        self_sums = fourth_stage(self_sums, cross_done)
+    with jax.named_scope("gather_mod"):
+        gathered = joined_rows(gathered, "x", *self_sums[1])
     grad_frames = grad_resid_one + norm_back(
-        normed_one, inverse_one, after(grad_first, cross_done) * (1.0 + scale_one)
-    )
-    self_done = summed(landed(self_sums, grad_frames)).astype(bf16)
-    shard_up, shard_down = rows_whole(feed_done)
-    shard_cout, shard_cquery, shard_ckey, shard_cvalue = columns_whole(cross_done)
-    shard_out, shard_query, shard_key, shard_value = columns_whole(self_done)
+        normed_one, inverse_one, after(grad_first, gathered) * (1.0 + scale_one)
+    )
+    with jax.named_scope("gather_mod"):
+        gathered = joined_rows(gathered, "y", grad_frames)
+    self_done = summed(landed(self_sums, gathered)).astype(bf16)
+    with jax.named_scope("gather_mod"):
+        gathered = joined_rows(gathered, "core", self_done)
+    grad_mod_all = gathered[:, : 6 * width]
+    digits = gathered[:, 6 * width : 6 * width + 2].astype(f32)
+    steps_all = digits[:, 0] * 256.0 + digits[:, 1]
+    up_shape, low_shape = up_weight.shape, out_w.shape
+    shard_up, shard_down = finish(feed_done, [up_shape, down_weight.shape])
+    shard_cout, shard_cquery, shard_ckey, shard_cvalue = finish(cross_done, [low_shape] * 4)
+    shard_out, shard_query, shard_key, shard_value = finish(self_done, [low_shape] * 4)
 
     choose_all = (
         steps_all[:, None] == jnp.arange(step_table.shape[0]).astype(f32)[None, :]
@@ -661,26 +713,23 @@
         choose_all.astype(f32), grad_cond, (((0,), (0,)), ((), ())), precision=highest
     )
 
-    def columns(value):
-        return value.T.astype(f32)
-
     return (
         layer_out,
         grad_frames,
-        grad_text.reshape(text.shape),
+        grad_text.reshape(rows_dev, CAPTION, SEGS, width).swapaxes(1, 2).reshape(text.shape),
         grad_table,
         grad_ada_w,
         grad_ada_b,
-        columns(shard_query),
-        columns(shard_key),
-        columns(shard_value),
-        shard_out.astype(f32),
-        columns(shard_cquery),
-        columns(shard_ckey),
-        columns(shard_cvalue),
-        shard_cout.astype(f32),
-        shard_up.astype(f32),
-        columns(shard_down),
+        shard_query.T,
+        shard_key.T,
+        shard_value.T,
+        shard_out,
+        shard_cquery.T,
+        shard_ckey.T,
+        shard_cvalue.T,
+        shard_cout,
+        shard_up,
+        shard_down,
     )
 
 

time: 376 us -> 347 us (0.923)
  waiting for transfers between devices: 103 us -> 78.1 us
  starting transfers between devices: 63.6 us -> 48.1 us
  between operations: 3.46 us -> 16.7 us
  other arithmetic: 80 us -> 68.6 us
  Pallas kernels: 71 us -> 77.5 us
  local copies, waits for them, and re-layouts: 32.4 us -> 38.2 us
  matrix products: 17.7 us -> 13.9 us
    ppermute x64 -> x57, waiting for transfers between devices: 103 us -> 78.1 us  [shifted(): lax.ppermute(value, axis, [(k, (k + steps) % count) for k in range(count)])]
    ppermute x64 -> x57, starting transfers between devices: 63.6 us -> 48.1 us  [shifted(): lax.ppermute(value, axis, [(k, (k + steps) % count) for k in range(count)])]
    another operation x60 -> x33, other arithmetic: 28.1 us -> 12.7 us  [gather_axis(): return jnp.stack([at(place) for place in range(count)])]
    pallas_call x0 -> x3, Pallas kernels: none -> 6.4 us  [finish(): pl.pallas_call(finish_kernel, grid=(1,), in_specs=[pl.BlockSpec(memory_sp...]
    dynamic_slice x4 -> x8, local copies, waits for them, and re-layouts: 0.32 us -> 5.57 us  [picked(): lax.dynamic_index_in_dim(t, which, dim, keepdims=False)]
    dot_general x6 -> x0, matrix products: 4.45 us -> none  [shards(): lax.dot_general(chooser, v, (((0,), (0,)), ((), ())), precision=highest)]
    convert_element_type x15, other arithmetic: 14.3 us -> 18.4 us  [launch(): summed(picked(terms, dim, (me + s) % count)).astype(bf16)]
    convert_element_type x7 -> x3, other arithmetic: 5.2 us -> 1.32 us  [the longest x1 1.24 us: shards(): feed_done = summed(landed(feed_sums, *cross_sums[1])).astype(bf16)]
  transfers between devices with their start and end apart: 64 -> 58, of which waited for: 29 -> 21; matrix products, arithmetic and copies ran while one was open for 30% -> 27% of each run, Pallas kernels for 14% -> 17%
where the time goes in v3:
time: 347 us; the launch traced here: 341 us
  waiting for transfers between devices  78.1 us (23%)
  Pallas kernels  77.5 us (22%)
  other arithmetic  68.6 us (20%)
  starting transfers between devices  48.1 us (14%)
  local copies, waits for them, and re-layouts  38.2 us (11%)
  between operations  16.7 us (5%)
  matrix products  13.9 us (4%)
    ppermute x57, waiting for transfers between devices, shifted(): lax.ppermute(value, axis, [(k, (k + steps) % count) for k in range(count)])  78.1 us
    ppermute x57, starting transfers between devices, shifted(): lax.ppermute(value, axis, [(k, (k + steps) % count) for k in range(count)])  48.1 us
    pallas_call x2, Pallas kernels, attend_back(): pl.pallas_call(backward_kernel, grid_spec=pltpu.PrefetchScalarGridSpec(nu...  38.7 us
    unnamed x284, local copies, waits for them, and re-layouts  21.7 us
    pallas_call x1, Pallas kernels, feed(): pl.pallas_call(feed_kernel, grid_spec=pltpu.PrefetchScalarGridSpec(num_sc...  20 us
    convert_element_type x15, other arithmetic, launch(): summed(picked(terms, dim, (me + s) % count)).astype(bf16)  18.4 us
    another operation x33, other arithmetic, gather_axis(): return jnp.stack([at(place) for place in range(count)])  12.7 us
    pallas_call x2, Pallas kernels, attend(): pl.pallas_call(forward_kernel, grid=(rows, pairs), in_specs=blocks + [pl....  11.2 us
  transfers between devices with their start and end apart: 58, of which 21 were waited for; matrix products, arithmetic and copies ran while one was open for 27% of the time, Pallas kernels for 17%

profile of v3, /device:TPU:0, one launch (start us, length us, event | category | flops | bytes accessed | tf_op | source)
XLA Modules:
  0.0 341.2 jit_solution(9160124524202321344)
XLA Ops:
  18.0 4.0 %collective-permute-start.3 = (bf16[3,24,768]{2,1,0:T(8,128)(2,1)S(1)}, bf16[3,24,768]{2,1,0:T(8,128)(2,1)}, u32[]{:S(2)}, u32[]{:S(2)}) collective-permute-start(bf16[3,24,768]{2,1,0:T(8,128)(2,1)S(1)} %get-tuple-element.84), channel_id=1, source_target_pairs={{0,4},{4,0},{1,5},{5,1},{2,6},{6,2},{3,7},{7,3},{8,12},{12,8},{9,1... | collective-permute-start | bytes 331784 | tf_op jit(solution)/shard_map/to_za_1/ppermute | solution.py:29
  38.5 10.9 %collective-permute-done.4 = bf16[2,3,24,768]{3,2,1,0:T(8,128)(2,1)S(1)} collective-permute-done((bf16[2,3,24,768]{3,2,1,0:T(8,128)(2,1)S(1)}, bf16[2,3,24,768]{3,2,1,0:T(8,128)(2,1)S(1)}, u32[]{:S(2)}, u32[]{:S(2)}) %collective-permute-start.4) | collective-permute-done | bytes 221216 | tf_op jit(solution)/shard_map/to_zb_1/ppermute | solution.py:29
  56.6 5.6 %collective-permute-done.8 = bf16[2,2,3,24,384]{4,3,2,1,0:T(8,128)(2,1)S(1)} collective-permute-done((bf16[2,2,3,24,384]{4,3,2,1,0:T(8,128)(2,1)S(1)}, bf16[2,2,3,24,384]{4,3,2,1,0:T(8,128)(2,1)S(1)}, u32[]{:S(2)}, u32[]{:S(2)}) %collective-permute-start.8) | collective-permute-done | bytes 221216 | tf_op jit(solution)/shard_map/to_y_1/ppermute | solution.py:29
  63.7 2.3 collective-permute-done.5
  67.9 2.5 collective-permute-start.12
  70.4 4.6 %collective-permute-done.9 = bf16[2,2,2,3,24,384]{5,4,3,2,1,0:T(8,128)(2,1)S(1)} collective-permute-done((bf16[2,2,2,3,24,384]{5,4,3,2,1,0:T(8,128)(2,1)S(1)}, bf16[2,2,2,3,24,384]{5,4,3,2,1,0:T(8,128)(2,1)S(1)}, u32[]{:S(2)}, u32[]{:S(2)}) %collective-permute-start.9) | collective-permute-done | bytes 442400 | tf_op jit(solution)/shard_map/to_x_1/ppermute | solution.py:29
  77.6 3.0 fusion.14
  80.7 13.1 %collective-permute-done.12 = bf16[2,2,96,768]{3,2,0,1:T(8,128)(2,1)S(1)} collective-permute-done((bf16[2,2,96,768]{3,2,0,1:T(8,128)(2,1)S(1)}, bf16[2,2,96,768]{3,2,0,1:T(8,128)(2,1)S(1)}, u32[]{:S(2)}, u32[]{:S(2)}) %collective-permute-start.12) | collective-permute-done | bytes 589856 | tf_op jit(solution)/shard_map/to_zb_1/ppermute | solution.py:29
  99.4 5.5 %shard_map.307.mix_ref = bf16[512,768]{1,0:T(8,128)(2,1)S(1)} custom-call(bf16[512,768]{1,0:T(8,128)(2,1)S(1)} %convolution_convert_fusion.3.q_ref, bf16[512,768]{1,0:T(8,128)(2,1)S(1)} %convolution_convert_fusion.2.k_ref, bf16[512,768]{1,0:T(8,128)(2,1)S(1)} %convolution_convert_fusion.1.v_ref, f32[1,512,512]{2,1,0:T(8,128)S(1)} %compare_select_fusion.bias_ref), custom_call_target="tpu_custom_call" | custom-call | tf_op jit(solution)/shard_map/pallas_call | solution.py:360
  112.4 3.2 fusion.146
  115.7 2.7 fusion.145
  121.9 5.7 %shard_map.308.mix_ref = bf16[512,768]{1,0:T(8,128)(2,1)S(1)} custom-call(bf16[512,768]{1,0:T(8,128)(2,1)S(1)} %convolution_convert_fusion.q_ref, bf16[308,768]{1,0:T(8,128)(2,1)S(1)} %fusion.18.k_ref, bf16[308,768]{1,0:T(8,128)(2,1)S(1)} %fusion.19.v_ref, f32[1,512,308]{2,1,0:T(8,128)S(1)} %and_select_fusion.bias_ref), custom_call_target="tpu_custom_call" | custom-call | tf_op jit(solution)/shard_map/pallas_call | solution.py:360
  127.7 3.6 %collective-permute-done.14 = bf16[2,2,2,96,768]{4,3,2,1,0:T(8,128)(2,1)} collective-permute-done((bf16[2,2,2,96,768]{4,3,2,1,0:T(8,128)(2,1)}, bf16[2,2,2,96,768]{4,3,2,1,0:T(8,128)(2,1)}, u32[]{:S(2)}, u32[]{:S(2)}) %collective-permute-start.14) | collective-permute-done | bytes 1179680 | tf_op jit(solution)/shard_map/to_y_1/ppermute | solution.py:29
  139.5 2.4 add_convert_fusion.3.x_ref
  142.0 2.2 collective-permute-done.18.down_far
  145.6 20.0 %shard_map.309 = (f32[512,768]{1,0:T(8,128)S(1)}, f32[512,768]{1,0:T(8,128)S(1)}, bf16[8,384,384]{2,1,0:T(8,128)(2,1)}, bf16[8,384,384]{2,1,0:T(8,128)(2,1)}, bf...) custom-call(s32[1]{0:T(128)} %bitcast.51.core_ref, bf16[512,768]{1,0:T(8,128)(2,1)S(1)} %add_convert_fusion.3.x_ref, ...), custom_call_target="tpu_custom_call" | custom-call | tf_op jit(solution)/shard_map/pallas_call | solution.py:456
  167.4 2.3 fusion.141
  169.8 3.3 fusion.144
  173.1 2.8 fusion.21
  177.6 2.8 fusion.22
  180.9 17.8 %shard_map.310 = (f32[308,768]{1,0:T(8,128)S(1)}, f32[512,768]{1,0:T(8,128)}, bf16[2,768,384]{2,1,0:T(8,128)(2,1)}, bf16[2,768,384]{2,1,0:T(8,128)(2,1)}, bf16[2...) custom-call(s32[1]{0:T(128)} %bitcast.51.core_ref, bf16[512,768]{1,0:T(8,128)(2,1)S(1)} %copy-done.20, ...), custom_call_target="tpu_custom_call" | custom-call | tf_op jit(solution)/shard_map/pallas_call | solution.py:383
  204.2 4.3 %collective-permute-done.24 = bf16[1,2,2,2,192,384]{5,4,2,1,3,0:T(8,128)(2,1)} collective-permute-done((bf16[1,2,2,2,192,384]{5,4,2,1,3,0:T(8,128)(2,1)}, bf16[1,2,2,2,192,384]{5,4,2,1,3,0:T(8,128)(2,1)}, u32[]{:S(2)}, u32[]{:S(2)}) %collective-permute-start.24) | collective-permute-done | bytes 1179680 | tf_op jit(solution)/shard_map/feed_sums_first_stage/to_y_1/ppermute | solution.py:29
  210.9 2.7 fusion.30
  216.7 2.3 fusion.29
  221.4 21.0 %shard_map.311 = (f32[512,768]{1,0:T(8,128)}, bf16[2,768,384]{2,1,0:T(8,128)(2,1)}, bf16[2,768,384]{2,1,0:T(8,128)(2,1)}, bf16[2,768,384]{2,1,0:T(8,128)(2,1)}, bf16[2,768,384]{2,1,0:T(8,128)(2,1)}) custom-call(s32[1]{0:T(128)} %bitcast.51.core_ref, bf16[512,768]{1,0:T(8,128)(2,1)S(1)} %copy-done.6, bf16[512,768]{1,0:T(8,128)(2,1)S(1)} %copy-done.8, ...), custom_call_target="tpu_custom_call" | custom-call | tf_op jit(solution)/shard_map/pallas_call | solution.py:383
  261.8 4.8 %collective-permute-done.34 = bf16[2,1,2,192,384]{4,3,0,2,1:T(8,128)(2,1)S(1)} collective-permute-done((bf16[2,1,2,192,384]{4,3,0,2,1:T(8,128)(2,1)S(1)}, bf16[2,1,2,192,384]{4,3,0,2,1:T(8,128)(2,1)S(1)}, u32[]{:S(2)}, u32[]{:S(2)}) %collective-permute-start.34) | collective-permute-done | bytes 589856 | tf_op jit(solution)/shard_map/feed_sums_third_stage/to_zb_1/ppermute | solution.py:29
  280.9 7.6 %collective-permute-done.40 = bf16[2,2,2,48,384]{4,3,1,0,2:T(8,128)(2,1)} collective-permute-done((bf16[2,2,2,48,384]{4,3,1,0,2:T(8,128)(2,1)}, bf16[2,2,2,48,384]{4,3,1,0,2:T(8,128)(2,1)}, u32[]{:S(2)}, u32[]{:S(2)}) %collective-permute-start.40) | collective-permute-done | bytes 294944 | tf_op jit(solution)/shard_map/cross_sums_third_stage/to_zb_1/ppermute | solution.py:29
  298.4 4.1 %collective-permute-done.43 = bf16[2,2,2,48,384]{4,3,1,0,2:T(8,128)(2,1)S(1)} collective-permute-done((bf16[2,2,2,48,384]{4,3,1,0,2:T(8,128)(2,1)S(1)}, bf16[2,2,2,48,384]{4,3,1,0,2:T(8,128)(2,1)S(1)}, u32[]{:S(2)}, u32[]{:S(2)}) %collective-permute-start.43) | collective-permute-done | bytes 294944 | tf_op jit(solution)/shard_map/self_sums_third_stage/to_zb_1/ppermute | solution.py:29
  313.5 4.3 %collective-permute-done.51.far_y = bf16[4,48,384]{2,1,0:T(8,128)(2,1)S(1)} collective-permute-done((bf16[4,48,384]{2,1,0:T(8,128)(2,1)S(1)}, bf16[4,48,384]{2,1,0:T(8,128)(2,1)S(1)}, u32[]{:S(2)}, u32[]{:S(2)}) %collective-permute-start.51) | collective-permute-done | bytes 147488 | tf_op jit(solution)/shard_map/to_y_1/ppermute | solution.py:29
  321.4 2.2 shard_map.314
  323.6 2.1 shard_map.313
  325.7 2.1 shard_map.312
  (538 shorter events, 146.6 us)
Async XLA Ops:
  7.2 105.1 %all-gather.2.cloned.1.call-start = ((), (), s32[]{:S(2)}) async-start(), calls=%async_computation | async-start | bytes 6082560 | tf_op jit(solution)/shard_map/all_gather | solution.py:522
  18.0 16.3 %collective-permute-start.3 = (bf16[3,24,768]{2,1,0:T(8,128)(2,1)S(1)}, bf16[3,24,768]{2,1,0:T(8,128)(2,1)}, u32[]{:S(2)}, u32[]{:S(2)}) collective-permute-start(bf16[3,24,768]{2,1,0:T(8,128)(2,1)S(1)} %get-tuple-element.84), channel_id=1, source_target_pairs={{0,4},{4,0},{1,5},{5,1},{2,6},{6,2},{3,7},{7,3},{8,12},{12,8},{9,1... | collective-permute-start | bytes 331784 | tf_op jit(solution)/shard_map/to_za_1/ppermute | solution.py:29
  23.6 13.3 %collective-permute-start = (f32[2,2,4,4608]{3,2,1,0:T(4,128)}, f32[2,2,4,4608]{3,2,1,0:T(4,128)S(1)}, u32[]{:S(2)}, u32[]{:S(2)}) collective-permute-start(f32[2,2,4,4608]{3,2,1,0:T(4,128)} %dynamic-slice_bitcast_fusion), channel_id=1, source_target_pairs={{0,1},{1,0},{2,3},{3,2},{4,5},{5,4},{6,7},{7,6},{8,9},{9,8},{10,11... | collective-permute-start | bytes 884744 | tf_op jit(solution)/shard_map/to_x_1/ppermute | solution.py:29
  25.1 41.7 %collective-permute-start.11 = (bf16[2,96,768]{2,1,0:T(8,128)(2,1)S(1)}, bf16[2,96,768]{2,1,0:T(8,128)(2,1)}, u32[]{:S(2)}, u32[]{:S(2)}) collective-permute-start(bf16[2,96,768]{2,1,0:T(8,128)(2,1)S(1)} %get-tuple-element.89), channel_id=1, source_target_pairs={{0,4},{4,0},{1,5},{5,1},{2,6},{6,2},{3,7},{7,3},{8,12},{12,8},{9,1... | collective-permute-start | bytes 884744 | tf_op jit(solution)/shard_map/to_za_1/ppermute | solution.py:29
  35.2 14.1 %collective-permute-start.4 = (bf16[2,3,24,768]{3,2,1,0:T(8,128)(2,1)S(1)}, bf16[2,3,24,768]{3,2,1,0:T(8,128)(2,1)S(1)}, u32[]{:S(2)}, u32[]{:S(2)}) collective-permute-start(bf16[2,3,24,768]{3,2,1,0:T(8,128)(2,1)S(1)} %pad_maximum_fusion.14), channel_id=1, source_target_pairs={{0,2},{2,0},{1,3},{3,1},{4,6},{6,4},{5,7},{7,5},{8,10},{10,8},{9,1... | collective-permute-start | bytes 663560 | tf_op jit(solution)/shard_map/to_zb_1/ppermute | solution.py:29
  37.9 12.7 %collective-permute-start.1 = (bf16[2,4,4608]{2,1,0:T(4,128)(2,1)S(1)}, bf16[2,4,4608]{2,1,0:T(4,128)(2,1)S(1)}, u32[]{:S(2)}, u32[]{:S(2)}) collective-permute-start(bf16[2,4,4608]{2,1,0:T(4,128)(2,1)S(1)} %dynamic-slice_bitcast_fusion.1), channel_id=1, source_target_pairs={{0,2},{2,0},{1,3},{3,1},{4,6},{6,4},{5,7},{7,5},{8,10},{10,8},{9,1... | collective-permute-start | bytes 221192 | tf_op jit(solution)/shard_map/to_zb_1/ppermute | solution.py:29
  62.3 12.7 %collective-permute-start.9 = (bf16[2,2,2,3,24,384]{5,4,3,2,1,0:T(8,128)(2,1)S(1)}, bf16[2,2,2,3,24,384]{5,4,3,2,1,0:T(8,128)(2,1)S(1)}, u32[]{:S(2)}, u32[]{:S(2)}) collective-permute-start(bf16[2,2,2,3,24,384]{5,4,3,2,1,0:T(8,128)(2,1)S(1)} %pad_maximum_fusion.12), channel_id=1, source_target_pairs={{0,1},{1,0},{2,3},{3,2},{4,5},{5,4},{6,7},{7,6},{8,9},{9,8},{10,11... | collective-permute-start | bytes 1327112 | tf_op jit(solution)/shard_map/to_x_1/ppermute | solution.py:29
  67.9 25.8 %collective-permute-start.12 = (bf16[2,2,96,768]{3,2,0,1:T(8,128)(2,1)S(1)}, bf16[2,2,96,768]{3,2,0,1:T(8,128)(2,1)S(1)}, u32[]{:S(2)}, u32[]{:S(2)}) collective-permute-start(bf16[2,2,96,768]{3,2,0,1:T(8,128)(2,1)S(1)} %pad_maximum_fusion.9), channel_id=1, source_target_pairs={{0,2},{2,0},{1,3},{3,1},{4,6},{6,4},{5,7},{7,5},{8,10},{10,8},{9,1... | collective-permute-start | bytes 1769480 | tf_op jit(solution)/shard_map/to_zb_1/ppermute | solution.py:29
  75.4 18.7 %collective-permute-start.10 = (bf16[2,2,2,2,3,24,384]{6,5,4,3,2,0,1:T(8,128)(2,1)S(1)}, bf16[2,2,2,2,3,24,384]{6,5,4,3,2,0,1:T(8,128)(2,1)S(1)}, u32[]{:S(2)}, u32[]{:S(2)}) collective-permute-start(bf16[2,2,2,2,3,24,384]{6,5,4,3,2,0,1:T(8,128)(2,1)S(1)} %copy.129), channel_id=1, source_target_pairs={{0,8},{8,0},{1,9},{9,1},{2,10},{10,2},{3,11},{11,3},{4,12},{12,4},... | collective-permute-start | bytes 2654216 | tf_op jit(solution)/shard_map/to_core_1/ppermute | solution.py:29
  77.4 16.7 %collective-permute-start.7 = (bf16[2,2,2,2,3,24,384]{6,5,4,3,2,0,1:T(8,128)(2,1)S(1)}, bf16[2,2,2,2,3,24,384]{6,5,4,3,2,0,1:T(8,128)(2,1)S(1)}, u32[]{:S(2)}, u32[]{:S(2)}) collective-permute-start(bf16[2,2,2,2,3,24,384]{6,5,4,3,2,0,1:T(8,128)(2,1)S(1)} %pad_maximum_fusion.5), channel_id=1, source_target_pairs={{0,8},{8,0},{1,9},{9,1},{2,10},{10,2},{3,11},{11,3},{4,12},{12,4},... | collective-permute-start | bytes 2654216 | tf_op jit(solution)/shard_map/to_core_1/ppermute | solution.py:29
  94.0 14.3 %collective-permute-start.15 = (bf16[2,2,96,768]{3,2,1,0:T(8,128)(2,1)S(1)}, bf16[2,2,96,768]{3,2,1,0:T(8,128)(2,1)S(1)}, u32[]{:S(2)}, u32[]{:S(2)}) collective-permute-start(bf16[2,2,96,768]{3,2,1,0:T(8,128)(2,1)S(1)} %get-tuple-element.228), channel_id=1, source_target_pairs={{0,16},{16,0},{1,17},{17,1},{2,18},{18,2},{3,19},{19,3},{4,20},{20... | collective-permute-start | bytes 1769480 | tf_op jit(solution)/shard_map/to_y_1/ppermute | solution.py:29
  107.2 24.1 %collective-permute-start.14 = (bf16[2,2,2,96,768]{4,3,2,1,0:T(8,128)(2,1)}, bf16[2,2,2,96,768]{4,3,2,1,0:T(8,128)(2,1)}, u32[]{:S(2)}, u32[]{:S(2)}) collective-permute-start(bf16[2,2,2,96,768]{4,3,2,1,0:T(8,128)(2,1)} %pad_maximum_fusion.3), channel_id=1, source_target_pairs={{0,16},{16,0},{1,17},{17,1},{2,18},{18,2},{3,19},{19,3},{4,20},{20... | collective-permute-start | bytes 3538952 | tf_op jit(solution)/shard_map/to_y_1/ppermute | solution.py:29
  110.4 24.2 %collective-permute-start.16 = (bf16[2,2,2,96,768]{4,3,2,1,0:T(8,128)(2,1)}, bf16[2,2,2,96,768]{4,3,2,1,0:T(8,128)(2,1)}, u32[]{:S(2)}, u32[]{:S(2)}) collective-permute-start(bf16[2,2,2,96,768]{4,3,2,1,0:T(8,128)(2,1)} %pad_maximum_fusion.4), channel_id=1, source_target_pairs={{0,1},{1,0},{2,3},{3,2},{4,5},{5,4},{6,7},{7,6},{8,9},{9,8},{10,11... | collective-permute-start | bytes 3538952 | tf_op jit(solution)/shard_map/to_x_1/ppermute | solution.py:29
  175.9 28.3 %collective-permute-start.23 = (bf16[1,2,2,2,192,384]{5,4,2,1,3,0:T(8,128)(2,1)}, bf16[1,2,2,2,192,384]{5,4,2,1,3,0:T(8,128)(2,1)}, u32[]{:S(2)}, u32[]{:S(2)}) collective-permute-start(bf16[1,2,2,2,192,384]{5,4,2,1,3,0:T(8,128)(2,1)} %fusion.21), channel_id=1, source_target_pairs={{0,1},{1,0},{2,3},{3,2},{4,5},{5,4},{6,7},{7,6},{8,9},{9,8},{10,11... | collective-permute-start | bytes 3538952 | tf_op jit(solution)/shard_map/feed_sums_first_stage/to_x_1/ppermute | solution.py:29
  180.4 28.0 %collective-permute-start.24 = (bf16[1,2,2,2,192,384]{5,4,2,1,3,0:T(8,128)(2,1)}, bf16[1,2,2,2,192,384]{5,4,2,1,3,0:T(8,128)(2,1)}, u32[]{:S(2)}, u32[]{:S(2)}) collective-permute-start(bf16[1,2,2,2,192,384]{5,4,2,1,3,0:T(8,128)(2,1)} %fusion.22), channel_id=1, source_target_pairs={{0,16},{16,0},{1,17},{17,1},{2,18},{18,2},{3,19},{19,3},{4,20},{20... | collective-permute-start | bytes 3538952 | tf_op jit(solution)/shard_map/feed_sums_first_stage/to_y_1/ppermute | solution.py:29
  198.8 14.8 %collective-permute-start.22 = (bf16[2,768,384]{2,1,0:T(8,128)(2,1)}, bf16[2,768,384]{2,1,0:T(8,128)(2,1)S(1)}, u32[]{:S(2)}, u32[]{:S(2)}) collective-permute-start(bf16[2,768,384]{2,1,0:T(8,128)(2,1)} %get-tuple-element.107), channel_id=1, source_target_pairs={{0,8},{8,0},{1,9},{9,1},{2,10},{10,2},{3,11},{11,3},{4,12},{12,4},... | collective-permute-start | bytes 3538952 | tf_op jit(solution)/shard_map/cross_sums_first_stage/to_core_1/ppermute | solution.py:29
  210.5 35.2 %collective-permute-start.26 = (bf16[2,2,2,2,48,384]{5,4,0,2,1,3:T(8,128)(2,1)}, bf16[2,2,2,2,48,384]{5,4,0,2,1,3:T(8,128)(2,1)}, u32[]{:S(2)}, u32[]{:S(2)}) collective-permute-start(bf16[2,2,2,2,48,384]{5,4,0,2,1,3:T(8,128)(2,1)} %fusion.52), channel_id=1, source_target_pairs={{0,1},{1,0},{2,3},{3,2},{4,5},{5,4},{6,7},{7,6},{8,9},{9,8},{10,11... | collective-permute-start | bytes 1769480 | tf_op jit(solution)/shard_map/cross_sums_first_stage/to_x_1/ppermute | solution.py:29
  214.6 31.2 %collective-permute-start.27 = (bf16[2,2,2,2,48,384]{5,4,0,2,1,3:T(8,128)(2,1)}, bf16[2,2,2,2,48,384]{5,4,0,2,1,3:T(8,128)(2,1)}, u32[]{:S(2)}, u32[]{:S(2)}) collective-permute-start(bf16[2,2,2,2,48,384]{5,4,0,2,1,3:T(8,128)(2,1)} %fusion.53), channel_id=1, source_target_pairs={{0,16},{16,0},{1,17},{17,1},{2,18},{18,2},{3,19},{19,3},{4,20},{20... | collective-permute-start | bytes 1769480 | tf_op jit(solution)/shard_map/cross_sums_first_stage/to_y_1/ppermute | solution.py:29
  215.1 30.7 %collective-permute-start.28 = (bf16[1,2,2,192,384]{4,3,2,1,0:T(8,128)(2,1)}, bf16[1,2,2,192,384]{4,3,2,1,0:T(8,128)(2,1)}, u32[]{:S(2)}, u32[]{:S(2)}) collective-permute-start(bf16[1,2,2,192,384]{4,3,2,1,0:T(8,128)(2,1)} %fusion.30), channel_id=1, source_target_pairs={{0,16},{16,0},{1,17},{17,1},{2,18},{18,2},{3,19},{19,3},{4,20},{20... | collective-permute-start | bytes 1769480 | tf_op jit(solution)/shard_map/feed_sums_second_stage/to_y_1/ppermute | solution.py:29
  219.0 26.8 %collective-permute-start.29 = (bf16[1,2,2,192,384]{4,3,2,1,0:T(8,128)(2,1)}, bf16[1,2,2,192,384]{4,3,2,1,0:T(8,128)(2,1)}, u32[]{:S(2)}, u32[]{:S(2)}) collective-permute-start(bf16[1,2,2,192,384]{4,3,2,1,0:T(8,128)(2,1)} %fusion.29), channel_id=1, source_target_pairs={{0,1},{1,0},{2,3},{3,2},{4,5},{5,4},{6,7},{7,6},{8,9},{9,8},{10,11... | collective-permute-start | bytes 1769480 | tf_op jit(solution)/shard_map/feed_sums_second_stage/to_x_1/ppermute | solution.py:29
  246.9 22.0 %collective-permute-start.33 = (bf16[2,2,2,48,384]{4,3,0,2,1:T(8,128)(2,1)S(1)}, bf16[2,2,2,48,384]{4,3,0,2,1:T(8,128)(2,1)S(1)}, u32[]{:S(2)}, u32[]{:S(2)}) collective-permute-start(bf16[2,2,2,48,384]{4,3,0,2,1:T(8,128)(2,1)S(1)} %fusion.77), channel_id=1, source_target_pairs={{0,16},{16,0},{1,17},{17,1},{2,18},{18,2},{3,19},{19,3},{4,20},{20... | collective-permute-start | bytes 884744 | tf_op jit(solution)/shard_map/cross_sums_second_stage/to_y_1/ppermute | solution.py:29
  251.1 15.5 %collective-permute-start.34 = (bf16[2,1,2,192,384]{4,3,0,2,1:T(8,128)(2,1)S(1)}, bf16[2,1,2,192,384]{4,3,0,2,1:T(8,128)(2,1)S(1)}, u32[]{:S(2)}, u32[]{:S(2)}) collective-permute-start(bf16[2,1,2,192,384]{4,3,0,2,1:T(8,128)(2,1)S(1)} %fusion.61), channel_id=1, source_target_pairs={{0,2},{2,0},{1,3},{3,1},{4,6},{6,4},{5,7},{7,5},{8,10},{10,8},{9,1... | collective-permute-start | bytes 1769480 | tf_op jit(solution)/shard_map/feed_sums_third_stage/to_zb_1/ppermute | solution.py:29
  253.3 17.0 %collective-permute-start.35 = (bf16[2,2,2,48,384]{4,3,0,2,1:T(8,128)(2,1)S(1)}, bf16[2,2,2,48,384]{4,3,0,2,1:T(8,128)(2,1)S(1)}, u32[]{:S(2)}, u32[]{:S(2)}) collective-permute-start(bf16[2,2,2,48,384]{4,3,0,2,1:T(8,128)(2,1)S(1)} %fusion.76), channel_id=1, source_target_pairs={{0,1},{1,0},{2,3},{3,2},{4,5},{5,4},{6,7},{7,6},{8,9},{9,8},{10,11... | collective-permute-start | bytes 884744 | tf_op jit(solution)/shard_map/cross_sums_second_stage/to_x_1/ppermute | solution.py:29
  254.2 20.8 %collective-permute-start.32 = (bf16[2,2,2,2,48,384]{5,4,0,2,1,3:T(8,128)(2,1)S(1)}, bf16[2,2,2,2,48,384]{5,4,0,2,1,3:T(8,128)(2,1)S(1)}, u32[]{:S(2)}, u32[]{:S(2)}) collective-permute-start(bf16[2,2,2,2,48,384]{5,4,0,2,1,3:T(8,128)(2,1)S(1)} %fusion.54), channel_id=1, source_target_pairs={{0,1},{1,0},{2,3},{3,2},{4,5},{5,4},{6,7},{7,6},{8,9},{9,8},{10,11... | collective-permute-start | bytes 1769480 | tf_op jit(solution)/shard_map/self_sums_first_stage/to_x_1/ppermute | solution.py:29
  255.8 19.3 %collective-permute-start.36 = (bf16[2,2,2,2,48,384]{5,4,0,2,1,3:T(8,128)(2,1)S(1)}, bf16[2,2,2,2,48,384]{5,4,0,2,1,3:T(8,128)(2,1)S(1)}, u32[]{:S(2)}, u32[]{:S(2)}) collective-permute-start(bf16[2,2,2,2,48,384]{5,4,0,2,1,3:T(8,128)(2,1)S(1)} %fusion.55), channel_id=1, source_target_pairs={{0,16},{16,0},{1,17},{17,1},{2,18},{18,2},{3,19},{19,3},{4,20},{20... | collective-permute-start | bytes 1769480 | tf_op jit(solution)/shard_map/self_sums_first_stage/to_y_1/ppermute | solution.py:29
  268.8 20.8 %collective-permute-start.39 = (bf16[2,1,192,384]{3,2,0,1:T(8,128)(2,1)}, bf16[2,1,192,384]{3,2,0,1:T(8,128)(2,1)}, u32[]{:S(2)}, u32[]{:S(2)}) collective-permute-start(bf16[2,1,192,384]{3,2,0,1:T(8,128)(2,1)} %fusion.73), channel_id=1, source_target_pairs={{0,4},{4,0},{1,5},{5,1},{2,6},{6,2},{3,7},{7,3},{8,12},{12,8},{9,1... | collective-permute-start | bytes 884744 | tf_op jit(solution)/shard_map/feed_sums_fourth_stage/to_za_1/ppermute | solution.py:29
  273.3 15.2 %collective-permute-start.40 = (bf16[2,2,2,48,384]{4,3,1,0,2:T(8,128)(2,1)}, bf16[2,2,2,48,384]{4,3,1,0,2:T(8,128)(2,1)}, u32[]{:S(2)}, u32[]{:S(2)}) collective-permute-start(bf16[2,2,2,48,384]{4,3,1,0,2:T(8,128)(2,1)} %fusion.85), channel_id=1, source_target_pairs={{0,2},{2,0},{1,3},{3,1},{4,6},{6,4},{5,7},{7,5},{8,10},{10,8},{9,1... | collective-permute-start | bytes 884744 | tf_op jit(solution)/shard_map/cross_sums_third_stage/to_zb_1/ppermute | solution.py:29
  275.9 16.9 %collective-permute-start.38 = (bf16[2,2,2,48,384]{4,3,0,2,1:T(8,128)(2,1)}, bf16[2,2,2,48,384]{4,3,0,2,1:T(8,128)(2,1)}, u32[]{:S(2)}, u32[]{:S(2)}) collective-permute-start(bf16[2,2,2,48,384]{4,3,0,2,1:T(8,128)(2,1)} %fusion.70), channel_id=1, source_target_pairs={{0,16},{16,0},{1,17},{17,1},{2,18},{18,2},{3,19},{19,3},{4,20},{20... | collective-permute-start | bytes 884744 | tf_op jit(solution)/shard_map/self_sums_second_stage/to_y_1/ppermute | solution.py:29
  278.4 14.4 %collective-permute-start.41 = (bf16[2,2,2,48,384]{4,3,0,2,1:T(8,128)(2,1)}, bf16[2,2,2,48,384]{4,3,0,2,1:T(8,128)(2,1)}, u32[]{:S(2)}, u32[]{:S(2)}) collective-permute-start(bf16[2,2,2,48,384]{4,3,0,2,1:T(8,128)(2,1)} %fusion.69), channel_id=1, source_target_pairs={{0,1},{1,0},{2,3},{3,2},{4,5},{5,4},{6,7},{7,6},{8,9},{9,8},{10,11... | collective-permute-start | bytes 884744 | tf_op jit(solution)/shard_map/self_sums_second_stage/to_x_1/ppermute | solution.py:29
  279.7 15.6 %collective-permute-start.37 = (bf16[8,4736]{1,0:T(8,128)(2,1)}, bf16[8,4736]{1,0:T(8,128)(2,1)S(1)}, u32[]{:S(2)}, u32[]{:S(2)}) collective-permute-start(bf16[8,4736]{1,0:T(8,128)(2,1)} %reshape.986), channel_id=1, source_target_pairs={{0,2},{2,0},{1,3},{3,1},{4,6},{6,4},{5,7},{7,5},{8,10},{10,8},{9,1... | collective-permute-start | bytes 227336 | tf_op jit(solution)/shard_map/gather_mod/to_zb_1/ppermute | solution.py:29
  290.9 21.2 %collective-permute-start.54 = (bf16[2,192,384]{2,1,0:T(8,128)(2,1)S(1)}, bf16[2,192,384]{2,1,0:T(8,128)(2,1)S(1)}, u32[]{:S(2)}, u32[]{:S(2)}) collective-permute-start(bf16[2,192,384]{2,1,0:T(8,128)(2,1)S(1)} %bitcast.370), channel_id=1, source_target_pairs={{0,16},{16,0},{1,17},{17,1},{2,18},{18,2},{3,19},{19,3},{4,20},{20... | collective-permute-start | bytes 884744 | tf_op jit(solution)/shard_map/to_y_1/ppermute | solution.py:29
  310.6 17.2 %collective-permute-start.46 = (bf16[64,4736]{1,0:T(8,128)(2,1)}, bf16[64,4736]{1,0:T(8,128)(2,1)}, u32[]{:S(2)}, u32[]{:S(2)}) collective-permute-start(bf16[64,4736]{1,0:T(8,128)(2,1)} %bitcast.145), channel_id=1, source_target_pairs={{0,8},{8,0},{1,9},{9,1},{2,10},{10,2},{3,11},{11,3},{4,12},{12,4},... | collective-permute-start | bytes 1818632 | tf_op jit(solution)/shard_map/gather_mod/to_core_1/ppermute | solution.py:29
  (168 other events, 1691.1 us)
Sparse Core Ops, SparseCore 0:
  25.2 77.7 all-gather.1

commit v4 on v3

--- a/solution.py
+++ b/solution.py
@@ -131,29 +131,38 @@
     return whole.reshape(whole.shape[0], -1, whole.shape[-1])
 
 
-def parts_kernel(mine_ref, *refs):
-    *sources, up_ref, down_ref, first_ref, more_ref, feed_ref, row_ref, tall_ref = refs
-    rows, hidden = first_ref.shape[1], feed_ref.shape[1]
-
-    def own(ref, count):
-        return ref[pl.ds(pl.multiple_of(mine_ref[0] * count, 8), count), :].astype(bf16)
-
+def rows_kernel(mine_ref, *refs):
+    *sources, first_ref, more_ref, sems = refs
+    rows = first_ref.shape[1]
+    own = pl.ds(pl.multiple_of(mine_ref[0] * rows, 8), rows)
+    copies = []
     for which, source in enumerate(sources):
-        row_ref[...] = source[...].astype(f32)
-        target, place = (first_ref, which) if which < 3 else (more_ref, which - 3)
-        target[place] = own(row_ref, rows)
-    tall_ref[...] = up_ref[...].astype(f32).T
-    feed_ref[0] = own(tall_ref, hidden)
-    tall_ref[...] = down_ref[...].astype(f32)
-    feed_ref[1] = own(tall_ref, hidden)
+        target = first_ref.at[which] if which < 3 else more_ref.at[which - 3]
+        copies.append(pltpu.make_async_copy(source.at[own, :], target, sems.at[which]))
+    for copy in copies:
+        copy.start()
+    for copy in copies:
+        copy.wait()
+
+
+def feed_rows_kernel(mine_ref, up_ref, down_ref, feed_ref, wide_ref, tall_ref, sems):
+    rows = feed_ref.shape[1]
+    own = pl.ds(pl.multiple_of(mine_ref[0] * rows, 8), rows)
+    down = pltpu.make_async_copy(down_ref.at[own, :], feed_ref.at[1], sems.at[0])
+    up = pltpu.make_async_copy(up_ref, wide_ref, sems.at[1])
+    down.start()
+    up.start()
+    up.wait()
+    tall_ref[...] = wide_ref[...].astype(f32).T
+    down.wait()
+    feed_ref[0] = tall_ref[own, :].astype(bf16)
 
 
 def weight_parts(weights, up_weight, down_weight):
     copies = lax.axis_size("y") * lax.axis_size("core")
     mine = lax.axis_index("y") * lax.axis_size("core") + lax.axis_index("core")
     hidden, width = down_weight.shape
-    shard = weights[0].shape[0]
-    rows = shard // copies
+    rows = weights[0].shape[0] // copies
     if rows % 8 or hidden // copies % 8:
 
         def own(value):
@@ -163,42 +172,47 @@
         kept = [own(w) for w in weights]
         feed_part = jnp.stack([own(up_weight.T), own(down_weight)])
         return jnp.stack(kept[:3]), jnp.stack(kept[3:]), feed_part
-    shapes = [
-        (3, rows, width),
-        (len(weights) - 3, rows, width),
-        (2, hidden // copies, width),
-    ]
-
-    def whole(shape):
-        return pl.BlockSpec(shape, lambda i: (0,) * len(shape))
-
-    sources = [*weights, up_weight, down_weight]
-    return pl.pallas_call(
-        parts_kernel,
-        grid=(1,),
-        in_specs=[pl.BlockSpec(memory_space=pltpu.SMEM)] + [whole(w.shape) for w in sources],
-        out_specs=[whole(shape) for shape in shapes],
-        out_shape=[jax.ShapeDtypeStruct(shape, bf16) for shape in shapes],
-        scratch_shapes=[pltpu.VMEM((shard, width), f32), pltpu.VMEM((hidden, width), f32)],
-        compiler_params=pltpu.CompilerParams(vmem_limit_bytes=VMEM),
-    )(mine.reshape(1), *sources)
+    smem, hbm = pl.BlockSpec(memory_space=pltpu.SMEM), pl.BlockSpec(memory_space=pltpu.HBM)
+    vmem = pl.BlockSpec(memory_space=pltpu.VMEM)
+    first, more = pl.pallas_call(
+        rows_kernel,
+        in_specs=[smem] + [hbm] * len(weights),
+        out_specs=[vmem] * 2,
+        out_shape=[
+            jax.ShapeDtypeStruct((3, rows, width), bf16),
+            jax.ShapeDtypeStruct((len(weights) - 3, rows, width), bf16),
+        ],
+        scratch_shapes=[pltpu.SemaphoreType.DMA((len(weights),))],
+    )(mine.reshape(1), *weights)
+    feed_part = pl.pallas_call(
+        feed_rows_kernel,
+        in_specs=[smem, hbm, hbm],
+        out_specs=vmem,
+        out_shape=jax.ShapeDtypeStruct((2, hidden // copies, width), bf16),
+        scratch_shapes=[
+            pltpu.VMEM((width, hidden), bf16),
+            pltpu.VMEM((hidden, width), f32),
+            pltpu.SemaphoreType.DMA((2,)),
+        ],
+    )(mine.reshape(1), up_weight, down_weight)
+    return first, more, feed_part
 
 
 def finish_kernel(me_ref, near, far_y, far_core, far_both, *refs):
     *outs, whole_ref = refs
     y, core = me_ref[0], me_ref[1]
     matrices, rows, lanes = near.shape
-    deep = rows == lanes // 2
+    by_rows = lanes == whole_ref.shape[1]
 
     def place(which, part, turn_y, turn_core):
-        if deep:
-            row = (core ^ turn_core) * 2 * rows + (y ^ turn_y) * rows
-            whole_ref[pl.ds(pl.multiple_of(row, 8), rows), :] = part[which].astype(f32)
+        here_y, here_core = y ^ turn_y, core ^ turn_core
+        row = (2 * here_y + here_core) * rows if by_rows else here_y * rows
+        row = pl.ds(pl.multiple_of(row, 8), rows)
+        if by_rows:
+            whole_ref[row, :] = part[which].astype(f32)
         else:
-            row, lane = (y ^ turn_y) * rows, (core ^ turn_core) * lanes
-            whole_ref[
-                pl.ds(pl.multiple_of(row, 8), rows), pl.ds(pl.multiple_of(lane, 128), lanes)
-            ] = part[which].astype(f32)
+            lane = pl.ds(pl.multiple_of(here_core * lanes, 128), lanes)
+            whole_ref[row, lane] = part[which].astype(f32)
 
     for which, out in enumerate(outs):
         for part, turns in ((near, (0, 0)), (far_y, (1, 0)), (far_core, (0, 1)), (far_both, (1, 1))):
@@ -206,16 +220,25 @@
         out[...] = whole_ref[...] if out.shape == whole_ref.shape else whole_ref[...].T
 
 
-def finish(done, shapes):
+def spread(done):
     done = done.reshape(-1, *done.shape[2:])
-    deep = done.shape[1] == done.shape[2] // 2
+    far_y = shifted(done, "y", 1)
+    return done, far_y, shifted(done, "core", 1), shifted(far_y, "core", 1)
+
+
+def finish(quarters, rows, shapes, *hold):
+    done, far_y, far_core, far_both = quarters
+    by_rows = lax.axis_size("y") * lax.axis_size("core") * done.shape[1] == rows
+    width = done.shape[2] if by_rows else 2 * done.shape[2]
     if lax.axis_size("y") != 2 or done.shape[1] % 8 or done.shape[2] % 128:
-        done = gather_axis(gather_axis(done, "y"), "core")
-        axes = (2, 0, 1, 3, 4) if deep else (2, 1, 3, 0, 4)
-        done = done.transpose(axes).reshape(done.shape[2], *shapes[0])
-        return [d.astype(f32) if s == shapes[0] else d.T.astype(f32) for d, s in zip(done, shapes)]
-    far_y = shifted(done, "y", 1)
-    far_core, far_both = shifted(done, "core", 1), shifted(far_y, "core", 1)
+        done = gather_axis(gather_axis(done, "core"), "y")
+        axes = (2, 0, 1, 3, 4) if by_rows else (2, 0, 3, 1, 4)
+        done = done.transpose(axes).reshape(done.shape[2], rows, width)
+        return [
+            (d if s == (rows, width) else d.T).astype(f32) for d, s in zip(done, shapes)
+        ]
+    if hold:
+        far_core, far_both = after(far_core, *hold), after(far_both, *hold)
     me = jnp.stack([lax.axis_index("y"), lax.axis_index("core")])
 
     def whole(shape):
@@ -227,7 +250,7 @@
         in_specs=[pl.BlockSpec(memory_space=pltpu.SMEM)] + [whole(done.shape)] * 4,
         out_specs=[whole(shape) for shape in shapes],
         out_shape=[jax.ShapeDtypeStruct(shape, f32) for shape in shapes],
-        scratch_shapes=[pltpu.VMEM(shapes[0], f32)],
+        scratch_shapes=[pltpu.VMEM((rows, width), f32)],
         compiler_params=pltpu.CompilerParams(vmem_limit_bytes=VMEM),
     )(me, done, far_y, far_core, far_both)
 
@@ -400,76 +423,149 @@
     )(core, query, keys, values, mix, bias, *weights, back, x, *([text] if cross else []))
 
 
-def feed_kernel(
-    core_ref, x_ref, g_ref, up_ref, down_ref, up_far, down_far, out_ref, back_ref, *rest
-):
-    *grads, xt_ref, gt_ref = rest
+def feed_kernel(paired, me_ref, x_ref, x_far, g_ref, g_far, *refs):
+    inputs, outs = refs[: 4 if paired else 2], refs[4 if paired else 2 :]
+    out_ref, back_ref, out_far, back_far, *grad_refs, out_sum, back_sum = outs
     slope = (2.0 / jnp.pi) ** 0.5
-
-    @pl.when(pl.program_id(0) == 0)
+    step = pl.program_id(0)
+
+    @pl.when(step == 0)
     def _():
-        out_ref[...] = jnp.zeros_like(out_ref)
-        back_ref[...] = jnp.zeros_like(back_ref)
-        xt_ref[...] = x_ref[...].T
-        gt_ref[...] = g_ref[...].T
-
-    def joined(near, far):
-        first = core_ref[0] == 0
-        parts = []
-        for x in range(near.shape[1]):
-            for y in range(near.shape[0]):
-                here, there = near[y, x, 0, 0], far[y, x, 0, 0]
-                parts += [jnp.where(first, here, there), jnp.where(first, there, here)]
-        return jnp.concatenate(parts, axis=0)
-
-    up, down = joined(up_ref, up_far), joined(down_ref, down_far)
-    pre = outer_cols(x_ref[...], up)
-    square = pre * pre
-    bent = jnp.tanh(slope * pre * (1.0 + 0.044715 * square))
-    rise = 0.5 * (1.0 + bent)
-    active = (pre * rise).astype(bf16)
-    steep = rise + 0.5 * pre * (1.0 - bent * bent) * (slope * (1.0 + 0.134145 * square))
-    grad_pre = (outer_cols(g_ref[...], down) * steep).astype(bf16)
-    out_ref[...] += matmul(active, down)
-    back_ref[...] += matmul(grad_pre, up)
-    shards, half, block = grads[0].shape
-    lanes = [slice(n * block, (n + 1) * block) for n in range(shards)]
-    for which, (left, right) in enumerate([(xt_ref, grad_pre), (gt_ref, active)]):
-        for target, core in ((grads[which], core_ref[0]), (grads[which + 2], 1 - core_ref[0])):
-            rows = left[pl.ds(pl.multiple_of(core * half, half), half), :]
-            product = matmul(rows, right).astype(bf16)
-            for n in range(shards):
-                target[n] = product[:, lanes[n]]
-
-
-def feed(core, third_in, grad_mlp, weights):
+        for ref in (out_ref, back_ref, out_sum, back_sum):
+            ref[...] = jnp.zeros_like(ref)
+
+    my_y, my_x = me_ref[0], me_ref[1]
+    if paired:
+        up_near, up_far, down_near, down_far = inputs
+        (nx, zb, _, rows, _), ny = up_near.shape, 2
+        up_at = lambda b, x, y: jnp.where(my_y == y, up_near[x, b, 0], up_far[x, b, 0])
+        down_at = lambda b, x, y: jnp.where(my_x == x, down_near[y, b, 0], down_far[y, b, 0])
+    else:
+        up_ref, down_ref = inputs
+        ny, nx, zb, _, rows, _ = up_ref.shape
+        up_at = lambda b, x, y: up_ref[y, x, b, 0]
+        down_at = lambda b, x, y: down_ref[y, x, b, 0]
+    places = [(b, x, y) for b in range(zb) for x in range(nx) for y in range(ny)]
+    up = jnp.concatenate([up_at(*p) for p in places], axis=0)
+    down = jnp.concatenate([down_at(*p) for p in places], axis=0)
+    up_parts, down_parts = [], []
+    for third, grad, out, back in (
+        (x_ref, g_ref, out_ref, back_ref),
+        (x_far, g_far, out_sum, back_sum),
+    ):
+        pre = outer_cols(third[...], up)
+        square = pre * pre
+        bent = jnp.tanh(slope * pre * (1.0 + 0.044715 * square))
+        rise = 0.5 * (1.0 + bent)
+        active = (pre * rise).astype(bf16)
+        steep = rise + 0.5 * pre * (1.0 - bent * bent) * (slope * (1.0 + 0.134145 * square))
+        grad_pre = (outer_cols(grad[...], down) * steep).astype(bf16)
+        out[...] += matmul(active, down)
+        back[...] += matmul(grad_pre, up)
+        up_parts.append(inner_rows(grad_pre, third[...]))
+        down_parts.append(inner_rows(active, grad[...]))
+    up_total = (up_parts[0] + up_parts[1]).astype(bf16)
+    down_total = (down_parts[0] + down_parts[1]).astype(bf16)
+    at = {p: slice(n * rows, (n + 1) * rows) for n, p in enumerate(places)}
+    if paired:
+        up_kept, up_sent, down_kept, down_sent = grad_refs
+        for b in range(zb):
+            for k in range(2):
+                zero, one = up_total[at[b, 0, k]], up_total[at[b, 1, k]]
+                up_kept[k, 0, b] = jnp.where(my_x == 0, zero, one)
+                up_sent[k, 0, b] = jnp.where(my_x == 0, one, zero)
+                zero, one = down_total[at[b, k, 0]], down_total[at[b, k, 1]]
+                down_kept[k, 0, b] = jnp.where(my_y == 0, zero, one)
+                down_sent[k, 0, b] = jnp.where(my_y == 0, one, zero)
+    else:
+        for ref, total in zip(grad_refs, (up_total, down_total)):
+            for b, x, y in places:
+                ref[0, b, x, y] = total[at[b, x, y]]
+
+    @pl.when(step == pl.num_programs(0) - 1)
+    def _():
+        out_far[...] = out_sum[...].astype(bf16)
+        back_far[...] = back_sum[...].astype(bf16)
+
+
+def feed(third_in, grad_mlp, up, down):
     tokens, width = third_in.shape
-    ny, nx, zb, za, rows, _ = weights[0].shape
-    nz = za * zb
-    block, half = ny * rows * 2, width // 2
+    nx, zb, za, rows, _ = up.shape
+    ny = lax.axis_size("y")
+    paired = nx == 2 and ny == 2
+    if paired:
+        weights = [up, shifted(up, "y", 1), down, shifted(down, "x", 1)]
+    else:
+        weights = [gather_axis(up, "y"), gather_axis(down, "x").swapaxes(0, 1)]
     whole = pl.BlockSpec((tokens, width), lambda j, c: (0, 0))
-    parts = pl.BlockSpec((nx, half, block), lambda j, c: (j, 0, 0))
-    matrix = pl.BlockSpec(
-        (ny, nx, 1, 1, rows, width), lambda j, c: (0, 0, j % zb, j // zb, 0, 0)
-    )
-    hidden = nx * nz * block
-    return pl.pallas_call(
-        feed_kernel,
+    half_shape, whole_shape = (2, za, zb, rows, width), (za, zb, nx, ny, rows, width)
+    grads_shape = half_shape if paired else whole_shape
+    matrix_shape = (2, zb, 1, rows, width) if paired else (ny, nx, zb, 1, rows, width)
+    zeros = len(matrix_shape) - 3
+    matrix = pl.BlockSpec(matrix_shape, lambda j, c: (0,) * zeros + (j, 0, 0))
+    if paired:
+        grads = pl.BlockSpec((2, 1, zb, rows, width), lambda j, c: (0, j, 0, 0, 0))
+    else:
+        grads = pl.BlockSpec((1, *whole_shape[1:]), lambda j, c: (j, 0, 0, 0, 0, 0))
+    count = 4 if paired else 2
+    me = jnp.stack([lax.axis_index("y"), lax.axis_index("x")])
+    out, back, out_far, back_far, *parts = pl.pallas_call(
+        partial(feed_kernel, paired),
         grid_spec=pltpu.PrefetchScalarGridSpec(
             num_scalar_prefetch=1,
-            grid=(nz,),
-            in_specs=[whole] * 2 + [matrix] * 4,
-            out_specs=[whole] * 2 + [parts] * 4,
-            scratch_shapes=[pltpu.VMEM((width, tokens), bf16)] * 2,
+            grid=(za,),
+            in_specs=[whole] * 4 + [matrix] * count,
+            out_specs=[whole] * 4 + [grads] * count,
+            scratch_shapes=[pltpu.VMEM((tokens, width), f32)] * 2,
         ),
-        out_shape=[
-            jax.ShapeDtypeStruct((tokens, width), f32),
-            jax.ShapeDtypeStruct((tokens, width), f32),
-        ]
-        + [jax.ShapeDtypeStruct((nx * nz, half, block), bf16)] * 4,
+        out_shape=[jax.ShapeDtypeStruct((tokens, width), f32)] * 2
+        + [jax.ShapeDtypeStruct((tokens, width), bf16)] * 2
+        + [jax.ShapeDtypeStruct(grads_shape, bf16)] * count,
+        compiler_params=pltpu.CompilerParams(vmem_limit_bytes=56 << 20),
+        cost_estimate=pl.CostEstimate(flops=0, transcendentals=0, bytes_accessed=0),
+    )(me, third_in, shifted(third_in, "core", 1), grad_mlp, shifted(grad_mlp, "core", 1), *weights)
+    if paired:
+        up_kept, up_sent, down_kept, down_sent = parts
+
+        def as_grid(part):
+            return part.transpose(1, 2, 0, 3, 4)[None]
+
+        sums = (
+            ([as_grid(up_kept)], [], [as_grid(shifted(up_sent, "x", 1))]),
+            ([as_grid(down_kept)], [], [as_grid(shifted(down_sent, "y", 1))]),
+        )
+    else:
+        sums = launch([parts[0][None]], "x", 3), launch([parts[1][None]], "y", 4)
+    out = out + shifted(out_far, "core", 1).astype(f32)
+    back = back + shifted(back_far, "core", 1).astype(f32)
+    return out, back, sums
+
+
+def clips_kernel(clip_ref, digits_ref, first, one, resid, mixed, third, three, up, mlp, out_ref):
+    clips, width = out_ref.shape[0], first.shape[1]
+    row = lax.broadcasted_iota(jnp.int32, (16, 1), 0)
+    chooser = (clip_ref[...] == row).astype(f32).astype(bf16)
+    parts = [
+        first[...],
+        first[...] * one[...],
+        resid[...] * mixed[...],
+        third[...],
+        third[...] * three[...],
+        up[...].astype(f32) * mlp[...],
+    ]
+    for place, part in enumerate(parts):
+        total = matmul(chooser, part.astype(bf16))[:clips]
+        out_ref[:, place * width : (place + 1) * width] = total.astype(bf16)
+    out_ref[:, len(parts) * width :] = digits_ref[...]
+
+
+def clip_sums(clips, clip, digits, *values):
+    width = values[0].shape[1]
+    return pl.pallas_call(
+        clips_kernel,
+        out_shape=jax.ShapeDtypeStruct((clips, 6 * width + digits.shape[1]), bf16),
         compiler_params=pltpu.CompilerParams(vmem_limit_bytes=VMEM),
-        cost_estimate=pl.CostEstimate(flops=0, transcendentals=0, bytes_accessed=0),
-    )(core, third_in, grad_mlp, *weights)
+    )(clip[None, :], digits, *values)
 
 
 def shards(
@@ -518,46 +614,14 @@
         up_weight,
         down_weight,
     )
-    more_rows = more.shape[0] * more.shape[1]
-    gathered_more = lax.all_gather(
-        more.reshape(more_rows, width), (*MP_AXES, "y", "core"), axis=0, tiled=True
-    )
-    first_in_column = gather_axis(gather_axis(first, "za"), "zb")
-    feed_part = after(feed_part, first_in_column)
-    first_left = gather_axis(first_in_column[..., :half], "x")
-    first_right = gather_axis(first_in_column[..., half:], "y")
-    feed_part = gather_axis(feed_part, "za", first_left, first_right)
-    first_left = gather_axis(first_left, "y")
-    first_right = gather_axis(first_right, "x")
-    feed_part = gather_axis(feed_part, "zb", first_left, first_right)
-    qkv = assemble(gather_axis(first_left, "core"), gather_axis(first_right, "core"))
-    qkv = qkv.reshape(-1, width)
-
-    table_low = step_table
-    step_ids = after(step_ids, first)
-    choose_step = (step_ids[:, None] == jnp.arange(step_table.shape[0])[None, :]).astype(bf16)
-    silu_mine = jax.nn.silu(matmul(choose_step, table_low)).astype(bf16)
-    partial_mod = matmul(silu_mine, ada_weight)
-    partial_mod = partial_mod.reshape(za, zb, nx, segs_dev, partial_mod.shape[1])
-    modulation = summed(landed(launch_wide(partial_mod, "x", 2))).astype(bf16)
-    modulation = summed(landed(launch([modulation], "zb", 1))).astype(bf16)
-    modulation = summed(landed(launch([modulation], "za", 0)))
-    modulation = modulation + ada_bias.astype(f32)
-    flat_ids = my_ids.reshape(-1)
-    row_of = jnp.arange(flat_ids.shape[0]) // frames_row
-    clip = flat_ids + row_of * SEGS
-    chosen = clip[:, None] == jnp.arange(segs_dev)[None, :]
-
-    def per_frame(index):
-        table = modulation[:, index * width : (index + 1) * width]
-        value = jnp.broadcast_to(table[0:1], (clip.shape[0], width))
-        for segment in range(1, segs_dev):
-            value = jnp.where(chosen[:, segment : segment + 1], table[segment : segment + 1], value)
-        return value
-
-    shift_one, scale_one, gate_one, shift_two, scale_two, gate_two = map(per_frame, range(6))
-
-    my_steps = lax.dynamic_slice_in_dim(step_ids, position * segs_dev, segs_dev, 0)
+    column = gather_axis(first, "za")
+    first_column = column
+    column = gather_axis(column, "zb")
+    more = gather_axis(after(more, column), "za")
+    feed_part = after(feed_part, more)
+    first_left = gather_axis(column[..., :half], "x")
+    first_right = gather_axis(column[..., half:], "y")
+    my_steps = lax.dynamic_slice_in_dim(after(step_ids, first_left, first_right), position * segs_dev, segs_dev, 0)
     digits = jnp.stack([my_steps // 256, my_steps % 256], axis=1).astype(bf16)
     digits = jnp.pad(digits, ((0, 0), (0, 126)))
 
@@ -571,19 +635,55 @@
     cross_bias = jnp.where(allowed, 0.0, masked_score).astype(f32)
     allowed_t = (my_ids[:, None, :] == key_segment[None, :, None]) & valid_key[:, :, None]
     cross_bias_t = jnp.where(allowed_t, 0.0, masked_score).astype(f32)
-    cross_bias = after(cross_bias, cross_bias_t, digits)
+
+    text = after(text, first_left, first_right)
+    text_flat = text.reshape(rows_dev, SEGS, CAPTION, width).swapaxes(1, 2).reshape(-1, width)
+    prepared = (digits, text_flat)
+    more = gather_axis(more, "zb", first_left, first_right, *prepared)
+    first_left = gather_axis(first_left, "y")
+    first_right = gather_axis(first_right, "x")
+    feed_part = gather_axis(feed_part, "za", first_left, first_right)
+    more_left = gather_axis(more[..., :half], "x", first_left, first_right)
+    more_right = gather_axis(more[..., half:], "y", first_left, first_right)
+    qkv = assemble(gather_axis(first_left, "core"), gather_axis(first_right, "core"))
+    qkv = qkv.reshape(-1, width)
+    table_low = step_table
+    step_ids = after(step_ids, first)
+    choose_step = (step_ids[:, None] == jnp.arange(step_table.shape[0])[None, :]).astype(bf16)
+    silu_mine = jax.nn.silu(matmul(choose_step, table_low)).astype(bf16)
+    partial_mod = matmul(silu_mine, ada_weight)
+    partial_mod = partial_mod.reshape(za, zb, nx, segs_dev, partial_mod.shape[1])
+    modulation = summed(landed(launch_wide(partial_mod, "x", 2), first_column)).astype(bf16)
+    modulation = summed(landed(launch([modulation], "zb", 1), column)).astype(bf16)
+    modulation = summed(landed(launch([modulation], "za", 0), first_left, first_right))
+    modulation = modulation + ada_bias.astype(f32)
+    flat_ids = my_ids.reshape(-1)
+    row_of = jnp.arange(flat_ids.shape[0]) // frames_row
+    clip = flat_ids + row_of * SEGS
+    chosen = clip[:, None] == jnp.arange(segs_dev)[None, :]
+
+    def per_frame(index):
+        table = modulation[:, index * width : (index + 1) * width]
+        value = jnp.broadcast_to(table[0:1], (clip.shape[0], width))
+        for segment in range(1, segs_dev):
+            value = jnp.where(chosen[:, segment : segment + 1], table[segment : segment + 1], value)
+        return value
+
+    shift_one, scale_one, gate_one, shift_two, scale_two, gate_two = map(per_frame, range(6))
 
     base = frames.astype(f32)
-    text_flat = text.reshape(rows_dev, SEGS, CAPTION, width).swapaxes(1, 2).reshape(-1, width)
     normed_one, inverse_one = normalize(base)
     first_in = (normed_one * (1.0 + scale_one) + shift_one).astype(bf16)
     query, keys, values = (
         outer_cols(first_in, qkv[i * width : (i + 1) * width]).astype(bf16) for i in range(3)
     )
     self_mix = attend(query, keys, values, self_bias)
-    feed_up = gather_axis(feed_part[:, :, 0], "x", self_mix)
-    feed_down = gather_axis(feed_part[:, :, 1], "y", self_mix)
-    whole = gathered_more.reshape(-1, *more.shape).swapaxes(0, 1).reshape(more.shape[0], -1, width)
+    more_left = gather_axis(more_left, "y", self_mix)
+    more_right = gather_axis(more_right, "x", self_mix)
+    feed_part = gather_axis(feed_part, "zb", self_mix)
+    feed_up = gather_axis(feed_part[:, :, 0], "x", more_left, more_right)
+    feed_down = gather_axis(feed_part[:, :, 1], "y", more_left, more_right)
+    whole = assemble(gather_axis(more_left, "core"), gather_axis(more_right, "core"))
     out_full, cquery_t, cout_full = whole[0], whole[1], whole[4]
     ckv_t = whole[2:4].reshape(-1, width)
     self_out = matmul(self_mix, out_full)
@@ -600,15 +700,9 @@
     upstream = out_grad.astype(f32)
     grad_mlp = (gate_two * upstream).astype(bf16)
     core = lax.axis_index("core").reshape(1)
-    feed_up = gather_axis(feed_up, "y", cross_mix)
-    feed_down = gather_axis(feed_down, "x", cross_mix).swapaxes(0, 1)
-    feed_weights = [feed_up, feed_down] + [shifted(w, "core", 1) for w in (feed_up, feed_down)]
-    mlp_out, grad_third, *ff_parts = feed(core, third_in, grad_mlp, feed_weights)
+    mlp_out, grad_third, feed_sums = feed(third_in, grad_mlp, feed_up, feed_down)
     layer_out = (resid_two + gate_two * mlp_out).astype(bf16)
 
-    grad_gate_two = upstream * mlp_out
-    with jax.named_scope("feed_sums_first_stage"):
-        feed_sums = first_stage(*[part[None] for part in ff_parts])
     grad_resid_two = upstream + norm_back(
         normed_three, inverse_three, grad_third * (1.0 + scale_two)
     )
@@ -630,7 +724,6 @@
     with jax.named_scope("feed_sums_second_stage"):
         feed_sums = second_stage(feed_sums, grad_second)
     grad_resid_one = grad_resid_two + norm_back(normed_two, inverse_two, grad_second)
-    grad_gate_one = grad_resid_one * self_out
     grad_self = after(
         (gate_one * grad_resid_one).astype(bf16), *sends(cross_sums), *sends(feed_sums)
     )
@@ -652,18 +745,19 @@
     with jax.named_scope("self_sums_first_stage"):
         self_sums = first_stage(*self_parts, *sends(cross_sums), *feed_sums[1])
 
-    chooser = chosen.astype(bf16)
     grad_first = after(grad_first, *sends(self_sums))
-    mod_parts = [
+    grad_mod = clip_sums(
+        segs_dev,
+        clip,
+        digits,
         grad_first,
-        grad_first * normed_one,
-        grad_gate_one,
+        normed_one,
+        grad_resid_one,
+        self_out,
         grad_third,
-        grad_third * normed_three,
-        grad_gate_two,
-    ]
-    grad_mod = jnp.concatenate(
-        [inner_rows(chooser, v.astype(bf16)).astype(bf16) for v in mod_parts] + [digits], axis=1
+        normed_three,
+        out_grad,
+        mlp_out,
     )
     with jax.named_scope("feed_sums_fourth_stage"):
         feed_sums = fourth_stage(feed_sums, grad_mod)
@@ -676,13 +770,17 @@
     with jax.named_scope("cross_sums_fourth_stage"):
         cross_sums = fourth_stage(cross_sums, gathered)
     feed_done = summed(landed(feed_sums, *cross_sums[1])).astype(bf16)
+    with jax.named_scope("feed_spread"):
+        feed_quarters = spread(feed_done)
     with jax.named_scope("self_sums_third_stage"):
         self_sums = third_stage(self_sums, feed_done)
     with jax.named_scope("gather_mod"):
         gathered = joined_rows(gathered, "zb", *self_sums[1])
     cross_done = summed(landed(cross_sums, gathered)).astype(bf16)
     with jax.named_scope("self_sums_fourth_stage"):
-        self_sums = fourth_stage(self_sums, cross_done)
+        self_sums = fourth_stage(self_sums, cross_done, feed_quarters[1])
+    with jax.named_scope("cross_spread"):
+        cross_quarters = spread(cross_done)
     with jax.named_scope("gather_mod"):
         gathered = joined_rows(gathered, "x", *self_sums[1])
     grad_frames = grad_resid_one + norm_back(
@@ -690,17 +788,14 @@
     )
     with jax.named_scope("gather_mod"):
         gathered = joined_rows(gathered, "y", grad_frames)
-    self_done = summed(landed(self_sums, gathered)).astype(bf16)
+    self_done = summed(landed(self_sums, gathered, cross_quarters[1])).astype(bf16)
+    with jax.named_scope("self_spread"):
+        self_quarters = spread(self_done)
     with jax.named_scope("gather_mod"):
         gathered = joined_rows(gathered, "core", self_done)
     grad_mod_all = gathered[:, : 6 * width]
     digits = gathered[:, 6 * width : 6 * width + 2].astype(f32)
     steps_all = digits[:, 0] * 256.0 + digits[:, 1]
-    up_shape, low_shape = up_weight.shape, out_w.shape
-    shard_up, shard_down = finish(feed_done, [up_shape, down_weight.shape])
-    shard_cout, shard_cquery, shard_ckey, shard_cvalue = finish(cross_done, [low_shape] * 4)
-    shard_out, shard_query, shard_key, shard_value = finish(self_done, [low_shape] * 4)
-
     choose_all = (
         steps_all[:, None] == jnp.arange(step_table.shape[0]).astype(f32)[None, :]
     ).astype(bf16)
@@ -711,6 +806,16 @@
     grad_cond = silu_back(cond_all, outer_cols(grad_mod_all, ada_weight))
     grad_table = lax.dot_general(
         choose_all.astype(f32), grad_cond, (((0,), (0,)), ((), ())), precision=highest
+    )
+
+    hidden, low = down_weight.shape[0], out_w.shape[0]
+    made = (grad_ada_w, grad_table)
+    shard_up, shard_down = finish(feed_quarters, hidden, [up_weight.shape, down_weight.shape])
+    shard_cout, shard_cquery, shard_ckey, shard_cvalue = finish(
+        cross_quarters, low, [out_w.shape] * 4
+    )
+    shard_out, shard_query, shard_key, shard_value = finish(
+        self_quarters, low, [out_w.shape] * 4, *made, shard_up, shard_cout
     )
 
     return (

time: 347 us -> 321 us (0.925)
  waiting for transfers between devices: 78.1 us -> 52.7 us
  local copies, waits for them, and re-layouts: 38.2 us -> 19.5 us
  between operations: 16.7 us -> 3.03 us
  starting transfers between devices: 48.1 us -> 60 us
  other arithmetic: 68.6 us -> 79.8 us
  Pallas kernels: 77.5 us -> 88.4 us
    ppermute x57 -> x65, waiting for transfers between devices: 78.1 us -> 52.7 us  [shifted(): lax.ppermute(value, axis, [(k, (k + steps) % count) for k in range(count)])]
    unnamed x284 -> x228, local copies, waits for them, and re-layouts: 21.7 us -> 7.64 us
    ppermute x57 -> x65, starting transfers between devices: 48.1 us -> 60 us  [shifted(): lax.ppermute(value, axis, [(k, (k + steps) % count) for k in range(count)])]
    pallas_call x2 -> x4, Pallas kernels: 21.2 us -> 31.3 us  [the longest x1 23.6 us: feed(): pl.pallas_call(partial(feed_kernel, paired), grid_spec=pltpu.PrefetchScal...]
    another operation x33 -> x45, other arithmetic: 12.7 us -> 20.7 us  [gather_axis(): return jnp.stack([at(place) for place in range(count)])]
    mul x0 -> x1, other arithmetic: none -> 5.15 us  [normalize(): return (centre * inverse, inverse)]
    convert_element_type x15 -> x13, other arithmetic: 18.4 us -> 14.7 us  [launch(): summed(picked(terms, dim, (me + s) % count)).astype(bf16)]
  transfers between devices with their start and end apart: 58 -> 65, of which waited for: 21 -> 16; matrix products, arithmetic and copies ran while one was open for 27% -> 33% of each run, Pallas kernels for 17% -> 19%
where the time goes in v4:
time: 321 us; the launch traced here: 316 us
  Pallas kernels  88.4 us (28%)
  other arithmetic  79.8 us (25%)
  starting transfers between devices  60 us (19%)
  waiting for transfers between devices  52.7 us (16%)
  local copies, waits for them, and re-layouts  19.5 us (6%)
  matrix products  12.6 us (4%)
    ppermute x65, starting transfers between devices, shifted(): lax.ppermute(value, axis, [(k, (k + steps) % count) for k in range(count)])  60 us
    ppermute x65, waiting for transfers between devices, shifted(): lax.ppermute(value, axis, [(k, (k + steps) % count) for k in range(count)])  52.7 us
    pallas_call x2, Pallas kernels, attend_back(): pl.pallas_call(backward_kernel, grid_spec=pltpu.PrefetchScalarGridSpec(nu...  39.4 us
    pallas_call x1, Pallas kernels, feed(): pl.pallas_call(partial(feed_kernel, paired), grid_spec=pltpu.PrefetchScal...  23.6 us
    another operation x45, other arithmetic, gather_axis(): return jnp.stack([at(place) for place in range(count)])  20.7 us
    convert_element_type x13, other arithmetic, launch(): summed(picked(terms, dim, (me + s) % count)).astype(bf16)  14.7 us
    pallas_call x2, Pallas kernels, attend(): pl.pallas_call(forward_kernel, grid=(rows, pairs), in_specs=blocks + [pl....  11.5 us
    reduce_sum x3, other arithmetic, norm_back(): mean_grad = jnp.mean(upstream, axis=-1, keepdims=True)  8.78 us
  transfers between devices with their start and end apart: 65, of which 16 were waited for; matrix products, arithmetic and copies ran while one was open for 33% of the time, Pallas kernels for 19%

profile of v4, /device:TPU:0, one launch (start us, length us, event | category | flops | bytes accessed | tf_op | source)
XLA Modules:
  0.0 316.0 jit_solution(18080251155429082907)
XLA Ops:
  2.4 4.1 %collective-permute-start.1 = (bf16[3,24,768]{2,1,0:T(8,128)(2,1)}, bf16[3,24,768]{2,1,0:T(8,128)(2,1)}, u32[]{:S(2)}, u32[]{:S(2)}) collective-permute-start(bf16[3,24,768]{2,1,0:T(8,128)(2,1)} %get-tuple-element.94), channel_id=1, source_target_pairs={{0,4},{4,0},{1,5},{5,1},{2,6},{6,2},{3,7},{7,3},{8,12},{12,8},{9,1... | collective-permute-start | bytes 331784 | tf_op jit(solution)/shard_map/to_za_1/ppermute | solution.py:29
  13.4 2.1 shard_map.309
  20.5 4.1 %collective-permute-done.3 = bf16[2,3,24,768]{3,2,1,0:T(8,128)(2,1)S(1)} collective-permute-done((bf16[2,3,24,768]{3,2,1,0:T(8,128)(2,1)S(1)}, bf16[2,3,24,768]{3,2,1,0:T(8,128)(2,1)S(1)}, u32[]{:S(2)}, u32[]{:S(2)}) %collective-permute-start.3) | collective-permute-done | bytes 221216 | tf_op jit(solution)/shard_map/to_zb_1/ppermute | solution.py:29
  28.0 2.6 collective-permute-start.4
  30.5 6.0 %collective-permute-done.11 = bf16[5,24,768]{2,1,0:T(8,128)(2,1)S(1)} collective-permute-done((bf16[5,24,768]{2,1,0:T(8,128)(2,1)S(1)}, bf16[5,24,768]{2,1,0:T(8,128)(2,1)S(1)}, u32[]{:S(2)}, u32[]{:S(2)}) %collective-permute-start.11) | collective-permute-done | bytes 184352 | tf_op jit(solution)/shard_map/to_za_1/ppermute | solution.py:29
  46.0 5.2 %collective-permute-done.12 = bf16[2,5,24,768]{3,2,1,0:T(8,128)(2,1)} collective-permute-done((bf16[2,5,24,768]{3,2,1,0:T(8,128)(2,1)}, bf16[2,5,24,768]{3,2,1,0:T(8,128)(2,1)}, u32[]{:S(2)}, u32[]{:S(2)}) %collective-permute-start.12) | collective-permute-done | bytes 368672 | tf_op jit(solution)/shard_map/to_zb_1/ppermute | solution.py:29
  60.3 5.2 %fusion = (f32[512,768]{1,0:T(8,128)}, bf16[512,768]{1,0:T(8,128)(2,1)S(1)}, bf16[512,768]{1,0:T(8,128)(2,1)S(1)}) fusion(bf16[512,768]{1,0:T(8,128)(2,1)S(1)} %copy-done.32, f32[512]{0:T(512)S(1)} %copy-done.84, f32[512]{0:T(512)S(1)} %broadcast_multiply_fusion.8, f32[768]{0:T(1024)S(1)} %get-tuple-element.190, f32[768]{0:T(1024)S(1)} %get-tuple-element.191, ...), kind=kLoop, calls=%fused_computation.20 | loop fusion | flops 7471104 | bytes 4761088 | tf_op jit(solution)/shard_map/mul | solution.py:261
  76.0 5.8 %shard_map.307.mix_ref = bf16[512,768]{1,0:T(8,128)(2,1)S(1)} custom-call(bf16[512,768]{1,0:T(8,128)(2,1)S(1)} %convolution_convert_fusion.3.q_ref, bf16[512,768]{1,0:T(8,128)(2,1)S(1)} %convolution_convert_fusion.2.k_ref, bf16[512,768]{1,0:T(8,128)(2,1)S(1)} %convolution_convert_fusion.1.v_ref, f32[1,512,512]{2,1,0:T(8,128)S(1)} %compare_select_fusion.bias_ref), custom_call_target="tpu_custom_call" | custom-call | tf_op jit(solution)/shard_map/pallas_call | solution.py:383
  87.1 2.0 collective-permute-start.25
  89.4 8.8 %collective-permute-done.23 = bf16[2,2,96,768]{3,2,1,0:T(8,128)(2,1)S(1)} collective-permute-done((bf16[2,2,96,768]{3,2,1,0:T(8,128)(2,1)S(1)}, bf16[2,2,96,768]{3,2,1,0:T(8,128)(2,1)S(1)}, u32[]{:S(2)}, u32[]{:S(2)}) %collective-permute-start.23) | collective-permute-done | bytes 589856 | tf_op jit(solution)/shard_map/to_x_1/ppermute | solution.py:29
  100.7 2.6 collective-permute-done.25
  109.0 2.2 fusion.125
  116.3 5.6 %shard_map.308.mix_ref = bf16[512,768]{1,0:T(8,128)(2,1)S(1)} custom-call(bf16[512,768]{1,0:T(8,128)(2,1)S(1)} %convolution_convert_fusion.q_ref, bf16[308,768]{1,0:T(8,128)(2,1)S(1)} %convolution_convert_fusion.5.k_ref, bf16[308,768]{1,0:T(8,128)(2,1)S(1)} %convolution_convert_fusion.4.v_ref, f32[1,512,308]{2,1,0:T(8,128)S(1)} %and_select_fusion.bias_ref), custom_call_target="tpu_custom_call" | custom-call | tf_op jit(solution)/shard_map/pallas_call | solution.py:383
  123.2 3.3 %add_convert_fusion.1 = (bf16[512,768]{1,0:T(8,128)(2,1)S(1)}, f32[512,768]{1,0:T(8,128)}) fusion(f32[768]{0:T(1024)S(1)} %get-tuple-element.179, f32[768]{0:T(1024)S(1)} %get-tuple-element.180, f32[768]{0:T(1024)S(1)} %get-tuple-element.181, f32[768]{0:T(1024)S(1)} %get-tuple-element.182, f32[768]{0:T(1024)S(1)} %get-tuple-element.183, ...), kind=kLoop, calls=%fused_computation.35 | loop fusion | flops 4718592 | bytes 3962368 | tf_op jit(solution)/shard_map/convert_element_type | solution.py:699
  128.2 3.6 %collective-permute-done.26.refs_3_ = bf16[2,2,2,96,768]{4,3,2,1,0:T(8,128)(2,1)} collective-permute-done((bf16[2,2,2,96,768]{4,3,2,1,0:T(8,128)(2,1)}, bf16[2,2,2,96,768]{4,3,2,1,0:T(8,128)(2,1)}, u32[]{:S(2)}, u32[]{:S(2)}) %collective-permute-start.26) | collective-permute-done | bytes 1179680 | tf_op jit(solution)/shard_map/to_x_1/ppermute | solution.py:29
  132.7 23.6 %shard_map.310 = (f32[512,768]{1,0:T(8,128)}, f32[512,768]{1,0:T(8,128)}, bf16[512,768]{1,0:T(8,128)(2,1)}, bf16[512,768]{1,0:T(8,128)(2,1)}, bf16[2,2,2,96,768]...) custom-call(s32[2]{0:T(128)} %pad_add_fusion.me_ref, ...), custom_call_target="tpu_custom_call" | custom-call | tf_op jit(solution)/shard_map/pallas_call | solution.py:512
  160.9 5.2 %fusion.122 = (f32[512]{0:T(512)S(1)}, f32[512]{0:T(512)S(1)}, f32[512,768]{1,0:T(8,128)S(1)}, bf16[512,768]{1,0:T(8,128)(2,1)}, f32[512,768]{1,0:T(8,128)}) fusion(f32[768]{0:T(1024)S(1)} %get-tuple-element.183, f32[768]{0:T(1024)S(1)} %get-tuple-element.184, pred[512]{0:T(512)(128)(4,1)} %get-tuple-element.203, f32[768]{0:T(1024)S(1)} %get-tuple-element.185, ...), kind=kLoop, calls=%fused_computation.392 | loop fusion | flops 7076864 | bytes 11826688 | tf_op jit(solution)/shard_map/reduce_sum | solution.py:265
  168.5 17.8 %shard_map.311 = (f32[308,768]{1,0:T(8,128)S(1)}, f32[512,768]{1,0:T(8,128)}, bf16[2,768,384]{2,1,0:T(8,128)(2,1)}, bf16[2,768,384]{2,1,0:T(8,128)(2,1)}, bf16[2...) custom-call(s32[1]{0:T(128)} %bitcast.78.core_ref, bf16[512,768]{1,0:T(8,128)(2,1)S(1)} %copy-done.19, ...), custom_call_target="tpu_custom_call" | custom-call | tf_op jit(solution)/shard_map/pallas_call | solution.py:406
  186.4 2.3 fusion.123
  191.0 2.2 fusion.19
  193.8 2.1 fusion.18
  201.5 21.6 %shard_map.312 = (f32[512,768]{1,0:T(8,128)}, bf16[2,768,384]{2,1,0:T(8,128)(2,1)}, bf16[2,768,384]{2,1,0:T(8,128)(2,1)}, bf16[2,768,384]{2,1,0:T(8,128)(2,1)}, bf16[2,768,384]{2,1,0:T(8,128)(2,1)}) custom-call(s32[1]{0:T(128)} %bitcast.78.core_ref, bf16[512,768]{1,0:T(8,128)(2,1)S(1)} %copy-done.9, bf16[512,768]{1,0:T(8,128)(2,1)S(1)} %copy-done.11, ...), custom_call_target="tpu_custom_call" | custom-call | tf_op jit(solution)/shard_map/pallas_call | solution.py:406
  240.2 3.8 %shard_map.313 = bf16[4,4736]{1,0:T(4,128)(2,1)S(1)} custom-call(s32[1,512]{1,0:T(1,128)S(1)} %get-tuple-element.205.clip_ref, bf16[4,128]{1,0:T(4,128)(2,1)S(1)} %fusion.115.digits_ref, f32[512,768]{1,0:T(8,128)S(1)} %copy-done.1, f32[512,768]{1,0:T(8,128)S(1)} %copy-done.5, f32[512,768]{1,0:T(8,128)S(1)} %get-tuple-element.208.resid, ...), custom_call_target="tpu_custom_call" | custom-call | tf_op jit(solution)/shard_map/pallas_call | solution.py:564
  254.6 2.9 collective-permute-done.40
  263.0 3.4 %collective-permute-done.48 = bf16[2,2,2,48,384]{4,3,1,0,2:T(8,128)(2,1)} collective-permute-done((bf16[2,2,2,48,384]{4,3,1,0,2:T(8,128)(2,1)}, bf16[2,2,2,48,384]{4,3,1,0,2:T(8,128)(2,1)}, u32[]{:S(2)}, u32[]{:S(2)}) %collective-permute-start.48) | collective-permute-done | bytes 294944 | tf_op jit(solution)/shard_map/cross_sums_third_stage/to_zb_1/ppermute | solution.py:29
  272.5 2.5 collective-permute-start.51
  278.5 1.9 collective-permute-done.51
  285.7 2.5 collective-permute-done.54
  291.6 4.0 %collective-permute-done.57.far_y = bf16[4,48,384]{2,1,0:T(8,128)(2,1)} collective-permute-done((bf16[4,48,384]{2,1,0:T(8,128)(2,1)S(1)}, bf16[4,48,384]{2,1,0:T(8,128)(2,1)}, u32[]{:S(2)}, u32[]{:S(2)}) %collective-permute-start.57) | collective-permute-done | bytes 147488 | tf_op jit(solution)/shard_map/cross_spread/to_y_1/ppermute | solution.py:29
  295.6 4.8 %collective-permute-done.56 = bf16[2,2,48,384]{3,2,1,0:T(8,128)(2,1)S(1)} collective-permute-done((bf16[2,2,48,384]{3,2,1,0:T(8,128)(2,1)S(1)}, bf16[2,2,48,384]{3,2,1,0:T(8,128)(2,1)S(1)}, u32[]{:S(2)}, u32[]{:S(2)}) %collective-permute-start.56) | collective-permute-done | bytes 147488 | tf_op jit(solution)/shard_map/self_sums_fourth_stage/to_za_1/ppermute | solution.py:29
  302.7 2.5 shard_map.314
  305.2 2.1 shard_map.315
  (509 shorter events, 144.4 us)
Async XLA Ops:
  24.8 14.5 %collective-permute-start.5 = (bf16[2,2,3,24,384]{4,3,2,1,0:T(8,128)(2,1)S(1)}, bf16[2,2,3,24,384]{4,3,2,1,0:T(8,128)(2,1)S(1)}, u32[]{:S(2)}, u32[]{:S(2)}) collective-permute-start(bf16[2,2,3,24,384]{4,3,2,1,0:T(8,128)(2,1)S(1)} %get-tuple-element.283), channel_id=1, source_target_pairs={{0,1},{1,0},{2,3},{3,2},{4,5},{5,4},{6,7},{7,6},{8,9},{9,8},{10,11... | collective-permute-start | bytes 663560 | tf_op jit(solution)/shard_map/to_x_1/ppermute | solution.py:29
  25.4 15.3 %collective-permute-start.7 = (bf16[2,2,3,24,384]{4,3,2,1,0:T(8,128)(2,1)S(1)}, bf16[2,2,3,24,384]{4,3,2,1,0:T(8,128)(2,1)S(1)}, u32[]{:S(2)}, u32[]{:S(2)}) collective-permute-start(bf16[2,2,3,24,384]{4,3,2,1,0:T(8,128)(2,1)S(1)} %get-tuple-element.282), channel_id=1, source_target_pairs={{0,16},{16,0},{1,17},{17,1},{2,18},{18,2},{3,19},{19,3},{4,20},{20... | collective-permute-start | bytes 663560 | tf_op jit(solution)/shard_map/to_y_1/ppermute | solution.py:29
  28.0 29.3 %collective-permute-start.4 = (bf16[4,4608]{1,0:T(4,128)(2,1)}, bf16[4,4608]{1,0:T(4,128)(2,1)}, u32[]{:S(2)}, u32[]{:S(2)}) collective-permute-start(bf16[4,4608]{1,0:T(4,128)(2,1)} %dynamic-slice_bitcast_fusion.2), channel_id=1, source_target_pairs={{0,4},{4,0},{1,5},{5,1},{2,6},{6,2},{3,7},{7,3},{8,12},{12,8},{9,1... | collective-permute-start | bytes 110600 | tf_op jit(solution)/shard_map/to_za_1/ppermute | solution.py:29
  37.4 13.8 %collective-permute-start.12 = (bf16[2,5,24,768]{3,2,1,0:T(8,128)(2,1)}, bf16[2,5,24,768]{3,2,1,0:T(8,128)(2,1)}, u32[]{:S(2)}, u32[]{:S(2)}) collective-permute-start(bf16[2,5,24,768]{3,2,1,0:T(8,128)(2,1)} %pad_maximum_fusion.18), channel_id=1, source_target_pairs={{0,2},{2,0},{1,3},{3,1},{4,6},{6,4},{5,7},{7,5},{8,10},{10,8},{9,1... | collective-permute-start | bytes 1105928 | tf_op jit(solution)/shard_map/to_zb_1/ppermute | solution.py:29
  37.4 21.5 %collective-permute-start.21 = (bf16[2,96,768]{2,1,0:T(8,128)(2,1)}, bf16[2,96,768]{2,1,0:T(8,128)(2,1)}, u32[]{:S(2)}, u32[]{:S(2)}) collective-permute-start(bf16[2,96,768]{2,1,0:T(8,128)(2,1)} %shard_map.309), channel_id=1, source_target_pairs={{0,4},{4,0},{1,5},{5,1},{2,6},{6,2},{3,7},{7,3},{8,12},{12,8},{9,1... | collective-permute-start | bytes 884744 | tf_op jit(solution)/shard_map/to_za_1/ppermute | solution.py:29
  53.1 14.1 %collective-permute-start.13 = (bf16[2,2,5,24,384]{4,3,2,1,0:T(8,128)(2,1)S(1)}, bf16[2,2,5,24,384]{4,3,2,1,0:T(8,128)(2,1)S(1)}, u32[]{:S(2)}, u32[]{:S(2)}) collective-permute-start(bf16[2,2,5,24,384]{4,3,2,1,0:T(8,128)(2,1)S(1)} %get-tuple-element.271), channel_id=1, source_target_pairs={{0,1},{1,0},{2,3},{3,2},{4,5},{5,4},{6,7},{7,6},{8,9},{9,8},{10,11... | collective-permute-start | bytes 1105928 | tf_op jit(solution)/shard_map/to_x_1/ppermute | solution.py:29
  60.1 21.7 %collective-permute-start.22 = (bf16[2,2,96,768]{3,2,0,1:T(8,128)(2,1)S(1)}, bf16[2,2,96,768]{3,2,0,1:T(8,128)(2,1)}, u32[]{:S(2)}, u32[]{:S(2)}) collective-permute-start(bf16[2,2,96,768]{3,2,0,1:T(8,128)(2,1)S(1)} %pad_maximum_fusion.13), channel_id=1, source_target_pairs={{0,2},{2,0},{1,3},{3,1},{4,6},{6,4},{5,7},{7,5},{8,10},{10,8},{9,1... | collective-permute-start | bytes 1769480 | tf_op jit(solution)/shard_map/to_zb_1/ppermute | solution.py:29
  66.7 18.7 %collective-permute-start.17 = (bf16[2,2,2,5,24,384]{5,4,3,2,1,0:T(8,128)(2,1)}, bf16[2,2,2,5,24,384]{5,4,3,2,1,0:T(8,128)(2,1)S(1)}, u32[]{:S(2)}, u32[]{:S(2)}) collective-permute-start(bf16[2,2,2,5,24,384]{5,4,3,2,1,0:T(8,128)(2,1)} %pad_maximum_fusion.10), channel_id=1, source_target_pairs={{0,1},{1,0},{2,3},{3,2},{4,5},{5,4},{6,7},{7,6},{8,9},{9,8},{10,11... | collective-permute-start | bytes 2211848 | tf_op jit(solution)/shard_map/to_x_1/ppermute | solution.py:29
  68.2 18.4 %collective-permute-start.14 = (bf16[2,2,2,5,24,384]{5,4,3,2,1,0:T(8,128)(2,1)}, bf16[2,2,2,5,24,384]{5,4,3,2,1,0:T(8,128)(2,1)S(1)}, u32[]{:S(2)}, u32[]{:S(2)}) collective-permute-start(bf16[2,2,2,5,24,384]{5,4,3,2,1,0:T(8,128)(2,1)} %pad_maximum_fusion.9), channel_id=1, source_target_pairs={{0,16},{16,0},{1,17},{17,1},{2,18},{18,2},{3,19},{19,3},{4,20},{20... | collective-permute-start | bytes 2211848 | tf_op jit(solution)/shard_map/to_y_1/ppermute | solution.py:29
  83.4 14.8 %collective-permute-start.23 = (bf16[2,2,96,768]{3,2,1,0:T(8,128)(2,1)S(1)}, bf16[2,2,96,768]{3,2,1,0:T(8,128)(2,1)S(1)}, u32[]{:S(2)}, u32[]{:S(2)}) collective-permute-start(bf16[2,2,96,768]{3,2,1,0:T(8,128)(2,1)S(1)} %get-tuple-element.257), channel_id=1, source_target_pairs={{0,1},{1,0},{2,3},{3,2},{4,5},{5,4},{6,7},{7,6},{8,9},{9,8},{10,11... | collective-permute-start | bytes 1769480 | tf_op jit(solution)/shard_map/to_x_1/ppermute | solution.py:29
  85.8 20.1 %collective-permute-start.18 = (bf16[2,2,2,2,5,24,384]{6,5,4,3,2,0,1:T(8,128)(2,1)S(1)}, bf16[2,2,2,2,5,24,384]{6,5,4,3,2,0,1:T(8,128)(2,1)S(1)}, u32[]{:S(2)}, u32[]{:S(2)}) collective-permute-start(bf16[2,2,2,2,5,24,384]{6,5,4,3,2,0,1:T(8,128)(2,1)S(1)} %copy.148), channel_id=1, source_target_pairs={{0,8},{8,0},{1,9},{9,1},{2,10},{10,2},{3,11},{11,3},{4,12},{12,4},... | collective-permute-start | bytes 4423688 | tf_op jit(solution)/shard_map/to_core_1/ppermute | solution.py:29
  87.0 19.2 %collective-permute-start.15 = (bf16[2,2,2,2,5,24,384]{6,5,4,3,2,0,1:T(8,128)(2,1)S(1)}, bf16[2,2,2,2,5,24,384]{6,5,4,3,2,0,1:T(8,128)(2,1)S(1)}, u32[]{:S(2)}, u32[]{:S(2)}) collective-permute-start(bf16[2,2,2,2,5,24,384]{6,5,4,3,2,0,1:T(8,128)(2,1)S(1)} %pad_maximum_fusion), channel_id=1, source_target_pairs={{0,8},{8,0},{1,9},{9,1},{2,10},{10,2},{3,11},{11,3},{4,12},{12,4},... | collective-permute-start | bytes 4423688 | tf_op jit(solution)/shard_map/to_core_1/ppermute | solution.py:29
  87.1 16.2 %collective-permute-start.25 = (bf16[2,2,96,768]{3,2,1,0:T(8,128)(2,1)S(1)}, bf16[2,2,96,768]{3,2,1,0:T(8,128)(2,1)S(1)}, u32[]{:S(2)}, u32[]{:S(2)}) collective-permute-start(bf16[2,2,96,768]{3,2,1,0:T(8,128)(2,1)S(1)} %get-tuple-element.256), channel_id=1, source_target_pairs={{0,16},{16,0},{1,17},{17,1},{2,18},{18,2},{3,19},{19,3},{4,20},{20... | collective-permute-start | bytes 1769480 | tf_op jit(solution)/shard_map/to_y_1/ppermute | solution.py:29
  89.3 38.0 %collective-permute-start.20 = (bf16[512,768]{1,0:T(8,128)(2,1)S(1)}, bf16[512,768]{1,0:T(8,128)(2,1)}, u32[]{:S(2)}, u32[]{:S(2)}) collective-permute-start(bf16[512,768]{1,0:T(8,128)(2,1)S(1)} %get-tuple-element.298.g_ref), channel_id=1, source_target_pairs={{0,8},{8,0},{1,9},{9,1},{2,10},{10,2},{3,11},{11,3},{4,12},{12,4},... | collective-permute-start | bytes 2359304 | tf_op jit(solution)/shard_map/to_core_1/ppermute | solution.py:29
  99.4 28.8 %collective-permute-start.24 = (bf16[2,2,2,96,768]{4,3,2,1,0:T(8,128)(2,1)}, bf16[2,2,2,96,768]{4,3,2,1,0:T(8,128)(2,1)}, u32[]{:S(2)}, u32[]{:S(2)}) collective-permute-start(bf16[2,2,2,96,768]{4,3,2,1,0:T(8,128)(2,1)} %pad_maximum_fusion.5.refs_0_), channel_id=1, source_target_pairs={{0,16},{16,0},{1,17},{17,1},{2,18},{18,2},{3,19},{19,3},{4,20},{20... | collective-permute-start | bytes 3538952 | tf_op jit(solution)/shard_map/to_y_1/ppermute | solution.py:29
  104.5 27.4 %collective-permute-start.26 = (bf16[2,2,2,96,768]{4,3,2,1,0:T(8,128)(2,1)}, bf16[2,2,2,96,768]{4,3,2,1,0:T(8,128)(2,1)}, u32[]{:S(2)}, u32[]{:S(2)}) collective-permute-start(bf16[2,2,2,96,768]{4,3,2,1,0:T(8,128)(2,1)} %pad_maximum_fusion.6.refs_2_), channel_id=1, source_target_pairs={{0,1},{1,0},{2,3},{3,2},{4,5},{5,4},{6,7},{7,6},{8,9},{9,8},{10,11... | collective-permute-start | bytes 3538952 | tf_op jit(solution)/shard_map/to_x_1/ppermute | solution.py:29
  157.8 33.2 %collective-permute-start.31 = (bf16[2,2,2,96,768]{4,3,2,1,0:T(8,128)(2,1)}, bf16[2,2,2,96,768]{4,3,2,1,0:T(8,128)(2,1)}, u32[]{:S(2)}, u32[]{:S(2)}) collective-permute-start(bf16[2,2,2,96,768]{4,3,2,1,0:T(8,128)(2,1)} %get-tuple-element.123), channel_id=1, source_target_pairs={{0,1},{1,0},{2,3},{3,2},{4,5},{5,4},{6,7},{7,6},{8,9},{9,8},{10,11... | collective-permute-start | bytes 3538952 | tf_op jit(solution)/shard_map/to_x_1/ppermute | solution.py:29
  159.3 34.5 %collective-permute-start.32 = (bf16[2,2,2,96,768]{4,3,2,1,0:T(8,128)(2,1)}, bf16[2,2,2,96,768]{4,3,2,1,0:T(8,128)(2,1)}, u32[]{:S(2)}, u32[]{:S(2)}) collective-permute-start(bf16[2,2,2,96,768]{4,3,2,1,0:T(8,128)(2,1)} %get-tuple-element.126), channel_id=1, source_target_pairs={{0,16},{16,0},{1,17},{17,1},{2,18},{18,2},{3,19},{19,3},{4,20},{20... | collective-permute-start | bytes 3538952 | tf_op jit(solution)/shard_map/to_y_1/ppermute | solution.py:29
  193.2 29.9 %collective-permute-start.36 = (bf16[1,2,2,96,768]{4,3,2,1,0:T(8,128)(2,1)}, bf16[1,2,2,96,768]{4,3,2,1,0:T(8,128)(2,1)}, u32[]{:S(2)}, u32[]{:S(2)}) collective-permute-start(bf16[1,2,2,96,768]{4,3,2,1,0:T(8,128)(2,1)} %fusion.19), channel_id=1, source_target_pairs={{0,16},{16,0},{1,17},{17,1},{2,18},{18,2},{3,19},{19,3},{4,20},{20... | collective-permute-start | bytes 1769480 | tf_op jit(solution)/shard_map/feed_sums_second_stage/to_y_1/ppermute | solution.py:29
  195.9 28.7 %collective-permute-start.37 = (bf16[1,2,2,96,768]{4,3,2,1,0:T(8,128)(2,1)}, bf16[1,2,2,96,768]{4,3,2,1,0:T(8,128)(2,1)}, u32[]{:S(2)}, u32[]{:S(2)}) collective-permute-start(bf16[1,2,2,96,768]{4,3,2,1,0:T(8,128)(2,1)} %fusion.18), channel_id=1, source_target_pairs={{0,1},{1,0},{2,3},{3,2},{4,5},{5,4},{6,7},{7,6},{8,9},{9,8},{10,11... | collective-permute-start | bytes 1769480 | tf_op jit(solution)/shard_map/feed_sums_second_stage/to_x_1/ppermute | solution.py:29
  198.7 33.2 %collective-permute-start.34 = (bf16[2,2,2,2,48,384]{5,4,0,2,1,3:T(8,128)(2,1)}, bf16[2,2,2,2,48,384]{5,4,0,2,1,3:T(8,128)(2,1)}, u32[]{:S(2)}, u32[]{:S(2)}) collective-permute-start(bf16[2,2,2,2,48,384]{5,4,0,2,1,3:T(8,128)(2,1)} %fusion.29), channel_id=1, source_target_pairs={{0,1},{1,0},{2,3},{3,2},{4,5},{5,4},{6,7},{7,6},{8,9},{9,8},{10,11... | collective-permute-start | bytes 1769480 | tf_op jit(solution)/shard_map/cross_sums_first_stage/to_x_1/ppermute | solution.py:29
  200.0 33.8 %collective-permute-start.35 = (bf16[2,2,2,2,48,384]{5,4,0,2,1,3:T(8,128)(2,1)}, bf16[2,2,2,2,48,384]{5,4,0,2,1,3:T(8,128)(2,1)}, u32[]{:S(2)}, u32[]{:S(2)}) collective-permute-start(bf16[2,2,2,2,48,384]{5,4,0,2,1,3:T(8,128)(2,1)} %fusion.30), channel_id=1, source_target_pairs={{0,16},{16,0},{1,17},{17,1},{2,18},{18,2},{3,19},{19,3},{4,20},{20... | collective-permute-start | bytes 1769480 | tf_op jit(solution)/shard_map/cross_sums_first_stage/to_y_1/ppermute | solution.py:29
  223.1 14.9 %collective-permute-start.33 = (bf16[2,768,384]{2,1,0:T(8,128)(2,1)}, bf16[2,768,384]{2,1,0:T(8,128)(2,1)S(1)}, u32[]{:S(2)}, u32[]{:S(2)}) collective-permute-start(bf16[2,768,384]{2,1,0:T(8,128)(2,1)} %get-tuple-element.131), channel_id=1, source_target_pairs={{0,8},{8,0},{1,9},{9,1},{2,10},{10,2},{3,11},{11,3},{4,12},{12,4},... | collective-permute-start | bytes 3538952 | tf_op jit(solution)/shard_map/self_sums_first_stage/to_core_1/ppermute | solution.py:29
  227.8 16.2 %collective-permute-start.42 = (bf16[2,1,2,96,768]{4,3,0,2,1:T(8,128)(2,1)}, bf16[2,1,2,96,768]{4,3,0,2,1:T(8,128)(2,1)}, u32[]{:S(2)}, u32[]{:S(2)}) collective-permute-start(bf16[2,1,2,96,768]{4,3,0,2,1:T(8,128)(2,1)} %fusion.38), channel_id=1, source_target_pairs={{0,2},{2,0},{1,3},{3,1},{4,6},{6,4},{5,7},{7,5},{8,10},{10,8},{9,1... | collective-permute-start | bytes 1769480 | tf_op jit(solution)/shard_map/feed_sums_third_stage/to_zb_1/ppermute | solution.py:29
  233.8 13.8 %collective-permute-start.41 = (bf16[2,2,2,48,384]{4,3,0,2,1:T(8,128)(2,1)}, bf16[2,2,2,48,384]{4,3,0,2,1:T(8,128)(2,1)S(1)}, u32[]{:S(2)}, u32[]{:S(2)}) collective-permute-start(bf16[2,2,2,48,384]{4,3,0,2,1:T(8,128)(2,1)} %fusion.54), channel_id=1, source_target_pairs={{0,16},{16,0},{1,17},{17,1},{2,18},{18,2},{3,19},{19,3},{4,20},{20... | collective-permute-start | bytes 884744 | tf_op jit(solution)/shard_map/cross_sums_second_stage/to_y_1/ppermute | solution.py:29
  238.2 19.4 %collective-permute-start.40 = (bf16[2,2,2,2,48,384]{5,4,0,2,1,3:T(8,128)(2,1)S(1)}, bf16[2,2,2,2,48,384]{5,4,0,2,1,3:T(8,128)(2,1)S(1)}, u32[]{:S(2)}, u32[]{:S(2)}) collective-permute-start(bf16[2,2,2,2,48,384]{5,4,0,2,1,3:T(8,128)(2,1)S(1)} %fusion.31), channel_id=1, source_target_pairs={{0,1},{1,0},{2,3},{3,2},{4,5},{5,4},{6,7},{7,6},{8,9},{9,8},{10,11... | collective-permute-start | bytes 1769480 | tf_op jit(solution)/shard_map/self_sums_first_stage/to_x_1/ppermute | solution.py:29
  238.7 18.9 %collective-permute-start.44 = (bf16[2,2,2,2,48,384]{5,4,0,2,1,3:T(8,128)(2,1)S(1)}, bf16[2,2,2,2,48,384]{5,4,0,2,1,3:T(8,128)(2,1)S(1)}, u32[]{:S(2)}, u32[]{:S(2)}) collective-permute-start(bf16[2,2,2,2,48,384]{5,4,0,2,1,3:T(8,128)(2,1)S(1)} %fusion.32), channel_id=1, source_target_pairs={{0,16},{16,0},{1,17},{17,1},{2,18},{18,2},{3,19},{19,3},{4,20},{20... | collective-permute-start | bytes 1769480 | tf_op jit(solution)/shard_map/self_sums_first_stage/to_y_1/ppermute | solution.py:29
  244.0 17.4 %collective-permute-start.39 = (bf16[4,4736]{1,0:T(4,128)(2,1)S(1)}, bf16[4,4736]{1,0:T(4,128)(2,1)S(1)}, u32[]{:S(2)}, u32[]{:S(2)}) collective-permute-start(bf16[4,4736]{1,0:T(4,128)(2,1)S(1)} %shard_map.313), channel_id=1, source_target_pairs={{0,4},{4,0},{1,5},{5,1},{2,6},{6,2},{3,7},{7,3},{8,12},{12,8},{9,1... | collective-permute-start | bytes 113672 | tf_op jit(solution)/shard_map/gather_mod/to_za_1/ppermute | solution.py:29
  247.6 20.2 %collective-permute-start.47 = (bf16[2,1,96,768]{3,2,0,1:T(8,128)(2,1)}, bf16[2,1,96,768]{3,2,0,1:T(8,128)(2,1)}, u32[]{:S(2)}, u32[]{:S(2)}) collective-permute-start(bf16[2,1,96,768]{3,2,0,1:T(8,128)(2,1)} %fusion.50), channel_id=1, source_target_pairs={{0,4},{4,0},{1,5},{5,1},{2,6},{6,2},{3,7},{7,3},{8,12},{12,8},{9,1... | collective-permute-start | bytes 884744 | tf_op jit(solution)/shard_map/feed_sums_fourth_stage/to_za_1/ppermute | solution.py:29
  252.0 14.4 %collective-permute-start.48 = (bf16[2,2,2,48,384]{4,3,1,0,2:T(8,128)(2,1)}, bf16[2,2,2,48,384]{4,3,1,0,2:T(8,128)(2,1)}, u32[]{:S(2)}, u32[]{:S(2)}) collective-permute-start(bf16[2,2,2,48,384]{4,3,1,0,2:T(8,128)(2,1)} %fusion.63), channel_id=1, source_target_pairs={{0,2},{2,0},{1,3},{3,1},{4,6},{6,4},{5,7},{7,5},{8,10},{10,8},{9,1... | collective-permute-start | bytes 884744 | tf_op jit(solution)/shard_map/cross_sums_third_stage/to_zb_1/ppermute | solution.py:29
  289.2 18.6 %collective-permute-start.55 = (bf16[64,4736]{1,0:T(8,128)(2,1)}, bf16[64,4736]{1,0:T(8,128)(2,1)}, u32[]{:S(2)}, u32[]{:S(2)}) collective-permute-start(bf16[64,4736]{1,0:T(8,128)(2,1)} %bitcast.147), channel_id=1, source_target_pairs={{0,8},{8,0},{1,9},{9,1},{2,10},{10,2},{3,11},{11,3},{4,12},{12,4},... | collective-permute-start | bytes 1818632 | tf_op jit(solution)/shard_map/gather_mod/to_core_1/ppermute | solution.py:29
  291.1 14.1 %collective-permute-start.62 = (bf16[4,48,384]{2,1,0:T(8,128)(2,1)S(1)}, bf16[4,48,384]{2,1,0:T(8,128)(2,1)}, u32[]{:S(2)}, u32[]{:S(2)}) collective-permute-start(bf16[4,48,384]{2,1,0:T(8,128)(2,1)S(1)} %bitcast.361), channel_id=1, source_target_pairs={{0,8},{8,0},{1,9},{9,1},{2,10},{10,2},{3,11},{11,3},{4,12},{12,4},... | collective-permute-start | bytes 442376 | tf_op jit(solution)/shard_map/cross_spread/to_core_1/ppermute | solution.py:29
  (147 other events, 1103.3 us)

commit v5 on v4

--- a/solution.py
+++ b/solution.py
@@ -158,23 +158,21 @@
     feed_ref[0] = tall_ref[own, :].astype(bf16)
 
 
-def weight_parts(weights, up_weight, down_weight):
+def own_rows(value, mine):
+    part = value.shape[0] // (lax.axis_size("y") * lax.axis_size("core"))
+    return lax.dynamic_slice_in_dim(value, mine * part, part, 0)
+
+
+def weight_parts(weights):
     copies = lax.axis_size("y") * lax.axis_size("core")
     mine = lax.axis_index("y") * lax.axis_size("core") + lax.axis_index("core")
-    hidden, width = down_weight.shape
-    rows = weights[0].shape[0] // copies
-    if rows % 8 or hidden // copies % 8:
-
-        def own(value):
-            part = value.shape[0] // copies
-            return lax.dynamic_slice_in_dim(value, mine * part, part, 0)
-
-        kept = [own(w) for w in weights]
-        feed_part = jnp.stack([own(up_weight.T), own(down_weight)])
-        return jnp.stack(kept[:3]), jnp.stack(kept[3:]), feed_part
+    width, rows = weights[0].shape[1], weights[0].shape[0] // copies
+    if rows % 8:
+        kept = [own_rows(w, mine) for w in weights]
+        return jnp.stack(kept[:3]), jnp.stack(kept[3:])
     smem, hbm = pl.BlockSpec(memory_space=pltpu.SMEM), pl.BlockSpec(memory_space=pltpu.HBM)
     vmem = pl.BlockSpec(memory_space=pltpu.VMEM)
-    first, more = pl.pallas_call(
+    return pl.pallas_call(
         rows_kernel,
         in_specs=[smem] + [hbm] * len(weights),
         out_specs=[vmem] * 2,
@@ -184,7 +182,18 @@
         ],
         scratch_shapes=[pltpu.SemaphoreType.DMA((len(weights),))],
     )(mine.reshape(1), *weights)
-    feed_part = pl.pallas_call(
+
+
+def feed_parts(up_weight, down_weight, *done):
+    copies = lax.axis_size("y") * lax.axis_size("core")
+    mine = lax.axis_index("y") * lax.axis_size("core") + lax.axis_index("core")
+    mine = after(mine, *done)
+    hidden, width = down_weight.shape
+    if hidden // copies % 8:
+        return jnp.stack([own_rows(up_weight.T, mine), own_rows(down_weight, mine)])
+    smem, hbm = pl.BlockSpec(memory_space=pltpu.SMEM), pl.BlockSpec(memory_space=pltpu.HBM)
+    vmem = pl.BlockSpec(memory_space=pltpu.VMEM)
+    return pl.pallas_call(
         feed_rows_kernel,
         in_specs=[smem, hbm, hbm],
         out_specs=vmem,
@@ -195,7 +204,6 @@
             pltpu.SemaphoreType.DMA((2,)),
         ],
     )(mine.reshape(1), up_weight, down_weight)
-    return first, more, feed_part
 
 
 def finish_kernel(me_ref, near, far_y, far_core, far_both, *refs):
@@ -220,9 +228,11 @@
         out[...] = whole_ref[...] if out.shape == whole_ref.shape else whole_ref[...].T
 
 
-def spread(done):
+def spread(done, *hold):
     done = done.reshape(-1, *done.shape[2:])
     far_y = shifted(done, "y", 1)
+    if hold:
+        far_y = after(far_y, *hold)
     return done, far_y, shifted(done, "core", 1), shifted(far_y, "core", 1)
 
 
@@ -425,7 +435,9 @@
 
 def feed_kernel(paired, me_ref, x_ref, x_far, g_ref, g_far, *refs):
     inputs, outs = refs[: 4 if paired else 2], refs[4 if paired else 2 :]
-    out_ref, back_ref, out_far, back_far, *grad_refs, out_sum, back_sum = outs
+    out_ref, back_ref, out_far, back_far, *grad_refs = outs[:-6]
+    out_sum, back_sum, third_both, grad_both, active_both, pre_both = outs[-6:]
+    tokens = x_ref.shape[0]
     slope = (2.0 / jnp.pi) ** 0.5
     step = pl.program_id(0)
 
@@ -433,6 +445,8 @@
     def _():
         for ref in (out_ref, back_ref, out_sum, back_sum):
             ref[...] = jnp.zeros_like(ref)
+        third_both[:tokens], third_both[tokens:] = x_ref[...], x_far[...]
+        grad_both[:tokens], grad_both[tokens:] = g_ref[...], g_far[...]
 
     my_y, my_x = me_ref[0], me_ref[1]
     if paired:
@@ -448,24 +462,21 @@
     places = [(b, x, y) for b in range(zb) for x in range(nx) for y in range(ny)]
     up = jnp.concatenate([up_at(*p) for p in places], axis=0)
     down = jnp.concatenate([down_at(*p) for p in places], axis=0)
-    up_parts, down_parts = [], []
-    for third, grad, out, back in (
-        (x_ref, g_ref, out_ref, back_ref),
-        (x_far, g_far, out_sum, back_sum),
-    ):
-        pre = outer_cols(third[...], up)
+    for which, (out, back) in enumerate(((out_ref, back_ref), (out_sum, back_sum))):
+        here = slice(which * tokens, (which + 1) * tokens)
+        pre = outer_cols(third_both[here], up)
         square = pre * pre
-        bent = jnp.tanh(slope * pre * (1.0 + 0.044715 * square))
-        rise = 0.5 * (1.0 + bent)
-        active = (pre * rise).astype(bf16)
-        steep = rise + 0.5 * pre * (1.0 - bent * bent) * (slope * (1.0 + 0.134145 * square))
-        grad_pre = (outer_cols(grad[...], down) * steep).astype(bf16)
+        rise = 0.5 + 0.5 * jnp.tanh(pre * (slope + (0.044715 * slope) * square))
+        active = pre * rise
+        steep = rise + active * (1.0 - rise) * (2.0 * slope + (0.26829 * slope) * square)
+        active = active.astype(bf16)
+        grad_pre = (outer_cols(grad_both[here], down) * steep).astype(bf16)
         out[...] += matmul(active, down)
         back[...] += matmul(grad_pre, up)
-        up_parts.append(inner_rows(grad_pre, third[...]))
-        down_parts.append(inner_rows(active, grad[...]))
-    up_total = (up_parts[0] + up_parts[1]).astype(bf16)
-    down_total = (down_parts[0] + down_parts[1]).astype(bf16)
+        active_both[here] = active
+        pre_both[here] = grad_pre
+    up_total = inner_rows(pre_both[...], third_both[...]).astype(bf16)
+    down_total = inner_rows(active_both[...], grad_both[...]).astype(bf16)
     at = {p: slice(n * rows, (n + 1) * rows) for n, p in enumerate(places)}
     if paired:
         up_kept, up_sent, down_kept, down_sent = grad_refs
@@ -516,7 +527,9 @@
             grid=(za,),
             in_specs=[whole] * 4 + [matrix] * count,
             out_specs=[whole] * 4 + [grads] * count,
-            scratch_shapes=[pltpu.VMEM((tokens, width), f32)] * 2,
+            scratch_shapes=[pltpu.VMEM((tokens, width), f32)] * 2
+            + [pltpu.VMEM((2 * tokens, width), bf16)] * 2
+            + [pltpu.VMEM((2 * tokens, zb * nx * ny * rows), bf16)] * 2,
         ),
         out_shape=[jax.ShapeDtypeStruct((tokens, width), f32)] * 2
         + [jax.ShapeDtypeStruct((tokens, width), bf16)] * 2
@@ -600,7 +613,7 @@
     my_lens = lax.dynamic_slice_in_dim(text_lens, position * segs_dev, segs_dev, 0)
 
     half = width // 2
-    first, more, feed_part = weight_parts(
+    first, more = weight_parts(
         [
             query_w.T,
             key_w.T,
@@ -610,18 +623,18 @@
             cross_key_w.T,
             cross_value_w.T,
             cross_out_w,
-        ],
-        up_weight,
-        down_weight,
-    )
-    column = gather_axis(first, "za")
-    first_column = column
-    column = gather_axis(column, "zb")
-    more = gather_axis(after(more, column), "za")
-    feed_part = after(feed_part, more)
+        ]
+    )
+    first_column = gather_axis(first, "za")
+    feed_part = feed_parts(up_weight, down_weight, first_column)
+    column = gather_axis(first_column, "zb")
+    more = after(more, column)
     first_left = gather_axis(column[..., :half], "x")
     first_right = gather_axis(column[..., half:], "y")
-    my_steps = lax.dynamic_slice_in_dim(after(step_ids, first_left, first_right), position * segs_dev, segs_dev, 0)
+    crossed = (first_left, first_right)
+    more = gather_axis(more, "za", *crossed)
+    feed_part = after(feed_part, more)
+    my_steps = lax.dynamic_slice_in_dim(after(step_ids, column), position * segs_dev, segs_dev, 0)
     digits = jnp.stack([my_steps // 256, my_steps % 256], axis=1).astype(bf16)
     digits = jnp.pad(digits, ((0, 0), (0, 126)))
 
@@ -636,25 +649,25 @@
     allowed_t = (my_ids[:, None, :] == key_segment[None, :, None]) & valid_key[:, :, None]
     cross_bias_t = jnp.where(allowed_t, 0.0, masked_score).astype(f32)
 
-    text = after(text, first_left, first_right)
+    text = after(text, column)
     text_flat = text.reshape(rows_dev, SEGS, CAPTION, width).swapaxes(1, 2).reshape(-1, width)
     prepared = (digits, text_flat)
+    first_left = gather_axis(first_left, "y", more)
+    first_right = gather_axis(first_right, "x", more)
     more = gather_axis(more, "zb", first_left, first_right, *prepared)
-    first_left = gather_axis(first_left, "y")
-    first_right = gather_axis(first_right, "x")
     feed_part = gather_axis(feed_part, "za", first_left, first_right)
     more_left = gather_axis(more[..., :half], "x", first_left, first_right)
     more_right = gather_axis(more[..., half:], "y", first_left, first_right)
     qkv = assemble(gather_axis(first_left, "core"), gather_axis(first_right, "core"))
     qkv = qkv.reshape(-1, width)
     table_low = step_table
-    step_ids = after(step_ids, first)
+    step_ids = after(step_ids, first_column)
     choose_step = (step_ids[:, None] == jnp.arange(step_table.shape[0])[None, :]).astype(bf16)
     silu_mine = jax.nn.silu(matmul(choose_step, table_low)).astype(bf16)
     partial_mod = matmul(silu_mine, ada_weight)
     partial_mod = partial_mod.reshape(za, zb, nx, segs_dev, partial_mod.shape[1])
-    modulation = summed(landed(launch_wide(partial_mod, "x", 2), first_column)).astype(bf16)
-    modulation = summed(landed(launch([modulation], "zb", 1), column)).astype(bf16)
+    modulation = summed(landed(launch_wide(partial_mod, "x", 2), column)).astype(bf16)
+    modulation = summed(landed(launch([modulation], "zb", 1), *crossed)).astype(bf16)
     modulation = summed(landed(launch([modulation], "za", 0), first_left, first_right))
     modulation = modulation + ada_bias.astype(f32)
     flat_ids = my_ids.reshape(-1)
@@ -777,20 +790,18 @@
     with jax.named_scope("gather_mod"):
         gathered = joined_rows(gathered, "zb", *self_sums[1])
     cross_done = summed(landed(cross_sums, gathered)).astype(bf16)
-    with jax.named_scope("self_sums_fourth_stage"):
-        self_sums = fourth_stage(self_sums, cross_done, feed_quarters[1])
     with jax.named_scope("cross_spread"):
         cross_quarters = spread(cross_done)
+    with jax.named_scope("self_sums_fourth_stage"):
+        self_sums = fourth_stage(self_sums, feed_quarters[1])
     with jax.named_scope("gather_mod"):
         gathered = joined_rows(gathered, "x", *self_sums[1])
     grad_frames = grad_resid_one + norm_back(
         normed_one, inverse_one, after(grad_first, gathered) * (1.0 + scale_one)
     )
+    self_done = summed(landed(self_sums, grad_frames)).astype(bf16)
     with jax.named_scope("gather_mod"):
-        gathered = joined_rows(gathered, "y", grad_frames)
-    self_done = summed(landed(self_sums, gathered, cross_quarters[1])).astype(bf16)
-    with jax.named_scope("self_spread"):
-        self_quarters = spread(self_done)
+        gathered = joined_rows(gathered, "y", self_done, cross_done)
     with jax.named_scope("gather_mod"):
         gathered = joined_rows(gathered, "core", self_done)
     grad_mod_all = gathered[:, : 6 * width]
@@ -810,12 +821,14 @@
 
     hidden, low = down_weight.shape[0], out_w.shape[0]
     made = (grad_ada_w, grad_table)
+    with jax.named_scope("self_spread"):
+        self_quarters = spread(self_done, *made)
     shard_up, shard_down = finish(feed_quarters, hidden, [up_weight.shape, down_weight.shape])
     shard_cout, shard_cquery, shard_ckey, shard_cvalue = finish(
         cross_quarters, low, [out_w.shape] * 4
     )
     shard_out, shard_query, shard_key, shard_value = finish(
-        self_quarters, low, [out_w.shape] * 4, *made, shard_up, shard_cout
+        self_quarters, low, [out_w.shape] * 4, shard_up, shard_cout
     )
 
     return (

time: 321 us -> 314 us (0.978)
  other arithmetic: 79.8 us -> 75.5 us
    another operation x45, other arithmetic: 20.7 us -> 16.5 us  [gather_axis(): return jnp.stack([at(place) for place in range(count)])]
    unnamed x228 -> x222, local copies, waits for them, and re-layouts: 7.64 us -> 7.47 us
  transfers between devices with their start and end apart: 65 -> 65, of which waited for: 16 -> 17; matrix products, arithmetic and copies ran while one was open for 33% -> 32% of each run, Pallas kernels for 19% -> 20%
where the time goes in v5:
time: 314 us; the launch traced here: 309 us
  Pallas kernels  87.4 us (28%)
  other arithmetic  75.5 us (24%)
  starting transfers between devices  59.5 us (19%)
  waiting for transfers between devices  52.3 us (17%)
  local copies, waits for them, and re-layouts  19.1 us (6%)
  matrix products  12.4 us (4%)
    ppermute x65, starting transfers between devices, shifted(): lax.ppermute(value, axis, [(k, (k + steps) % count) for k in range(count)])  59.5 us
    ppermute x65, waiting for transfers between devices, shifted(): lax.ppermute(value, axis, [(k, (k + steps) % count) for k in range(count)])  52.3 us
    pallas_call x2, Pallas kernels, attend_back(): pl.pallas_call(backward_kernel, grid_spec=pltpu.PrefetchScalarGridSpec(nu...  39.2 us
    pallas_call x1, Pallas kernels, feed(): pl.pallas_call(partial(feed_kernel, paired), grid_spec=pltpu.PrefetchScal...  23 us
    another operation x45, other arithmetic, gather_axis(): return jnp.stack([at(place) for place in range(count)])  16.5 us
    convert_element_type x13, other arithmetic, launch(): summed(picked(terms, dim, (me + s) % count)).astype(bf16)  14.7 us
    pallas_call x2, Pallas kernels, attend(): pl.pallas_call(forward_kernel, grid=(rows, pairs), in_specs=blocks + [pl....  11.3 us
    reduce_sum x3, other arithmetic, norm_back(): mean_grad = jnp.mean(upstream, axis=-1, keepdims=True)  8.76 us
  transfers between devices with their start and end apart: 65, of which 17 were waited for; matrix products, arithmetic and copies ran while one was open for 32% of the time, Pallas kernels for 20%

profile of v5, /device:TPU:0, one launch (start us, length us, event | category | flops | bytes accessed | tf_op | source)
XLA Modules:
  0.0 309.2 jit_solution(4609885879584569460)
XLA Ops:
  2.5 4.1 %collective-permute-start = (bf16[3,24,768]{2,1,0:T(8,128)(2,1)}, bf16[3,24,768]{2,1,0:T(8,128)(2,1)S(1)}, u32[]{:S(2)}, u32[]{:S(2)}) collective-permute-start(bf16[3,24,768]{2,1,0:T(8,128)(2,1)} %get-tuple-element.99), channel_id=1, source_target_pairs={{0,4},{4,0},{1,5},{5,1},{2,6},{6,2},{3,7},{7,3},{8,12},{12,8},{9,1... | collective-permute-start | bytes 331784 | tf_op jit(solution)/shard_map/to_za_1/ppermute | solution.py:29
  18.7 2.1 shard_map.309
  24.8 3.3 %collective-permute-start.8 = (bf16[5,24,768]{2,1,0:T(8,128)(2,1)}, bf16[5,24,768]{2,1,0:T(8,128)(2,1)}, u32[]{:S(2)}, u32[]{:S(2)}) collective-permute-start(bf16[5,24,768]{2,1,0:T(8,128)(2,1)} %get-tuple-element.104), channel_id=1, source_target_pairs={{0,4},{4,0},{1,5},{5,1},{2,6},{6,2},{3,7},{7,3},{8,12},{12,8},{9,1... | collective-permute-start | bytes 552968 | tf_op jit(solution)/shard_map/to_za_1/ppermute | solution.py:29
  28.3 1.9 reshape.790.rest_0_
  37.4 2.4 collective-permute-start.6
  42.1 3.5 %collective-permute-done.7 = bf16[2,2,2,3,24,384]{5,4,3,2,1,0:T(8,128)(2,1)S(1)} collective-permute-done((bf16[2,2,2,3,24,384]{5,4,3,2,1,0:T(8,128)(2,1)S(1)}, bf16[2,2,2,3,24,384]{5,4,3,2,1,0:T(8,128)(2,1)S(1)}, u32[]{:S(2)}, u32[]{:S(2)}) %collective-permute-start.7) | collective-permute-done | bytes 442400 | tf_op jit(solution)/shard_map/to_y_1/ppermute | solution.py:29
  46.8 9.2 %collective-permute-done.12 = bf16[2,5,24,768]{3,2,1,0:T(8,128)(2,1)S(1)} collective-permute-done((bf16[2,5,24,768]{3,2,1,0:T(8,128)(2,1)S(1)}, bf16[2,5,24,768]{3,2,1,0:T(8,128)(2,1)S(1)}, u32[]{:S(2)}, u32[]{:S(2)}) %collective-permute-start.12) | collective-permute-done | bytes 368672 | tf_op jit(solution)/shard_map/to_zb_1/ppermute | solution.py:29
  59.5 5.2 %fusion = (f32[512,768]{1,0:T(8,128)}, bf16[512,768]{1,0:T(8,128)(2,1)S(1)}, bf16[512,768]{1,0:T(8,128)(2,1)S(1)}) fusion(bf16[512,768]{1,0:T(8,128)(2,1)S(1)} %copy-done.32, f32[512]{0:T(512)S(1)} %copy-done.81, f32[512]{0:T(512)S(1)} %broadcast_multiply_fusion.8, f32[768]{0:T(1024)S(1)} %get-tuple-element.200, f32[768]{0:T(1024)S(1)} %get-tuple-element.201, ...), kind=kLoop, calls=%fused_computation.20 | loop fusion | flops 7471104 | bytes 4761088 | tf_op jit(solution)/shard_map/mul | solution.py:271
  74.9 5.9 %shard_map.307.mix_ref = bf16[512,768]{1,0:T(8,128)(2,1)S(1)} custom-call(bf16[512,768]{1,0:T(8,128)(2,1)S(1)} %convolution_convert_fusion.3.q_ref, bf16[512,768]{1,0:T(8,128)(2,1)S(1)} %convolution_convert_fusion.2.k_ref, bf16[512,768]{1,0:T(8,128)(2,1)S(1)} %convolution_convert_fusion.1.v_ref, f32[1,512,512]{2,1,0:T(8,128)S(1)} %compare_select_fusion.bias_ref), custom_call_target="tpu_custom_call" | custom-call | tf_op jit(solution)/shard_map/pallas_call | solution.py:393
  86.4 9.7 %collective-permute-done.23 = bf16[2,2,96,768]{3,2,1,0:T(8,128)(2,1)S(1)} collective-permute-done((bf16[2,2,96,768]{3,2,1,0:T(8,128)(2,1)S(1)}, bf16[2,2,96,768]{3,2,1,0:T(8,128)(2,1)S(1)}, u32[]{:S(2)}, u32[]{:S(2)}) %collective-permute-start.23) | collective-permute-done | bytes 589856 | tf_op jit(solution)/shard_map/to_x_1/ppermute | solution.py:29
  98.8 2.4 collective-permute-done.25
  102.4 2.3 collective-permute-start.26
  107.4 2.2 fusion.125
  114.8 5.4 %shard_map.308.mix_ref = bf16[512,768]{1,0:T(8,128)(2,1)S(1)} custom-call(bf16[512,768]{1,0:T(8,128)(2,1)S(1)} %convolution_convert_fusion.q_ref, bf16[308,768]{1,0:T(8,128)(2,1)S(1)} %convolution_convert_fusion.5.k_ref, bf16[308,768]{1,0:T(8,128)(2,1)S(1)} %convolution_convert_fusion.4.v_ref, f32[1,512,308]{2,1,0:T(8,128)S(1)} %and_select_fusion.bias_ref), custom_call_target="tpu_custom_call" | custom-call | tf_op jit(solution)/shard_map/pallas_call | solution.py:393
  121.4 3.3 %add_convert_fusion.1 = (bf16[512,768]{1,0:T(8,128)(2,1)S(1)}, f32[512,768]{1,0:T(8,128)}) fusion(f32[768]{0:T(1024)S(1)} %get-tuple-element.189, f32[768]{0:T(1024)S(1)} %get-tuple-element.190, f32[768]{0:T(1024)S(1)} %get-tuple-element.191, f32[768]{0:T(1024)S(1)} %get-tuple-element.192, f32[768]{0:T(1024)S(1)} %get-tuple-element.193, ...), kind=kLoop, calls=%fused_computation.35 | loop fusion | flops 4718592 | bytes 3962368 | tf_op jit(solution)/shard_map/convert_element_type | solution.py:712
  126.1 4.2 %collective-permute-done.26.refs_3_ = bf16[2,2,2,96,768]{4,3,2,1,0:T(8,128)(2,1)} collective-permute-done((bf16[2,2,2,96,768]{4,3,2,1,0:T(8,128)(2,1)}, bf16[2,2,2,96,768]{4,3,2,1,0:T(8,128)(2,1)}, u32[]{:S(2)}, u32[]{:S(2)}) %collective-permute-start.26) | collective-permute-done | bytes 1179680 | tf_op jit(solution)/shard_map/to_x_1/ppermute | solution.py:29
  131.2 23.0 %shard_map.310 = (f32[512,768]{1,0:T(8,128)}, f32[512,768]{1,0:T(8,128)}, bf16[512,768]{1,0:T(8,128)(2,1)}, bf16[512,768]{1,0:T(8,128)(2,1)}, bf16[2,2,2,96,768]...) custom-call(s32[2]{0:T(128)} %pad_add_fusion.me_ref, ...), custom_call_target="tpu_custom_call" | custom-call | tf_op jit(solution)/shard_map/pallas_call | solution.py:523
  158.0 5.2 %fusion.122 = (f32[512]{0:T(512)S(1)}, f32[512]{0:T(512)S(1)}, f32[512,768]{1,0:T(8,128)S(1)}, bf16[512,768]{1,0:T(8,128)(2,1)}, f32[512,768]{1,0:T(8,128)}) fusion(f32[768]{0:T(1024)S(1)} %get-tuple-element.193, f32[768]{0:T(1024)S(1)} %get-tuple-element.194, pred[512]{0:T(512)(128)(4,1)} %get-tuple-element.213, f32[768]{0:T(1024)S(1)} %get-tuple-element.195, ...), kind=kLoop, calls=%fused_computation.392 | loop fusion | flops 7076864 | bytes 11826688 | tf_op jit(solution)/shard_map/reduce_sum | solution.py:275
  165.6 17.7 %shard_map.311 = (f32[308,768]{1,0:T(8,128)S(1)}, f32[512,768]{1,0:T(8,128)}, bf16[2,768,384]{2,1,0:T(8,128)(2,1)}, bf16[2,768,384]{2,1,0:T(8,128)(2,1)}, bf16[2...) custom-call(s32[1]{0:T(128)} %bitcast.79.core_ref, bf16[512,768]{1,0:T(8,128)(2,1)S(1)} %copy-done.19, ...), custom_call_target="tpu_custom_call" | custom-call | tf_op jit(solution)/shard_map/pallas_call | solution.py:416
  183.4 2.2 fusion.123
  187.9 2.2 fusion.19
  191.7 2.0 fusion.18
  198.4 21.5 %shard_map.312 = (f32[512,768]{1,0:T(8,128)}, bf16[2,768,384]{2,1,0:T(8,128)(2,1)}, bf16[2,768,384]{2,1,0:T(8,128)(2,1)}, bf16[2,768,384]{2,1,0:T(8,128)(2,1)}, bf16[2,768,384]{2,1,0:T(8,128)(2,1)}) custom-call(s32[1]{0:T(128)} %bitcast.79.core_ref, bf16[512,768]{1,0:T(8,128)(2,1)S(1)} %copy-done.9, bf16[512,768]{1,0:T(8,128)(2,1)S(1)} %copy-done.11, ...), custom_call_target="tpu_custom_call" | custom-call | tf_op jit(solution)/shard_map/pallas_call | solution.py:416
  236.5 3.8 %shard_map.313 = bf16[4,4736]{1,0:T(4,128)(2,1)S(1)} custom-call(s32[1,512]{1,0:T(1,128)S(1)} %get-tuple-element.215.clip_ref, bf16[4,128]{1,0:T(4,128)(2,1)S(1)} %fusion.115.digits_ref, f32[512,768]{1,0:T(8,128)S(1)} %copy-done.1, f32[512,768]{1,0:T(8,128)S(1)} %copy-done.5, f32[512,768]{1,0:T(8,128)S(1)} %get-tuple-element.218.resid, ...), custom_call_target="tpu_custom_call" | custom-call | tf_op jit(solution)/shard_map/pallas_call | solution.py:577
  242.9 2.2 collective-permute-start.47
  250.8 3.9 %collective-permute-done.40 = bf16[2,2,2,2,48,384]{5,4,0,2,1,3:T(8,128)(2,1)S(1)} collective-permute-done((bf16[2,2,2,2,48,384]{5,4,0,2,1,3:T(8,128)(2,1)S(1)}, bf16[2,2,2,2,48,384]{5,4,0,2,1,3:T(8,128)(2,1)S(1)}, u32[]{:S(2)}, u32[]{:S(2)}) %collective-permute-start.40) | collective-permute-done | bytes 589856 | tf_op jit(solution)/shard_map/self_sums_first_stage/to_x_1/ppermute | solution.py:29
  259.8 3.2 %collective-permute-done.48 = bf16[2,2,2,48,384]{4,3,1,0,2:T(8,128)(2,1)} collective-permute-done((bf16[2,2,2,48,384]{4,3,1,0,2:T(8,128)(2,1)}, bf16[2,2,2,48,384]{4,3,1,0,2:T(8,128)(2,1)}, u32[]{:S(2)}, u32[]{:S(2)}) %collective-permute-start.48) | collective-permute-done | bytes 294944 | tf_op jit(solution)/shard_map/cross_sums_third_stage/to_zb_1/ppermute | solution.py:29
  272.4 4.7 %collective-permute-done.51 = bf16[2,2,2,48,384]{4,3,1,0,2:T(8,128)(2,1)S(1)} collective-permute-done((bf16[2,2,2,48,384]{4,3,1,0,2:T(8,128)(2,1)S(1)}, bf16[2,2,2,48,384]{4,3,1,0,2:T(8,128)(2,1)S(1)}, u32[]{:S(2)}, u32[]{:S(2)}) %collective-permute-start.51) | collective-permute-done | bytes 294944 | tf_op jit(solution)/shard_map/self_sums_third_stage/to_zb_1/ppermute | solution.py:29
  283.1 2.3 collective-permute-done.54
  288.7 4.0 %collective-permute-done.61.far_y = bf16[4,48,384]{2,1,0:T(8,128)(2,1)} collective-permute-done((bf16[4,48,384]{2,1,0:T(8,128)(2,1)S(1)}, bf16[4,48,384]{2,1,0:T(8,128)(2,1)}, u32[]{:S(2)}, u32[]{:S(2)}) %collective-permute-start.61) | collective-permute-done | bytes 147488 | tf_op jit(solution)/shard_map/cross_spread/to_y_1/ppermute | solution.py:29
  294.6 2.5 shard_map.314
  297.0 2.1 shard_map.315
  (503 shorter events, 136.7 us)
Async XLA Ops:
  17.2 13.1 %collective-permute-start.1 = (f32[2,2,4,4608]{3,2,1,0:T(4,128)}, f32[2,2,4,4608]{3,2,1,0:T(4,128)}, u32[]{:S(2)}, u32[]{:S(2)}) collective-permute-start(f32[2,2,4,4608]{3,2,1,0:T(4,128)} %dynamic-slice_bitcast_fusion), channel_id=1, source_target_pairs={{0,1},{1,0},{2,3},{3,2},{4,5},{5,4},{6,7},{7,6},{8,9},{9,8},{10,11... | collective-permute-start | bytes 884744 | tf_op jit(solution)/shard_map/to_x_1/ppermute | solution.py:29
  24.8 15.0 %collective-permute-start.8 = (bf16[5,24,768]{2,1,0:T(8,128)(2,1)}, bf16[5,24,768]{2,1,0:T(8,128)(2,1)}, u32[]{:S(2)}, u32[]{:S(2)}) collective-permute-start(bf16[5,24,768]{2,1,0:T(8,128)(2,1)} %get-tuple-element.104), channel_id=1, source_target_pairs={{0,4},{4,0},{1,5},{5,1},{2,6},{6,2},{3,7},{7,3},{8,12},{12,8},{9,1... | collective-permute-start | bytes 552968 | tf_op jit(solution)/shard_map/to_za_1/ppermute | solution.py:29
  40.8 15.3 %collective-permute-start.12 = (bf16[2,5,24,768]{3,2,1,0:T(8,128)(2,1)S(1)}, bf16[2,5,24,768]{3,2,1,0:T(8,128)(2,1)S(1)}, u32[]{:S(2)}, u32[]{:S(2)}) collective-permute-start(bf16[2,5,24,768]{3,2,1,0:T(8,128)(2,1)S(1)} %pad_maximum_fusion.18), channel_id=1, source_target_pairs={{0,2},{2,0},{1,3},{3,1},{4,6},{6,4},{5,7},{7,5},{8,10},{10,8},{9,1... | collective-permute-start | bytes 1105928 | tf_op jit(solution)/shard_map/to_zb_1/ppermute | solution.py:29
  41.9 16.6 %collective-permute-start.21 = (bf16[2,96,768]{2,1,0:T(8,128)(2,1)S(1)}, bf16[2,96,768]{2,1,0:T(8,128)(2,1)S(1)}, u32[]{:S(2)}, u32[]{:S(2)}) collective-permute-start(bf16[2,96,768]{2,1,0:T(8,128)(2,1)S(1)} %copy-done.65), channel_id=1, source_target_pairs={{0,4},{4,0},{1,5},{5,1},{2,6},{6,2},{3,7},{7,3},{8,12},{12,8},{9,1... | collective-permute-start | bytes 884744 | tf_op jit(solution)/shard_map/to_za_1/ppermute | solution.py:29
  46.3 22.9 %collective-permute-start.10 = (bf16[2,2,2,2,3,24,384]{6,5,4,3,2,0,1:T(8,128)(2,1)S(1)}, bf16[2,2,2,2,3,24,384]{6,5,4,3,2,0,1:T(8,128)(2,1)S(1)}, u32[]{:S(2)}, u32[]{:S(2)}) collective-permute-start(bf16[2,2,2,2,3,24,384]{6,5,4,3,2,0,1:T(8,128)(2,1)S(1)} %pad_maximum_fusion.7), channel_id=1, source_target_pairs={{0,8},{8,0},{1,9},{9,1},{2,10},{10,2},{3,11},{11,3},{4,12},{12,4},... | collective-permute-start | bytes 2654216 | tf_op jit(solution)/shard_map/to_core_1/ppermute | solution.py:29
  46.4 22.2 %collective-permute-start.11 = (bf16[2,2,2,2,3,24,384]{6,5,4,3,2,0,1:T(8,128)(2,1)S(1)}, bf16[2,2,2,2,3,24,384]{6,5,4,3,2,0,1:T(8,128)(2,1)S(1)}, u32[]{:S(2)}, u32[]{:S(2)}) collective-permute-start(bf16[2,2,2,2,3,24,384]{6,5,4,3,2,0,1:T(8,128)(2,1)S(1)} %copy.137), channel_id=1, source_target_pairs={{0,8},{8,0},{1,9},{9,1},{2,10},{10,2},{3,11},{11,3},{4,12},{12,4},... | collective-permute-start | bytes 2654216 | tf_op jit(solution)/shard_map/to_core_1/ppermute | solution.py:29
  59.5 21.3 %collective-permute-start.22 = (bf16[2,2,96,768]{3,2,0,1:T(8,128)(2,1)}, bf16[2,2,96,768]{3,2,0,1:T(8,128)(2,1)}, u32[]{:S(2)}, u32[]{:S(2)}) collective-permute-start(bf16[2,2,96,768]{3,2,0,1:T(8,128)(2,1)} %pad_maximum_fusion.13), channel_id=1, source_target_pairs={{0,2},{2,0},{1,3},{3,1},{4,6},{6,4},{5,7},{7,5},{8,10},{10,8},{9,1... | collective-permute-start | bytes 1769480 | tf_op jit(solution)/shard_map/to_zb_1/ppermute | solution.py:29
  66.2 17.5 %collective-permute-start.17 = (bf16[2,2,2,5,24,384]{5,4,3,2,1,0:T(8,128)(2,1)S(1)}, bf16[2,2,2,5,24,384]{5,4,3,2,1,0:T(8,128)(2,1)S(1)}, u32[]{:S(2)}, u32[]{:S(2)}) collective-permute-start(bf16[2,2,2,5,24,384]{5,4,3,2,1,0:T(8,128)(2,1)S(1)} %pad_maximum_fusion.10), channel_id=1, source_target_pairs={{0,1},{1,0},{2,3},{3,2},{4,5},{5,4},{6,7},{7,6},{8,9},{9,8},{10,11... | collective-permute-start | bytes 2211848 | tf_op jit(solution)/shard_map/to_x_1/ppermute | solution.py:29
  68.2 17.5 %collective-permute-start.14 = (bf16[2,2,2,5,24,384]{5,4,3,2,1,0:T(8,128)(2,1)S(1)}, bf16[2,2,2,5,24,384]{5,4,3,2,1,0:T(8,128)(2,1)S(1)}, u32[]{:S(2)}, u32[]{:S(2)}) collective-permute-start(bf16[2,2,2,5,24,384]{5,4,3,2,1,0:T(8,128)(2,1)S(1)} %pad_maximum_fusion.9), channel_id=1, source_target_pairs={{0,16},{16,0},{1,17},{17,1},{2,18},{18,2},{3,19},{19,3},{4,20},{20... | collective-permute-start | bytes 2211848 | tf_op jit(solution)/shard_map/to_y_1/ppermute | solution.py:29
  82.3 13.7 %collective-permute-start.23 = (bf16[2,2,96,768]{3,2,1,0:T(8,128)(2,1)S(1)}, bf16[2,2,96,768]{3,2,1,0:T(8,128)(2,1)S(1)}, u32[]{:S(2)}, u32[]{:S(2)}) collective-permute-start(bf16[2,2,96,768]{3,2,1,0:T(8,128)(2,1)S(1)} %get-tuple-element.267), channel_id=1, source_target_pairs={{0,1},{1,0},{2,3},{3,2},{4,5},{5,4},{6,7},{7,6},{8,9},{9,8},{10,11... | collective-permute-start | bytes 1769480 | tf_op jit(solution)/shard_map/to_x_1/ppermute | solution.py:29
  84.2 20.5 %collective-permute-start.18 = (bf16[2,2,2,2,5,24,384]{6,5,4,3,2,0,1:T(8,128)(2,1)S(1)}, bf16[2,2,2,2,5,24,384]{6,5,4,3,2,0,1:T(8,128)(2,1)S(1)}, u32[]{:S(2)}, u32[]{:S(2)}) collective-permute-start(bf16[2,2,2,2,5,24,384]{6,5,4,3,2,0,1:T(8,128)(2,1)S(1)} %copy.148), channel_id=1, source_target_pairs={{0,8},{8,0},{1,9},{9,1},{2,10},{10,2},{3,11},{11,3},{4,12},{12,4},... | collective-permute-start | bytes 4423688 | tf_op jit(solution)/shard_map/to_core_1/ppermute | solution.py:29
  84.9 40.6 %collective-permute-start.20 = (bf16[512,768]{1,0:T(8,128)(2,1)S(1)}, bf16[512,768]{1,0:T(8,128)(2,1)}, u32[]{:S(2)}, u32[]{:S(2)}) collective-permute-start(bf16[512,768]{1,0:T(8,128)(2,1)S(1)} %get-tuple-element.308.g_ref), channel_id=1, source_target_pairs={{0,8},{8,0},{1,9},{9,1},{2,10},{10,2},{3,11},{11,3},{4,12},{12,4},... | collective-permute-start | bytes 2359304 | tf_op jit(solution)/shard_map/to_core_1/ppermute | solution.py:29
  85.0 16.1 %collective-permute-start.25 = (bf16[2,2,96,768]{3,2,1,0:T(8,128)(2,1)S(1)}, bf16[2,2,96,768]{3,2,1,0:T(8,128)(2,1)S(1)}, u32[]{:S(2)}, u32[]{:S(2)}) collective-permute-start(bf16[2,2,96,768]{3,2,1,0:T(8,128)(2,1)S(1)} %get-tuple-element.266), channel_id=1, source_target_pairs={{0,16},{16,0},{1,17},{17,1},{2,18},{18,2},{3,19},{19,3},{4,20},{20... | collective-permute-start | bytes 1769480 | tf_op jit(solution)/shard_map/to_y_1/ppermute | solution.py:29
  86.1 19.4 %collective-permute-start.15 = (bf16[2,2,2,2,5,24,384]{6,5,4,3,2,0,1:T(8,128)(2,1)S(1)}, bf16[2,2,2,2,5,24,384]{6,5,4,3,2,0,1:T(8,128)(2,1)S(1)}, u32[]{:S(2)}, u32[]{:S(2)}) collective-permute-start(bf16[2,2,2,2,5,24,384]{6,5,4,3,2,0,1:T(8,128)(2,1)S(1)} %pad_maximum_fusion), channel_id=1, source_target_pairs={{0,8},{8,0},{1,9},{9,1},{2,10},{10,2},{3,11},{11,3},{4,12},{12,4},... | collective-permute-start | bytes 4423688 | tf_op jit(solution)/shard_map/to_core_1/ppermute | solution.py:29
  97.3 28.8 %collective-permute-start.24 = (bf16[2,2,2,96,768]{4,3,2,1,0:T(8,128)(2,1)}, bf16[2,2,2,96,768]{4,3,2,1,0:T(8,128)(2,1)}, u32[]{:S(2)}, u32[]{:S(2)}) collective-permute-start(bf16[2,2,2,96,768]{4,3,2,1,0:T(8,128)(2,1)} %pad_maximum_fusion.5.refs_0_), channel_id=1, source_target_pairs={{0,16},{16,0},{1,17},{17,1},{2,18},{18,2},{3,19},{19,3},{4,20},{20... | collective-permute-start | bytes 3538952 | tf_op jit(solution)/shard_map/to_y_1/ppermute | solution.py:29
  102.4 27.9 %collective-permute-start.26 = (bf16[2,2,2,96,768]{4,3,2,1,0:T(8,128)(2,1)}, bf16[2,2,2,96,768]{4,3,2,1,0:T(8,128)(2,1)}, u32[]{:S(2)}, u32[]{:S(2)}) collective-permute-start(bf16[2,2,2,96,768]{4,3,2,1,0:T(8,128)(2,1)} %pad_maximum_fusion.6.refs_2_), channel_id=1, source_target_pairs={{0,1},{1,0},{2,3},{3,2},{4,5},{5,4},{6,7},{7,6},{8,9},{9,8},{10,11... | collective-permute-start | bytes 3538952 | tf_op jit(solution)/shard_map/to_x_1/ppermute | solution.py:29
  155.6 32.3 %collective-permute-start.31 = (bf16[2,2,2,96,768]{4,3,2,1,0:T(8,128)(2,1)}, bf16[2,2,2,96,768]{4,3,2,1,0:T(8,128)(2,1)}, u32[]{:S(2)}, u32[]{:S(2)}) collective-permute-start(bf16[2,2,2,96,768]{4,3,2,1,0:T(8,128)(2,1)} %get-tuple-element.132), channel_id=1, source_target_pairs={{0,1},{1,0},{2,3},{3,2},{4,5},{5,4},{6,7},{7,6},{8,9},{9,8},{10,11... | collective-permute-start | bytes 3538952 | tf_op jit(solution)/shard_map/to_x_1/ppermute | solution.py:29
  157.4 34.3 %collective-permute-start.32 = (bf16[2,2,2,96,768]{4,3,2,1,0:T(8,128)(2,1)}, bf16[2,2,2,96,768]{4,3,2,1,0:T(8,128)(2,1)}, u32[]{:S(2)}, u32[]{:S(2)}) collective-permute-start(bf16[2,2,2,96,768]{4,3,2,1,0:T(8,128)(2,1)} %get-tuple-element.135), channel_id=1, source_target_pairs={{0,16},{16,0},{1,17},{17,1},{2,18},{18,2},{3,19},{19,3},{4,20},{20... | collective-permute-start | bytes 3538952 | tf_op jit(solution)/shard_map/to_y_1/ppermute | solution.py:29
  190.1 29.9 %collective-permute-start.36 = (bf16[1,2,2,96,768]{4,3,2,1,0:T(8,128)(2,1)}, bf16[1,2,2,96,768]{4,3,2,1,0:T(8,128)(2,1)}, u32[]{:S(2)}, u32[]{:S(2)}) collective-permute-start(bf16[1,2,2,96,768]{4,3,2,1,0:T(8,128)(2,1)} %fusion.19), channel_id=1, source_target_pairs={{0,16},{16,0},{1,17},{17,1},{2,18},{18,2},{3,19},{19,3},{4,20},{20... | collective-permute-start | bytes 1769480 | tf_op jit(solution)/shard_map/feed_sums_second_stage/to_y_1/ppermute | solution.py:29
  193.7 27.8 %collective-permute-start.37 = (bf16[1,2,2,96,768]{4,3,2,1,0:T(8,128)(2,1)}, bf16[1,2,2,96,768]{4,3,2,1,0:T(8,128)(2,1)}, u32[]{:S(2)}, u32[]{:S(2)}) collective-permute-start(bf16[1,2,2,96,768]{4,3,2,1,0:T(8,128)(2,1)} %fusion.18), channel_id=1, source_target_pairs={{0,1},{1,0},{2,3},{3,2},{4,5},{5,4},{6,7},{7,6},{8,9},{9,8},{10,11... | collective-permute-start | bytes 1769480 | tf_op jit(solution)/shard_map/feed_sums_second_stage/to_x_1/ppermute | solution.py:29
  195.4 32.9 %collective-permute-start.34 = (bf16[2,2,2,2,48,384]{5,4,0,2,1,3:T(8,128)(2,1)}, bf16[2,2,2,2,48,384]{5,4,0,2,1,3:T(8,128)(2,1)}, u32[]{:S(2)}, u32[]{:S(2)}) collective-permute-start(bf16[2,2,2,2,48,384]{5,4,0,2,1,3:T(8,128)(2,1)} %fusion.29), channel_id=1, source_target_pairs={{0,1},{1,0},{2,3},{3,2},{4,5},{5,4},{6,7},{7,6},{8,9},{9,8},{10,11... | collective-permute-start | bytes 1769480 | tf_op jit(solution)/shard_map/cross_sums_first_stage/to_x_1/ppermute | solution.py:29
  197.8 32.2 %collective-permute-start.35 = (bf16[2,2,2,2,48,384]{5,4,0,2,1,3:T(8,128)(2,1)}, bf16[2,2,2,2,48,384]{5,4,0,2,1,3:T(8,128)(2,1)}, u32[]{:S(2)}, u32[]{:S(2)}) collective-permute-start(bf16[2,2,2,2,48,384]{5,4,0,2,1,3:T(8,128)(2,1)} %fusion.30), channel_id=1, source_target_pairs={{0,16},{16,0},{1,17},{17,1},{2,18},{18,2},{3,19},{19,3},{4,20},{20... | collective-permute-start | bytes 1769480 | tf_op jit(solution)/shard_map/cross_sums_first_stage/to_y_1/ppermute | solution.py:29
  220.0 13.9 %collective-permute-start.33 = (bf16[2,768,384]{2,1,0:T(8,128)(2,1)}, bf16[2,768,384]{2,1,0:T(8,128)(2,1)S(1)}, u32[]{:S(2)}, u32[]{:S(2)}) collective-permute-start(bf16[2,768,384]{2,1,0:T(8,128)(2,1)} %get-tuple-element.140), channel_id=1, source_target_pairs={{0,8},{8,0},{1,9},{9,1},{2,10},{10,2},{3,11},{11,3},{4,12},{12,4},... | collective-permute-start | bytes 3538952 | tf_op jit(solution)/shard_map/self_sums_first_stage/to_core_1/ppermute | solution.py:29
  224.7 15.7 %collective-permute-start.42 = (bf16[2,1,2,96,768]{4,3,0,2,1:T(8,128)(2,1)}, bf16[2,1,2,96,768]{4,3,0,2,1:T(8,128)(2,1)}, u32[]{:S(2)}, u32[]{:S(2)}) collective-permute-start(bf16[2,1,2,96,768]{4,3,0,2,1:T(8,128)(2,1)} %fusion.38), channel_id=1, source_target_pairs={{0,2},{2,0},{1,3},{3,1},{4,6},{6,4},{5,7},{7,5},{8,10},{10,8},{9,1... | collective-permute-start | bytes 1769480 | tf_op jit(solution)/shard_map/feed_sums_third_stage/to_zb_1/ppermute | solution.py:29
  230.1 12.8 %collective-permute-start.41 = (bf16[2,2,2,48,384]{4,3,0,2,1:T(8,128)(2,1)}, bf16[2,2,2,48,384]{4,3,0,2,1:T(8,128)(2,1)S(1)}, u32[]{:S(2)}, u32[]{:S(2)}) collective-permute-start(bf16[2,2,2,48,384]{4,3,0,2,1:T(8,128)(2,1)} %fusion.54), channel_id=1, source_target_pairs={{0,16},{16,0},{1,17},{17,1},{2,18},{18,2},{3,19},{19,3},{4,20},{20... | collective-permute-start | bytes 884744 | tf_op jit(solution)/shard_map/cross_sums_second_stage/to_y_1/ppermute | solution.py:29
  234.0 20.8 %collective-permute-start.40 = (bf16[2,2,2,2,48,384]{5,4,0,2,1,3:T(8,128)(2,1)S(1)}, bf16[2,2,2,2,48,384]{5,4,0,2,1,3:T(8,128)(2,1)S(1)}, u32[]{:S(2)}, u32[]{:S(2)}) collective-permute-start(bf16[2,2,2,2,48,384]{5,4,0,2,1,3:T(8,128)(2,1)S(1)} %fusion.31), channel_id=1, source_target_pairs={{0,1},{1,0},{2,3},{3,2},{4,5},{5,4},{6,7},{7,6},{8,9},{9,8},{10,11... | collective-permute-start | bytes 1769480 | tf_op jit(solution)/shard_map/self_sums_first_stage/to_x_1/ppermute | solution.py:29
  235.9 18.8 %collective-permute-start.44 = (bf16[2,2,2,2,48,384]{5,4,0,2,1,3:T(8,128)(2,1)S(1)}, bf16[2,2,2,2,48,384]{5,4,0,2,1,3:T(8,128)(2,1)S(1)}, u32[]{:S(2)}, u32[]{:S(2)}) collective-permute-start(bf16[2,2,2,2,48,384]{5,4,0,2,1,3:T(8,128)(2,1)S(1)} %fusion.32), channel_id=1, source_target_pairs={{0,16},{16,0},{1,17},{17,1},{2,18},{18,2},{3,19},{19,3},{4,20},{20... | collective-permute-start | bytes 1769480 | tf_op jit(solution)/shard_map/self_sums_first_stage/to_y_1/ppermute | solution.py:29
  240.3 17.9 %collective-permute-start.39 = (bf16[4,4736]{1,0:T(4,128)(2,1)S(1)}, bf16[4,4736]{1,0:T(4,128)(2,1)S(1)}, u32[]{:S(2)}, u32[]{:S(2)}) collective-permute-start(bf16[4,4736]{1,0:T(4,128)(2,1)S(1)} %shard_map.313), channel_id=1, source_target_pairs={{0,4},{4,0},{1,5},{5,1},{2,6},{6,2},{3,7},{7,3},{8,12},{12,8},{9,1... | collective-permute-start | bytes 113672 | tf_op jit(solution)/shard_map/gather_mod/to_za_1/ppermute | solution.py:29
  242.9 21.3 %collective-permute-start.47 = (bf16[2,1,96,768]{3,2,0,1:T(8,128)(2,1)}, bf16[2,1,96,768]{3,2,0,1:T(8,128)(2,1)}, u32[]{:S(2)}, u32[]{:S(2)}) collective-permute-start(bf16[2,1,96,768]{3,2,0,1:T(8,128)(2,1)} %fusion.50), channel_id=1, source_target_pairs={{0,4},{4,0},{1,5},{5,1},{2,6},{6,2},{3,7},{7,3},{8,12},{12,8},{9,1... | collective-permute-start | bytes 884744 | tf_op jit(solution)/shard_map/feed_sums_fourth_stage/to_za_1/ppermute | solution.py:29
  248.3 14.8 %collective-permute-start.48 = (bf16[2,2,2,48,384]{4,3,1,0,2:T(8,128)(2,1)}, bf16[2,2,2,48,384]{4,3,1,0,2:T(8,128)(2,1)}, u32[]{:S(2)}, u32[]{:S(2)}) collective-permute-start(bf16[2,2,2,48,384]{4,3,1,0,2:T(8,128)(2,1)} %fusion.63), channel_id=1, source_target_pairs={{0,2},{2,0},{1,3},{3,1},{4,6},{6,4},{5,7},{7,5},{8,10},{10,8},{9,1... | collective-permute-start | bytes 884744 | tf_op jit(solution)/shard_map/cross_sums_third_stage/to_zb_1/ppermute | solution.py:29
  258.4 12.2 %collective-permute-start.45 = (bf16[8,4736]{1,0:T(8,128)(2,1)S(1)}, bf16[8,4736]{1,0:T(8,128)(2,1)S(1)}, u32[]{:S(2)}, u32[]{:S(2)}) collective-permute-start(bf16[8,4736]{1,0:T(8,128)(2,1)S(1)} %reshape.801), channel_id=1, source_target_pairs={{0,2},{2,0},{1,3},{3,1},{4,6},{6,4},{5,7},{7,5},{8,10},{10,8},{9,1... | collective-permute-start | bytes 227336 | tf_op jit(solution)/shard_map/gather_mod/to_zb_1/ppermute | solution.py:29
  286.4 14.1 %collective-permute-start.56 = (bf16[64,4736]{1,0:T(8,128)(2,1)}, bf16[64,4736]{1,0:T(8,128)(2,1)}, u32[]{:S(2)}, u32[]{:S(2)}) collective-permute-start(bf16[64,4736]{1,0:T(8,128)(2,1)} %bitcast.150), channel_id=1, source_target_pairs={{0,8},{8,0},{1,9},{9,1},{2,10},{10,2},{3,11},{11,3},{4,12},{12,4},... | collective-permute-start | bytes 1818632 | tf_op jit(solution)/shard_map/gather_mod/to_core_1/ppermute | solution.py:29
  (144 other events, 1044.6 us)

commit v6 on v5

--- a/solution.py
+++ b/solution.py
@@ -1,4 +1,5 @@
 from functools import partial
+from typing import Any, NamedTuple
 
 import jax
 import jax.numpy as jnp
@@ -55,14 +56,28 @@
     return lax.optimization_barrier((value, *done))[0]
 
 
+class Term(NamedTuple):
+    value: Any
+    picks: tuple = ()
+    done: tuple = ()
+
+    def piece(self):
+        value = after(self.value, *self.done) if self.done else self.value
+        for dim, which in self.picks:
+            value = lax.dynamic_index_in_dim(value, which, dim, keepdims=False)
+        return value
+
+
 def picked(terms, dim, which):
-    return [lax.dynamic_index_in_dim(t, which, dim, keepdims=False) for t in terms]
+    terms = [t if isinstance(t, Term) else Term(t) for t in terms]
+    return [t._replace(picks=(*t.picks, (dim, which))) for t in terms]
 
 
 def summed(terms):
-    total = terms[0].astype(f32)
-    for term in terms[1:]:
-        total = total + term.astype(f32)
+    pieces = [t.piece() for t in terms]
+    total = pieces[0].astype(f32)
+    for piece in pieces[1:]:
+        total = total + piece.astype(f32)
     return total
 
 
@@ -79,16 +94,18 @@
 def launch_wide(value, axis, dim):
     count = lax.axis_size(axis)
     me = lax.axis_index(axis)
-    sent = [picked([value], dim, (me + s) % count)[0] for s in range(1, count)]
+    sent = [picked([value], dim, (me + s) % count)[0].piece() for s in range(1, count)]
     arrived = [shifted(part, axis, s) for s, part in enumerate(sent, 1)]
     return picked([value], dim, me), sent, arrived
 
 
 def landed(started, *done):
     kept, _, arrived = started
+    kept = [t if isinstance(t, Term) else Term(t) for t in kept]
     if done:
+        kept = [t._replace(done=done) for t in kept]
         arrived = [after(part, *done) for part in arrived]
-    return kept + arrived
+    return kept + [Term(part) for part in arrived]
 
 
 def split_rows(part):
@@ -549,12 +566,11 @@
         )
     else:
         sums = launch([parts[0][None]], "x", 3), launch([parts[1][None]], "y", 4)
-    out = out + shifted(out_far, "core", 1).astype(f32)
     back = back + shifted(back_far, "core", 1).astype(f32)
-    return out, back, sums
-
-
-def clips_kernel(clip_ref, digits_ref, first, one, resid, mixed, third, three, up, mlp, out_ref):
+    return out, shifted(out_far, "core", 1), back, sums
+
+
+def clips_kernel(clip_ref, digits_ref, first, one, resid, mixed, third, three, up, mlp, mlp_far, out_ref):
     clips, width = out_ref.shape[0], first.shape[1]
     row = lax.broadcasted_iota(jnp.int32, (16, 1), 0)
     chooser = (clip_ref[...] == row).astype(f32).astype(bf16)
@@ -564,7 +580,7 @@
         resid[...] * mixed[...],
         third[...],
         third[...] * three[...],
-        up[...].astype(f32) * mlp[...],
+        up[...].astype(f32) * (mlp[...] + mlp_far[...].astype(f32)),
     ]
     for place, part in enumerate(parts):
         total = matmul(chooser, part.astype(bf16))[:clips]
@@ -713,8 +729,7 @@
     upstream = out_grad.astype(f32)
     grad_mlp = (gate_two * upstream).astype(bf16)
     core = lax.axis_index("core").reshape(1)
-    mlp_out, grad_third, feed_sums = feed(third_in, grad_mlp, feed_up, feed_down)
-    layer_out = (resid_two + gate_two * mlp_out).astype(bf16)
+    mlp_near, mlp_far, grad_third, feed_sums = feed(third_in, grad_mlp, feed_up, feed_down)
 
     grad_resid_two = upstream + norm_back(
         normed_three, inverse_three, grad_third * (1.0 + scale_two)
@@ -732,10 +747,10 @@
         second_in,
         text_flat,
     )
-    with jax.named_scope("cross_sums_first_stage"):
-        cross_sums = first_stage(*cross_parts)
     with jax.named_scope("feed_sums_second_stage"):
         feed_sums = second_stage(feed_sums, grad_second)
+    with jax.named_scope("cross_sums_first_stage"):
+        cross_sums = first_stage(*cross_parts, *sends(feed_sums))
     grad_resid_one = grad_resid_two + norm_back(normed_two, inverse_two, grad_second)
     grad_self = after(
         (gate_one * grad_resid_one).astype(bf16), *sends(cross_sums), *sends(feed_sums)
@@ -751,10 +766,10 @@
         grad_self,
         first_in,
     )
-    with jax.named_scope("feed_sums_third_stage"):
-        feed_sums = third_stage(feed_sums, grad_first)
     with jax.named_scope("cross_sums_second_stage"):
         cross_sums = second_stage(cross_sums, grad_first)
+    with jax.named_scope("feed_sums_third_stage"):
+        feed_sums = third_stage(feed_sums, grad_first, *sends(cross_sums))
     with jax.named_scope("self_sums_first_stage"):
         self_sums = first_stage(*self_parts, *sends(cross_sums), *feed_sums[1])
 
@@ -770,32 +785,37 @@
         grad_third,
         normed_three,
         out_grad,
-        mlp_out,
+        mlp_near,
+        mlp_far,
     )
     with jax.named_scope("feed_sums_fourth_stage"):
         feed_sums = fourth_stage(feed_sums, grad_mod)
+    with jax.named_scope("self_sums_second_stage"):
+        self_sums = second_stage(self_sums, *feed_sums[1])
     with jax.named_scope("cross_sums_third_stage"):
-        cross_sums = third_stage(cross_sums, *feed_sums[1])
-    with jax.named_scope("self_sums_second_stage"):
-        self_sums = second_stage(self_sums, *cross_sums[1])
+        cross_sums = third_stage(cross_sums, *sends(self_sums))
     with jax.named_scope("gather_mod"):
-        gathered = joined_rows(grad_mod, "za", *sends(self_sums))
-    with jax.named_scope("cross_sums_fourth_stage"):
-        cross_sums = fourth_stage(cross_sums, gathered)
-    feed_done = summed(landed(feed_sums, *cross_sums[1])).astype(bf16)
+        gathered = joined_rows(grad_mod, "za", *cross_sums[1])
+    feed_done = summed(landed(feed_sums, gathered)).astype(bf16)
     with jax.named_scope("feed_spread"):
         feed_quarters = spread(feed_done)
     with jax.named_scope("self_sums_third_stage"):
         self_sums = third_stage(self_sums, feed_done)
+    with jax.named_scope("cross_sums_fourth_stage"):
+        cross_sums = fourth_stage(cross_sums, *self_sums[1])
+    layer_out = resid_two + gate_two * (after(mlp_near, *cross_sums[1]) + mlp_far.astype(f32))
+    layer_out = layer_out.astype(bf16)
     with jax.named_scope("gather_mod"):
-        gathered = joined_rows(gathered, "zb", *self_sums[1])
-    cross_done = summed(landed(cross_sums, gathered)).astype(bf16)
-    with jax.named_scope("cross_spread"):
-        cross_quarters = spread(cross_done)
+        gathered = joined_rows(gathered, "zb", *cross_sums[1])
+    hidden, low = down_weight.shape[0], out_w.shape[0]
+    shard_up, shard_down = finish(feed_quarters, hidden, [up_weight.shape, down_weight.shape])
+    grad_text = grad_text.reshape(rows_dev, CAPTION, SEGS, width).swapaxes(1, 2)
+    grad_text = after(grad_text.reshape(text.shape), *self_sums[1])
     with jax.named_scope("self_sums_fourth_stage"):
-        self_sums = fourth_stage(self_sums, feed_quarters[1])
+        self_sums = fourth_stage(self_sums, gathered, shard_up, grad_text)
+    cross_done = summed(landed(cross_sums, *self_sums[1])).astype(bf16)
     with jax.named_scope("gather_mod"):
-        gathered = joined_rows(gathered, "x", *self_sums[1])
+        gathered = joined_rows(gathered, "x", cross_done)
     grad_frames = grad_resid_one + norm_back(
         normed_one, inverse_one, after(grad_first, gathered) * (1.0 + scale_one)
     )
@@ -819,11 +839,11 @@
         choose_all.astype(f32), grad_cond, (((0,), (0,)), ((), ())), precision=highest
     )
 
-    hidden, low = down_weight.shape[0], out_w.shape[0]
     made = (grad_ada_w, grad_table)
+    with jax.named_scope("cross_spread"):
+        cross_quarters = spread(cross_done, *made)
     with jax.named_scope("self_spread"):
         self_quarters = spread(self_done, *made)
-    shard_up, shard_down = finish(feed_quarters, hidden, [up_weight.shape, down_weight.shape])
     shard_cout, shard_cquery, shard_ckey, shard_cvalue = finish(
         cross_quarters, low, [out_w.shape] * 4
     )
@@ -834,7 +854,7 @@
     return (
         layer_out,
         grad_frames,
-        grad_text.reshape(rows_dev, CAPTION, SEGS, width).swapaxes(1, 2).reshape(text.shape),
+        grad_text,
         grad_table,
         grad_ada_w,
         grad_ada_b,

time: 314 us -> 310 us (0.987)
  other arithmetic: 75.5 us -> 80.7 us
  local copies, waits for them, and re-layouts: 19.1 us -> 15.8 us
  starting transfers between devices: 59.5 us -> 56.3 us
    convert_element_type x13, other arithmetic: 14.7 us -> 20.5 us  [launch(): summed(picked(terms, dim, (me + s) % count)).astype(bf16)]
    another operation x45 -> x46, other arithmetic: 16.5 us -> 11.5 us  [gather_axis(): return jnp.stack([at(place) for place in range(count)])]
    another operation x6 -> x9, other arithmetic: 7.79 us -> 10.2 us  [third_stage(): return launch([jnp.stack([left, right])], 'zb', 3)]
    unnamed x222 -> x176, local copies, waits for them, and re-layouts: 7.47 us -> 6.69 us
  transfers between devices with their start and end apart: 65 -> 65, of which waited for: 17 -> 20; matrix products, arithmetic and copies ran while one was open for 32% -> 33% of each run, Pallas kernels for 20% -> 20%
where the time goes in v6:
time: 310 us; the launch traced here: 305 us
  Pallas kernels  86.7 us (28%)
  other arithmetic  80.7 us (26%)
  starting transfers between devices  56.3 us (18%)
  waiting for transfers between devices  50.7 us (16%)
  local copies, waits for them, and re-layouts  15.8 us (5%)
  matrix products  11.6 us (4%)
    ppermute x65, starting transfers between devices, shifted(): lax.ppermute(value, axis, [(k, (k + steps) % count) for k in range(count)])  56.3 us
    ppermute x65, waiting for transfers between devices, shifted(): lax.ppermute(value, axis, [(k, (k + steps) % count) for k in range(count)])  50.7 us
    pallas_call x2, Pallas kernels, attend_back(): pl.pallas_call(backward_kernel, grid_spec=pltpu.PrefetchScalarGridSpec(nu...  38.6 us
    pallas_call x1, Pallas kernels, feed(): pl.pallas_call(partial(feed_kernel, paired), grid_spec=pltpu.PrefetchScal...  23.2 us
    convert_element_type x13, other arithmetic, launch(): summed(picked(terms, dim, (me + s) % count)).astype(bf16)  20.5 us
    another operation x46, other arithmetic, gather_axis(): return jnp.stack([at(place) for place in range(count)])  11.5 us
    pallas_call x2, Pallas kernels, attend(): pl.pallas_call(forward_kernel, grid=(rows, pairs), in_specs=blocks + [pl....  10.9 us
    another operation x9, other arithmetic, third_stage(): return launch([jnp.stack([left, right])], 'zb', 3)  10.2 us
  transfers between devices with their start and end apart: 65, of which 20 were waited for; matrix products, arithmetic and copies ran while one was open for 33% of the time, Pallas kernels for 20%

profile of v6, /device:TPU:0, one launch (start us, length us, event | category | flops | bytes accessed | tf_op | source)
XLA Modules:
  0.0 304.5 jit_solution(11259272438267522671)
XLA Ops:
  2.5 4.1 %collective-permute-start = (bf16[3,24,768]{2,1,0:T(8,128)(2,1)}, bf16[3,24,768]{2,1,0:T(8,128)(2,1)S(1)}, u32[]{:S(2)}, u32[]{:S(2)}) collective-permute-start(bf16[3,24,768]{2,1,0:T(8,128)(2,1)} %get-tuple-element.142), channel_id=1, source_target_pairs={{0,4},{4,0},{1,5},{5,1},{2,6},{6,2},{3,7},{7,3},{8,12},{12,8},{9,1... | collective-permute-start | bytes 331784 | tf_op jit(solution)/shard_map/to_za_1/ppermute | solution.py:30
  16.8 2.1 shard_map.309
  23.9 3.3 %collective-permute-start.7 = (bf16[5,24,768]{2,1,0:T(8,128)(2,1)}, bf16[5,24,768]{2,1,0:T(8,128)(2,1)}, u32[]{:S(2)}, u32[]{:S(2)}) collective-permute-start(bf16[5,24,768]{2,1,0:T(8,128)(2,1)} %get-tuple-element.149), channel_id=1, source_target_pairs={{0,4},{4,0},{1,5},{5,1},{2,6},{6,2},{3,7},{7,3},{8,12},{12,8},{9,1... | collective-permute-start | bytes 552968 | tf_op jit(solution)/shard_map/to_za_1/ppermute | solution.py:30
  39.1 2.5 collective-permute-start.12
  41.6 2.0 collective-permute-done.6
  45.0 9.6 %collective-permute-done.12 = bf16[2,5,24,768]{3,2,1,0:T(8,128)(2,1)S(1)} collective-permute-done((bf16[2,5,24,768]{3,2,1,0:T(8,128)(2,1)S(1)}, bf16[2,5,24,768]{3,2,1,0:T(8,128)(2,1)S(1)}, u32[]{:S(2)}, u32[]{:S(2)}) %collective-permute-start.12) | collective-permute-done | bytes 368672 | tf_op jit(solution)/shard_map/to_zb_1/ppermute | solution.py:30
  57.7 4.8 %fusion = (f32[512,768]{1,0:T(8,128)}, bf16[512,768]{1,0:T(8,128)(2,1)S(1)}, bf16[512,768]{1,0:T(8,128)(2,1)}) fusion(bf16[512,768]{1,0:T(8,128)(2,1)S(1)} %copy-done.23, f32[512]{0:T(512)S(1)} %copy-done.75, f32[512]{0:T(512)S(1)} %copy-done.65, f32[768]{0:T(1024)S(1)} %get-tuple-element.286, f32[768]{0:T(1024)S(1)} %get-tuple-element.287, ...), kind=kLoop, calls=%fused_computation.20 | loop fusion | flops 7471104 | bytes 4761088 | tf_op jit(solution)/shard_map/mul | solution.py:288
  72.6 5.5 %shard_map.307.mix_ref = bf16[512,768]{1,0:T(8,128)(2,1)S(1)} custom-call(bf16[512,768]{1,0:T(8,128)(2,1)S(1)} %convolution_convert_fusion.3.q_ref, bf16[512,768]{1,0:T(8,128)(2,1)S(1)} %convolution_convert_fusion.2.k_ref, bf16[512,768]{1,0:T(8,128)(2,1)S(1)} %convolution_convert_fusion.1.v_ref, f32[1,512,512]{2,1,0:T(8,128)S(1)} %compare_select_fusion.bias_ref), custom_call_target="tpu_custom_call" | custom-call | tf_op jit(solution)/shard_map/pallas_call | solution.py:410
  85.2 8.1 %collective-permute-done.23 = bf16[2,2,96,768]{3,2,1,0:T(8,128)(2,1)S(1)} collective-permute-done((bf16[2,2,96,768]{3,2,1,0:T(8,128)(2,1)S(1)}, bf16[2,2,96,768]{3,2,1,0:T(8,128)(2,1)S(1)}, u32[]{:S(2)}, u32[]{:S(2)}) %collective-permute-start.23) | collective-permute-done | bytes 589856 | tf_op jit(solution)/shard_map/to_x_1/ppermute | solution.py:30
  94.6 5.1 %collective-permute-done.25 = bf16[2,2,96,768]{3,2,1,0:T(8,128)(2,1)S(1)} collective-permute-done((bf16[2,2,96,768]{3,2,1,0:T(8,128)(2,1)S(1)}, bf16[2,2,96,768]{3,2,1,0:T(8,128)(2,1)S(1)}, u32[]{:S(2)}, u32[]{:S(2)}) %collective-permute-start.25) | collective-permute-done | bytes 589856 | tf_op jit(solution)/shard_map/to_y_1/ppermute | solution.py:30
  103.8 2.2 fusion.111
  110.6 5.4 %shard_map.308.mix_ref = bf16[512,768]{1,0:T(8,128)(2,1)S(1)} custom-call(bf16[512,768]{1,0:T(8,128)(2,1)S(1)} %convolution_convert_fusion.q_ref, bf16[308,768]{1,0:T(8,128)(2,1)S(1)} %convolution_convert_fusion.5.k_ref, bf16[308,768]{1,0:T(8,128)(2,1)S(1)} %convolution_convert_fusion.4.v_ref, f32[1,512,308]{2,1,0:T(8,128)S(1)} %and_select_fusion.bias_ref), custom_call_target="tpu_custom_call" | custom-call | tf_op jit(solution)/shard_map/pallas_call | solution.py:410
  117.2 3.3 %add_convert_fusion.1 = (bf16[512,768]{1,0:T(8,128)(2,1)S(1)}, f32[512,768]{1,0:T(8,128)}) fusion(f32[768]{0:T(1024)S(1)} %get-tuple-element.275, f32[768]{0:T(1024)S(1)} %get-tuple-element.276, f32[768]{0:T(1024)S(1)} %get-tuple-element.277, f32[768]{0:T(1024)S(1)} %get-tuple-element.278, f32[768]{0:T(1024)S(1)} %get-tuple-element.279, ...), kind=kLoop, calls=%fused_computation.34 | loop fusion | flops 4718592 | bytes 3962368 | tf_op jit(solution)/shard_map/convert_element_type | solution.py:728
  121.1 3.4 %collective-permute-done.24.refs_1_ = bf16[2,2,2,96,768]{4,3,2,1,0:T(8,128)(2,1)} collective-permute-done((bf16[2,2,2,96,768]{4,3,2,1,0:T(8,128)(2,1)S(1)}, bf16[2,2,2,96,768]{4,3,2,1,0:T(8,128)(2,1)}, u32[]{:S(2)}, u32[]{:S(2)}) %collective-permute-start.24) | collective-permute-done | bytes 1179680 | tf_op jit(solution)/shard_map/to_y_1/ppermute | solution.py:30
  124.6 3.7 %collective-permute-done.26.refs_3_ = bf16[2,2,2,96,768]{4,3,2,1,0:T(8,128)(2,1)} collective-permute-done((bf16[2,2,2,96,768]{4,3,2,1,0:T(8,128)(2,1)}, bf16[2,2,2,96,768]{4,3,2,1,0:T(8,128)(2,1)}, u32[]{:S(2)}, u32[]{:S(2)}) %collective-permute-start.26) | collective-permute-done | bytes 1179680 | tf_op jit(solution)/shard_map/to_x_1/ppermute | solution.py:30
  128.3 23.2 %shard_map.310 = (f32[512,768]{1,0:T(8,128)}, f32[512,768]{1,0:T(8,128)}, bf16[512,768]{1,0:T(8,128)(2,1)}, bf16[512,768]{1,0:T(8,128)(2,1)}, bf16[2,2,2,96,768]...) custom-call(s32[2]{0:T(128)} %pad_add_fusion.me_ref, ...), custom_call_target="tpu_custom_call" | custom-call | tf_op jit(solution)/shard_map/pallas_call | solution.py:540
  154.0 3.0 fusion.108
  159.0 17.6 %shard_map.311 = (f32[308,768]{1,0:T(8,128)S(1)}, f32[512,768]{1,0:T(8,128)}, bf16[2,768,384]{2,1,0:T(8,128)(2,1)}, bf16[2,768,384]{2,1,0:T(8,128)(2,1)}, bf16[2...) custom-call(s32[1]{0:T(128)} %bitcast.79.core_ref, bf16[512,768]{1,0:T(8,128)(2,1)S(1)} %convolution_convert_fusion.q_ref, ...), custom_call_target="tpu_custom_call" | custom-call | tf_op jit(solution)/shard_map/pallas_call | solution.py:433
  178.1 2.5 fusion.109
  180.6 2.2 fusion.25
  183.9 2.0 fusion.26
  193.6 2.4 multiply_convert_fusion
  196.1 20.9 %shard_map.312 = (f32[512,768]{1,0:T(8,128)}, bf16[2,768,384]{2,1,0:T(8,128)(2,1)}, bf16[2,768,384]{2,1,0:T(8,128)(2,1)}, bf16[2,768,384]{2,1,0:T(8,128)(2,1)}, bf16[2,768,384]{2,1,0:T(8,128)(2,1)}) custom-call(s32[1]{0:T(128)} %bitcast.79.core_ref, bf16[512,768]{1,0:T(8,128)(2,1)S(1)} %copy-done.7, bf16[512,768]{1,0:T(8,128)(2,1)S(1)} %copy-done.9, ...), custom_call_target="tpu_custom_call" | custom-call | tf_op jit(solution)/shard_map/pallas_call | solution.py:433
  219.0 2.1 fusion.51
  226.9 2.1 fusion.29
  229.5 2.2 fusion.30
  239.5 4.5 %shard_map.313 = bf16[4,4736]{1,0:T(4,128)(2,1)S(1)} custom-call(s32[1,512]{1,0:T(1,128)S(1)} %get-tuple-element.301.clip_ref, bf16[4,128]{1,0:T(4,128)(2,1)S(1)} %fusion.101.digits_ref, f32[512,768]{1,0:T(8,128)S(1)} %copy-done.1, f32[512,768]{1,0:T(8,128)S(1)} %copy-done.3, f32[512,768]{1,0:T(8,128)} %get-tuple-element.304.resid, ...), custom_call_target="tpu_custom_call" | custom-call | tf_op jit(solution)/shard_map/pallas_call | solution.py:593
  246.2 2.6 collective-permute-start.45
  273.7 2.5 shard_map.314
  276.2 3.9 %collective-permute-done.54 = bf16[2,2,2,48,384]{4,3,1,0,2:T(8,128)(2,1)S(1)} collective-permute-done((bf16[2,2,2,48,384]{4,3,1,0,2:T(8,128)(2,1)S(1)}, bf16[2,2,2,48,384]{4,3,1,0,2:T(8,128)(2,1)S(1)}, u32[]{:S(2)}, u32[]{:S(2)}) %collective-permute-start.54) | collective-permute-done | bytes 294944 | tf_op jit(solution)/shard_map/self_sums_third_stage/to_zb_1/ppermute | solution.py:30
  283.5 3.9 %fusion.107 = (f32[512]{0:T(512)S(1)}, f32[512]{0:T(512)S(1)}, bf16[512,768]{1,0:T(8,128)(2,1)}) fusion(f32[512,768]{1,0:T(8,128)S(1)} %copy-done.1, f32[768]{0:T(1024)S(1)} %copy-done.59, f32[768]{0:T(1024)S(1)} %copy-done.61, pred[512]{0:T(512)(128)(4,1)S(1)} %copy-done.80, f32[768]{0:T(1024)S(1)} %copy-done.63, pred[512]{0:T(512)(128)(4,1)S(1)} %copy-done.82, ...), kind=kLoop, calls=%fused_computation.351 | loop fusion | flops 7470080 | bytes 7112192 | tf_op jit(solution)/shard_map/reduce_sum | solution.py:292
  296.9 2.8 collective-permute-done.59.far_y
  (454 shorter events, 136.4 us)
Async XLA Ops:
  15.3 14.1 %collective-permute-start.2 = (f32[2,2,4,4608]{3,2,1,0:T(4,128)}, f32[2,2,4,4608]{3,2,1,0:T(4,128)}, u32[]{:S(2)}, u32[]{:S(2)}) collective-permute-start(f32[2,2,4,4608]{3,2,1,0:T(4,128)} %dynamic-slice_bitcast_fusion), channel_id=1, source_target_pairs={{0,1},{1,0},{2,3},{3,2},{4,5},{5,4},{6,7},{7,6},{8,9},{9,8},{10,11... | collective-permute-start | bytes 884744 | tf_op jit(solution)/shard_map/to_x_1/ppermute | solution.py:30
  23.9 14.1 %collective-permute-start.7 = (bf16[5,24,768]{2,1,0:T(8,128)(2,1)}, bf16[5,24,768]{2,1,0:T(8,128)(2,1)}, u32[]{:S(2)}, u32[]{:S(2)}) collective-permute-start(bf16[5,24,768]{2,1,0:T(8,128)(2,1)} %get-tuple-element.149), channel_id=1, source_target_pairs={{0,4},{4,0},{1,5},{5,1},{2,6},{6,2},{3,7},{7,3},{8,12},{12,8},{9,1... | collective-permute-start | bytes 552968 | tf_op jit(solution)/shard_map/to_za_1/ppermute | solution.py:30
  39.1 15.6 %collective-permute-start.12 = (bf16[2,5,24,768]{3,2,1,0:T(8,128)(2,1)S(1)}, bf16[2,5,24,768]{3,2,1,0:T(8,128)(2,1)S(1)}, u32[]{:S(2)}, u32[]{:S(2)}) collective-permute-start(bf16[2,5,24,768]{3,2,1,0:T(8,128)(2,1)S(1)} %pad_maximum_fusion.21), channel_id=1, source_target_pairs={{0,2},{2,0},{1,3},{3,1},{4,6},{6,4},{5,7},{7,5},{8,10},{10,8},{9,1... | collective-permute-start | bytes 1105928 | tf_op jit(solution)/shard_map/to_zb_1/ppermute | solution.py:30
  41.6 14.7 %collective-permute-start.21 = (bf16[2,96,768]{2,1,0:T(8,128)(2,1)S(1)}, bf16[2,96,768]{2,1,0:T(8,128)(2,1)S(1)}, u32[]{:S(2)}, u32[]{:S(2)}) collective-permute-start(bf16[2,96,768]{2,1,0:T(8,128)(2,1)S(1)} %copy-done.49), channel_id=1, source_target_pairs={{0,4},{4,0},{1,5},{5,1},{2,6},{6,2},{3,7},{7,3},{8,12},{12,8},{9,1... | collective-permute-start | bytes 884744 | tf_op jit(solution)/shard_map/to_za_1/ppermute | solution.py:30
  44.5 22.8 %collective-permute-start.10 = (bf16[2,2,2,2,3,24,384]{6,5,4,3,2,0,1:T(8,128)(2,1)S(1)}, bf16[2,2,2,2,3,24,384]{6,5,4,3,2,0,1:T(8,128)(2,1)S(1)}, u32[]{:S(2)}, u32[]{:S(2)}) collective-permute-start(bf16[2,2,2,2,3,24,384]{6,5,4,3,2,0,1:T(8,128)(2,1)S(1)} %pad_maximum_fusion.8), channel_id=1, source_target_pairs={{0,8},{8,0},{1,9},{9,1},{2,10},{10,2},{3,11},{11,3},{4,12},{12,4},... | collective-permute-start | bytes 2654216 | tf_op jit(solution)/shard_map/to_core_1/ppermute | solution.py:30
  44.5 22.1 %collective-permute-start.11 = (bf16[2,2,2,2,3,24,384]{6,5,4,3,2,0,1:T(8,128)(2,1)S(1)}, bf16[2,2,2,2,3,24,384]{6,5,4,3,2,0,1:T(8,128)(2,1)S(1)}, u32[]{:S(2)}, u32[]{:S(2)}) collective-permute-start(bf16[2,2,2,2,3,24,384]{6,5,4,3,2,0,1:T(8,128)(2,1)S(1)} %copy.137), channel_id=1, source_target_pairs={{0,8},{8,0},{1,9},{9,1},{2,10},{10,2},{3,11},{11,3},{4,12},{12,4},... | collective-permute-start | bytes 2654216 | tf_op jit(solution)/shard_map/to_core_1/ppermute | solution.py:30
  57.3 20.8 %collective-permute-start.22 = (bf16[2,2,96,768]{3,2,0,1:T(8,128)(2,1)}, bf16[2,2,96,768]{3,2,0,1:T(8,128)(2,1)}, u32[]{:S(2)}, u32[]{:S(2)}) collective-permute-start(bf16[2,2,96,768]{3,2,0,1:T(8,128)(2,1)} %pad_maximum_fusion.16), channel_id=1, source_target_pairs={{0,2},{2,0},{1,3},{3,1},{4,6},{6,4},{5,7},{7,5},{8,10},{10,8},{9,1... | collective-permute-start | bytes 1769480 | tf_op jit(solution)/shard_map/to_zb_1/ppermute | solution.py:30
  64.3 17.8 %collective-permute-start.17 = (bf16[2,2,2,5,24,384]{5,4,3,2,1,0:T(8,128)(2,1)S(1)}, bf16[2,2,2,5,24,384]{5,4,3,2,1,0:T(8,128)(2,1)S(1)}, u32[]{:S(2)}, u32[]{:S(2)}) collective-permute-start(bf16[2,2,2,5,24,384]{5,4,3,2,1,0:T(8,128)(2,1)S(1)} %pad_maximum_fusion.11), channel_id=1, source_target_pairs={{0,1},{1,0},{2,3},{3,2},{4,5},{5,4},{6,7},{7,6},{8,9},{9,8},{10,11... | collective-permute-start | bytes 2211848 | tf_op jit(solution)/shard_map/to_x_1/ppermute | solution.py:30
  65.1 19.5 %collective-permute-start.14 = (bf16[2,2,2,5,24,384]{5,4,3,2,1,0:T(8,128)(2,1)S(1)}, bf16[2,2,2,5,24,384]{5,4,3,2,1,0:T(8,128)(2,1)S(1)}, u32[]{:S(2)}, u32[]{:S(2)}) collective-permute-start(bf16[2,2,2,5,24,384]{5,4,3,2,1,0:T(8,128)(2,1)S(1)} %pad_maximum_fusion.10), channel_id=1, source_target_pairs={{0,16},{16,0},{1,17},{17,1},{2,18},{18,2},{3,19},{19,3},{4,20},{20... | collective-permute-start | bytes 2211848 | tf_op jit(solution)/shard_map/to_y_1/ppermute | solution.py:30
  79.6 13.6 %collective-permute-start.23 = (bf16[2,2,96,768]{3,2,1,0:T(8,128)(2,1)S(1)}, bf16[2,2,96,768]{3,2,1,0:T(8,128)(2,1)S(1)}, u32[]{:S(2)}, u32[]{:S(2)}) collective-permute-start(bf16[2,2,96,768]{3,2,1,0:T(8,128)(2,1)S(1)} %get-tuple-element.335), channel_id=1, source_target_pairs={{0,1},{1,0},{2,3},{3,2},{4,5},{5,4},{6,7},{7,6},{8,9},{9,8},{10,11... | collective-permute-start | bytes 1769480 | tf_op jit(solution)/shard_map/to_x_1/ppermute | solution.py:30
  82.7 18.3 %collective-permute-start.18 = (bf16[2,2,2,2,5,24,384]{6,5,4,3,2,0,1:T(8,128)(2,1)S(1)}, bf16[2,2,2,2,5,24,384]{6,5,4,3,2,0,1:T(8,128)(2,1)S(1)}, u32[]{:S(2)}, u32[]{:S(2)}) collective-permute-start(bf16[2,2,2,2,5,24,384]{6,5,4,3,2,0,1:T(8,128)(2,1)S(1)} %copy.148), channel_id=1, source_target_pairs={{0,8},{8,0},{1,9},{9,1},{2,10},{10,2},{3,11},{11,3},{4,12},{12,4},... | collective-permute-start | bytes 4423688 | tf_op jit(solution)/shard_map/to_core_1/ppermute | solution.py:30
  83.4 37.8 %collective-permute-start.20 = (bf16[512,768]{1,0:T(8,128)(2,1)}, bf16[512,768]{1,0:T(8,128)(2,1)}, u32[]{:S(2)}, u32[]{:S(2)}) collective-permute-start(bf16[512,768]{1,0:T(8,128)(2,1)} %get-tuple-element.376.g_ref), channel_id=1, source_target_pairs={{0,8},{8,0},{1,9},{9,1},{2,10},{10,2},{3,11},{11,3},{4,12},{12,4},... | collective-permute-start | bytes 2359304 | tf_op jit(solution)/shard_map/to_core_1/ppermute | solution.py:30
  83.5 16.1 %collective-permute-start.25 = (bf16[2,2,96,768]{3,2,1,0:T(8,128)(2,1)S(1)}, bf16[2,2,96,768]{3,2,1,0:T(8,128)(2,1)S(1)}, u32[]{:S(2)}, u32[]{:S(2)}) collective-permute-start(bf16[2,2,96,768]{3,2,1,0:T(8,128)(2,1)S(1)} %get-tuple-element.334), channel_id=1, source_target_pairs={{0,16},{16,0},{1,17},{17,1},{2,18},{18,2},{3,19},{19,3},{4,20},{20... | collective-permute-start | bytes 1769480 | tf_op jit(solution)/shard_map/to_y_1/ppermute | solution.py:30
  84.9 17.0 %collective-permute-start.15 = (bf16[2,2,2,2,5,24,384]{6,5,4,3,2,0,1:T(8,128)(2,1)S(1)}, bf16[2,2,2,2,5,24,384]{6,5,4,3,2,0,1:T(8,128)(2,1)S(1)}, u32[]{:S(2)}, u32[]{:S(2)}) collective-permute-start(bf16[2,2,2,2,5,24,384]{6,5,4,3,2,0,1:T(8,128)(2,1)S(1)} %pad_maximum_fusion), channel_id=1, source_target_pairs={{0,8},{8,0},{1,9},{9,1},{2,10},{10,2},{3,11},{11,3},{4,12},{12,4},... | collective-permute-start | bytes 4423688 | tf_op jit(solution)/shard_map/to_core_1/ppermute | solution.py:30
  93.5 31.1 %collective-permute-start.24 = (bf16[2,2,2,96,768]{4,3,2,1,0:T(8,128)(2,1)S(1)}, bf16[2,2,2,96,768]{4,3,2,1,0:T(8,128)(2,1)}, u32[]{:S(2)}, u32[]{:S(2)}) collective-permute-start(bf16[2,2,2,96,768]{4,3,2,1,0:T(8,128)(2,1)S(1)} %pad_maximum_fusion.6.refs_0_), channel_id=1, source_target_pairs={{0,16},{16,0},{1,17},{17,1},{2,18},{18,2},{3,19},{19,3},{4,20},{20... | collective-permute-start | bytes 3538952 | tf_op jit(solution)/shard_map/to_y_1/ppermute | solution.py:30
  100.9 27.4 %collective-permute-start.26 = (bf16[2,2,2,96,768]{4,3,2,1,0:T(8,128)(2,1)}, bf16[2,2,2,96,768]{4,3,2,1,0:T(8,128)(2,1)}, u32[]{:S(2)}, u32[]{:S(2)}) collective-permute-start(bf16[2,2,2,96,768]{4,3,2,1,0:T(8,128)(2,1)} %pad_maximum_fusion.7.refs_2_), channel_id=1, source_target_pairs={{0,1},{1,0},{2,3},{3,2},{4,5},{5,4},{6,7},{7,6},{8,9},{9,8},{10,11... | collective-permute-start | bytes 3538952 | tf_op jit(solution)/shard_map/to_x_1/ppermute | solution.py:30
  151.7 28.9 %collective-permute-start.29 = (bf16[2,2,2,96,768]{4,3,2,1,0:T(8,128)(2,1)}, bf16[2,2,2,96,768]{4,3,2,1,0:T(8,128)(2,1)}, u32[]{:S(2)}, u32[]{:S(2)}) collective-permute-start(bf16[2,2,2,96,768]{4,3,2,1,0:T(8,128)(2,1)} %get-tuple-element.176), channel_id=1, source_target_pairs={{0,1},{1,0},{2,3},{3,2},{4,5},{5,4},{6,7},{7,6},{8,9},{9,8},{10,11... | collective-permute-start | bytes 3538952 | tf_op jit(solution)/shard_map/to_x_1/ppermute | solution.py:30
  152.1 28.5 %collective-permute-start.30 = (bf16[2,2,2,96,768]{4,3,2,1,0:T(8,128)(2,1)}, bf16[2,2,2,96,768]{4,3,2,1,0:T(8,128)(2,1)}, u32[]{:S(2)}, u32[]{:S(2)}) collective-permute-start(bf16[2,2,2,96,768]{4,3,2,1,0:T(8,128)(2,1)} %get-tuple-element.180), channel_id=1, source_target_pairs={{0,16},{16,0},{1,17},{17,1},{2,18},{18,2},{3,19},{19,3},{4,20},{20... | collective-permute-start | bytes 3538952 | tf_op jit(solution)/shard_map/to_y_1/ppermute | solution.py:30
  182.8 38.3 %collective-permute-start.34 = (bf16[1,2,2,96,768]{4,3,2,1,0:T(8,128)(2,1)}, bf16[1,2,2,96,768]{4,3,2,1,0:T(8,128)(2,1)}, u32[]{:S(2)}, u32[]{:S(2)}) collective-permute-start(bf16[1,2,2,96,768]{4,3,2,1,0:T(8,128)(2,1)} %fusion.25), channel_id=1, source_target_pairs={{0,16},{16,0},{1,17},{17,1},{2,18},{18,2},{3,19},{19,3},{4,20},{20... | collective-permute-start | bytes 1769480 | tf_op jit(solution)/shard_map/feed_sums_second_stage/to_y_1/ppermute | solution.py:30
  185.9 35.2 %collective-permute-start.35 = (bf16[1,2,2,96,768]{4,3,2,1,0:T(8,128)(2,1)}, bf16[1,2,2,96,768]{4,3,2,1,0:T(8,128)(2,1)}, u32[]{:S(2)}, u32[]{:S(2)}) collective-permute-start(bf16[1,2,2,96,768]{4,3,2,1,0:T(8,128)(2,1)} %fusion.26), channel_id=1, source_target_pairs={{0,1},{1,0},{2,3},{3,2},{4,5},{5,4},{6,7},{7,6},{8,9},{9,8},{10,11... | collective-permute-start | bytes 1769480 | tf_op jit(solution)/shard_map/feed_sums_second_stage/to_x_1/ppermute | solution.py:30
  189.8 27.4 %collective-permute-start.32 = (bf16[2,2,2,2,48,384]{5,4,0,2,1,3:T(8,128)(2,1)}, bf16[2,2,2,2,48,384]{5,4,0,2,1,3:T(8,128)(2,1)}, u32[]{:S(2)}, u32[]{:S(2)}) collective-permute-start(bf16[2,2,2,2,48,384]{5,4,0,2,1,3:T(8,128)(2,1)} %fusion.27), channel_id=1, source_target_pairs={{0,1},{1,0},{2,3},{3,2},{4,5},{5,4},{6,7},{7,6},{8,9},{9,8},{10,11... | collective-permute-start | bytes 1769480 | tf_op jit(solution)/shard_map/cross_sums_first_stage/to_x_1/ppermute | solution.py:30
  192.6 26.3 %collective-permute-start.33 = (bf16[2,2,2,2,48,384]{5,4,0,2,1,3:T(8,128)(2,1)}, bf16[2,2,2,2,48,384]{5,4,0,2,1,3:T(8,128)(2,1)}, u32[]{:S(2)}, u32[]{:S(2)}) collective-permute-start(bf16[2,2,2,2,48,384]{5,4,0,2,1,3:T(8,128)(2,1)} %fusion.28), channel_id=1, source_target_pairs={{0,16},{16,0},{1,17},{17,1},{2,18},{18,2},{3,19},{19,3},{4,20},{20... | collective-permute-start | bytes 1769480 | tf_op jit(solution)/shard_map/cross_sums_first_stage/to_y_1/ppermute | solution.py:30
  218.8 17.7 %collective-permute-start.38 = (bf16[512,768]{1,0:T(8,128)(2,1)}, bf16[512,768]{1,0:T(8,128)(2,1)}, u32[]{:S(2)}, u32[]{:S(2)}) collective-permute-start(bf16[512,768]{1,0:T(8,128)(2,1)} %get-tuple-element.207), channel_id=1, source_target_pairs={{0,8},{8,0},{1,9},{9,1},{2,10},{10,2},{3,11},{11,3},{4,12},{12,4},... | collective-permute-start | bytes 2359304 | tf_op jit(solution)/shard_map/to_core_1/ppermute | solution.py:30
  225.4 18.6 %collective-permute-start.39 = (bf16[2,1,2,96,768]{4,3,0,2,1:T(8,128)(2,1)}, bf16[2,1,2,96,768]{4,3,0,2,1:T(8,128)(2,1)}, u32[]{:S(2)}, u32[]{:S(2)}) collective-permute-start(bf16[2,1,2,96,768]{4,3,0,2,1:T(8,128)(2,1)} %fusion.36), channel_id=1, source_target_pairs={{0,2},{2,0},{1,3},{3,1},{4,6},{6,4},{5,7},{7,5},{8,10},{10,8},{9,1... | collective-permute-start | bytes 1769480 | tf_op jit(solution)/shard_map/feed_sums_third_stage/to_zb_1/ppermute | solution.py:30
  229.1 17.1 %collective-permute-start.40 = (bf16[2,2,2,2,48,384]{5,4,0,2,1,3:T(8,128)(2,1)}, bf16[2,2,2,2,48,384]{5,4,0,2,1,3:T(8,128)(2,1)}, u32[]{:S(2)}, u32[]{:S(2)}) collective-permute-start(bf16[2,2,2,2,48,384]{5,4,0,2,1,3:T(8,128)(2,1)} %fusion.29), channel_id=1, source_target_pairs={{0,1},{1,0},{2,3},{3,2},{4,5},{5,4},{6,7},{7,6},{8,9},{9,8},{10,11... | collective-permute-start | bytes 1769480 | tf_op jit(solution)/shard_map/self_sums_first_stage/to_x_1/ppermute | solution.py:30
  231.7 19.0 %collective-permute-start.41 = (bf16[2,2,2,2,48,384]{5,4,0,2,1,3:T(8,128)(2,1)}, bf16[2,2,2,2,48,384]{5,4,0,2,1,3:T(8,128)(2,1)}, u32[]{:S(2)}, u32[]{:S(2)}) collective-permute-start(bf16[2,2,2,2,48,384]{5,4,0,2,1,3:T(8,128)(2,1)} %fusion.30), channel_id=1, source_target_pairs={{0,16},{16,0},{1,17},{17,1},{2,18},{18,2},{3,19},{19,3},{4,20},{20... | collective-permute-start | bytes 1769480 | tf_op jit(solution)/shard_map/self_sums_first_stage/to_y_1/ppermute | solution.py:30
  234.6 19.6 %collective-permute-start.42 = (bf16[2,2,2,48,384]{4,3,0,2,1:T(8,128)(2,1)S(1)}, bf16[2,2,2,48,384]{4,3,0,2,1:T(8,128)(2,1)S(1)}, u32[]{:S(2)}, u32[]{:S(2)}) collective-permute-start(bf16[2,2,2,48,384]{4,3,0,2,1:T(8,128)(2,1)S(1)} %fusion.52), channel_id=1, source_target_pairs={{0,16},{16,0},{1,17},{17,1},{2,18},{18,2},{3,19},{19,3},{4,20},{20... | collective-permute-start | bytes 884744 | tf_op jit(solution)/shard_map/cross_sums_second_stage/to_y_1/ppermute | solution.py:30
  236.5 17.6 %collective-permute-start.43 = (bf16[2,2,2,48,384]{4,3,0,2,1:T(8,128)(2,1)S(1)}, bf16[2,2,2,48,384]{4,3,0,2,1:T(8,128)(2,1)S(1)}, u32[]{:S(2)}, u32[]{:S(2)}) collective-permute-start(bf16[2,2,2,48,384]{4,3,0,2,1:T(8,128)(2,1)S(1)} %copy-done.50), channel_id=1, source_target_pairs={{0,1},{1,0},{2,3},{3,2},{4,5},{5,4},{6,7},{7,6},{8,9},{9,8},{10,11... | collective-permute-start | bytes 884744 | tf_op jit(solution)/shard_map/cross_sums_second_stage/to_x_1/ppermute | solution.py:30
  244.0 14.7 %collective-permute-start.44 = (bf16[4,4736]{1,0:T(4,128)(2,1)S(1)}, bf16[4,4736]{1,0:T(4,128)(2,1)S(1)}, u32[]{:S(2)}, u32[]{:S(2)}) collective-permute-start(bf16[4,4736]{1,0:T(4,128)(2,1)S(1)} %shard_map.313), channel_id=1, source_target_pairs={{0,4},{4,0},{1,5},{5,1},{2,6},{6,2},{3,7},{7,3},{8,12},{12,8},{9,1... | collective-permute-start | bytes 113672 | tf_op jit(solution)/shard_map/gather_mod/to_za_1/ppermute | solution.py:30
  246.2 16.0 %collective-permute-start.45 = (bf16[2,1,96,768]{3,2,0,1:T(8,128)(2,1)}, bf16[2,1,96,768]{3,2,0,1:T(8,128)(2,1)}, u32[]{:S(2)}, u32[]{:S(2)}) collective-permute-start(bf16[2,1,96,768]{3,2,0,1:T(8,128)(2,1)} %fusion.50), channel_id=1, source_target_pairs={{0,4},{4,0},{1,5},{5,1},{2,6},{6,2},{3,7},{7,3},{8,12},{12,8},{9,1... | collective-permute-start | bytes 884744 | tf_op jit(solution)/shard_map/feed_sums_fourth_stage/to_za_1/ppermute | solution.py:30
  257.6 13.1 %collective-permute-start.48 = (bf16[2,2,2,48,384]{4,3,1,0,2:T(8,128)(2,1)}, bf16[2,2,2,48,384]{4,3,1,0,2:T(8,128)(2,1)}, u32[]{:S(2)}, u32[]{:S(2)}) collective-permute-start(bf16[2,2,2,48,384]{4,3,1,0,2:T(8,128)(2,1)} %fusion.61), channel_id=1, source_target_pairs={{0,2},{2,0},{1,3},{3,1},{4,6},{6,4},{5,7},{7,5},{8,10},{10,8},{9,1... | collective-permute-start | bytes 884744 | tf_op jit(solution)/shard_map/cross_sums_third_stage/to_zb_1/ppermute | solution.py:30
  258.8 13.1 %collective-permute-start.49 = (bf16[8,4736]{1,0:T(8,128)(2,1)S(1)}, bf16[8,4736]{1,0:T(8,128)(2,1)S(1)}, u32[]{:S(2)}, u32[]{:S(2)}) collective-permute-start(bf16[8,4736]{1,0:T(8,128)(2,1)S(1)} %reshape.853), channel_id=1, source_target_pairs={{0,2},{2,0},{1,3},{3,1},{4,6},{6,4},{5,7},{7,5},{8,10},{10,8},{9,1... | collective-permute-start | bytes 227336 | tf_op jit(solution)/shard_map/gather_mod/to_zb_1/ppermute | solution.py:30
  (121 other events, 745.5 us)

commit v7 on v6

--- a/solution.py
+++ b/solution.py
@@ -551,7 +551,7 @@
         out_shape=[jax.ShapeDtypeStruct((tokens, width), f32)] * 2
         + [jax.ShapeDtypeStruct((tokens, width), bf16)] * 2
         + [jax.ShapeDtypeStruct(grads_shape, bf16)] * count,
-        compiler_params=pltpu.CompilerParams(vmem_limit_bytes=56 << 20),
+        compiler_params=pltpu.CompilerParams(vmem_limit_bytes=50 << 20),
         cost_estimate=pl.CostEstimate(flops=0, transcendentals=0, bytes_accessed=0),
     )(me, third_in, shifted(third_in, "core", 1), grad_mlp, shifted(grad_mlp, "core", 1), *weights)
     if paired:

time: 310 us -> 311 us (level)
    another operation x46, other arithmetic: 11.5 us -> 16.7 us  [gather_axis(): return jnp.stack([at(place) for place in range(count)])]
    unnamed x176 -> x214, local copies, waits for them, and re-layouts: 6.69 us -> 6.19 us
  transfers between devices with their start and end apart: 65 -> 65, of which waited for: 20 -> 23; matrix products, arithmetic and copies ran while one was open for 33% -> 34% of each run, Pallas kernels for 20% -> 20%
where the time goes in v7:
time: 311 us; the launch traced here: 305 us
  Pallas kernels  85.5 us (27%)
  other arithmetic  83.7 us (27%)
  starting transfers between devices  53.9 us (17%)
  waiting for transfers between devices  52.4 us (17%)
  local copies, waits for them, and re-layouts  15.3 us (5%)
  matrix products  11.7 us (4%)
    ppermute x65, starting transfers between devices, shifted(): lax.ppermute(value, axis, [(k, (k + steps) % count) for k in range(count)])  53.9 us
    ppermute x65, waiting for transfers between devices, shifted(): lax.ppermute(value, axis, [(k, (k + steps) % count) for k in range(count)])  52.4 us
    pallas_call x2, Pallas kernels, attend_back(): pl.pallas_call(backward_kernel, grid_spec=pltpu.PrefetchScalarGridSpec(nu...  38.7 us
    pallas_call x1, Pallas kernels, feed(): pl.pallas_call(partial(feed_kernel, paired), grid_spec=pltpu.PrefetchScal...  21.7 us
    convert_element_type x13, other arithmetic, launch(): summed(picked(terms, dim, (me + s) % count)).astype(bf16)  20.5 us
    another operation x46, other arithmetic, gather_axis(): return jnp.stack([at(place) for place in range(count)])  16.7 us
    pallas_call x2, Pallas kernels, attend(): pl.pallas_call(forward_kernel, grid=(rows, pairs), in_specs=blocks + [pl....  11 us
    another operation x9, other arithmetic, third_stage(): return launch([jnp.stack([left, right])], 'zb', 3)  10.2 us
  transfers between devices with their start and end apart: 65, of which 23 were waited for; matrix products, arithmetic and copies ran while one was open for 34% of the time, Pallas kernels for 20%

profile of v7, /device:TPU:0, one launch (start us, length us, event | category | flops | bytes accessed | tf_op | source)
XLA Modules:
  0.0 305.4 jit_solution(9469672976506361978)
XLA Ops:
  2.5 4.1 %collective-permute-start = (bf16[3,24,768]{2,1,0:T(8,128)(2,1)}, bf16[3,24,768]{2,1,0:T(8,128)(2,1)S(1)}, u32[]{:S(2)}, u32[]{:S(2)}) collective-permute-start(bf16[3,24,768]{2,1,0:T(8,128)(2,1)} %get-tuple-element.142), channel_id=1, source_target_pairs={{0,4},{4,0},{1,5},{5,1},{2,6},{6,2},{3,7},{7,3},{8,12},{12,8},{9,1... | collective-permute-start | bytes 331784 | tf_op jit(solution)/shard_map/to_za_1/ppermute | solution.py:30
  16.8 2.1 shard_map.309
  23.9 3.3 %collective-permute-start.7 = (bf16[5,24,768]{2,1,0:T(8,128)(2,1)}, bf16[5,24,768]{2,1,0:T(8,128)(2,1)}, u32[]{:S(2)}, u32[]{:S(2)}) collective-permute-start(bf16[5,24,768]{2,1,0:T(8,128)(2,1)} %get-tuple-element.149), channel_id=1, source_target_pairs={{0,4},{4,0},{1,5},{5,1},{2,6},{6,2},{3,7},{7,3},{8,12},{12,8},{9,1... | collective-permute-start | bytes 552968 | tf_op jit(solution)/shard_map/to_za_1/ppermute | solution.py:30
  39.1 2.5 collective-permute-start.12
  45.0 9.6 %collective-permute-done.12 = bf16[2,5,24,768]{3,2,1,0:T(8,128)(2,1)S(1)} collective-permute-done((bf16[2,5,24,768]{3,2,1,0:T(8,128)(2,1)S(1)}, bf16[2,5,24,768]{3,2,1,0:T(8,128)(2,1)S(1)}, u32[]{:S(2)}, u32[]{:S(2)}) %collective-permute-start.12) | collective-permute-done | bytes 368672 | tf_op jit(solution)/shard_map/to_zb_1/ppermute | solution.py:30
  57.7 4.8 %fusion = (f32[512,768]{1,0:T(8,128)}, bf16[512,768]{1,0:T(8,128)(2,1)S(1)}, bf16[512,768]{1,0:T(8,128)(2,1)S(1)}) fusion(bf16[512,768]{1,0:T(8,128)(2,1)S(1)} %copy-done.24, f32[512]{0:T(512)S(1)} %copy-done.84, f32[512]{0:T(512)S(1)} %copy-done.74, f32[768]{0:T(1024)S(1)} %get-tuple-element.286, f32[768]{0:T(1024)S(1)} %get-tuple-element.287, ...), kind=kLoop, calls=%fused_computation.20 | loop fusion | flops 7471104 | bytes 4761088 | tf_op jit(solution)/shard_map/mul | solution.py:288
  72.8 5.5 %shard_map.307.mix_ref = bf16[512,768]{1,0:T(8,128)(2,1)S(1)} custom-call(bf16[512,768]{1,0:T(8,128)(2,1)S(1)} %convolution_convert_fusion.3.q_ref, bf16[512,768]{1,0:T(8,128)(2,1)S(1)} %convolution_convert_fusion.2.k_ref, bf16[512,768]{1,0:T(8,128)(2,1)S(1)} %convolution_convert_fusion.1.v_ref, f32[1,512,512]{2,1,0:T(8,128)S(1)} %compare_select_fusion.bias_ref), custom_call_target="tpu_custom_call" | custom-call | tf_op jit(solution)/shard_map/pallas_call | solution.py:410
  81.2 2.1 collective-permute-done.17
  87.8 6.5 %collective-permute-done.23 = bf16[2,2,96,768]{3,2,1,0:T(8,128)(2,1)S(1)} collective-permute-done((bf16[2,2,96,768]{3,2,1,0:T(8,128)(2,1)S(1)}, bf16[2,2,96,768]{3,2,1,0:T(8,128)(2,1)S(1)}, u32[]{:S(2)}, u32[]{:S(2)}) %collective-permute-start.23) | collective-permute-done | bytes 589856 | tf_op jit(solution)/shard_map/to_x_1/ppermute | solution.py:30
  96.0 6.0 %collective-permute-done.25 = bf16[2,2,96,768]{3,2,1,0:T(8,128)(2,1)S(1)} collective-permute-done((bf16[2,2,96,768]{3,2,1,0:T(8,128)(2,1)S(1)}, bf16[2,2,96,768]{3,2,1,0:T(8,128)(2,1)S(1)}, u32[]{:S(2)}, u32[]{:S(2)}) %collective-permute-start.25) | collective-permute-done | bytes 589856 | tf_op jit(solution)/shard_map/to_y_1/ppermute | solution.py:30
  106.1 2.2 fusion.111
  113.0 5.5 %shard_map.308.mix_ref = bf16[512,768]{1,0:T(8,128)(2,1)S(1)} custom-call(bf16[512,768]{1,0:T(8,128)(2,1)S(1)} %convolution_convert_fusion.q_ref, bf16[308,768]{1,0:T(8,128)(2,1)S(1)} %convolution_convert_fusion.5.k_ref, bf16[308,768]{1,0:T(8,128)(2,1)S(1)} %convolution_convert_fusion.4.v_ref, f32[1,512,308]{2,1,0:T(8,128)S(1)} %and_select_fusion.bias_ref), custom_call_target="tpu_custom_call" | custom-call | tf_op jit(solution)/shard_map/pallas_call | solution.py:410
  119.8 2.4 add_convert_fusion.1
  122.4 4.5 %collective-permute-done.24.refs_1_ = bf16[2,2,2,96,768]{4,3,2,1,0:T(8,128)(2,1)} collective-permute-done((bf16[2,2,2,96,768]{4,3,2,1,0:T(8,128)(2,1)}, bf16[2,2,2,96,768]{4,3,2,1,0:T(8,128)(2,1)}, u32[]{:S(2)}, u32[]{:S(2)}) %collective-permute-start.24) | collective-permute-done | bytes 1179680 | tf_op jit(solution)/shard_map/to_y_1/ppermute | solution.py:30
  126.9 3.7 %collective-permute-done.26.refs_3_ = bf16[2,2,2,96,768]{4,3,2,1,0:T(8,128)(2,1)} collective-permute-done((bf16[2,2,2,96,768]{4,3,2,1,0:T(8,128)(2,1)}, bf16[2,2,2,96,768]{4,3,2,1,0:T(8,128)(2,1)}, u32[]{:S(2)}, u32[]{:S(2)}) %collective-permute-start.26) | collective-permute-done | bytes 1179680 | tf_op jit(solution)/shard_map/to_x_1/ppermute | solution.py:30
  130.6 21.7 %shard_map.310 = (f32[512,768]{1,0:T(8,128)}, f32[512,768]{1,0:T(8,128)}, bf16[512,768]{1,0:T(8,128)(2,1)S(1)}, bf16[512,768]{1,0:T(8,128)(2,1)S(1)}, bf16[2,2,2...) custom-call(s32[2]{0:T(128)S(1)} %pad_add_fusion.me_ref, ...), custom_call_target="tpu_custom_call" | custom-call | tf_op jit(solution)/shard_map/pallas_call | solution.py:540
  154.7 2.4 fusion.108
  159.1 17.7 %shard_map.311 = (f32[308,768]{1,0:T(8,128)S(1)}, f32[512,768]{1,0:T(8,128)}, bf16[2,768,384]{2,1,0:T(8,128)(2,1)}, bf16[2,768,384]{2,1,0:T(8,128)(2,1)}, bf16[2...) custom-call(s32[1]{0:T(128)} %bitcast.79.core_ref, bf16[512,768]{1,0:T(8,128)(2,1)S(1)} %convolution_convert_fusion.q_ref, ...), custom_call_target="tpu_custom_call" | custom-call | tf_op jit(solution)/shard_map/pallas_call | solution.py:433
  178.3 2.5 fusion.109
  181.4 2.1 fusion.25
  184.0 2.0 fusion.26
  194.5 2.4 multiply_convert_fusion
  197.0 21.0 %shard_map.312 = (f32[512,768]{1,0:T(8,128)}, bf16[2,768,384]{2,1,0:T(8,128)(2,1)}, bf16[2,768,384]{2,1,0:T(8,128)(2,1)}, bf16[2,768,384]{2,1,0:T(8,128)(2,1)}, bf16[2,768,384]{2,1,0:T(8,128)(2,1)}) custom-call(s32[1]{0:T(128)} %bitcast.79.core_ref, bf16[512,768]{1,0:T(8,128)(2,1)S(1)} %copy-done.7, bf16[512,768]{1,0:T(8,128)(2,1)S(1)} %copy-done.9, ...), custom_call_target="tpu_custom_call" | custom-call | tf_op jit(solution)/shard_map/pallas_call | solution.py:433
  220.0 2.1 fusion.51
  228.2 2.1 fusion.29
  230.7 2.2 fusion.30
  240.8 4.5 %shard_map.313 = bf16[4,4736]{1,0:T(4,128)(2,1)S(1)} custom-call(s32[1,512]{1,0:T(1,128)S(1)} %get-tuple-element.301.clip_ref, bf16[4,128]{1,0:T(4,128)(2,1)S(1)} %fusion.101.digits_ref, f32[512,768]{1,0:T(8,128)S(1)} %copy-done.1, f32[512,768]{1,0:T(8,128)S(1)} %copy-done.3, f32[512,768]{1,0:T(8,128)} %get-tuple-element.304.resid, ...), custom_call_target="tpu_custom_call" | custom-call | tf_op jit(solution)/shard_map/pallas_call | solution.py:593
  247.2 2.9 collective-permute-start.45
  274.9 2.5 shard_map.314
  277.3 4.0 %collective-permute-done.54 = bf16[2,2,2,48,384]{4,3,1,0,2:T(8,128)(2,1)S(1)} collective-permute-done((bf16[2,2,2,48,384]{4,3,1,0,2:T(8,128)(2,1)S(1)}, bf16[2,2,2,48,384]{4,3,1,0,2:T(8,128)(2,1)S(1)}, u32[]{:S(2)}, u32[]{:S(2)}) %collective-permute-start.54) | collective-permute-done | bytes 294944 | tf_op jit(solution)/shard_map/self_sums_third_stage/to_zb_1/ppermute | solution.py:30
  284.4 3.9 %fusion.107 = (f32[512]{0:T(512)S(1)}, f32[512]{0:T(512)S(1)}, bf16[512,768]{1,0:T(8,128)(2,1)}) fusion(f32[512,768]{1,0:T(8,128)S(1)} %copy-done.1, f32[768]{0:T(1024)S(1)} %copy-done.68, f32[768]{0:T(1024)S(1)} %copy-done.70, pred[512]{0:T(512)(128)(4,1)S(1)} %copy-done.90, f32[768]{0:T(1024)S(1)} %copy-done.72, pred[512]{0:T(512)(128)(4,1)S(1)} %copy-done.93, ...), kind=kLoop, calls=%fused_computation.351 | loop fusion | flops 7470080 | bytes 7112192 | tf_op jit(solution)/shard_map/reduce_sum | solution.py:292
  297.8 2.8 collective-permute-done.59.far_y
  (492 shorter events, 138.9 us)
Async XLA Ops:
  15.3 14.1 %collective-permute-start.2 = (f32[2,2,4,4608]{3,2,1,0:T(4,128)}, f32[2,2,4,4608]{3,2,1,0:T(4,128)}, u32[]{:S(2)}, u32[]{:S(2)}) collective-permute-start(f32[2,2,4,4608]{3,2,1,0:T(4,128)} %dynamic-slice_bitcast_fusion), channel_id=1, source_target_pairs={{0,1},{1,0},{2,3},{3,2},{4,5},{5,4},{6,7},{7,6},{8,9},{9,8},{10,11... | collective-permute-start | bytes 884744 | tf_op jit(solution)/shard_map/to_x_1/ppermute | solution.py:30
  23.9 14.1 %collective-permute-start.7 = (bf16[5,24,768]{2,1,0:T(8,128)(2,1)}, bf16[5,24,768]{2,1,0:T(8,128)(2,1)}, u32[]{:S(2)}, u32[]{:S(2)}) collective-permute-start(bf16[5,24,768]{2,1,0:T(8,128)(2,1)} %get-tuple-element.149), channel_id=1, source_target_pairs={{0,4},{4,0},{1,5},{5,1},{2,6},{6,2},{3,7},{7,3},{8,12},{12,8},{9,1... | collective-permute-start | bytes 552968 | tf_op jit(solution)/shard_map/to_za_1/ppermute | solution.py:30
  39.1 15.5 %collective-permute-start.12 = (bf16[2,5,24,768]{3,2,1,0:T(8,128)(2,1)S(1)}, bf16[2,5,24,768]{3,2,1,0:T(8,128)(2,1)S(1)}, u32[]{:S(2)}, u32[]{:S(2)}) collective-permute-start(bf16[2,5,24,768]{3,2,1,0:T(8,128)(2,1)S(1)} %pad_maximum_fusion.21), channel_id=1, source_target_pairs={{0,2},{2,0},{1,3},{3,1},{4,6},{6,4},{5,7},{7,5},{8,10},{10,8},{9,1... | collective-permute-start | bytes 1105928 | tf_op jit(solution)/shard_map/to_zb_1/ppermute | solution.py:30
  41.6 14.8 %collective-permute-start.21 = (bf16[2,96,768]{2,1,0:T(8,128)(2,1)S(1)}, bf16[2,96,768]{2,1,0:T(8,128)(2,1)S(1)}, u32[]{:S(2)}, u32[]{:S(2)}) collective-permute-start(bf16[2,96,768]{2,1,0:T(8,128)(2,1)S(1)} %copy-done.58), channel_id=1, source_target_pairs={{0,4},{4,0},{1,5},{5,1},{2,6},{6,2},{3,7},{7,3},{8,12},{12,8},{9,1... | collective-permute-start | bytes 884744 | tf_op jit(solution)/shard_map/to_za_1/ppermute | solution.py:30
  44.4 23.8 %collective-permute-start.10 = (bf16[2,2,2,2,3,24,384]{6,5,4,3,2,0,1:T(8,128)(2,1)S(1)}, bf16[2,2,2,2,3,24,384]{6,5,4,3,2,0,1:T(8,128)(2,1)S(1)}, u32[]{:S(2)}, u32[]{:S(2)}) collective-permute-start(bf16[2,2,2,2,3,24,384]{6,5,4,3,2,0,1:T(8,128)(2,1)S(1)} %pad_maximum_fusion.8), channel_id=1, source_target_pairs={{0,8},{8,0},{1,9},{9,1},{2,10},{10,2},{3,11},{11,3},{4,12},{12,4},... | collective-permute-start | bytes 2654216 | tf_op jit(solution)/shard_map/to_core_1/ppermute | solution.py:30
  44.5 23.1 %collective-permute-start.11 = (bf16[2,2,2,2,3,24,384]{6,5,4,3,2,0,1:T(8,128)(2,1)S(1)}, bf16[2,2,2,2,3,24,384]{6,5,4,3,2,0,1:T(8,128)(2,1)S(1)}, u32[]{:S(2)}, u32[]{:S(2)}) collective-permute-start(bf16[2,2,2,2,3,24,384]{6,5,4,3,2,0,1:T(8,128)(2,1)S(1)} %copy.137), channel_id=1, source_target_pairs={{0,8},{8,0},{1,9},{9,1},{2,10},{10,2},{3,11},{11,3},{4,12},{12,4},... | collective-permute-start | bytes 2654216 | tf_op jit(solution)/shard_map/to_core_1/ppermute | solution.py:30
  57.3 21.0 %collective-permute-start.22 = (bf16[2,2,96,768]{3,2,0,1:T(8,128)(2,1)}, bf16[2,2,96,768]{3,2,0,1:T(8,128)(2,1)}, u32[]{:S(2)}, u32[]{:S(2)}) collective-permute-start(bf16[2,2,96,768]{3,2,0,1:T(8,128)(2,1)} %pad_maximum_fusion.16), channel_id=1, source_target_pairs={{0,2},{2,0},{1,3},{3,1},{4,6},{6,4},{5,7},{7,5},{8,10},{10,8},{9,1... | collective-permute-start | bytes 1769480 | tf_op jit(solution)/shard_map/to_zb_1/ppermute | solution.py:30
  65.2 18.1 %collective-permute-start.17 = (bf16[2,2,2,5,24,384]{5,4,3,2,1,0:T(8,128)(2,1)}, bf16[2,2,2,5,24,384]{5,4,3,2,1,0:T(8,128)(2,1)}, u32[]{:S(2)}, u32[]{:S(2)}) collective-permute-start(bf16[2,2,2,5,24,384]{5,4,3,2,1,0:T(8,128)(2,1)} %pad_maximum_fusion.11), channel_id=1, source_target_pairs={{0,1},{1,0},{2,3},{3,2},{4,5},{5,4},{6,7},{7,6},{8,9},{9,8},{10,11... | collective-permute-start | bytes 2211848 | tf_op jit(solution)/shard_map/to_x_1/ppermute | solution.py:30
  67.0 18.9 %collective-permute-start.14 = (bf16[2,2,2,5,24,384]{5,4,3,2,1,0:T(8,128)(2,1)}, bf16[2,2,2,5,24,384]{5,4,3,2,1,0:T(8,128)(2,1)}, u32[]{:S(2)}, u32[]{:S(2)}) collective-permute-start(bf16[2,2,2,5,24,384]{5,4,3,2,1,0:T(8,128)(2,1)} %pad_maximum_fusion.10), channel_id=1, source_target_pairs={{0,16},{16,0},{1,17},{17,1},{2,18},{18,2},{3,19},{19,3},{4,20},{20... | collective-permute-start | bytes 2211848 | tf_op jit(solution)/shard_map/to_y_1/ppermute | solution.py:30
  79.9 14.4 %collective-permute-start.23 = (bf16[2,2,96,768]{3,2,1,0:T(8,128)(2,1)S(1)}, bf16[2,2,96,768]{3,2,1,0:T(8,128)(2,1)S(1)}, u32[]{:S(2)}, u32[]{:S(2)}) collective-permute-start(bf16[2,2,96,768]{3,2,1,0:T(8,128)(2,1)S(1)} %get-tuple-element.335), channel_id=1, source_target_pairs={{0,1},{1,0},{2,3},{3,2},{4,5},{5,4},{6,7},{7,6},{8,9},{9,8},{10,11... | collective-permute-start | bytes 1769480 | tf_op jit(solution)/shard_map/to_x_1/ppermute | solution.py:30
  85.0 18.3 %collective-permute-start.18 = (bf16[2,2,2,2,5,24,384]{6,5,4,3,2,0,1:T(8,128)(2,1)S(1)}, bf16[2,2,2,2,5,24,384]{6,5,4,3,2,0,1:T(8,128)(2,1)S(1)}, u32[]{:S(2)}, u32[]{:S(2)}) collective-permute-start(bf16[2,2,2,2,5,24,384]{6,5,4,3,2,0,1:T(8,128)(2,1)S(1)} %copy.148), channel_id=1, source_target_pairs={{0,8},{8,0},{1,9},{9,1},{2,10},{10,2},{3,11},{11,3},{4,12},{12,4},... | collective-permute-start | bytes 4423688 | tf_op jit(solution)/shard_map/to_core_1/ppermute | solution.py:30
  85.7 36.7 %collective-permute-start.20 = (bf16[512,768]{1,0:T(8,128)(2,1)S(1)}, bf16[512,768]{1,0:T(8,128)(2,1)}, u32[]{:S(2)}, u32[]{:S(2)}) collective-permute-start(bf16[512,768]{1,0:T(8,128)(2,1)S(1)} %get-tuple-element.376.g_ref), channel_id=1, source_target_pairs={{0,8},{8,0},{1,9},{9,1},{2,10},{10,2},{3,11},{11,3},{4,12},{12,4},... | collective-permute-start | bytes 2359304 | tf_op jit(solution)/shard_map/to_core_1/ppermute | solution.py:30
  85.9 16.1 %collective-permute-start.25 = (bf16[2,2,96,768]{3,2,1,0:T(8,128)(2,1)S(1)}, bf16[2,2,96,768]{3,2,1,0:T(8,128)(2,1)S(1)}, u32[]{:S(2)}, u32[]{:S(2)}) collective-permute-start(bf16[2,2,96,768]{3,2,1,0:T(8,128)(2,1)S(1)} %get-tuple-element.334), channel_id=1, source_target_pairs={{0,16},{16,0},{1,17},{17,1},{2,18},{18,2},{3,19},{19,3},{4,20},{20... | collective-permute-start | bytes 1769480 | tf_op jit(solution)/shard_map/to_y_1/ppermute | solution.py:30
  87.4 16.8 %collective-permute-start.15 = (bf16[2,2,2,2,5,24,384]{6,5,4,3,2,0,1:T(8,128)(2,1)S(1)}, bf16[2,2,2,2,5,24,384]{6,5,4,3,2,0,1:T(8,128)(2,1)S(1)}, u32[]{:S(2)}, u32[]{:S(2)}) collective-permute-start(bf16[2,2,2,2,5,24,384]{6,5,4,3,2,0,1:T(8,128)(2,1)S(1)} %pad_maximum_fusion), channel_id=1, source_target_pairs={{0,8},{8,0},{1,9},{9,1},{2,10},{10,2},{3,11},{11,3},{4,12},{12,4},... | collective-permute-start | bytes 4423688 | tf_op jit(solution)/shard_map/to_core_1/ppermute | solution.py:30
  95.6 31.4 %collective-permute-start.24 = (bf16[2,2,2,96,768]{4,3,2,1,0:T(8,128)(2,1)}, bf16[2,2,2,96,768]{4,3,2,1,0:T(8,128)(2,1)}, u32[]{:S(2)}, u32[]{:S(2)}) collective-permute-start(bf16[2,2,2,96,768]{4,3,2,1,0:T(8,128)(2,1)} %pad_maximum_fusion.6.refs_0_), channel_id=1, source_target_pairs={{0,16},{16,0},{1,17},{17,1},{2,18},{18,2},{3,19},{19,3},{4,20},{20... | collective-permute-start | bytes 3538952 | tf_op jit(solution)/shard_map/to_y_1/ppermute | solution.py:30
  103.2 27.4 %collective-permute-start.26 = (bf16[2,2,2,96,768]{4,3,2,1,0:T(8,128)(2,1)}, bf16[2,2,2,96,768]{4,3,2,1,0:T(8,128)(2,1)}, u32[]{:S(2)}, u32[]{:S(2)}) collective-permute-start(bf16[2,2,2,96,768]{4,3,2,1,0:T(8,128)(2,1)} %pad_maximum_fusion.7.refs_2_), channel_id=1, source_target_pairs={{0,1},{1,0},{2,3},{3,2},{4,5},{5,4},{6,7},{7,6},{8,9},{9,8},{10,11... | collective-permute-start | bytes 3538952 | tf_op jit(solution)/shard_map/to_x_1/ppermute | solution.py:30
  152.6 28.7 %collective-permute-start.29 = (bf16[2,2,2,96,768]{4,3,2,1,0:T(8,128)(2,1)}, bf16[2,2,2,96,768]{4,3,2,1,0:T(8,128)(2,1)}, u32[]{:S(2)}, u32[]{:S(2)}) collective-permute-start(bf16[2,2,2,96,768]{4,3,2,1,0:T(8,128)(2,1)} %get-tuple-element.176), channel_id=1, source_target_pairs={{0,1},{1,0},{2,3},{3,2},{4,5},{5,4},{6,7},{7,6},{8,9},{9,8},{10,11... | collective-permute-start | bytes 3538952 | tf_op jit(solution)/shard_map/to_x_1/ppermute | solution.py:30
  152.9 28.5 %collective-permute-start.30 = (bf16[2,2,2,96,768]{4,3,2,1,0:T(8,128)(2,1)}, bf16[2,2,2,96,768]{4,3,2,1,0:T(8,128)(2,1)}, u32[]{:S(2)}, u32[]{:S(2)}) collective-permute-start(bf16[2,2,2,96,768]{4,3,2,1,0:T(8,128)(2,1)} %get-tuple-element.180), channel_id=1, source_target_pairs={{0,16},{16,0},{1,17},{17,1},{2,18},{18,2},{3,19},{19,3},{4,20},{20... | collective-permute-start | bytes 3538952 | tf_op jit(solution)/shard_map/to_y_1/ppermute | solution.py:30
  183.5 38.5 %collective-permute-start.34 = (bf16[1,2,2,96,768]{4,3,2,1,0:T(8,128)(2,1)}, bf16[1,2,2,96,768]{4,3,2,1,0:T(8,128)(2,1)}, u32[]{:S(2)}, u32[]{:S(2)}) collective-permute-start(bf16[1,2,2,96,768]{4,3,2,1,0:T(8,128)(2,1)} %fusion.25), channel_id=1, source_target_pairs={{0,16},{16,0},{1,17},{17,1},{2,18},{18,2},{3,19},{19,3},{4,20},{20... | collective-permute-start | bytes 1769480 | tf_op jit(solution)/shard_map/feed_sums_second_stage/to_y_1/ppermute | solution.py:30
  186.0 36.0 %collective-permute-start.35 = (bf16[1,2,2,96,768]{4,3,2,1,0:T(8,128)(2,1)}, bf16[1,2,2,96,768]{4,3,2,1,0:T(8,128)(2,1)}, u32[]{:S(2)}, u32[]{:S(2)}) collective-permute-start(bf16[1,2,2,96,768]{4,3,2,1,0:T(8,128)(2,1)} %fusion.26), channel_id=1, source_target_pairs={{0,1},{1,0},{2,3},{3,2},{4,5},{5,4},{6,7},{7,6},{8,9},{9,8},{10,11... | collective-permute-start | bytes 1769480 | tf_op jit(solution)/shard_map/feed_sums_second_stage/to_x_1/ppermute | solution.py:30
  190.0 28.0 %collective-permute-start.32 = (bf16[2,2,2,2,48,384]{5,4,0,2,1,3:T(8,128)(2,1)}, bf16[2,2,2,2,48,384]{5,4,0,2,1,3:T(8,128)(2,1)}, u32[]{:S(2)}, u32[]{:S(2)}) collective-permute-start(bf16[2,2,2,2,48,384]{5,4,0,2,1,3:T(8,128)(2,1)} %fusion.27), channel_id=1, source_target_pairs={{0,1},{1,0},{2,3},{3,2},{4,5},{5,4},{6,7},{7,6},{8,9},{9,8},{10,11... | collective-permute-start | bytes 1769480 | tf_op jit(solution)/shard_map/cross_sums_first_stage/to_x_1/ppermute | solution.py:30
  192.8 27.0 %collective-permute-start.33 = (bf16[2,2,2,2,48,384]{5,4,0,2,1,3:T(8,128)(2,1)}, bf16[2,2,2,2,48,384]{5,4,0,2,1,3:T(8,128)(2,1)}, u32[]{:S(2)}, u32[]{:S(2)}) collective-permute-start(bf16[2,2,2,2,48,384]{5,4,0,2,1,3:T(8,128)(2,1)} %fusion.28), channel_id=1, source_target_pairs={{0,16},{16,0},{1,17},{17,1},{2,18},{18,2},{3,19},{19,3},{4,20},{20... | collective-permute-start | bytes 1769480 | tf_op jit(solution)/shard_map/cross_sums_first_stage/to_y_1/ppermute | solution.py:30
  219.8 17.9 %collective-permute-start.38 = (bf16[512,768]{1,0:T(8,128)(2,1)}, bf16[512,768]{1,0:T(8,128)(2,1)}, u32[]{:S(2)}, u32[]{:S(2)}) collective-permute-start(bf16[512,768]{1,0:T(8,128)(2,1)} %copy-done.17), channel_id=1, source_target_pairs={{0,8},{8,0},{1,9},{9,1},{2,10},{10,2},{3,11},{11,3},{4,12},{12,4},... | collective-permute-start | bytes 2359304 | tf_op jit(solution)/shard_map/to_core_1/ppermute | solution.py:30
  226.4 18.9 %collective-permute-start.39 = (bf16[2,1,2,96,768]{4,3,0,2,1:T(8,128)(2,1)}, bf16[2,1,2,96,768]{4,3,0,2,1:T(8,128)(2,1)}, u32[]{:S(2)}, u32[]{:S(2)}) collective-permute-start(bf16[2,1,2,96,768]{4,3,0,2,1:T(8,128)(2,1)} %fusion.36), channel_id=1, source_target_pairs={{0,2},{2,0},{1,3},{3,1},{4,6},{6,4},{5,7},{7,5},{8,10},{10,8},{9,1... | collective-permute-start | bytes 1769480 | tf_op jit(solution)/shard_map/feed_sums_third_stage/to_zb_1/ppermute | solution.py:30
  230.3 16.8 %collective-permute-start.40 = (bf16[2,2,2,2,48,384]{5,4,0,2,1,3:T(8,128)(2,1)}, bf16[2,2,2,2,48,384]{5,4,0,2,1,3:T(8,128)(2,1)}, u32[]{:S(2)}, u32[]{:S(2)}) collective-permute-start(bf16[2,2,2,2,48,384]{5,4,0,2,1,3:T(8,128)(2,1)} %fusion.29), channel_id=1, source_target_pairs={{0,1},{1,0},{2,3},{3,2},{4,5},{5,4},{6,7},{7,6},{8,9},{9,8},{10,11... | collective-permute-start | bytes 1769480 | tf_op jit(solution)/shard_map/self_sums_first_stage/to_x_1/ppermute | solution.py:30
  232.9 19.1 %collective-permute-start.41 = (bf16[2,2,2,2,48,384]{5,4,0,2,1,3:T(8,128)(2,1)}, bf16[2,2,2,2,48,384]{5,4,0,2,1,3:T(8,128)(2,1)}, u32[]{:S(2)}, u32[]{:S(2)}) collective-permute-start(bf16[2,2,2,2,48,384]{5,4,0,2,1,3:T(8,128)(2,1)} %fusion.30), channel_id=1, source_target_pairs={{0,16},{16,0},{1,17},{17,1},{2,18},{18,2},{3,19},{19,3},{4,20},{20... | collective-permute-start | bytes 1769480 | tf_op jit(solution)/shard_map/self_sums_first_stage/to_y_1/ppermute | solution.py:30
  235.8 19.7 %collective-permute-start.42 = (bf16[2,2,2,48,384]{4,3,0,2,1:T(8,128)(2,1)S(1)}, bf16[2,2,2,48,384]{4,3,0,2,1:T(8,128)(2,1)S(1)}, u32[]{:S(2)}, u32[]{:S(2)}) collective-permute-start(bf16[2,2,2,48,384]{4,3,0,2,1:T(8,128)(2,1)S(1)} %fusion.52), channel_id=1, source_target_pairs={{0,16},{16,0},{1,17},{17,1},{2,18},{18,2},{3,19},{19,3},{4,20},{20... | collective-permute-start | bytes 884744 | tf_op jit(solution)/shard_map/cross_sums_second_stage/to_y_1/ppermute | solution.py:30
  237.7 17.8 %collective-permute-start.43 = (bf16[2,2,2,48,384]{4,3,0,2,1:T(8,128)(2,1)S(1)}, bf16[2,2,2,48,384]{4,3,0,2,1:T(8,128)(2,1)S(1)}, u32[]{:S(2)}, u32[]{:S(2)}) collective-permute-start(bf16[2,2,2,48,384]{4,3,0,2,1:T(8,128)(2,1)S(1)} %copy-done.59), channel_id=1, source_target_pairs={{0,1},{1,0},{2,3},{3,2},{4,5},{5,4},{6,7},{7,6},{8,9},{9,8},{10,11... | collective-permute-start | bytes 884744 | tf_op jit(solution)/shard_map/cross_sums_second_stage/to_x_1/ppermute | solution.py:30
  245.3 14.4 %collective-permute-start.44 = (bf16[4,4736]{1,0:T(4,128)(2,1)S(1)}, bf16[4,4736]{1,0:T(4,128)(2,1)S(1)}, u32[]{:S(2)}, u32[]{:S(2)}) collective-permute-start(bf16[4,4736]{1,0:T(4,128)(2,1)S(1)} %shard_map.313), channel_id=1, source_target_pairs={{0,4},{4,0},{1,5},{5,1},{2,6},{6,2},{3,7},{7,3},{8,12},{12,8},{9,1... | collective-permute-start | bytes 113672 | tf_op jit(solution)/shard_map/gather_mod/to_za_1/ppermute | solution.py:30
  247.2 15.9 %collective-permute-start.45 = (bf16[2,1,96,768]{3,2,0,1:T(8,128)(2,1)}, bf16[2,1,96,768]{3,2,0,1:T(8,128)(2,1)}, u32[]{:S(2)}, u32[]{:S(2)}) collective-permute-start(bf16[2,1,96,768]{3,2,0,1:T(8,128)(2,1)} %fusion.50), channel_id=1, source_target_pairs={{0,4},{4,0},{1,5},{5,1},{2,6},{6,2},{3,7},{7,3},{8,12},{12,8},{9,1... | collective-permute-start | bytes 884744 | tf_op jit(solution)/shard_map/feed_sums_fourth_stage/to_za_1/ppermute | solution.py:30
  258.9 12.8 %collective-permute-start.48 = (bf16[2,2,2,48,384]{4,3,1,0,2:T(8,128)(2,1)}, bf16[2,2,2,48,384]{4,3,1,0,2:T(8,128)(2,1)}, u32[]{:S(2)}, u32[]{:S(2)}) collective-permute-start(bf16[2,2,2,48,384]{4,3,1,0,2:T(8,128)(2,1)} %fusion.61), channel_id=1, source_target_pairs={{0,2},{2,0},{1,3},{3,1},{4,6},{6,4},{5,7},{7,5},{8,10},{10,8},{9,1... | collective-permute-start | bytes 884744 | tf_op jit(solution)/shard_map/cross_sums_third_stage/to_zb_1/ppermute | solution.py:30
  259.9 13.4 %collective-permute-start.49 = (bf16[8,4736]{1,0:T(8,128)(2,1)S(1)}, bf16[8,4736]{1,0:T(8,128)(2,1)S(1)}, u32[]{:S(2)}, u32[]{:S(2)}) collective-permute-start(bf16[8,4736]{1,0:T(8,128)(2,1)S(1)} %reshape.853), channel_id=1, source_target_pairs={{0,2},{2,0},{1,3},{3,1},{4,6},{6,4},{5,7},{7,5},{8,10},{10,8},{9,1... | collective-permute-start | bytes 227336 | tf_op jit(solution)/shard_map/gather_mod/to_zb_1/ppermute | solution.py:30
  (140 other events, 1022.5 us)
